TPU v7x, 128 devices: a whole 4x4x4 slice. The times are simulated.
128 devices in a mesh: dy: 16 (over y, x), dx: 8 (over z, core).
Axes of the slice: x: 4, y: 4, z: 4, core: 2. Of those that a mesh axis runs over, the one named last changes fastest.
Arguments:
- heights: float32 [8192, 4096], P('dy', 'dx'), may hold values from -4 to 4
- albedo: float32 [8192, 4096], P('dy', 'dx'), may hold values from 0.5 to 1.5
- observed: bfloat16 [2048, 384, 384], P(('dy', 'dx')), may hold values from -2 to 2
- resample: bfloat16 [2048, 2, 384, 384], P(('dy', 'dx')), may hold values from -1 to 1
- exposure: float32 [8, 16], P('dx'), may hold values from -0.5 to 0.5
- sun_azimuth: float32 [8, 16], P('dx'), may hold values from -3.140625 to 3.140625
- sun_elevation: float32 [8, 16], P('dx'), may hold values from 0.02 to 0.3
- send_plan: int32 [16, 8, 4, 32], P('dy', 'dx'), may hold values from 0 to 128, as said below
- recv_plan: int32 [16, 8, 16], P('dy', 'dx'), may hold values from 0 to 31, as said below
Outputs:
- height_gradient: float32 [8192, 4096], P('dy', 'dx')
- camera_gradient: float32 [8, 16, 7], P('dx', 'dy')
Inputs may be any that keep to these rules, and one draw needn't show every extreme that they name: send_plan[s, c, :, r * 2 + j] describes slot j of the crops that the DEM tile (s, c) serves to the device (r, c): row offset and column offset of the crop's window in the tile (multiples of 128, at most 128 and 128), the image m, and 1; unused slots are all zeros. Every device is served exactly 2 crops by at least one tile. recv_plan[r, c, m] = s * 2 + j names the used slot send_plan[s, c, :, r * 2 + j] whose image is m; the values of one device are distinct.
All inputs are finite; a program needn't handle non-finite values.
Results may differ from a plain program's by a relative error of at most 0.005.
Values may be sent and summed in bfloat16 or wider, within the bound.
No kernel may reach another device: no remote copies, remote signals or barrier semaphores. Data moves between devices by JAX's collectives and lax.ppermute only.
A program may use at most 384 MiB of HBM per device.

v0:
```python
import jax
import jax.numpy as jnp
from jax import lax
from jax.sharding import PartitionSpec as P

BLK = 128


SMOOTHING_WEIGHT = 0.02
HIGHEST = lax.Precision.HIGHEST


def padded_2(block, sides, width):
    for axis, dim in sides:
        count = lax.axis_size(axis)
        forward = [(i, i + 1) for i in range(count - 1)]
        backward = [(target, source) for source, target in forward]
        low = lax.ppermute(
            lax.slice_in_dim(block, block.shape[dim] - width, None, axis=dim), axis, forward
        )
        high = lax.ppermute(lax.slice_in_dim(block, 0, width, axis=dim), axis, backward)
        block = jnp.concatenate([low, block, high], axis=dim)
    return block


def split_up(shard, dim, peers):
    lengths = shard.shape
    blocks = shard.reshape(*lengths[:dim], peers, lengths[dim] // peers, *lengths[dim + 1 :])
    return jnp.moveaxis(blocks, dim, 0)


def summed_on_arrival(shard, axis, dim):
    blocks = split_up(shard, dim, lax.axis_size(axis))
    arrived = lax.all_to_all(blocks, axis, split_axis=0, concat_axis=0, tiled=True)
    return arrived.sum(axis=0)


def extended(shard, sides, width):
    edges = {}
    for axis, dim in sides:
        peers, length = (lax.axis_size(axis), shard.shape[dim])
        up = [(i, (i + 1) % peers) for i in range(peers - 1)]
        last = lax.slice_in_dim(shard, length - width, length, axis=dim)
        leading = lax.slice_in_dim(shard, 0, width, axis=dim)
        edges[dim] = (
            lax.ppermute(last, axis, up),
            lax.ppermute(leading, axis, [(b, a) for a, b in up]),
        )
    done = []
    for _, dim in sides:
        low, high = edges[dim]
        around = [(width, width) if d in done else (0, 0) for d in range(shard.ndim)]
        shard = jnp.concatenate([jnp.pad(low, around), shard, jnp.pad(high, around)], axis=dim)
        done.append(dim)
    return shard


def slopes(padded):
    slope_x = (padded[1:-1, 2:] - padded[1:-1, :-2]) * 0.5
    slope_y = (padded[2:, 1:-1] - padded[:-2, 1:-1]) * 0.5
    return (slope_x, slope_y)


def laplace(padded):
    return (
        padded[:-2, 1:-1]
        + padded[2:, 1:-1]
        + padded[1:-1, :-2]
        + padded[1:-1, 2:]
        - 4.0 * padded[1:-1, 1:-1]
    )


def shading(slope_x, slope_y, albedo):
    length = jnp.sqrt(1.0 + slope_x * slope_x + slope_y * slope_y)
    normal = jnp.stack([-slope_x, -slope_y, jnp.ones_like(slope_x)])
    return albedo[None] * normal / length[None]


def sun_vectors(solar_azimuth, elevation):
    return jnp.stack(
        [
            jnp.cos(elevation) * jnp.cos(solar_azimuth),
            jnp.cos(elevation) * jnp.sin(solar_azimuth),
            jnp.sin(elevation),
        ]
    )


def edge_diff(values):
    step_diff = values[..., 1:] - values[..., :-1]
    return jnp.concatenate(
        [step_diff[..., :1], 0.5 * (step_diff[..., 1:] + step_diff[..., :-1]), step_diff[..., -1:]],
        axis=-1,
    )


def crop_terms(predicted, residual):
    crop_size = predicted.shape[-1]
    coordinate = (jnp.arange(crop_size, dtype=jnp.float32) - 0.5 * (crop_size - 1)) / crop_size
    deriv_u = edge_diff(predicted)
    deriv_v = jnp.swapaxes(edge_diff(jnp.swapaxes(predicted, -1, -2)), -1, -2)
    resid_u = residual * deriv_u
    resid_v = residual * deriv_v
    col_coord = coordinate[None, None, :]
    row_coord = coordinate[None, :, None]
    sum_list = [
        jnp.sum(resid_u, axis=(1, 2)),
        jnp.sum(resid_u * col_coord, axis=(1, 2)),
        jnp.sum(resid_u * row_coord, axis=(1, 2)),
        jnp.sum(resid_v, axis=(1, 2)),
        jnp.sum(resid_v * col_coord, axis=(1, 2)),
        jnp.sum(resid_v * row_coord, axis=(1, 2)),
    ]
    pose_part = jnp.stack(sum_list, axis=-1) / crop_size
    exposure_part = jnp.sum(residual * predicted, axis=(1, 2)) / (crop_size * crop_size)
    return jnp.concatenate([pose_part, exposure_part[:, None]], axis=-1)


def render(shaded, observed, resample, exposure_gain):
    first_pass = jnp.einsum(
        "nij,njk->nik", resample[:, 0], shaded, preferred_element_type=jnp.float32
    ).astype(jnp.bfloat16)
    predicted = exposure_gain[:, None, None] * jnp.einsum(
        "nil,nkl->nik", first_pass, resample[:, 1], preferred_element_type=jnp.float32
    )
    residual = predicted - observed.astype(jnp.float32)
    crop_sums = crop_terms(predicted, residual)
    weighted = (exposure_gain[:, None, None] * residual).astype(jnp.bfloat16)
    back_pass = jnp.einsum(
        "nji,njk->nik", resample[:, 0], weighted, preferred_element_type=jnp.float32
    ).astype(jnp.bfloat16)
    crop_grad = jnp.einsum(
        "njk,nkl->njl", back_pass, resample[:, 1], preferred_element_type=jnp.float32
    ).astype(jnp.bfloat16)
    return (crop_sums, crop_grad)


def to_blocks(fields):
    channels, rows_all, cols_all = fields.shape
    shaped = fields.reshape(channels, rows_all // BLK, BLK, cols_all // BLK, BLK)
    return shaped.transpose(0, 1, 3, 2, 4).reshape(channels, -1, BLK * BLK)


def from_blocks(blocks, rows_all, cols_all):
    channels = blocks.shape[0]
    shaped = blocks.reshape(channels, rows_all // BLK, cols_all // BLK, BLK, BLK)
    return shaped.transpose(0, 1, 3, 2, 4).reshape(channels, rows_all, cols_all)


def crops_to_blocks(crops):
    item_count, crop_size = (crops.shape[0], crops.shape[-1])
    per_side = crop_size // BLK
    shaped = crops.reshape(item_count, per_side, BLK, per_side, BLK)
    return shaped.transpose(0, 1, 3, 2, 4).reshape(item_count * per_side * per_side, BLK * BLK)


def blocks_to_crops(blocks, item_count, crop_size):
    per_side = crop_size // BLK
    shaped = blocks.reshape(item_count, per_side, per_side, BLK, BLK)
    return shaped.transpose(0, 1, 3, 2, 4).reshape(item_count, crop_size, crop_size)


def block_index(row_off, col_off, crop_size, tile_cols):
    per_side = crop_size // BLK
    blocks_across = tile_cols // BLK
    inner_steps = jnp.arange(per_side, dtype=jnp.int32)
    target_block = (
        (row_off[:, None, None] // BLK + inner_steps[None, :, None]) * blocks_across
        + col_off[:, None, None] // BLK
        + inner_steps[None, None, :]
    ).reshape(-1)
    return target_block


def per_device(
    heights, albedo, observed, resample, exposure, sun_azimuth, sun_elevation, send_plan, recv_plan
):
    tile_rows, tile_cols = heights.shape
    crop_size = observed.shape[-1]
    slot_plan = send_plan[0, 0]
    row_off, col_off, slot_image, slot_used = (
        slot_plan[0],
        slot_plan[1],
        slot_plan[2],
        slot_plan[3],
    )
    slot_count = row_off.shape[0]
    receive = recv_plan[0, 0]
    sun_table = sun_vectors(sun_azimuth[0], sun_elevation[0])
    exposure_gain = jnp.exp(exposure[0])
    image_pick = (
        (slot_image[:, None] == jnp.arange(sun_table.shape[1], dtype=jnp.int32)[None, :])
        & (slot_used[:, None] == 1)
    ).astype(jnp.float32)
    slot_sun = jnp.dot(sun_table, image_pick.T, precision=HIGHEST)
    wide_rim = padded_2(heights, (("dy", 0), ("dx", 1)), 2)
    slope_x, slope_y = slopes(wide_rim[1:-1, 1:-1])
    lap_field = laplace(wide_rim)
    row_ids = jnp.arange(tile_rows + 2)
    col_ids = jnp.arange(tile_cols + 2)
    row_keep = ~(
        (row_ids == 0) & (lax.axis_index("dy") == 0)
        | (row_ids == tile_rows + 1) & (lax.axis_index("dy") == lax.axis_size("dy") - 1)
    )
    col_keep = ~(
        (col_ids == 0) & (lax.axis_index("dx") == 0)
        | (col_ids == tile_cols + 1) & (lax.axis_index("dx") == lax.axis_size("dx") - 1)
    )
    keep_mask = row_keep[:, None] & col_keep[None, :]
    smoothness_term = laplace(jnp.where(keep_mask, lap_field, 0.0))
    fields = shading(slope_x, slope_y, albedo)
    field_blocks = to_blocks(fields)
    total_blocks = field_blocks.shape[1]
    block_ids = block_index(row_off, col_off, crop_size, tile_cols)
    per_crop = crop_size // BLK * (crop_size // BLK)
    block_sun = jnp.repeat(slot_sun, per_crop, axis=1)
    shaded_blocks = block_sun[0][:, None] * jnp.take(field_blocks[0], block_ids, axis=0)
    for component in range(1, 3):
        shaded_blocks = shaded_blocks + block_sun[component][:, None] * jnp.take(
            field_blocks[component], block_ids, axis=0
        )
    shaded = blocks_to_crops(shaded_blocks, slot_count, crop_size).astype(jnp.bfloat16)
    arrived = lax.all_to_all(shaded, "dy", split_axis=0, concat_axis=0, tiled=True)
    own_crops = jnp.take(arrived, receive, axis=0)
    crop_sums, crop_grad = render(own_crops, observed, resample, exposure_gain)
    outgoing = (
        jnp.zeros((slot_count, crop_size, crop_size), jnp.bfloat16).at[receive].set(crop_grad)
    )
    slot_grads = lax.all_to_all(outgoing, "dy", split_axis=0, concat_axis=0, tiled=True)
    camera_model = summed_on_arrival(crop_sums, "dy", 0)
    grad_blocks = crops_to_blocks(slot_grads.astype(jnp.float32))
    grad_parts = []
    for component in range(3):
        empty_blocks = jnp.zeros((total_blocks, grad_blocks.shape[1]), jnp.float32)
        grad_parts.append(
            empty_blocks.at[block_ids].add(block_sun[component][:, None] * grad_blocks)
        )
    field_grads = from_blocks(jnp.stack(grad_parts), tile_rows, tile_cols)

    def shade_local(slope_a, slope_b):
        return shading(slope_a, slope_b, albedo)

    _, pull_back = jax.vjp(shade_local, slope_x, slope_y)
    grad_x, grad_y = pull_back(field_grads)
    grad_rims = extended(
        jnp.stack([grad_x, grad_y]).astype(jnp.bfloat16), (("dy", 1), ("dx", 2)), 1
    ).astype(jnp.float32)
    data_term_gradient = (grad_rims[0, 1:-1, :-2] - grad_rims[0, 1:-1, 2:]) * 0.5 + (
        grad_rims[1, :-2, 1:-1] - grad_rims[1, 2:, 1:-1]
    ) * 0.5
    height_gradient = data_term_gradient + SMOOTHING_WEIGHT * smoothness_term
    return (height_gradient, camera_model[None])


def solution(mesh):
    placed = (
        P("dy", "dx"),
        P("dy", "dx"),
        P(("dy", "dx"), None, None),
        P(("dy", "dx"), None, None, None),
        P("dx", None),
        P("dx", None),
        P("dx", None),
        P("dy", "dx", None, None),
        P("dy", "dx", None),
    )
    return jax.shard_map(
        per_device,
        mesh=mesh,
        in_specs=placed,
        out_specs=(P("dy", "dx"), P("dx", "dy", None)),
        check_vma=False,
    )
```

profile of v0, /device:TPU:7, one launch (start us, length us, event | category | flops | bytes accessed | tf_op | source)
XLA Modules:
  0.0 723.6 jit_solution(5084659198977324627)
XLA Ops:
  1.5 3.1 collective-permute-start
  13.3 3.6 collective-permute-start.2
  17.0 3.4 collective-permute-start.3
  26.2 2.8 multiply_divide_fusion
  30.5 2.5 stack.66
  34.4 2.9 stack.67
  42.5 11.7 %gather_fusion.1 = f32[288,16384]{1,0:T(8,128)} fusion(f32[16,16384]{1,0:T(8,128)S(1)} %bitcast.149, s32[1024]{0:T(1024)S(1)} %pad_clamp_fusion.1), kind=kCustom, calls=%fused_computation.clone | custom fusion | bytes 37749888 | tf_op jit(solution)/shard_map/jit(_take)/gather | solution.py:218
  54.2 11.6 %gather_fusion.2 = f32[288,16384]{1,0:T(8,128)} fusion(f32[16,16384]{1,0:T(8,128)S(1)} %bitcast.150, s32[1024]{0:T(1024)S(1)} %pad_clamp_fusion.1), kind=kCustom, calls=%fused_computation.1.clone | custom fusion | bytes 37749888 | tf_op jit(solution)/shard_map/jit(_take)/gather | solution.py:220
  66.5 11.8 %gather_fusion.3 = f32[288,16384]{1,0:T(8,128)} fusion(f32[16,16384]{1,0:T(8,128)S(1)} %bitcast.151, s32[1024]{0:T(1024)S(1)} %pad_clamp_fusion.1), kind=kCustom, calls=%fused_computation.2.clone | custom fusion | bytes 37749888 | tf_op jit(solution)/shard_map/jit(_take)/gather | solution.py:220
  78.3 22.3 %fusion.3 = bf16[36,8,128,128]{3,1,2,0:T(8,128)(2,1)} fusion(f32[288,16384]{1,0:T(8,128)} %gather_fusion.3, f32[288,16384]{1,0:T(8,128)} %gather_fusion.2, f32[288,16384]{1,0:T(8,128)} %gather_fusion.1, f32[288]{0:T(512)S(1)} %copy-done.32, f32[288]{0:T(512)S(1)} %copy-done.30, f32[288]{0:T(512)S(1)} %copy-done.28, pred[288]{0:T(512)(128)(4,1)S(1)} %copy-done.36), kind=kLoop, calls=%fused_computation.18 | loop fusion | flops 42467328 | bytes 66064032
  100.7 10.2 %copy.75 = bf16[36,8,128,128]{3,2,1,0:T(8,128)(2,1)} copy(bf16[36,8,128,128]{3,1,2,0:T(8,128)(2,1)} %fusion.3) | data formatting | bytes 18874368
  110.8 13.9 %copy.93 = bf16[32,3,3,128,128]{4,2,3,1,0:T(4,128)(2,1)} copy(bf16[32,3,3,128,128]{4,3,2,1,0:T(8,128)(2,1)} %bitcast.156) | data formatting | bytes 18874368 | tf_op jit(solution)/shard_map/convert_element_type | solution.py:223
  124.7 24.5 %convert_element_type.41 = bf16[32,384,384]{2,1,0:T(8,128)(2,1)} reshape(bf16[32,3,128,3,128]{4,3,2,1,0:T(4,128)(2,1)} %bitcast.155) | data formatting | bytes 18874368 | tf_op jit(solution)/shard_map/convert_element_type | solution.py:223
  149.2 7.1 all-to-all-start
  156.4 138.8 %all-to-all-done = bf16[32,384,384]{2,1,0:T(8,128)(2,1)} async-done(((bf16[32,384,384]{2,1,0:T(8,128)(2,1)}), bf16[32,384,384]{2,1,0:T(8,128)(2,1)}, u32[]{:S(2)}, u32[]{:S(2)}) %all-to-all-start) | async-done | bytes 9437216 | tf_op jit(solution)/shard_map/all_to_all | solution.py:224
  295.2 7.1 gather_fusion
  302.3 12.6 %broadcast_multiply_fusion = f32[16,384,384]{2,1,0:T(8,128)} fusion(f32[16]{0:T(128)S(1)} %exponential_bitcast_fusion, bf16[16,2,384,384]{3,2,1,0:T(8,128)(2,1)} %param.14, bf16[16,384,384]{2,1,0:T(8,128)(2,1)} %gather_fusion, pred[16]{0:T(512)(128)(4,1)S(1)} %compare_and_fusion.1), kind=kOutput, calls=%fused_computation.47 | convolution fusion | flops 3630956544 | bytes 23593040 | tf_op jit(solution)/shard_map/nil,nkl->nik/dot_general | solution.py:124
  314.9 12.5 %fusion.32 = bf16[16,384,384]{2,1,0:T(8,128)(2,1)} fusion(bf16[16,2,384,384]{3,2,1,0:T(8,128)(2,1)} %param.14, f32[16,384,384]{2,1,0:T(8,128)} %broadcast_multiply_fusion, bf16[16,384,384]{2,1,0:T(8,128)(2,1)} %param.13, f32[16]{0:T(128)S(1)} %exponential_bitcast_fusion), kind=kOutput, calls=%fused_computation.58 | convolution fusion | flops 3638034432 | bytes 28311616 | tf_op jit(solution)/shard_map/njk,nkl->njl/dot_general | solution.py:133
  327.4 4.9 broadcast_in_dim.62
  332.3 11.5 %scatter_fusion = bf16[32,384,384]{2,1,0:T(8,128)(2,1)} fusion(bf16[32,384,384]{2,1,0:T(8,128)(2,1)} %broadcast_in_dim.62, s32[16]{0:T(128)S(1)} %fusion.100, bf16[16,384,384]{2,1,0:T(8,128)(2,1)} %fusion.32), kind=kCustom, calls=%fused_computation.4 | custom fusion | bytes 14155840 | tf_op jit(solution)/shard_map/scatter | solution.py:228
  343.9 9.6 %all-to-all-start.1 = ((bf16[32,384,384]{2,1,0:T(8,128)(2,1)}), bf16[32,384,384]{2,1,0:T(8,128)(2,1)}, u32[]{:S(2)}, u32[]{:S(2)}) async-start(bf16[32,384,384]{2,1,0:T(8,128)(2,1)} %scatter_fusion), calls=%async_computation.1 | async-start | bytes 18874368 | tf_op jit(solution)/shard_map/all_to_all | solution.py:230
  356.7 9.6 %copy.63 = f32[16,384,384]{1,2,0:T(8,128)} copy(f32[16,384,384]{2,1,0:T(8,128)} %broadcast_multiply_fusion) | data formatting | bytes 18874368 | tf_op jit(solution)/shard_map/mul | solution.py:124
  366.3 12.7 %slice_subtract_fusion = f32[16,384,383]{2,1,0:T(8,128)} fusion(f32[16,384,384]{2,1,0:T(8,128)} %bitcast.153), kind=kLoop, calls=%fused_computation.21 | loop fusion | flops 2353152 | bytes 28237824 | tf_op jit(solution)/shard_map/sub | solution.py:91
  379.0 6.5 fusion.106
  385.5 12.7 %fusion.4 = f32[16,384,382]{2,1,0:T(8,128)} fusion(f32[16,384,383]{2,1,0:T(8,128)} %slice_subtract_fusion), kind=kLoop, calls=%fused_computation.20 | loop fusion | flops 4694016 | bytes 28164096 | tf_op jit(solution)/shard_map/mul | solution.py:93
  398.2 12.5 %maximum_bitcast_fusion = f32[16,384,384]{1,2,0:T(8,128)} fusion(f32[16,384,1]{2,1,0:T(8,128)} %get-tuple-element.23, f32[16,384,382]{2,1,0:T(8,128)} %fusion.4, f32[16,384,1]{2,1,0:T(8,128)} %get-tuple-element.22), kind=kLoop, calls=%fused_computation.26 | loop fusion | flops 4718592 | bytes 18874368 | tf_op jit(solution)/shard_map/transpose | solution.py:102
  410.6 9.8 %copy.64 = f32[16,384,384]{2,1,0:T(8,128)} copy(f32[16,384,384]{1,2,0:T(8,128)} %maximum_bitcast_fusion) | data formatting | bytes 18874368 | tf_op jit(solution)/shard_map/transpose | solution.py:102
  420.4 12.6 %slice_subtract_fusion.1 = f32[16,384,383]{2,1,0:T(8,128)} fusion(f32[16,384,384]{2,1,0:T(8,128)} %broadcast_multiply_fusion), kind=kLoop, calls=%fused_computation.24 | loop fusion | flops 2353152 | bytes 28237824 | tf_op jit(solution)/shard_map/sub | solution.py:91
  433.1 6.6 fusion.105
  439.6 12.9 %fusion.5 = f32[16,384,382]{2,1,0:T(8,128)} fusion(f32[16,384,383]{2,1,0:T(8,128)} %slice_subtract_fusion.1), kind=kLoop, calls=%fused_computation.23 | loop fusion | flops 4694016 | bytes 28164096 | tf_op jit(solution)/shard_map/mul | solution.py:93
  452.5 18.3 %maximum_multiply_fusion = (f32[16,384,384]{2,1,0:T(8,128)S(1)}, f32[16,384,384]{2,1,0:T(8,128)}, f32[16]{0:T(128)S(1)}) fusion(f32[16,384,1]{2,1,0:T(8,128)} %get-tuple-element.21, f32[16,384,382]{2,1,0:T(8,128)} %fusion.5, f32[16,384,1]{2,1,0:T(8,128)} %get-tuple-element.20, f32[16,384,384]{2,1,0:T(8,128)} %broadcast_multiply_fusion, ...), kind=kLoop, calls=%fused_computation.25 | loop fusion | flops 18874352 | bytes 51904576 | tf_op jit(solution)/shard_map/mul | solution.py:103
  470.8 6.7 multiply_reduce_fusion.1
  478.2 13.1 %all-to-all-done.1 = bf16[32,384,384]{2,1,0:T(8,128)(2,1)} async-done(((bf16[32,384,384]{2,1,0:T(8,128)(2,1)}), bf16[32,384,384]{2,1,0:T(8,128)(2,1)}, u32[]{:S(2)}, u32[]{:S(2)}) %all-to-all-start.1) | async-done | bytes 9437216 | tf_op jit(solution)/shard_map/all_to_all | solution.py:230
  491.4 6.8 all-to-all-start.2
  498.2 26.3 %reshape.395 = f32[32,3,128,3,128]{4,3,2,1,0:T(4,128)} reshape(bf16[32,384,384]{2,1,0:T(8,128)(2,1)} %all-to-all-done.1) | data formatting | bytes 28311552 | tf_op jit(solution)/shard_map/reshape | solution.py:155
  524.6 10.1 %copy.59 = f32[32,3,3,128,128]{4,3,2,1,0:T(8,128)S(1)} copy(f32[32,3,3,128,128]{4,2,3,1,0:T(4,128)} %bitcast.152) | data formatting | bytes 37748736 | tf_op jit(solution)/shard_map/reshape | solution.py:155
  534.7 27.0 %bitcast_multiply_fusion.2 = (f32[288,16384]{1,0:T(8,128)}, f32[288,16384]{1,0:T(8,128)}, f32[288,16384]{1,0:T(8,128)}) fusion(f32[36,8,128,128]{3,2,1,0:T(8,128)S(1)} %bitcast.154, f32[288]{0:T(512)S(1)} %copy-done.29, f32[288]{0:T(512)S(1)} %copy-done.33, f32[288]{0:T(512)S(1)} %copy-done.31), kind=kLoop, calls=%fused_computation.10 | loop fusion | flops 14155776 | bytes 75500928 | tf_op jit(solution)/shard_map/mul | solution.py:237
  561.6 28.1 %scatter_custom_fusion.1 = f32[16,16384]{1,0:T(8,128)} fusion(s32[288]{0:T(512)S(1)} %fusion.99, f32[288,16384]{1,0:T(8,128)} %get-tuple-element.14, f32[]{:T(128)} %constant.35.clone.1), kind=kCustom, calls=%fused_computation.120 | custom fusion | flops 4718592 | bytes 1049088 | tf_op jit(solution)/shard_map/scatter-add | solution.py:237
  592.1 42.8 %scatter_custom_fusion.2 = f32[16,16384]{1,0:T(8,128)} fusion(s32[288]{0:T(512)S(1)} %fusion.99, f32[288,16384]{1,0:T(8,128)} %get-tuple-element.16, f32[]{:T(128)} %constant.35.clone.1), kind=kCustom, calls=%fused_computation.118 | custom fusion | flops 4718592 | bytes 1049088 | tf_op jit(solution)/shard_map/scatter-add | solution.py:237
  637.3 42.7 %scatter_custom_fusion.3 = f32[16,16384]{1,0:T(8,128)} fusion(s32[288]{0:T(512)S(1)} %fusion.99, f32[288,16384]{1,0:T(8,128)} %get-tuple-element.15, f32[]{:T(128)} %constant.35.clone.1), kind=kCustom, calls=%fused_computation.116 | custom fusion | flops 4718592 | bytes 1049088 | tf_op jit(solution)/shard_map/scatter-add | solution.py:237
  686.9 3.7 copy.60
  690.6 5.0 reshape.389
  695.6 3.3 divide_multiply_fusion
  701.7 3.1 collective-permute-start.5
  707.0 3.1 collective-permute-start.4
  710.1 2.9 collective-permute-start.7
  714.9 3.2 collective-permute-done.7
  720.2 3.0 fusion.60
  (151 shorter events, 48.3 us)
Async XLA Ops:
  0.6 24.0 %copy-start = (f32[512,512]{1,0:T(8,128)S(1)}, f32[512,512]{1,0:T(8,128)}, u32[]{:S(2)}) copy-start(f32[512,512]{1,0:T(8,128)} %param.11) | copy-start | bytes 3145732
  1.5 10.0 %collective-permute-start = (f32[2,512]{1,0:T(2,128)S(1)}, f32[2,512]{1,0:T(2,128)S(1)}, u32[]{:S(2)}, u32[]{:S(2)}) collective-permute-start(f32[2,512]{1,0:T(2,128)S(1)} %get-tuple-element.39), channel_id=1, source_target_pairs={{0,8},{8,16},{16,24},{24,32},{32,40},{40,48},{48,56},{56,64},{64,7... | collective-permute-start | bytes 12296 | tf_op jit(solution)/shard_map/ppermute | solution.py:18
  4.6 6.8 collective-permute-start.1
  9.1 11.3 %copy-start.22 = (s32[32,3,3]{2,1,0:T(4,128)}, s32[32,3,3]{2,1,0:T(4,128)S(1)}, u32[]{:S(2)}) copy-start(s32[32,3,3]{2,1,0:T(4,128)S(1)} %iota_add_fusion) | copy-start | bytes 3460
  11.4 14.8 %copy-start.24 = (f32[2,512]{1,0:T(2,128)}, f32[2,512]{1,0:T(2,128)S(1)}, u32[]{:S(2)}) copy-start(f32[2,512]{1,0:T(2,128)S(1)} %collective-permute-done) | copy-start | bytes 12292
  11.4 14.8 %copy-start.26 = (f32[2,512]{1,0:T(2,128)}, f32[2,512]{1,0:T(2,128)S(1)}, u32[]{:S(2)}) copy-start(f32[2,512]{1,0:T(2,128)S(1)} %collective-permute-done.1) | copy-start | bytes 12292
  13.3 11.3 %collective-permute-start.2 = (f32[516,2]{1,0:T(8,128)}, f32[516,2]{1,0:T(8,128)S(1)}, u32[]{:S(2)}, u32[]{:S(2)}) collective-permute-start(f32[516,2]{1,0:T(8,128)} %get-tuple-element.34), channel_id=1, source_target_pairs={{1,0},{2,1},{3,2},{4,3},{5,4},{6,5},{7,6},{9,8},{10,9},{11,10},{12... | collective-permute-start | bytes 12392 | tf_op jit(solution)/shard_map/ppermute | solution.py:21
  17.0 7.7 %collective-permute-start.3 = (f32[516,2]{1,0:T(8,128)}, f32[516,2]{1,0:T(8,128)}, u32[]{:S(2)}, u32[]{:S(2)}) collective-permute-start(f32[516,2]{1,0:T(8,128)} %get-tuple-element.33), channel_id=1, source_target_pairs={{0,1},{1,2},{2,3},{3,4},{4,5},{5,6},{6,7},{8,9},{9,10},{10,11},{11... | collective-permute-start | bytes 12392 | tf_op jit(solution)/shard_map/ppermute | solution.py:18
  22.1 16.5 %copy-start.10 = (f32[4,128,4,128]{3,1,2,0:T(8,128)}, f32[4,128,4,128]{3,1,2,0:T(8,128)S(1)}, u32[]{:S(2)}) copy-start(f32[4,128,4,128]{3,1,2,0:T(8,128)S(1)} %copy.48) | copy-start | bytes 3145732
  24.6 14.0 %copy-start.34 = (f32[3]{0:T(128)}, f32[3]{0:T(128)S(1)}, u32[]{:S(2)}) copy-start(f32[3]{0:T(128)S(1)} %pad.35.clone) | copy-start | bytes 40
  24.6 4.3 copy-start.20
  26.2 2.8 copy-start.2
  26.2 2.8 copy-start.4
  29.0 8.3 %copy-start.6 = (f32[512,512]{1,0:T(8,128)}, f32[512,512]{1,0:T(8,128)S(1)}, u32[]{:S(2)}) copy-start(f32[512,512]{1,0:T(8,128)S(1)} %get-tuple-element.13) | copy-start | bytes 3145732
  34.4 6.6 copy-start.12
  66.4 11.9 %copy-start.28 = (f32[288]{0:T(512)S(1)}, f32[288]{0:T(512)}, u32[]{:S(2)}) copy-start(f32[288]{0:T(512)} %broadcast_in_dim.61) | copy-start | bytes 3460
  66.4 11.9 %copy-start.30 = (f32[288]{0:T(512)S(1)}, f32[288]{0:T(512)}, u32[]{:S(2)}) copy-start(f32[288]{0:T(512)} %broadcast_in_dim.65) | copy-start | bytes 3460
  66.4 11.9 %copy-start.32 = (f32[288]{0:T(512)S(1)}, f32[288]{0:T(512)}, u32[]{:S(2)}) copy-start(f32[288]{0:T(512)} %broadcast_in_dim.67) | copy-start | bytes 3460
  66.5 11.9 %copy-start.36 = (pred[288]{0:T(512)(128)(4,1)S(1)}, pred[288]{0:T(512)(128)(4,1)}, u32[]{:S(2)}) copy-start(pred[288]{0:T(512)(128)(4,1)} %compare_and_fusion) | copy-start | bytes 868
  149.2 7.1 copy-start.37
  149.2 7.2 copy-start.38
  149.2 146.0 %all-to-all-start = ((bf16[32,384,384]{2,1,0:T(8,128)(2,1)}), bf16[32,384,384]{2,1,0:T(8,128)(2,1)}, u32[]{:S(2)}, u32[]{:S(2)}) async-start(bf16[32,384,384]{2,1,0:T(8,128)(2,1)} %convert_element_type.41), calls=%async_computation | async-start | bytes 18874368 | tf_op jit(solution)/shard_map/all_to_all | solution.py:224
  343.9 9.6 %copy-start.23 = (s32[32,3,3]{2,1,0:T(4,128)S(1)}, s32[32,3,3]{2,1,0:T(4,128)}, u32[]{:S(2)}) copy-start(s32[32,3,3]{2,1,0:T(4,128)} %copy-done.22) | copy-start | bytes 3460
  343.9 9.9 %copy-start.19 = (f32[512,512]{1,0:T(8,128)S(1)}, f32[512,512]{1,0:T(8,128)}, u32[]{:S(2)}) copy-start(f32[512,512]{1,0:T(8,128)} %get-tuple-element.12) | copy-start | bytes 3145732
  343.9 11.4 %copy-start.21 = (f32[516,2]{1,0:T(8,128)S(1)}, f32[516,2]{1,0:T(8,128)}, u32[]{:S(2)}) copy-start(f32[516,2]{1,0:T(8,128)} %copy-done.20) | copy-start | bytes 12388
  343.9 11.4 %copy-start.25 = (f32[2,512]{1,0:T(2,128)S(1)}, f32[2,512]{1,0:T(2,128)}, u32[]{:S(2)}) copy-start(f32[2,512]{1,0:T(2,128)} %copy-done.24) | copy-start | bytes 12292
  343.9 11.4 %copy-start.27 = (f32[2,512]{1,0:T(2,128)S(1)}, f32[2,512]{1,0:T(2,128)}, u32[]{:S(2)}) copy-start(f32[2,512]{1,0:T(2,128)} %copy-done.26) | copy-start | bytes 12292
  343.9 147.5 %all-to-all-start.1 = ((bf16[32,384,384]{2,1,0:T(8,128)(2,1)}), bf16[32,384,384]{2,1,0:T(8,128)(2,1)}, u32[]{:S(2)}, u32[]{:S(2)}) async-start(bf16[32,384,384]{2,1,0:T(8,128)(2,1)} %scatter_fusion), calls=%async_computation.1 | async-start | bytes 18874368 | tf_op jit(solution)/shard_map/all_to_all | solution.py:230
  491.4 223.0 %all-to-all-start.2 = ((f32[16,1,7]{2,1,0:T(1,128)}), f32[16,1,7]{2,1,0:T(1,128)S(1)}, u32[]{:S(2)}, u32[]{:S(2)}) async-start(f32[16,1,7]{2,1,0:T(1,128)} %copy.65), calls=%async_computation.2 | async-start | bytes 16384 | tf_op jit(solution)/shard_map/all_to_all | solution.py:34
  524.6 10.1 %copy-start.29 = (f32[288]{0:T(512)S(1)}, f32[288]{0:T(512)}, u32[]{:S(2)}) copy-start(f32[288]{0:T(512)} %broadcast_in_dim.61) | copy-start | bytes 3460
  524.6 10.1 %copy-start.31 = (f32[288]{0:T(512)S(1)}, f32[288]{0:T(512)}, u32[]{:S(2)}) copy-start(f32[288]{0:T(512)} %broadcast_in_dim.65) | copy-start | bytes 3460
  524.6 10.1 %copy-start.33 = (f32[288]{0:T(512)S(1)}, f32[288]{0:T(512)}, u32[]{:S(2)}) copy-start(f32[288]{0:T(512)} %broadcast_in_dim.67) | copy-start | bytes 3460
  637.3 46.8 %copy-start.35 = (f32[3]{0:T(128)S(1)}, f32[3]{0:T(128)}, u32[]{:S(2)}) copy-start(f32[3]{0:T(128)} %copy-done.34) | copy-start | bytes 40
  680.1 4.1 copy-start.8
  680.1 4.1 copy-start.9
  680.1 4.1 copy-start.11
  680.1 4.1 copy-start.13
  680.1 4.1 copy-start.15
  680.1 4.1 copy-start.17
  695.6 3.4 copy-start.3
  695.6 3.4 copy-start.5
  695.6 3.6 copy-start.7
  695.6 3.9 copy-start.18
  700.7 12.4 %copy-start.16 = (bf16[1,512,512]{2,1,0:T(8,128)(2,1)}, bf16[1,512,512]{2,1,0:T(8,128)(2,1)S(1)}, u32[]{:S(2)}) copy-start(bf16[1,512,512]{2,1,0:T(8,128)(2,1)S(1)} %get-tuple-element.25) | copy-start | bytes 1572868
  701.7 13.2 %collective-permute-start.5 = (bf16[2,1,512]{2,1,0:T(2,128)(2,1)S(1)}, bf16[2,1,512]{2,1,0:T(2,128)(2,1)S(1)}, u32[]{:S(2)}, u32[]{:S(2)}) collective-permute-start(bf16[2,1,512]{2,1,0:T(2,128)(2,1)S(1)} %get-tuple-element.35), channel_id=1, source_target_pairs={{0,8},{8,16},{16,24},{24,32},{32,40},{40,48},{48,56},{56,64},{64,7... | collective-permute-start | bytes 6152 | tf_op jit(solution)/shard_map/ppermute | solution.py:46
  704.8 10.1 %collective-permute-start.6 = (bf16[2,1,512]{2,1,0:T(2,128)(2,1)S(1)}, bf16[2,1,512]{2,1,0:T(2,128)(2,1)S(1)}, u32[]{:S(2)}, u32[]{:S(2)}) collective-permute-start(bf16[2,1,512]{2,1,0:T(2,128)(2,1)S(1)} %get-tuple-element.36), channel_id=1, source_target_pairs={{8,0},{16,8},{24,16},{32,24},{40,32},{48,40},{56,48},{64,56},{72,6... | collective-permute-start | bytes 6152 | tf_op jit(solution)/shard_map/ppermute | solution.py:47
  707.0 7.9 %collective-permute-start.4 = (bf16[2,512,1]{2,1,0:T(8,128)(2,1)}, bf16[2,512,1]{2,1,0:T(8,128)(2,1)S(1)}, u32[]{:S(2)}, u32[]{:S(2)}) collective-permute-start(bf16[2,512,1]{2,1,0:T(8,128)(2,1)} %get-tuple-element.37), channel_id=1, source_target_pairs={{0,1},{1,2},{2,3},{3,4},{4,5},{5,6},{6,7},{8,9},{9,10},{10,11},{11... | collective-permute-start | bytes 6152 | tf_op jit(solution)/shard_map/ppermute | solution.py:46
  710.1 8.0 %collective-permute-start.7 = (bf16[2,512,1]{2,1,0:T(8,128)(2,1)}, bf16[2,512,1]{2,1,0:T(8,128)(2,1)}, u32[]{:S(2)}, u32[]{:S(2)}) collective-permute-start(bf16[2,512,1]{2,1,0:T(8,128)(2,1)} %get-tuple-element.38), channel_id=1, source_target_pairs={{1,0},{2,1},{3,2},{4,3},{5,4},{6,5},{7,6},{9,8},{10,9},{11,10},{12... | collective-permute-start | bytes 6152 | tf_op jit(solution)/shard_map/ppermute | solution.py:47
  (2 other events, 4.4 us)
where the time goes:
time: 734 us; the launch traced here: 724 us
  other arithmetic  280 us (38%)
  local copies, waits for them, and re-layouts  214 us (29%)
  waiting for transfers between devices  155 us (21%)
  starting transfers between devices  47.1 us (6%)
  matrix products  25.2 us (3%)
    all_to_all x1, waiting for transfers between devices, per_device(): lax.all_to_all(shaded, 'dy', split_axis=0, concat_axis=0, tiled=True)  139 us
    scatter-add x3, other arithmetic, per_device(): empty_blocks.at[block_ids].add(block_sun[component][:, None] * grad_blocks)  114 us
    convert_element_type x2, local copies, waits for them, and re-layouts, per_device(): blocks_to_crops(shaded_blocks, slot_count, crop_size).astype(jnp.bfloat16)  38.4 us
    reshape x2, local copies, waits for them, and re-layouts, crops_to_blocks(): shaped.transpose(0, 1, 3, 2, 4)  36.4 us
    mul x1, other arithmetic, per_device(): block_sun[component][:, None] * grad_blocks  27 us
    mul x2, other arithmetic, edge_diff(): 0.5 * (step_diff[..., 1:] + step_diff[..., :-1])  25.6 us
    sub x2, other arithmetic, edge_diff(): step_diff = values[..., 1:] - values[..., :-1]  25.3 us
    gather x2, local copies, waits for them, and re-layouts, per_device(): jnp.take(field_blocks[component], block_ids, axis=0)  23.4 us
  transfers between devices with their start and end apart: 11, of which 3 were waited for; matrix products, arithmetic and copies ran while one was open for 47% of the time, Pallas kernels for 0%

commit v1 on v0

v1 whole, which is shorter than its diff:
```python
import jax
import jax.numpy as jnp
from jax import lax
from jax.experimental import pallas as pl
from jax.experimental.pallas import tpu as pltpu
from jax.sharding import PartitionSpec as P

SMOOTHING_WEIGHT = 0.02
H_SCALE = 8191.0
A_SCALE = 65534.0
T = 512
C = 384
EXTRA = 8
SPILL = 16
CH = 32
F32 = jnp.float32
BF16 = jnp.bfloat16
I32 = jnp.int32


def pack(high, low):
    return lax.shift_left(high, 16) | (low & 0xFFFF)


def high_of(word):
    return lax.shift_right_arithmetic(word, 16).astype(F32)


def low_of(word):
    return lax.shift_right_arithmetic(lax.shift_left(word, 16), 16).astype(F32)


def tile_kernel(
    used, image, row_off, col_off, sun, gain,
    tile_ref, res_ref, obs_ref,
    out_ref, sums_ref,
    hbuf, halo, sx_ref, sy_ref, w_ref, r2_ref, gx_ref, gy_ref,
    shaded, pbuf, weighted, grad,
):
    step = pl.program_id(0)
    first = (step // 2) * 2
    slot_odd = step % 2
    mine = used[step] == 1
    any_used = used[first] + used[first + 1] > 0

    @pl.when(step == 0)
    def _():
        sums_ref[...] = jnp.zeros_like(sums_ref)

    @pl.when((slot_odd == 0) & any_used)
    def _():
        words = tile_ref[0, T : T + EXTRA]
        halo[0:8] = high_of(words)
        halo[8:16] = low_of(words)
        hbuf[7:8] = halo[1:2]
        hbuf[T + 8 : T + 9] = halo[2:3]

        def unpack(k, _):
            base = pl.multiple_of(k * CH, CH)
            hbuf[pl.ds(base + 8, CH)] = high_of(tile_ref[0, pl.ds(base, CH)])
            gx_ref[pl.ds(base, CH)] = jnp.zeros((CH, T), F32)
            gy_ref[pl.ds(base + 8, CH)] = jnp.zeros((CH, T), F32)
            return 0

        lax.fori_loop(0, T // CH, unpack, 0)
        gy_ref[0:8] = jnp.zeros((8, T), F32)
        gy_ref[T + 8 : T + 16] = jnp.zeros((8, T), F32)

        def slope(k, _):
            base = pl.multiple_of(k * CH, CH)
            block = pl.multiple_of((k * CH // 128) * 128, 128)
            rows = hbuf[pl.ds(base, CH + 16)]
            h = rows[8 : 8 + CH]
            lane = lax.broadcasted_iota(I32, (CH, T), 1)
            pick = (
                lax.broadcasted_iota(I32, (CH, 128), 0) + (base - block)
                == lax.broadcasted_iota(I32, (CH, 128), 1)
            )
            left_col = jnp.sum(
                jnp.where(pick, halo[0:1, pl.ds(block, 128)], 0.0), axis=1, keepdims=True
            )
            right_col = jnp.sum(
                jnp.where(pick, halo[8:9, pl.ds(block, 128)], 0.0), axis=1, keepdims=True
            )
            left = jnp.where(lane == 0, left_col, pltpu.roll(h, 1, 1))
            right = jnp.where(lane == T - 1, right_col, pltpu.roll(h, T - 1, 1))
            sx = (right - left) * (0.5 / H_SCALE)
            sy = (rows[9 : 9 + CH] - rows[7 : 7 + CH]) * (0.5 / H_SCALE)
            albedo = low_of(tile_ref[0, pl.ds(base, CH)]) * (1.0 / A_SCALE) + 1.0
            r = lax.rsqrt(1.0 + sx * sx + sy * sy)
            sx_ref[pl.ds(base, CH)] = sx
            sy_ref[pl.ds(base, CH)] = sy
            w_ref[pl.ds(base, CH)] = albedo * r
            r2_ref[pl.ds(base, CH)] = r * r
            return 0

        lax.fori_loop(0, T // CH, slope, 0)

    @pl.when(mine)
    def _():
        m = image[step]
        oy = pl.multiple_of(row_off[step], 128)
        ox = pl.multiple_of(col_off[step], 128)
        s1 = sun[m]
        s2 = sun[16 + m]
        s3 = sun[32 + m]
        e = gain[m]
        cols = pl.ds(ox, C)

        def shade(k, _):
            base = pl.multiple_of(k * CH, CH)
            rows = pl.ds(pl.multiple_of(oy + base, CH), CH)
            q = s3 - s1 * sx_ref[rows, cols] - s2 * sy_ref[rows, cols]
            shaded[pl.ds(base, CH)] = (w_ref[rows, cols] * q).astype(BF16)
            return 0

        lax.fori_loop(0, C // CH, shade, 0)
        row_mat = res_ref[0, 0]
        col_mat = res_ref[0, 1]
        first_pass = jnp.dot(row_mat, shaded[...], preferred_element_type=F32).astype(BF16)
        pbuf[8 : 8 + C] = e * lax.dot_general(
            first_pass, col_mat, (((1,), (1,)), ((), ())), preferred_element_type=F32
        )
        pbuf[7:8] = 2.0 * pbuf[8:9] - pbuf[9:10]
        pbuf[C + 8 : C + 9] = 2.0 * pbuf[C + 7 : C + 8] - pbuf[C + 6 : C + 7]

        def fold(v):
            return v.reshape(CH // 8, 8, C)

        def terms(k, carry):
            a_x, a_xg, a_y, a_yg, a_e = carry
            base = pl.multiple_of(k * CH, CH)
            rows = pbuf[pl.ds(base, CH + 16)]
            p = rows[8 : 8 + CH]
            lane = lax.broadcasted_iota(I32, (CH, C), 1)
            residual = p - obs_ref[0, pl.ds(base, CH)].astype(F32)
            left = jnp.where(lane == 0, p, pltpu.roll(p, 1, 1))
            right = jnp.where(lane == C - 1, p, pltpu.roll(p, C - 1, 1))
            xs = fold(residual * (right - left))
            ys = fold(residual * (rows[9 : 9 + CH] - rows[7 : 7 + CH]))
            es = fold(residual * p)
            weighted[pl.ds(base, CH)] = (e * residual).astype(BF16)
            for g in range(CH // 8):
                at = (base + 8 * g).astype(F32)
                a_x = a_x + xs[g]
                a_xg = a_xg + xs[g] * at
                a_y = a_y + ys[g]
                a_yg = a_yg + ys[g] * at
                a_e = a_e + es[g]
            return a_x, a_xg, a_y, a_yg, a_e

        zero = jnp.zeros((8, C), F32)
        parts = lax.fori_loop(0, C // CH, terms, (zero,) * 5)
        for n in range(5):
            sums_ref[m, n] = parts[n]
        back_pass = lax.dot_general(
            row_mat, weighted[...], (((0,), (0,)), ((), ())), preferred_element_type=F32
        ).astype(BF16)
        grad[...] = jnp.dot(back_pass, col_mat, preferred_element_type=F32).astype(BF16)

        def pull(k, _):
            base = pl.multiple_of(k * CH, CH)
            rows = pl.ds(pl.multiple_of(oy + base, CH), CH)
            rows_y = pl.ds(pl.multiple_of(oy + base + 8, 8), CH)
            sx = sx_ref[rows, cols]
            sy = sy_ref[rows, cols]
            t = (s3 - s1 * sx - s2 * sy) * r2_ref[rows, cols]
            wg = w_ref[rows, cols] * grad[pl.ds(base, CH)].astype(F32)
            gx_ref[rows, cols] = gx_ref[rows, cols] - wg * (s1 + t * sx)
            gy_ref[rows_y, cols] = gy_ref[rows_y, cols] - wg * (s2 + t * sy)
            return 0

        lax.fori_loop(0, C // CH, pull, 0)

    @pl.when((slot_odd == 1) & any_used)
    def _():
        def stencil(k, _):
            base = pl.multiple_of(k * CH, CH)
            lane = lax.broadcasted_iota(I32, (CH, T), 1)
            gx = gx_ref[pl.ds(base, CH)]
            rows = gy_ref[pl.ds(base, CH + 16)]
            left = jnp.where(lane == 0, 0.0, pltpu.roll(gx, 1, 1))
            right = jnp.where(lane == T - 1, 0.0, pltpu.roll(gx, T - 1, 1))
            total = (left - right) + (rows[7 : 7 + CH] - rows[9 : 9 + CH])
            out_ref[0, pl.ds(base, CH)] = (0.5 * total).astype(BF16)
            return 0

        lax.fori_loop(0, T // CH, stencil, 0)
        eye = lax.broadcasted_iota(I32, (128, 128), 0) == lax.broadcasted_iota(
            I32, (128, 128), 1
        )
        low = []
        high = []
        for b in range(T // 128):
            first_col = gx_ref[128 * b : 128 * (b + 1), 0:128][:, 0:1]
            last_col = gx_ref[128 * b : 128 * (b + 1), T - 128 : T][:, 127:128]
            low.append(jnp.sum(jnp.where(eye, first_col, 0.0), axis=0, keepdims=True))
            high.append(jnp.sum(jnp.where(eye, last_col, 0.0), axis=0, keepdims=True))
        spill = jnp.concatenate(
            [
                -0.5 * gy_ref[8:9],
                0.5 * gy_ref[T + 7 : T + 8],
                -0.5 * jnp.concatenate(low, axis=1),
                0.5 * jnp.concatenate(high, axis=1),
                jnp.zeros((SPILL - 4, T), F32),
            ],
            axis=0,
        )
        out_ref[0, T : T + SPILL] = spill.astype(BF16)

    @pl.when((slot_odd == 1) & jnp.logical_not(any_used))
    def _():
        out_ref[...] = jnp.zeros_like(out_ref)


def run_tiles(tiles, resample, observed, used, image, row_off, col_off, sun, gain):
    count = tiles.shape[0]
    grid_spec = pltpu.PrefetchScalarGridSpec(
        num_scalar_prefetch=6,
        grid=(2 * count,),
        in_specs=[
            pl.BlockSpec((1, T + EXTRA, T), lambda i, *s: (i // 2, 0, 0)),
            pl.BlockSpec((1, 2, C, C), lambda i, u, m, *s: (m[i], 0, 0, 0)),
            pl.BlockSpec((1, C, C), lambda i, u, m, *s: (m[i], 0, 0)),
        ],
        out_specs=[
            pl.BlockSpec((1, T + SPILL, T), lambda i, *s: (i // 2, 0, 0)),
            pl.BlockSpec((16, 5, 8, C), lambda i, *s: (0, 0, 0, 0)),
        ],
        scratch_shapes=[
            pltpu.VMEM((T + 16, T), F32),
            pltpu.VMEM((16, T), F32),
            pltpu.VMEM((T, T), F32),
            pltpu.VMEM((T, T), F32),
            pltpu.VMEM((T, T), F32),
            pltpu.VMEM((T, T), F32),
            pltpu.VMEM((T, T), F32),
            pltpu.VMEM((T + 16, T), F32),
            pltpu.VMEM((C, C), BF16),
            pltpu.VMEM((C + 16, C), F32),
            pltpu.VMEM((C, C), BF16),
            pltpu.VMEM((C, C), BF16),
        ],
    )
    return pl.pallas_call(
        tile_kernel,
        grid_spec=grid_spec,
        out_shape=[
            jax.ShapeDtypeStruct((count, T + SPILL, T), BF16),
            jax.ShapeDtypeStruct((16, 5, 8, C), F32),
        ],
        compiler_params=pltpu.CompilerParams(dimension_semantics=("arbitrary",)),
        name="tiles",
    )(used, image, row_off, col_off, sun, gain, tiles, resample, observed)


def next_images(used, image):
    count = used.shape[0]
    ids = jnp.arange(count, dtype=I32)
    is_used = used == 1
    ahead = jnp.min(
        jnp.where(is_used[None, :] & (ids[None, :] >= ids[:, None]), ids[None, :], count), axis=1
    )
    last = jnp.maximum(jnp.max(jnp.where(is_used, ids, -1)), 0)
    at = jnp.where(ahead < count, ahead, last)
    return jnp.sum(jnp.where(at[:, None] == ids[None, :], image[None, :], 0), axis=1)


def sun_vectors(azimuth, elevation):
    return jnp.stack(
        [
            jnp.cos(elevation) * jnp.cos(azimuth),
            jnp.cos(elevation) * jnp.sin(azimuth),
            jnp.sin(elevation),
        ]
    )


def laplace(padded):
    return (
        padded[:-2, 1:-1]
        + padded[2:, 1:-1]
        + padded[1:-1, :-2]
        + padded[1:-1, 2:]
        - 4.0 * padded[1:-1, 1:-1]
    )


def shifted(value, axis, up):
    count = lax.axis_size(axis)
    pairs = [(i, i + 1) for i in range(count - 1)]
    return lax.ppermute(value, axis, pairs if up else [(b, a) for a, b in pairs])


def quantize(heights):
    return jnp.round(heights * H_SCALE).astype(I32)


def smoothness(heights, top, bottom):
    tall = jnp.concatenate([top, heights, bottom], axis=0)
    left = shifted(tall[:, -2:], "dx", True)
    right = shifted(tall[:, :2], "dx", False)
    wide = jnp.concatenate([left, tall, right], axis=1)
    field = laplace(wide)
    rows, cols = heights.shape
    row_ids = jnp.arange(rows + 2)
    col_ids = jnp.arange(cols + 2)
    row_keep = ~(
        (row_ids == 0) & (lax.axis_index("dy") == 0)
        | (row_ids == rows + 1) & (lax.axis_index("dy") == lax.axis_size("dy") - 1)
    )
    col_keep = ~(
        (col_ids == 0) & (lax.axis_index("dx") == 0)
        | (col_ids == cols + 1) & (lax.axis_index("dx") == lax.axis_size("dx") - 1)
    )
    return SMOOTHING_WEIGHT * laplace(jnp.where(row_keep[:, None] & col_keep[None, :], field, 0.0))


def finish_sums(parts):
    ids = jnp.arange(C, dtype=F32)
    coord = (ids - 0.5 * (C - 1)) / C
    edge = jnp.where((ids == 0) | (ids == C - 1), 1.0, 0.5)
    start = (jnp.arange(8, dtype=F32) - 0.5 * (C - 1)) / C
    x_sum, x_row, y_sum, y_row, e_sum = (parts[:, n] for n in range(5))
    x_v = x_row / C + x_sum * start[None, :, None]
    y_v = y_row / C + y_sum * start[None, :, None]

    def total(v):
        return jnp.sum(v, axis=(1, 2))

    pose = [
        total(x_sum * edge),
        total(x_sum * (edge * coord)),
        total(x_v * edge),
        total(y_sum) * 0.5,
        total(y_sum * coord) * 0.5,
        total(y_v) * 0.5,
    ]
    return jnp.concatenate(
        [jnp.stack(pose, axis=-1) / C, (total(e_sum) / (C * C))[:, None]], axis=-1
    )


def per_device(
    heights, albedo, observed, resample, exposure, sun_azimuth, sun_elevation, send_plan, recv_plan
):
    offsets = send_plan[0, 0, 0:2].reshape(2, 16, 2).transpose(1, 0, 2)
    offsets = lax.all_to_all(offsets, "dy", split_axis=0, concat_axis=0, tiled=True)
    row_off = offsets[:, 0].reshape(-1)
    col_off = offsets[:, 1].reshape(-1)
    slots = jnp.arange(32, dtype=I32)
    match = recv_plan[0, 0][None, :] == slots[:, None]
    used = jnp.any(match, axis=1).astype(I32)
    image = jnp.sum(jnp.where(match, jnp.arange(16, dtype=I32)[None, :], 0), axis=1)
    image = next_images(used, image)
    sun = sun_vectors(sun_azimuth[0], sun_elevation[0]).reshape(-1)
    gain = jnp.exp(exposure[0])

    top = shifted(heights[-2:], "dy", True)
    bottom = shifted(heights[:2], "dy", False)
    left = shifted(heights[:, -1], "dx", True)
    right = shifted(heights[:, 0], "dx", False)
    rims = jnp.stack(
        [
            pack(quantize(left), quantize(right)),
            pack(quantize(top[1]), jnp.zeros_like(quantize(top[1]))),
            pack(quantize(bottom[0]), jnp.zeros_like(quantize(bottom[0]))),
        ]
    )
    words = pack(quantize(heights), jnp.round((albedo - 1.0) * A_SCALE).astype(I32))
    words = jnp.concatenate([words, rims, jnp.zeros((EXTRA - 3, T), I32)], axis=0)
    tiles = lax.all_gather(words, "dy", axis=0)
    smooth = smoothness(heights, top, bottom)
    outs, parts = run_tiles(
        tiles, resample, observed, used, image, row_off, col_off, sun, gain
    )
    crop_sums = finish_sums(parts)
    arrived = lax.all_to_all(crop_sums[:, None], "dy", split_axis=0, concat_axis=0, tiled=True)
    camera = arrived.sum(axis=0)
    own = lax.psum_scatter(outs, "dy", scatter_dimension=0).astype(F32)
    from_below = shifted(own[T], "dy", False)
    from_above = shifted(own[T + 1], "dy", True)
    from_right = shifted(own[T + 2], "dx", False)
    from_left = shifted(own[T + 3], "dx", True)
    row_ids = lax.broadcasted_iota(I32, (T, T), 0)
    col_ids = lax.broadcasted_iota(I32, (T, T), 1)
    data = own[:T]
    data = data + jnp.where(row_ids == T - 1, from_below[None, :], 0.0)
    data = data + jnp.where(row_ids == 0, from_above[None, :], 0.0)
    data = data + jnp.where(col_ids == T - 1, from_right[:, None], 0.0)
    data = data + jnp.where(col_ids == 0, from_left[:, None], 0.0)
    return (data + smooth, camera[None])


def solution(mesh):
    placed = (
        P("dy", "dx"),
        P("dy", "dx"),
        P(("dy", "dx"), None, None),
        P(("dy", "dx"), None, None, None),
        P("dx", None),
        P("dx", None),
        P("dx", None),
        P("dy", "dx", None, None),
        P("dy", "dx", None),
    )
    return jax.shard_map(
        per_device,
        mesh=mesh,
        in_specs=placed,
        out_specs=(P("dy", "dx"), P("dx", "dy", None)),
        check_vma=False,
    )
```

time: 734 us -> 379 us (0.52); the launches traced: 724 us -> 378 us
  other arithmetic: 280 us -> 13.8 us
  local copies, waits for them, and re-layouts: 214 us -> 10.1 us
  Pallas kernels: 0 us -> 115 us
  matrix products: 25.2 us -> 0 us
  waiting for transfers between devices: 155 us -> 174 us
  between operations: 1.78 us -> 15 us
    all_to_all x3 -> x2, waiting for transfers between devices: 152 us -> 0.65 us  [the longest x1 0.64 us: per_device(): lax.all_to_all(offsets, 'dy', split_axis=0, concat_axis=0, tiled=True)]
    pallas_call x0 -> x1, Pallas kernels: none -> 115 us  [run_tiles(): pl.pallas_call(tile_kernel, grid_spec=grid_spec, out_shape=[jax.ShapeDtyp...]
    scatter-add x3 -> x0, other arithmetic: 114 us -> none  [per_device(): empty_blocks.at[block_ids].add(block_sun[component][:, None] * grad_blocks)]
    all_gather x0 -> x1, waiting for transfers between devices: none -> 100 us  [per_device(): tiles = lax.all_gather(words, 'dy', axis=0)]
    mul x6 -> x4, other arithmetic: 74.8 us -> 0.06 us  [the longest x1 0.04 us: sun_vectors(): jnp.cos(elevation) * jnp.cos(azimuth)]
    unnamed x0 -> x3, waiting for transfers between devices: none -> 65.8 us
    gather x4 -> x0, local copies, waits for them, and re-layouts: 42.3 us -> none  [the longest x2 23.4 us: per_device(): jnp.take(field_blocks[component], block_ids, axis=0)]
    reshape x4 -> x1, local copies, waits for them, and re-layouts: 42.1 us -> 0.6 us  [per_device(): sun = sun_vectors(sun_azimuth[0], sun_elevation[0]).reshape(-1)]
  transfers between devices with their start and end apart: 11 -> 14, of which waited for: 3 -> 6; matrix products, arithmetic and copies ran while one was open for 47% -> 5% of each run, Pallas kernels for 0% -> 0%
where the time goes in v1:
time: 379 us; the launch traced here: 378 us
  waiting for transfers between devices  174 us (46%)
  Pallas kernels  115 us (30%)
  starting transfers between devices  49.5 us (13%)
  between operations  15 us (4%)
  other arithmetic  13.8 us (4%)
  local copies, waits for them, and re-layouts  10.1 us (3%)
    pallas_call x1, Pallas kernels, run_tiles(): pl.pallas_call(tile_kernel, grid_spec=grid_spec, out_shape=[jax.ShapeDtyp...  115 us
    all_gather x1, waiting for transfers between devices, per_device(): tiles = lax.all_gather(words, 'dy', axis=0)  100 us
    unnamed x3, waiting for transfers between devices  65.8 us
    ppermute x10, starting transfers between devices, shifted(): lax.ppermute(value, axis, pairs if up else [(b, a) for a, b in pairs])  38.9 us
  transfers between devices with their start and end apart: 14, of which 6 were waited for; matrix products, arithmetic and copies ran while one was open for 5% of the time, Pallas kernels for 0%

profile of v1, /device:TPU:7, one launch (start us, length us, event | category | flops | bytes accessed | tf_op | source)
XLA Modules:
  0.0 377.9 jit_solution(6611933883970323411)
XLA Ops:
  7.2 0.0 all-gather.3.cloned.1.call-start
  7.2 0.7 fusion.36
  8.0 2.4 collective-permute-start.3
  10.4 4.9 %collective-permute-start.2 = (f32[2,512]{1,0:T(2,128)S(1)}, f32[2,512]{1,0:T(2,128)S(1)}, u32[]{:S(2)}, u32[]{:S(2)}) collective-permute-start(f32[2,512]{1,0:T(2,128)S(1)} %get-tuple-element.20), channel_id=1, source_target_pairs={{0,8},{8,16},{16,24},{24,32},{32,40},{40,48},{48,56},{56,64},{64,7... | collective-permute-start | bytes 12296 | tf_op jit(solution)/shard_map/ppermute | solution.py:292
  15.3 1.3 slice_reduce_fusion.1
  16.7 4.7 %collective-permute-start = (f32[512]{0:T(512)S(1)}, f32[512]{0:T(512)S(1)}, u32[]{:S(2)}, u32[]{:S(2)}) collective-permute-start(f32[512]{0:T(512)S(1)} %get-tuple-element.6), channel_id=1, source_target_pairs={{0,1},{1,2},{2,3},{3,4},{4,5},{5,6},{6,7},{8,9},{9,10},{10,11},{11... | collective-permute-start | bytes 6152 | tf_op jit(solution)/shard_map/ppermute | solution.py:292
  21.4 1.9 collective-permute-start.1
  23.3 1.8 and_or_fusion
  25.1 1.2 collective-permute-done.1
  26.4 2.2 concatenate.18
  28.6 0.1 reshape_squeeze.9
  28.7 0.6 copy.25
  29.4 6.6 %all-to-all-start = ((s32[16,2,2]{2,1,0:T(2,128)}), s32[16,2,2]{2,1,0:T(2,128)S(1)}, u32[]{:S(2)}, u32[]{:S(2)}) async-start(s32[16,2,2]{2,1,0:T(2,128)} %copy.25), calls=%async_computation | async-start | bytes 32768 | tf_op jit(solution)/shard_map/all_to_all | solution.py:348
  36.0 0.1 fusion.18
  36.1 0.6 select_reduce_fusion.3
  37.4 0.5 broadcast_compare_fusion
  37.9 0.1 select_reduce_fusion.1
  38.0 0.1 select_reduce_fusion.2
  38.1 0.7 select_reduce_fusion.image
  38.9 0.5 exponential_bitcast_fusion.gain
  39.5 0.6 reshape.116.sun
  40.1 0.6 all-to-all-done
  40.8 0.6 reshape_squeeze.10.row_off
  41.4 0.6 reshape_squeeze.11.col_off
  42.0 100.2 %all-gather.3.cloned.1.call-done = s32[8320,512]{1,0:T(8,128)} async-done(((s32[520,512]{1,0:T(8,128)}), s32[8320,512]{1,0:T(8,128)}) %all-gather.3.cloned.1.call-update) | async-done | bytes 17039376 | tf_op jit(solution)/shard_map/all_gather | solution.py:372
  142.2 115.3 %tiles.1 = (bf16[16,528,512]{2,1,0:T(8,128)(2,1)}, f32[16,5,8,384]{3,2,1,0:T(8,128)}) custom-call(s32[32]{0:T(128)} %get-tuple-element.31.used, s32[32]{0:T(128)} %select_reduce_fusion.image, s32[32]{0:T(128)} %reshape_squeeze.10.row_off, s32[32]{0:T(128)} %reshape_squeeze.11.col_off, f32[48]{0:T(128)} %reshape.116.sun, f32[16]{0:T(128)} %exponential_bitcast_fusion.gain, ...), custom_call_target="tpu_custom_call" | custom-call | tf_op jit(solution)/shard_map/tiles/pallas_call | solution.py:245
  257.6 1.1 copy-done
  258.7 0.1 pad_maximum_fusion.9
  258.9 7.9 %collective-permute-start.8 = (f32[516,2]{1,0:T(8,128)S(1)}, f32[516,2]{1,0:T(8,128)S(1)}, u32[]{:S(2)}, u32[]{:S(2)}) collective-permute-start(f32[516,2]{1,0:T(8,128)S(1)} %get-tuple-element.18), channel_id=1, source_target_pairs={{0,1},{1,2},{2,3},{3,4},{4,5},{5,6},{6,7},{8,9},{9,10},{10,11},{11... | collective-permute-start | bytes 12392 | tf_op jit(solution)/shard_map/ppermute | solution.py:292
  266.7 1.9 collective-permute-start.9
  268.7 1.4 collective-permute-done.8
  270.1 4.8 %collective-permute-done.9 = f32[516,2]{1,0:T(8,128)S(1)} collective-permute-done((f32[516,2]{1,0:T(8,128)S(1)}, f32[516,2]{1,0:T(8,128)S(1)}, u32[]{:S(2)}, u32[]{:S(2)}) %collective-permute-start.9) | collective-permute-done | bytes 4160 | tf_op jit(solution)/shard_map/ppermute | solution.py:292
  274.9 1.6 pad_maximum_fusion.6
  276.5 0.2 slice_reduce_fusion.3
  276.7 0.3 fusion.16
  277.0 0.2 slice_reduce_fusion.2
  277.2 0.7 copy.30
  277.9 4.0 %all-to-all-start.1 = ((f32[16,1,7]{2,1,0:T(1,128)}), f32[16,1,7]{2,1,0:T(1,128)S(1)}, u32[]{:S(2)}, u32[]{:S(2)}) async-start(f32[16,1,7]{2,1,0:T(1,128)} %copy.30), calls=%async_computation.1 | async-start | bytes 16384 | tf_op jit(solution)/shard_map/all_to_all | solution.py:378
  281.9 65.8 %reduce-scatter.4.cloned.1.call-done = bf16[1,528,512]{2,1,0:T(8,128)(2,1)} async-done(((bf16[16,528,512]{2,1,0:T(8,128)(2,1)}), bf16[1,528,512]{2,1,0:T(8,128)(2,1)}) %reduce-scatter.4.cloned.1.call-update) | async-done | bytes 540688
  347.7 0.9 fusion.37
  348.5 2.4 collective-permute-start.4
  350.9 5.0 %collective-permute-start.5 = (f32[512]{0:T(512)S(1)}, f32[512]{0:T(512)S(1)}, u32[]{:S(2)}, u32[]{:S(2)}) collective-permute-start(f32[512]{0:T(512)S(1)} %bitcast.76), channel_id=1, source_target_pairs={{0,8},{8,16},{16,24},{24,32},{32,40},{40,48},{48,56},{56,64},{64,7... | collective-permute-start | bytes 6152 | tf_op jit(solution)/shard_map/ppermute | solution.py:292
  355.9 4.7 %collective-permute-start.6 = (f32[512]{0:T(512)S(1)}, f32[512]{0:T(512)S(1)}, u32[]{:S(2)}, u32[]{:S(2)}) collective-permute-start(f32[512]{0:T(512)S(1)} %bitcast.75), channel_id=1, source_target_pairs={{1,0},{2,1},{3,2},{4,3},{5,4},{6,5},{7,6},{9,8},{10,9},{11,10},{12... | collective-permute-start | bytes 6152 | tf_op jit(solution)/shard_map/ppermute | solution.py:292
  360.6 3.1 collective-permute-start.7
  363.7 4.1 %fusion.1 = f32[514,514]{1,0:T(8,128)S(1)} fusion(f32[516,516]{1,0:T(8,128)} %pad_maximum_fusion.6, f32[516,2]{1,0:T(8,128)S(1)} %collective-permute-done.9, f32[2,512]{1,0:T(2,128)S(1)} %collective-permute-done.3, f32[512,512]{1,0:T(8,128)S(1)} %copy-done, f32[2,512]{1,0:T(2,128)S(1)} %collective-permute-done.2, f32[516,2]{1,0:T(8,128)S(1)} %collective-permute-done.8, ...), kind=kLoop, calls=%fused_computation.2 | loop fusion | flops 3434548 | bytes 5293188 | tf_op jit(solution)/shard_map/jit(_where)/select_n | solution.py:316
  367.9 0.5 reduce_sum.99
  368.5 0.1 convert_element_type.34
  368.6 2.4 fusion.6
  (47 shorter events, 0.4 us)
Async XLA Ops:
  7.2 135.0 %all-gather.3.cloned.1.call-start = ((), (), s32[]{:S(2)}) async-start(), calls=%async_computation.3 | async-start | bytes 18104320 | tf_op jit(solution)/shard_map/all_gather | solution.py:372
  8.0 18.3 %collective-permute-start.3 = (f32[2,512]{1,0:T(2,128)S(1)}, f32[2,512]{1,0:T(2,128)S(1)}, u32[]{:S(2)}, u32[]{:S(2)}) collective-permute-start(f32[2,512]{1,0:T(2,128)S(1)} %get-tuple-element.21), channel_id=1, source_target_pairs={{8,0},{16,8},{24,16},{32,24},{40,32},{48,40},{56,48},{64,56},{72,6... | collective-permute-start | bytes 12296 | tf_op jit(solution)/shard_map/ppermute | solution.py:292
  10.4 15.9 %collective-permute-start.2 = (f32[2,512]{1,0:T(2,128)S(1)}, f32[2,512]{1,0:T(2,128)S(1)}, u32[]{:S(2)}, u32[]{:S(2)}) collective-permute-start(f32[2,512]{1,0:T(2,128)S(1)} %get-tuple-element.20), channel_id=1, source_target_pairs={{0,8},{8,16},{16,24},{24,32},{32,40},{40,48},{48,56},{56,64},{64,7... | collective-permute-start | bytes 12296 | tf_op jit(solution)/shard_map/ppermute | solution.py:292
  16.7 8.4 %collective-permute-start = (f32[512]{0:T(512)S(1)}, f32[512]{0:T(512)S(1)}, u32[]{:S(2)}, u32[]{:S(2)}) collective-permute-start(f32[512]{0:T(512)S(1)} %get-tuple-element.6), channel_id=1, source_target_pairs={{0,1},{1,2},{2,3},{3,4},{4,5},{5,6},{6,7},{8,9},{9,10},{10,11},{11... | collective-permute-start | bytes 6152 | tf_op jit(solution)/shard_map/ppermute | solution.py:292
  21.4 4.9 %collective-permute-start.1 = (f32[512]{0:T(512)S(1)}, f32[512]{0:T(512)S(1)}, u32[]{:S(2)}, u32[]{:S(2)}) collective-permute-start(f32[512]{0:T(512)S(1)} %get-tuple-element.7), channel_id=1, source_target_pairs={{1,0},{2,1},{3,2},{4,3},{5,4},{6,5},{7,6},{9,8},{10,9},{11,10},{12... | collective-permute-start | bytes 6152 | tf_op jit(solution)/shard_map/ppermute | solution.py:292
  26.3 2.3 slice-start
  26.3 9.7 %copy-start.4 = (s32[1,1,16]{2,1,0:T(1,128)S(1)}, s32[1,1,16]{2,1,0:T(1,128)}, u32[]{:S(2)}) copy-start(s32[1,1,16]{2,1,0:T(1,128)} %param.17) | copy-start | bytes 196
  26.4 12.5 %copy-start.5 = (f32[1,16]{1,0:T(1,128)S(1)}, f32[1,16]{1,0:T(1,128)}, u32[]{:S(2)}) copy-start(f32[1,16]{1,0:T(1,128)} %param.13) | copy-start | bytes 196
  26.4 13.0 %copy-start.6 = (f32[1,16]{1,0:T(1,128)S(1)}, f32[1,16]{1,0:T(1,128)}, u32[]{:S(2)}) copy-start(f32[1,16]{1,0:T(1,128)} %param.15) | copy-start | bytes 196
  26.4 13.0 %copy-start.3 = (f32[1,16]{1,0:T(1,128)S(1)}, f32[1,16]{1,0:T(1,128)}, u32[]{:S(2)}) copy-start(f32[1,16]{1,0:T(1,128)} %param.14) | copy-start | bytes 196
  29.4 11.4 %all-to-all-start = ((s32[16,2,2]{2,1,0:T(2,128)}), s32[16,2,2]{2,1,0:T(2,128)S(1)}, u32[]{:S(2)}, u32[]{:S(2)}) async-start(s32[16,2,2]{2,1,0:T(2,128)} %copy.25), calls=%async_computation | async-start | bytes 32768 | tf_op jit(solution)/shard_map/all_to_all | solution.py:348
  36.0 311.7 %reduce-scatter.4.cloned.1.call-start = ((), (), s32[]{:S(2)}) async-start(), calls=%async_computation.4 | async-start | bytes 9191424
  257.5 1.2 copy-start
  258.9 11.2 %collective-permute-start.8 = (f32[516,2]{1,0:T(8,128)S(1)}, f32[516,2]{1,0:T(8,128)S(1)}, u32[]{:S(2)}, u32[]{:S(2)}) collective-permute-start(f32[516,2]{1,0:T(8,128)S(1)} %get-tuple-element.18), channel_id=1, source_target_pairs={{0,1},{1,2},{2,3},{3,4},{4,5},{5,6},{6,7},{8,9},{9,10},{10,11},{11... | collective-permute-start | bytes 12392 | tf_op jit(solution)/shard_map/ppermute | solution.py:292
  266.7 8.1 %collective-permute-start.9 = (f32[516,2]{1,0:T(8,128)S(1)}, f32[516,2]{1,0:T(8,128)S(1)}, u32[]{:S(2)}, u32[]{:S(2)}) collective-permute-start(f32[516,2]{1,0:T(8,128)S(1)} %get-tuple-element.19), channel_id=1, source_target_pairs={{1,0},{2,1},{3,2},{4,3},{5,4},{6,5},{7,6},{9,8},{10,9},{11,10},{12... | collective-permute-start | bytes 12392 | tf_op jit(solution)/shard_map/ppermute | solution.py:292
  268.7 7.8 %copy-start.1 = (f32[16,5,8,384]{3,2,1,0:T(8,128)S(1)}, f32[16,5,8,384]{3,2,1,0:T(8,128)}, u32[]{:S(2)}) copy-start(f32[16,5,8,384]{3,2,1,0:T(8,128)} %get-tuple-element.5) | copy-start | bytes 2949124
  277.9 90.0 %all-to-all-start.1 = ((f32[16,1,7]{2,1,0:T(1,128)}), f32[16,1,7]{2,1,0:T(1,128)S(1)}, u32[]{:S(2)}, u32[]{:S(2)}) async-start(f32[16,1,7]{2,1,0:T(1,128)} %copy.30), calls=%async_computation.1 | async-start | bytes 16384 | tf_op jit(solution)/shard_map/all_to_all | solution.py:378
  348.5 20.1 %collective-permute-start.4 = (f32[512]{0:T(512)S(1)}, f32[512]{0:T(512)S(1)}, u32[]{:S(2)}, u32[]{:S(2)}) collective-permute-start(f32[512]{0:T(512)S(1)} %bitcast.77), channel_id=1, source_target_pairs={{8,0},{16,8},{24,16},{32,24},{40,32},{48,40},{56,48},{64,56},{72,6... | collective-permute-start | bytes 6152 | tf_op jit(solution)/shard_map/ppermute | solution.py:292
  350.9 17.7 %collective-permute-start.5 = (f32[512]{0:T(512)S(1)}, f32[512]{0:T(512)S(1)}, u32[]{:S(2)}, u32[]{:S(2)}) collective-permute-start(f32[512]{0:T(512)S(1)} %bitcast.76), channel_id=1, source_target_pairs={{0,8},{8,16},{16,24},{24,32},{32,40},{40,48},{48,56},{56,64},{64,7... | collective-permute-start | bytes 6152 | tf_op jit(solution)/shard_map/ppermute | solution.py:292
  355.9 12.7 %collective-permute-start.6 = (f32[512]{0:T(512)S(1)}, f32[512]{0:T(512)S(1)}, u32[]{:S(2)}, u32[]{:S(2)}) collective-permute-start(f32[512]{0:T(512)S(1)} %bitcast.75), channel_id=1, source_target_pairs={{1,0},{2,1},{3,2},{4,3},{5,4},{6,5},{7,6},{9,8},{10,9},{11,10},{12... | collective-permute-start | bytes 6152 | tf_op jit(solution)/shard_map/ppermute | solution.py:292
  360.6 8.0 %collective-permute-start.7 = (f32[512]{0:T(512)S(1)}, f32[512]{0:T(512)S(1)}, u32[]{:S(2)}, u32[]{:S(2)}) collective-permute-start(f32[512]{0:T(512)S(1)} %bitcast.74), channel_id=1, source_target_pairs={{0,1},{1,2},{2,3},{3,4},{4,5},{5,6},{6,7},{8,9},{9,10},{10,11},{11... | collective-permute-start | bytes 6152 | tf_op jit(solution)/shard_map/ppermute | solution.py:292
  363.7 4.7 %copy-start.2 = (bf16[1,528,512]{2,1,0:T(8,128)(2,1)S(1)}, bf16[1,528,512]{2,1,0:T(8,128)(2,1)}, u32[]{:S(2)}) copy-start(bf16[1,528,512]{2,1,0:T(8,128)(2,1)} %reduce-scatter.4.cloned.1.call-done) | copy-start | bytes 1622020
Sparse Core Ops, SparseCore 0:
  28.8 113.3 all-gather.2
  257.6 89.9 reduce-scatter.3

commit v2 on v1

--- a/solution.py
+++ b/solution.py
@@ -34,14 +34,20 @@
     used, image, row_off, col_off, sun, gain,
     tile_ref, res_ref, obs_ref,
     out_ref, sums_ref,
-    hbuf, halo, sx_ref, sy_ref, w_ref, r2_ref, gx_ref, gy_ref,
-    shaded, pbuf, weighted, grad,
+    hbuf, hcol, sx_ref, sy_ref, w_ref, r2_ref, gx_ref, gy_ref,
+    shaded, tbuf, pbuf, weighted, grad,
 ):
     step = pl.program_id(0)
     first = (step // 2) * 2
     slot_odd = step % 2
     mine = used[step] == 1
     any_used = used[first] + used[first + 1] > 0
+    lane = lax.broadcasted_iota(I32, (CH, 128), 1)
+    at_first = lane == 0
+    at_last = lane == 127
+
+    def lanes(b):
+        return slice(128 * b, 128 * (b + 1))
 
     @pl.when(step == 0)
     def _():
@@ -50,167 +56,220 @@
     @pl.when((slot_odd == 0) & any_used)
     def _():
         words = tile_ref[0, T : T + EXTRA]
-        halo[0:8] = high_of(words)
-        halo[8:16] = low_of(words)
-        hbuf[7:8] = halo[1:2]
-        hbuf[T + 8 : T + 9] = halo[2:3]
+        high = lax.shift_right_arithmetic(words, 16)
+        low = lax.shift_right_arithmetic(lax.shift_left(words, 16), 16)
+        pieces = jnp.concatenate(
+            [
+                lax.shift_right_arithmetic(high, 8),
+                high & 255,
+                lax.shift_right_arithmetic(low, 8),
+                low & 255,
+            ],
+            axis=0,
+        ).astype(F32).astype(BF16)
+        row_id = lax.broadcasted_iota(I32, (32, 256), 0)
+        side = lax.broadcasted_iota(I32, (32, 256), 1) // 128
+        scale = jnp.where(row_id == 16 * side, 256.0, 0.0) + jnp.where(
+            row_id == 16 * side + 8, 1.0, 0.0
+        )
+        columns = lax.dot_general(
+            pieces, scale.astype(BF16), (((0,), (0,)), ((), ())), preferred_element_type=F32
+        )
+        for side_id in range(2):
+            hcol[side_id] = columns[:, lanes(side_id)]
+        rims = high.astype(F32)
+        for b in range(4):
+            hbuf[b, 7:8] = rims[1:2, lanes(b)]
+            hbuf[b, T + 8 : T + 9] = rims[2:3, lanes(b)]
+            gy_ref[b, 0:8] = jnp.zeros((8, 128), F32)
+            gy_ref[b, T + 8 : T + 16] = jnp.zeros((8, 128), F32)
 
         def unpack(k, _):
             base = pl.multiple_of(k * CH, CH)
-            hbuf[pl.ds(base + 8, CH)] = high_of(tile_ref[0, pl.ds(base, CH)])
-            gx_ref[pl.ds(base, CH)] = jnp.zeros((CH, T), F32)
-            gy_ref[pl.ds(base + 8, CH)] = jnp.zeros((CH, T), F32)
+            for b in range(4):
+                hbuf[b, pl.ds(base + 8, CH)] = high_of(tile_ref[0, pl.ds(base, CH), lanes(b)])
             return 0
 
-        lax.fori_loop(0, T // CH, unpack, 0)
-        gy_ref[0:8] = jnp.zeros((8, T), F32)
-        gy_ref[T + 8 : T + 16] = jnp.zeros((8, T), F32)
+        lax.fori_loop(0, T // CH, unpack, 0, unroll=2)
 
         def slope(k, _):
             base = pl.multiple_of(k * CH, CH)
-            block = pl.multiple_of((k * CH // 128) * 128, 128)
-            rows = hbuf[pl.ds(base, CH + 16)]
-            h = rows[8 : 8 + CH]
-            lane = lax.broadcasted_iota(I32, (CH, T), 1)
-            pick = (
-                lax.broadcasted_iota(I32, (CH, 128), 0) + (base - block)
-                == lax.broadcasted_iota(I32, (CH, 128), 1)
-            )
-            left_col = jnp.sum(
-                jnp.where(pick, halo[0:1, pl.ds(block, 128)], 0.0), axis=1, keepdims=True
-            )
-            right_col = jnp.sum(
-                jnp.where(pick, halo[8:9, pl.ds(block, 128)], 0.0), axis=1, keepdims=True
-            )
-            left = jnp.where(lane == 0, left_col, pltpu.roll(h, 1, 1))
-            right = jnp.where(lane == T - 1, right_col, pltpu.roll(h, T - 1, 1))
-            sx = (right - left) * (0.5 / H_SCALE)
-            sy = (rows[9 : 9 + CH] - rows[7 : 7 + CH]) * (0.5 / H_SCALE)
-            albedo = low_of(tile_ref[0, pl.ds(base, CH)]) * (1.0 / A_SCALE) + 1.0
-            r = lax.rsqrt(1.0 + sx * sx + sy * sy)
-            sx_ref[pl.ds(base, CH)] = sx
-            sy_ref[pl.ds(base, CH)] = sy
-            w_ref[pl.ds(base, CH)] = albedo * r
-            r2_ref[pl.ds(base, CH)] = r * r
+            rows = pl.ds(base, CH)
+            here = [hbuf[b, pl.ds(base + 8, CH)] for b in range(4)]
+            right_turn = [pltpu.roll(h, 1, 1) for h in here]
+            left_turn = [pltpu.roll(h, 127, 1) for h in here]
+            before = [hcol[0, rows]] + right_turn[:3]
+            after = left_turn[1:] + [hcol[1, rows]]
+            for b in range(4):
+                left = jnp.where(at_first, before[b], right_turn[b])
+                right = jnp.where(at_last, after[b], left_turn[b])
+                sx = (right - left) * (0.5 / H_SCALE)
+                sy = (hbuf[b, pl.ds(base + 9, CH)] - hbuf[b, pl.ds(base + 7, CH)]) * (
+                    0.5 / H_SCALE
+                )
+                albedo = low_of(tile_ref[0, rows, lanes(b)]) * (1.0 / A_SCALE) + 1.0
+                r = lax.rsqrt(1.0 + sx * sx + sy * sy)
+                sx_ref[b, rows] = sx
+                sy_ref[b, rows] = sy
+                w_ref[b, rows] = albedo * r
+                r2_ref[b, rows] = r * r
+                gx_ref[b, rows] = jnp.zeros((CH, 128), F32)
+                gy_ref[b, pl.ds(base + 8, CH)] = jnp.zeros((CH, 128), F32)
             return 0
 
-        lax.fori_loop(0, T // CH, slope, 0)
+        lax.fori_loop(0, T // CH, slope, 0, unroll=4)
 
     @pl.when(mine)
     def _():
         m = image[step]
         oy = pl.multiple_of(row_off[step], 128)
-        ox = pl.multiple_of(col_off[step], 128)
+        ob = col_off[step] // 128
         s1 = sun[m]
         s2 = sun[16 + m]
         s3 = sun[32 + m]
         e = gain[m]
-        cols = pl.ds(ox, C)
 
         def shade(k, _):
             base = pl.multiple_of(k * CH, CH)
             rows = pl.ds(pl.multiple_of(oy + base, CH), CH)
-            q = s3 - s1 * sx_ref[rows, cols] - s2 * sy_ref[rows, cols]
-            shaded[pl.ds(base, CH)] = (w_ref[rows, cols] * q).astype(BF16)
+            for b in range(3):
+                q = s3 - s1 * sx_ref[ob + b, rows] - s2 * sy_ref[ob + b, rows]
+                shaded[pl.ds(base, CH), lanes(b)] = (w_ref[ob + b, rows] * q).astype(BF16)
+                tbuf[b, pl.ds(base, CH)] = q * r2_ref[ob + b, rows]
             return 0
 
-        lax.fori_loop(0, C // CH, shade, 0)
+        lax.fori_loop(0, C // CH, shade, 0, unroll=4)
         row_mat = res_ref[0, 0]
         col_mat = res_ref[0, 1]
         first_pass = jnp.dot(row_mat, shaded[...], preferred_element_type=F32).astype(BF16)
-        pbuf[8 : 8 + C] = e * lax.dot_general(
+        predicted = e * lax.dot_general(
             first_pass, col_mat, (((1,), (1,)), ((), ())), preferred_element_type=F32
         )
-        pbuf[7:8] = 2.0 * pbuf[8:9] - pbuf[9:10]
-        pbuf[C + 8 : C + 9] = 2.0 * pbuf[C + 7 : C + 8] - pbuf[C + 6 : C + 7]
-
-        def fold(v):
-            return v.reshape(CH // 8, 8, C)
+        for b in range(3):
+            pbuf[b, 8 : 8 + C] = predicted[:, lanes(b)]
+            pbuf[b, 7:8] = 2.0 * pbuf[b, 8:9] - pbuf[b, 9:10]
+            pbuf[b, C + 8 : C + 9] = 2.0 * pbuf[b, C + 7 : C + 8] - pbuf[b, C + 6 : C + 7]
+
+        def add_up(v, base, total, by_row):
+            groups = [v[8 * g : 8 * g + 8] for g in range(CH // 8)]
+            tail = groups[-1]
+            lead = tail
+            for g in range(CH // 8 - 2, 0, -1):
+                tail = groups[g] + tail
+                lead = lead + tail
+            tail = groups[0] + tail
+            return total + tail, by_row + lead * 8.0 + tail * base
 
         def terms(k, carry):
-            a_x, a_xg, a_y, a_yg, a_e = carry
-            base = pl.multiple_of(k * CH, CH)
-            rows = pbuf[pl.ds(base, CH + 16)]
-            p = rows[8 : 8 + CH]
-            lane = lax.broadcasted_iota(I32, (CH, C), 1)
-            residual = p - obs_ref[0, pl.ds(base, CH)].astype(F32)
-            left = jnp.where(lane == 0, p, pltpu.roll(p, 1, 1))
-            right = jnp.where(lane == C - 1, p, pltpu.roll(p, C - 1, 1))
-            xs = fold(residual * (right - left))
-            ys = fold(residual * (rows[9 : 9 + CH] - rows[7 : 7 + CH]))
-            es = fold(residual * p)
-            weighted[pl.ds(base, CH)] = (e * residual).astype(BF16)
-            for g in range(CH // 8):
-                at = (base + 8 * g).astype(F32)
-                a_x = a_x + xs[g]
-                a_xg = a_xg + xs[g] * at
-                a_y = a_y + ys[g]
-                a_yg = a_yg + ys[g] * at
-                a_e = a_e + es[g]
-            return a_x, a_xg, a_y, a_yg, a_e
-
-        zero = jnp.zeros((8, C), F32)
-        parts = lax.fori_loop(0, C // CH, terms, (zero,) * 5)
-        for n in range(5):
-            sums_ref[m, n] = parts[n]
+            base = pl.multiple_of(k * CH, CH)
+            at = base.astype(F32)
+            rows = pl.ds(base, CH)
+            here = [pbuf[b, pl.ds(base + 8, CH)] for b in range(3)]
+            right_turn = [pltpu.roll(p, 1, 1) for p in here]
+            left_turn = [pltpu.roll(p, 127, 1) for p in here]
+            before = [here[0]] + right_turn[:2]
+            after = left_turn[1:] + [here[2]]
+            result = []
+            for b in range(3):
+                a_x, a_xg, a_y, a_yg, a_e = carry[b]
+                p = here[b]
+                residual = p - obs_ref[0, rows, lanes(b)].astype(F32)
+                weighted[rows, lanes(b)] = (e * residual).astype(BF16)
+                left = jnp.where(at_first, before[b], right_turn[b])
+                right = jnp.where(at_last, after[b], left_turn[b])
+                a_x, a_xg = add_up(residual * (right - left), at, a_x, a_xg)
+                down = pbuf[b, pl.ds(base + 9, CH)]
+                up = pbuf[b, pl.ds(base + 7, CH)]
+                a_y, a_yg = add_up(residual * (down - up), at, a_y, a_yg)
+                squares = residual * p
+                a_e = a_e + squares.reshape(CH // 8, 8, 128).sum(axis=0)
+                result.append((a_x, a_xg, a_y, a_yg, a_e))
+            return tuple(result)
+
+        zero = jnp.zeros((8, 128), F32)
+        parts = lax.fori_loop(0, C // CH, terms, ((zero,) * 5,) * 3, unroll=3)
+        for b in range(3):
+            for n in range(5):
+                sums_ref[m, n, :, lanes(b)] = parts[b][n]
         back_pass = lax.dot_general(
             row_mat, weighted[...], (((0,), (0,)), ((), ())), preferred_element_type=F32
         ).astype(BF16)
-        grad[...] = jnp.dot(back_pass, col_mat, preferred_element_type=F32).astype(BF16)
+        crop_grad = jnp.dot(back_pass, col_mat, preferred_element_type=F32)
+        for b in range(3):
+            grad[b] = crop_grad[:, lanes(b)]
 
         def pull(k, _):
             base = pl.multiple_of(k * CH, CH)
             rows = pl.ds(pl.multiple_of(oy + base, CH), CH)
             rows_y = pl.ds(pl.multiple_of(oy + base + 8, 8), CH)
-            sx = sx_ref[rows, cols]
-            sy = sy_ref[rows, cols]
-            t = (s3 - s1 * sx - s2 * sy) * r2_ref[rows, cols]
-            wg = w_ref[rows, cols] * grad[pl.ds(base, CH)].astype(F32)
-            gx_ref[rows, cols] = gx_ref[rows, cols] - wg * (s1 + t * sx)
-            gy_ref[rows_y, cols] = gy_ref[rows_y, cols] - wg * (s2 + t * sy)
+            for b in range(3):
+                t = tbuf[b, pl.ds(base, CH)]
+                wg = w_ref[ob + b, rows] * grad[b, pl.ds(base, CH)]
+                gx_ref[ob + b, rows] = gx_ref[ob + b, rows] - wg * (s1 + t * sx_ref[ob + b, rows])
+                gy_ref[ob + b, rows_y] = gy_ref[ob + b, rows_y] - wg * (
+                    s2 + t * sy_ref[ob + b, rows]
+                )
             return 0
 
-        lax.fori_loop(0, C // CH, pull, 0)
+        lax.fori_loop(0, C // CH, pull, 0, unroll=4)
 
     @pl.when((slot_odd == 1) & any_used)
     def _():
         def stencil(k, _):
             base = pl.multiple_of(k * CH, CH)
-            lane = lax.broadcasted_iota(I32, (CH, T), 1)
-            gx = gx_ref[pl.ds(base, CH)]
-            rows = gy_ref[pl.ds(base, CH + 16)]
-            left = jnp.where(lane == 0, 0.0, pltpu.roll(gx, 1, 1))
-            right = jnp.where(lane == T - 1, 0.0, pltpu.roll(gx, T - 1, 1))
-            total = (left - right) + (rows[7 : 7 + CH] - rows[9 : 9 + CH])
-            out_ref[0, pl.ds(base, CH)] = (0.5 * total).astype(BF16)
+            rows = pl.ds(base, CH)
+            here = [gx_ref[b, rows] for b in range(4)]
+            right_turn = [pltpu.roll(g, 1, 1) for g in here]
+            left_turn = [pltpu.roll(g, 127, 1) for g in here]
+            blank = jnp.zeros((CH, 128), F32)
+            before = [blank] + right_turn[:3]
+            after = left_turn[1:] + [blank]
+            for b in range(4):
+                left = jnp.where(at_first, before[b], right_turn[b])
+                right = jnp.where(at_last, after[b], left_turn[b])
+                up = gy_ref[b, pl.ds(base + 7, CH)]
+                down = gy_ref[b, pl.ds(base + 9, CH)]
+                total = (left - right) + (up - down)
+                out_ref[0, rows, lanes(b)] = (0.5 * total).astype(BF16)
             return 0
 
-        lax.fori_loop(0, T // CH, stencil, 0)
-        eye = lax.broadcasted_iota(I32, (128, 128), 0) == lax.broadcasted_iota(
-            I32, (128, 128), 1
-        )
-        low = []
-        high = []
-        for b in range(T // 128):
-            first_col = gx_ref[128 * b : 128 * (b + 1), 0:128][:, 0:1]
-            last_col = gx_ref[128 * b : 128 * (b + 1), T - 128 : T][:, 127:128]
-            low.append(jnp.sum(jnp.where(eye, first_col, 0.0), axis=0, keepdims=True))
-            high.append(jnp.sum(jnp.where(eye, last_col, 0.0), axis=0, keepdims=True))
-        spill = jnp.concatenate(
-            [
-                -0.5 * gy_ref[8:9],
-                0.5 * gy_ref[T + 7 : T + 8],
-                -0.5 * jnp.concatenate(low, axis=1),
-                0.5 * jnp.concatenate(high, axis=1),
-                jnp.zeros((SPILL - 4, T), F32),
-            ],
-            axis=0,
-        )
-        out_ref[0, T : T + SPILL] = spill.astype(BF16)
+        lax.fori_loop(0, T // CH, stencil, 0, unroll=4)
+        sub = lax.broadcasted_iota(I32, (16, 128), 0)
+        lane16 = lax.broadcasted_iota(I32, (16, 128), 1)
+        pick_low = jnp.where((sub == 2) & (lane16 == 0), -0.5, 0.0).astype(BF16)
+        pick_high = jnp.where((sub == 3) & (lane16 == 127), 0.5, 0.0).astype(BF16)
+        cross = (((1,), (1,)), ((), ()))
+        spill = lax.dot_general(
+            pick_low, gx_ref[0].astype(BF16), cross, preferred_element_type=F32
+        ) + lax.dot_general(pick_high, gx_ref[3].astype(BF16), cross, preferred_element_type=F32)
+        for b in range(4):
+            rims = jnp.where(
+                sub == 0,
+                -0.5 * gy_ref[b, 8:9],
+                jnp.where(sub == 1, 0.5 * gy_ref[b, T + 7 : T + 8], spill[:, lanes(b)]),
+            )
+            out_ref[0, T : T + SPILL, lanes(b)] = rims.astype(BF16)
 
     @pl.when((slot_odd == 1) & jnp.logical_not(any_used))
     def _():
         out_ref[...] = jnp.zeros_like(out_ref)
+
+
+SCRATCH = [
+    pltpu.VMEM((4, T + 16, 128), F32),
+    pltpu.VMEM((2, T, 128), F32),
+    pltpu.VMEM((4, T, 128), F32),
+    pltpu.VMEM((4, T, 128), F32),
+    pltpu.VMEM((4, T, 128), F32),
+    pltpu.VMEM((4, T, 128), F32),
+    pltpu.VMEM((4, T, 128), F32),
+    pltpu.VMEM((4, T + 16, 128), F32),
+    pltpu.VMEM((C, C), BF16),
+    pltpu.VMEM((3, C, 128), F32),
+    pltpu.VMEM((3, C + 16, 128), F32),
+    pltpu.VMEM((C, C), BF16),
+    pltpu.VMEM((3, C, 128), F32),
+]
 
 
 def run_tiles(tiles, resample, observed, used, image, row_off, col_off, sun, gain):
@@ -227,20 +286,7 @@
             pl.BlockSpec((1, T + SPILL, T), lambda i, *s: (i // 2, 0, 0)),
             pl.BlockSpec((16, 5, 8, C), lambda i, *s: (0, 0, 0, 0)),
         ],
-        scratch_shapes=[
-            pltpu.VMEM((T + 16, T), F32),
-            pltpu.VMEM((16, T), F32),
-            pltpu.VMEM((T, T), F32),
-            pltpu.VMEM((T, T), F32),
-            pltpu.VMEM((T, T), F32),
-            pltpu.VMEM((T, T), F32),
-            pltpu.VMEM((T, T), F32),
-            pltpu.VMEM((T + 16, T), F32),
-            pltpu.VMEM((C, C), BF16),
-            pltpu.VMEM((C + 16, C), F32),
-            pltpu.VMEM((C, C), BF16),
-            pltpu.VMEM((C, C), BF16),
-        ],
+        scratch_shapes=SCRATCH,
     )
     return pl.pallas_call(
         tile_kernel,

time: 379 us -> 339 us (0.89)
  Pallas kernels: 115 us -> 78.4 us
    pallas_call x1, Pallas kernels: 115 us -> 78.4 us  [run_tiles(): pl.pallas_call(tile_kernel, grid_spec=grid_spec, out_shape=[jax.ShapeDtyp...]
where the time goes in v2:
time: 339 us; the launch traced here: 338 us
  waiting for transfers between devices  171 us (50%)
  Pallas kernels  78.4 us (23%)
  starting transfers between devices  49.6 us (15%)
  between operations  15 us (4%)
  other arithmetic  13.8 us (4%)
  local copies, waits for them, and re-layouts  10.1 us (3%)
    all_gather x1, waiting for transfers between devices, per_device(): tiles = lax.all_gather(words, 'dy', axis=0)  100 us
    pallas_call x1, Pallas kernels, run_tiles(): pl.pallas_call(tile_kernel, grid_spec=grid_spec, out_shape=[jax.ShapeDtyp...  78.4 us
    unnamed x3, waiting for transfers between devices  62.9 us
    ppermute x10, starting transfers between devices, shifted(): lax.ppermute(value, axis, pairs if up else [(b, a) for a, b in pairs])  35.9 us
    ppermute x10, waiting for transfers between devices, shifted(): lax.ppermute(value, axis, pairs if up else [(b, a) for a, b in pairs])  7.36 us
    all_to_all x1, starting transfers between devices, per_device(): lax.all_to_all(crop_sums[:, None], 'dy', split_axis=0, concat_axis=0, til...  7.07 us
  transfers between devices with their start and end apart: 14, of which 6 were waited for; matrix products, arithmetic and copies ran while one was open for 5% of the time, Pallas kernels for 0%

profile of v2, /device:TPU:7, one launch (start us, length us, event | category | flops | bytes accessed | tf_op | source)
XLA Modules:
  0.0 338.0 jit_solution(8628571510964808176)
XLA Ops:
  7.2 0.7 fusion.36
  8.0 2.4 collective-permute-start.3
  10.4 4.9 %collective-permute-start.2 = (f32[2,512]{1,0:T(2,128)S(1)}, f32[2,512]{1,0:T(2,128)S(1)}, u32[]{:S(2)}, u32[]{:S(2)}) collective-permute-start(f32[2,512]{1,0:T(2,128)S(1)} %get-tuple-element.20), channel_id=1, source_target_pairs={{0,8},{8,16},{16,24},{24,32},{32,40},{40,48},{48,56},{56,64},{64,7... | collective-permute-start | bytes 12296 | tf_op jit(solution)/shard_map/ppermute | solution.py:338
  15.3 1.3 slice_reduce_fusion.1
  16.7 4.7 %collective-permute-start = (f32[512]{0:T(512)S(1)}, f32[512]{0:T(512)S(1)}, u32[]{:S(2)}, u32[]{:S(2)}) collective-permute-start(f32[512]{0:T(512)S(1)} %get-tuple-element.6), channel_id=1, source_target_pairs={{0,1},{1,2},{2,3},{3,4},{4,5},{5,6},{6,7},{8,9},{9,10},{10,11},{11... | collective-permute-start | bytes 6152 | tf_op jit(solution)/shard_map/ppermute | solution.py:338
  21.4 1.9 collective-permute-start.1
  23.3 1.8 and_or_fusion
  25.1 1.2 collective-permute-done.1
  26.4 2.2 concatenate.18
  28.6 0.1 reshape_squeeze.9
  28.7 0.6 copy.25
  29.4 6.6 %all-to-all-start = ((s32[16,2,2]{2,1,0:T(2,128)}), s32[16,2,2]{2,1,0:T(2,128)S(1)}, u32[]{:S(2)}, u32[]{:S(2)}) async-start(s32[16,2,2]{2,1,0:T(2,128)} %copy.25), calls=%async_computation | async-start | bytes 32768 | tf_op jit(solution)/shard_map/all_to_all | solution.py:394
  36.0 0.0 reduce-scatter.4.cloned.1.call-start
  36.0 0.1 fusion.18
  36.1 0.6 select_reduce_fusion.3
  37.4 0.5 broadcast_compare_fusion
  37.9 0.1 select_reduce_fusion.1
  38.0 0.1 select_reduce_fusion.2
  38.1 0.7 select_reduce_fusion.image
  38.9 0.5 exponential_bitcast_fusion.gain
  39.5 0.6 reshape.116.sun
  40.1 0.6 all-to-all-done
  40.8 0.6 reshape_squeeze.10.row_off
  41.4 0.6 reshape_squeeze.11.col_off
  42.0 100.2 %all-gather.3.cloned.1.call-done = s32[8320,512]{1,0:T(8,128)} async-done(((s32[520,512]{1,0:T(8,128)}), s32[8320,512]{1,0:T(8,128)}) %all-gather.3.cloned.1.call-update) | async-done | bytes 17039376 | tf_op jit(solution)/shard_map/all_gather | solution.py:418
  142.2 78.4 %tiles.1 = (bf16[16,528,512]{2,1,0:T(8,128)(2,1)}, f32[16,5,8,384]{3,2,1,0:T(8,128)}) custom-call(s32[32]{0:T(128)} %get-tuple-element.31.used, s32[32]{0:T(128)} %select_reduce_fusion.image, s32[32]{0:T(128)} %reshape_squeeze.10.row_off, s32[32]{0:T(128)} %reshape_squeeze.11.col_off, f32[48]{0:T(128)} %reshape.116.sun, f32[16]{0:T(128)} %exponential_bitcast_fusion.gain, ...), custom_call_target="tpu_custom_call" | custom-call | tf_op jit(solution)/shard_map/tiles/pallas_call | solution.py:291
  220.7 1.1 copy-done
  221.8 0.1 pad_maximum_fusion.9
  221.9 4.9 %collective-permute-start.8 = (f32[516,2]{1,0:T(8,128)S(1)}, f32[516,2]{1,0:T(8,128)S(1)}, u32[]{:S(2)}, u32[]{:S(2)}) collective-permute-start(f32[516,2]{1,0:T(8,128)S(1)} %get-tuple-element.18), channel_id=1, source_target_pairs={{0,1},{1,2},{2,3},{3,4},{4,5},{5,6},{6,7},{8,9},{9,10},{10,11},{11... | collective-permute-start | bytes 12392 | tf_op jit(solution)/shard_map/ppermute | solution.py:338
  226.8 1.9 collective-permute-start.9
  228.8 1.4 collective-permute-done.8
  230.1 4.8 %collective-permute-done.9 = f32[516,2]{1,0:T(8,128)S(1)} collective-permute-done((f32[516,2]{1,0:T(8,128)S(1)}, f32[516,2]{1,0:T(8,128)S(1)}, u32[]{:S(2)}, u32[]{:S(2)}) %collective-permute-start.9) | collective-permute-done | bytes 4160 | tf_op jit(solution)/shard_map/ppermute | solution.py:338
  234.9 1.6 pad_maximum_fusion.6
  236.5 0.2 slice_reduce_fusion.3
  236.7 0.3 fusion.16
  237.1 0.2 slice_reduce_fusion.2
  237.3 0.7 copy.30
  238.0 7.1 %all-to-all-start.1 = ((f32[16,1,7]{2,1,0:T(1,128)}), f32[16,1,7]{2,1,0:T(1,128)S(1)}, u32[]{:S(2)}, u32[]{:S(2)}) async-start(f32[16,1,7]{2,1,0:T(1,128)} %copy.30), calls=%async_computation.1 | async-start | bytes 16384 | tf_op jit(solution)/shard_map/all_to_all | solution.py:424
  245.1 62.9 %reduce-scatter.4.cloned.1.call-done = bf16[1,528,512]{2,1,0:T(8,128)(2,1)} async-done(((bf16[16,528,512]{2,1,0:T(8,128)(2,1)}), bf16[1,528,512]{2,1,0:T(8,128)(2,1)}) %reduce-scatter.4.cloned.1.call-update) | async-done | bytes 540688
  307.9 0.9 fusion.37
  308.8 2.4 collective-permute-start.4
  311.2 5.0 %collective-permute-start.5 = (f32[512]{0:T(512)S(1)}, f32[512]{0:T(512)S(1)}, u32[]{:S(2)}, u32[]{:S(2)}) collective-permute-start(f32[512]{0:T(512)S(1)} %bitcast.76), channel_id=1, source_target_pairs={{0,8},{8,16},{16,24},{24,32},{32,40},{40,48},{48,56},{56,64},{64,7... | collective-permute-start | bytes 6152 | tf_op jit(solution)/shard_map/ppermute | solution.py:338
  316.2 4.7 %collective-permute-start.6 = (f32[512]{0:T(512)S(1)}, f32[512]{0:T(512)S(1)}, u32[]{:S(2)}, u32[]{:S(2)}) collective-permute-start(f32[512]{0:T(512)S(1)} %bitcast.75), channel_id=1, source_target_pairs={{1,0},{2,1},{3,2},{4,3},{5,4},{6,5},{7,6},{9,8},{10,9},{11,10},{12... | collective-permute-start | bytes 6152 | tf_op jit(solution)/shard_map/ppermute | solution.py:338
  320.9 3.0 collective-permute-start.7
  323.9 4.1 %fusion.1 = f32[514,514]{1,0:T(8,128)S(1)} fusion(f32[516,516]{1,0:T(8,128)} %pad_maximum_fusion.6, f32[516,2]{1,0:T(8,128)S(1)} %collective-permute-done.9, f32[2,512]{1,0:T(2,128)S(1)} %collective-permute-done.3, f32[512,512]{1,0:T(8,128)S(1)} %copy-done, f32[2,512]{1,0:T(2,128)S(1)} %collective-permute-done.2, f32[516,2]{1,0:T(8,128)S(1)} %collective-permute-done.8, ...), kind=kLoop, calls=%fused_computation.2 | loop fusion | flops 3434548 | bytes 5293188 | tf_op jit(solution)/shard_map/jit(_where)/select_n | solution.py:362
  328.1 0.5 reduce_sum.99
  328.6 0.1 convert_element_type.34
  328.8 2.4 fusion.6
  (47 shorter events, 0.4 us)
Async XLA Ops:
  7.2 135.0 %all-gather.3.cloned.1.call-start = ((), (), s32[]{:S(2)}) async-start(), calls=%async_computation.3 | async-start | bytes 18104320 | tf_op jit(solution)/shard_map/all_gather | solution.py:418
  8.0 18.3 %collective-permute-start.3 = (f32[2,512]{1,0:T(2,128)S(1)}, f32[2,512]{1,0:T(2,128)S(1)}, u32[]{:S(2)}, u32[]{:S(2)}) collective-permute-start(f32[2,512]{1,0:T(2,128)S(1)} %get-tuple-element.21), channel_id=1, source_target_pairs={{8,0},{16,8},{24,16},{32,24},{40,32},{48,40},{56,48},{64,56},{72,6... | collective-permute-start | bytes 12296 | tf_op jit(solution)/shard_map/ppermute | solution.py:338
  10.4 15.9 %collective-permute-start.2 = (f32[2,512]{1,0:T(2,128)S(1)}, f32[2,512]{1,0:T(2,128)S(1)}, u32[]{:S(2)}, u32[]{:S(2)}) collective-permute-start(f32[2,512]{1,0:T(2,128)S(1)} %get-tuple-element.20), channel_id=1, source_target_pairs={{0,8},{8,16},{16,24},{24,32},{32,40},{40,48},{48,56},{56,64},{64,7... | collective-permute-start | bytes 12296 | tf_op jit(solution)/shard_map/ppermute | solution.py:338
  16.7 8.4 %collective-permute-start = (f32[512]{0:T(512)S(1)}, f32[512]{0:T(512)S(1)}, u32[]{:S(2)}, u32[]{:S(2)}) collective-permute-start(f32[512]{0:T(512)S(1)} %get-tuple-element.6), channel_id=1, source_target_pairs={{0,1},{1,2},{2,3},{3,4},{4,5},{5,6},{6,7},{8,9},{9,10},{10,11},{11... | collective-permute-start | bytes 6152 | tf_op jit(solution)/shard_map/ppermute | solution.py:338
  21.4 4.9 %collective-permute-start.1 = (f32[512]{0:T(512)S(1)}, f32[512]{0:T(512)S(1)}, u32[]{:S(2)}, u32[]{:S(2)}) collective-permute-start(f32[512]{0:T(512)S(1)} %get-tuple-element.7), channel_id=1, source_target_pairs={{1,0},{2,1},{3,2},{4,3},{5,4},{6,5},{7,6},{9,8},{10,9},{11,10},{12... | collective-permute-start | bytes 6152 | tf_op jit(solution)/shard_map/ppermute | solution.py:338
  26.3 2.3 slice-start
  26.3 9.7 %copy-start.4 = (s32[1,1,16]{2,1,0:T(1,128)S(1)}, s32[1,1,16]{2,1,0:T(1,128)}, u32[]{:S(2)}) copy-start(s32[1,1,16]{2,1,0:T(1,128)} %param.17) | copy-start | bytes 196
  26.4 12.5 %copy-start.5 = (f32[1,16]{1,0:T(1,128)S(1)}, f32[1,16]{1,0:T(1,128)}, u32[]{:S(2)}) copy-start(f32[1,16]{1,0:T(1,128)} %param.13) | copy-start | bytes 196
  26.4 13.0 %copy-start.6 = (f32[1,16]{1,0:T(1,128)S(1)}, f32[1,16]{1,0:T(1,128)}, u32[]{:S(2)}) copy-start(f32[1,16]{1,0:T(1,128)} %param.15) | copy-start | bytes 196
  26.4 13.0 %copy-start.3 = (f32[1,16]{1,0:T(1,128)S(1)}, f32[1,16]{1,0:T(1,128)}, u32[]{:S(2)}) copy-start(f32[1,16]{1,0:T(1,128)} %param.14) | copy-start | bytes 196
  29.4 11.4 %all-to-all-start = ((s32[16,2,2]{2,1,0:T(2,128)}), s32[16,2,2]{2,1,0:T(2,128)S(1)}, u32[]{:S(2)}, u32[]{:S(2)}) async-start(s32[16,2,2]{2,1,0:T(2,128)} %copy.25), calls=%async_computation | async-start | bytes 32768 | tf_op jit(solution)/shard_map/all_to_all | solution.py:394
  36.0 272.0 %reduce-scatter.4.cloned.1.call-start = ((), (), s32[]{:S(2)}) async-start(), calls=%async_computation.4 | async-start | bytes 9191424
  220.5 1.2 copy-start
  221.9 8.2 %collective-permute-start.8 = (f32[516,2]{1,0:T(8,128)S(1)}, f32[516,2]{1,0:T(8,128)S(1)}, u32[]{:S(2)}, u32[]{:S(2)}) collective-permute-start(f32[516,2]{1,0:T(8,128)S(1)} %get-tuple-element.18), channel_id=1, source_target_pairs={{0,1},{1,2},{2,3},{3,4},{4,5},{5,6},{6,7},{8,9},{9,10},{10,11},{11... | collective-permute-start | bytes 12392 | tf_op jit(solution)/shard_map/ppermute | solution.py:338
  226.8 8.1 %collective-permute-start.9 = (f32[516,2]{1,0:T(8,128)S(1)}, f32[516,2]{1,0:T(8,128)S(1)}, u32[]{:S(2)}, u32[]{:S(2)}) collective-permute-start(f32[516,2]{1,0:T(8,128)S(1)} %get-tuple-element.19), channel_id=1, source_target_pairs={{1,0},{2,1},{3,2},{4,3},{5,4},{6,5},{7,6},{9,8},{10,9},{11,10},{12... | collective-permute-start | bytes 12392 | tf_op jit(solution)/shard_map/ppermute | solution.py:338
  228.7 7.8 %copy-start.1 = (f32[16,5,8,384]{3,2,1,0:T(8,128)S(1)}, f32[16,5,8,384]{3,2,1,0:T(8,128)}, u32[]{:S(2)}) copy-start(f32[16,5,8,384]{3,2,1,0:T(8,128)} %get-tuple-element.5) | copy-start | bytes 2949124
  238.0 90.1 %all-to-all-start.1 = ((f32[16,1,7]{2,1,0:T(1,128)}), f32[16,1,7]{2,1,0:T(1,128)S(1)}, u32[]{:S(2)}, u32[]{:S(2)}) async-start(f32[16,1,7]{2,1,0:T(1,128)} %copy.30), calls=%async_computation.1 | async-start | bytes 16384 | tf_op jit(solution)/shard_map/all_to_all | solution.py:424
  308.8 20.0 %collective-permute-start.4 = (f32[512]{0:T(512)S(1)}, f32[512]{0:T(512)S(1)}, u32[]{:S(2)}, u32[]{:S(2)}) collective-permute-start(f32[512]{0:T(512)S(1)} %bitcast.77), channel_id=1, source_target_pairs={{8,0},{16,8},{24,16},{32,24},{40,32},{48,40},{56,48},{64,56},{72,6... | collective-permute-start | bytes 6152 | tf_op jit(solution)/shard_map/ppermute | solution.py:338
  311.2 17.6 %collective-permute-start.5 = (f32[512]{0:T(512)S(1)}, f32[512]{0:T(512)S(1)}, u32[]{:S(2)}, u32[]{:S(2)}) collective-permute-start(f32[512]{0:T(512)S(1)} %bitcast.76), channel_id=1, source_target_pairs={{0,8},{8,16},{16,24},{24,32},{32,40},{40,48},{48,56},{56,64},{64,7... | collective-permute-start | bytes 6152 | tf_op jit(solution)/shard_map/ppermute | solution.py:338
  316.2 12.6 %collective-permute-start.6 = (f32[512]{0:T(512)S(1)}, f32[512]{0:T(512)S(1)}, u32[]{:S(2)}, u32[]{:S(2)}) collective-permute-start(f32[512]{0:T(512)S(1)} %bitcast.75), channel_id=1, source_target_pairs={{1,0},{2,1},{3,2},{4,3},{5,4},{6,5},{7,6},{9,8},{10,9},{11,10},{12... | collective-permute-start | bytes 6152 | tf_op jit(solution)/shard_map/ppermute | solution.py:338
  320.9 7.9 %collective-permute-start.7 = (f32[512]{0:T(512)S(1)}, f32[512]{0:T(512)S(1)}, u32[]{:S(2)}, u32[]{:S(2)}) collective-permute-start(f32[512]{0:T(512)S(1)} %bitcast.74), channel_id=1, source_target_pairs={{0,1},{1,2},{2,3},{3,4},{4,5},{5,6},{6,7},{8,9},{9,10},{10,11},{11... | collective-permute-start | bytes 6152 | tf_op jit(solution)/shard_map/ppermute | solution.py:338
  323.9 4.7 %copy-start.2 = (bf16[1,528,512]{2,1,0:T(8,128)(2,1)S(1)}, bf16[1,528,512]{2,1,0:T(8,128)(2,1)}, u32[]{:S(2)}) copy-start(bf16[1,528,512]{2,1,0:T(8,128)(2,1)} %reduce-scatter.4.cloned.1.call-done) | copy-start | bytes 1622020
Sparse Core Ops, SparseCore 0:
  28.8 113.3 all-gather.2
  220.7 87.1 reduce-scatter.3

commit v3 on v2

--- a/solution.py
+++ b/solution.py
@@ -1,3 +1,5 @@
+import functools
+
 import jax
 import jax.numpy as jnp
 from jax import lax
@@ -5,13 +7,15 @@
 from jax.experimental.pallas import tpu as pltpu
 from jax.sharding import PartitionSpec as P
 
+
 SMOOTHING_WEIGHT = 0.02
 H_SCALE = 8191.0
 A_SCALE = 65534.0
 T = 512
 C = 384
-EXTRA = 8
-SPILL = 16
+HALF = 256
+PIECE = 264
+BACK = 272
 CH = 32
 F32 = jnp.float32
 BF16 = jnp.bfloat16
@@ -30,13 +34,15 @@
     return lax.shift_right_arithmetic(lax.shift_left(word, 16), 16).astype(F32)
 
 
-def tile_kernel(
-    used, image, row_off, col_off, sun, gain,
-    tile_ref, res_ref, obs_ref,
-    out_ref, sums_ref,
-    hbuf, hcol, sx_ref, sy_ref, w_ref, r2_ref, gx_ref, gy_ref,
-    shaded, tbuf, pbuf, weighted, grad,
-):
+def tile_kernel(pieces, operands, *refs):
+    used, image, row_off, col_off, sun, gain = refs[:6]
+    tiles = refs[6 : 6 + operands]
+    (
+        res_ref, obs_ref,
+        out_ref, sums_ref,
+        rim, hbuf, hcol, sx_ref, sy_ref, w_ref, r2_ref, gx_ref, gy_ref,
+        shaded, tbuf, pbuf, weighted, grad,
+    ) = refs[6 + operands :]
     step = pl.program_id(0)
     first = (step // 2) * 2
     slot_odd = step % 2
@@ -53,44 +59,57 @@
     def _():
         sums_ref[...] = jnp.zeros_like(sums_ref)
 
+    for t, sources in enumerate(pieces):
+
+        @pl.when((step == 2 * t) & any_used)
+        def _(sources=sources):
+            for half, (operand, at) in enumerate(sources):
+                ref = tiles[operand]
+                rim[half] = ref[at, HALF:PIECE]
+
+                def unpack(k, _, ref=ref, at=at, half=half):
+                    base = pl.multiple_of(k * CH, CH)
+                    to = pl.multiple_of(base + HALF * half, CH)
+                    for b in range(4):
+                        words = ref[at, pl.ds(base, CH), lanes(b)]
+                        hbuf[b, pl.ds(to + 8, CH)] = high_of(words)
+                        w_ref[b, pl.ds(to, CH)] = low_of(words) * (1.0 / A_SCALE) + 1.0
+                    return 0
+
+                lax.fori_loop(0, HALF // CH, unpack, 0)
+
     @pl.when((slot_odd == 0) & any_used)
     def _():
-        words = tile_ref[0, T : T + EXTRA]
-        high = lax.shift_right_arithmetic(words, 16)
-        low = lax.shift_right_arithmetic(lax.shift_left(words, 16), 16)
-        pieces = jnp.concatenate(
-            [
-                lax.shift_right_arithmetic(high, 8),
-                high & 255,
-                lax.shift_right_arithmetic(low, 8),
-                low & 255,
-            ],
-            axis=0,
-        ).astype(F32).astype(BF16)
         row_id = lax.broadcasted_iota(I32, (32, 256), 0)
         side = lax.broadcasted_iota(I32, (32, 256), 1) // 128
         scale = jnp.where(row_id == 16 * side, 256.0, 0.0) + jnp.where(
             row_id == 16 * side + 8, 1.0, 0.0
         )
-        columns = lax.dot_general(
-            pieces, scale.astype(BF16), (((0,), (0,)), ((), ())), preferred_element_type=F32
-        )
-        for side_id in range(2):
-            hcol[side_id] = columns[:, lanes(side_id)]
-        rims = high.astype(F32)
+        for half in range(2):
+            words = rim[half, :, 0:HALF]
+            high = lax.shift_right_arithmetic(words, 16)
+            low = lax.shift_right_arithmetic(lax.shift_left(words, 16), 16)
+            parts = jnp.concatenate(
+                [
+                    lax.shift_right_arithmetic(high, 8),
+                    high & 255,
+                    lax.shift_right_arithmetic(low, 8),
+                    low & 255,
+                ],
+                axis=0,
+            ).astype(F32).astype(BF16)
+            columns = lax.dot_general(
+                parts, scale.astype(BF16), (((0,), (0,)), ((), ())), preferred_element_type=F32
+            )
+            for side_id in range(2):
+                hcol[side_id, HALF * half : HALF * (half + 1)] = columns[:, lanes(side_id)]
+        top = high_of(rim[0])
+        bottom = high_of(rim[1])
         for b in range(4):
-            hbuf[b, 7:8] = rims[1:2, lanes(b)]
-            hbuf[b, T + 8 : T + 9] = rims[2:3, lanes(b)]
+            hbuf[b, 7:8] = top[1:2, lanes(b)]
+            hbuf[b, T + 8 : T + 9] = bottom[1:2, lanes(b)]
             gy_ref[b, 0:8] = jnp.zeros((8, 128), F32)
             gy_ref[b, T + 8 : T + 16] = jnp.zeros((8, 128), F32)
-
-        def unpack(k, _):
-            base = pl.multiple_of(k * CH, CH)
-            for b in range(4):
-                hbuf[b, pl.ds(base + 8, CH)] = high_of(tile_ref[0, pl.ds(base, CH), lanes(b)])
-            return 0
-
-        lax.fori_loop(0, T // CH, unpack, 0, unroll=2)
 
         def slope(k, _):
             base = pl.multiple_of(k * CH, CH)
@@ -107,17 +126,16 @@
                 sy = (hbuf[b, pl.ds(base + 9, CH)] - hbuf[b, pl.ds(base + 7, CH)]) * (
                     0.5 / H_SCALE
                 )
-                albedo = low_of(tile_ref[0, rows, lanes(b)]) * (1.0 / A_SCALE) + 1.0
                 r = lax.rsqrt(1.0 + sx * sx + sy * sy)
                 sx_ref[b, rows] = sx
                 sy_ref[b, rows] = sy
-                w_ref[b, rows] = albedo * r
+                w_ref[b, rows] = w_ref[b, rows] * r
                 r2_ref[b, rows] = r * r
                 gx_ref[b, rows] = jnp.zeros((CH, 128), F32)
                 gy_ref[b, pl.ds(base + 8, CH)] = jnp.zeros((CH, 128), F32)
             return 0
 
-        lax.fori_loop(0, T // CH, slope, 0, unroll=4)
+        lax.fori_loop(0, T // CH, slope, 0, unroll=2)
 
     @pl.when(mine)
     def _():
@@ -138,7 +156,7 @@
                 tbuf[b, pl.ds(base, CH)] = q * r2_ref[ob + b, rows]
             return 0
 
-        lax.fori_loop(0, C // CH, shade, 0, unroll=4)
+        lax.fori_loop(0, C // CH, shade, 0, unroll=2)
         row_mat = res_ref[0, 0]
         col_mat = res_ref[0, 1]
         first_pass = jnp.dot(row_mat, shaded[...], preferred_element_type=F32).astype(BF16)
@@ -211,13 +229,15 @@
                 )
             return 0
 
-        lax.fori_loop(0, C // CH, pull, 0, unroll=4)
+        lax.fori_loop(0, C // CH, pull, 0, unroll=2)
 
     @pl.when((slot_odd == 1) & any_used)
     def _():
         def stencil(k, _):
             base = pl.multiple_of(k * CH, CH)
             rows = pl.ds(base, CH)
+            half = k // (HALF // CH)
+            to = pl.ds(pl.multiple_of(base - half * HALF, CH), CH)
             here = [gx_ref[b, rows] for b in range(4)]
             right_turn = [pltpu.roll(g, 1, 1) for g in here]
             left_turn = [pltpu.roll(g, 127, 1) for g in here]
@@ -230,25 +250,28 @@
                 up = gy_ref[b, pl.ds(base + 7, CH)]
                 down = gy_ref[b, pl.ds(base + 9, CH)]
                 total = (left - right) + (up - down)
-                out_ref[0, rows, lanes(b)] = (0.5 * total).astype(BF16)
+                out_ref[0, half, to, lanes(b)] = (0.5 * total).astype(BF16)
             return 0
 
-        lax.fori_loop(0, T // CH, stencil, 0, unroll=4)
+        lax.fori_loop(0, T // CH, stencil, 0, unroll=2)
         sub = lax.broadcasted_iota(I32, (16, 128), 0)
         lane16 = lax.broadcasted_iota(I32, (16, 128), 1)
-        pick_low = jnp.where((sub == 2) & (lane16 == 0), -0.5, 0.0).astype(BF16)
-        pick_high = jnp.where((sub == 3) & (lane16 == 127), 0.5, 0.0).astype(BF16)
+        pick_low = jnp.where((sub == 1) & (lane16 == 0), -0.5, 0.0).astype(BF16)
+        pick_high = jnp.where((sub == 2) & (lane16 == 127), 0.5, 0.0).astype(BF16)
         cross = (((1,), (1,)), ((), ()))
-        spill = lax.dot_general(
-            pick_low, gx_ref[0].astype(BF16), cross, preferred_element_type=F32
-        ) + lax.dot_general(pick_high, gx_ref[3].astype(BF16), cross, preferred_element_type=F32)
-        for b in range(4):
-            rims = jnp.where(
-                sub == 0,
-                -0.5 * gy_ref[b, 8:9],
-                jnp.where(sub == 1, 0.5 * gy_ref[b, T + 7 : T + 8], spill[:, lanes(b)]),
+        for half in range(2):
+            rows = slice(HALF * half, HALF * (half + 1))
+            spill = lax.dot_general(
+                pick_low, gx_ref[0, rows].astype(BF16), cross, preferred_element_type=F32
+            ) + lax.dot_general(
+                pick_high, gx_ref[3, rows].astype(BF16), cross, preferred_element_type=F32
             )
-            out_ref[0, T : T + SPILL, lanes(b)] = rims.astype(BF16)
+            for b in range(4):
+                edge = 0.5 * gy_ref[b, T + 7 : T + 8] if half else -0.5 * gy_ref[b, 8:9]
+                rest = spill[:, lanes(b)] if b < 2 else jnp.zeros((16, 128), F32)
+                out_ref[0, half, HALF:BACK, lanes(b)] = jnp.where(sub == 0, edge, rest).astype(
+                    BF16
+                )
 
     @pl.when((slot_odd == 1) & jnp.logical_not(any_used))
     def _():
@@ -256,6 +279,7 @@
 
 
 SCRATCH = [
+    pltpu.VMEM((2, PIECE - HALF, T), I32),
     pltpu.VMEM((4, T + 16, 128), F32),
     pltpu.VMEM((2, T, 128), F32),
     pltpu.VMEM((4, T, 128), F32),
@@ -272,32 +296,151 @@
 ]
 
 
-def run_tiles(tiles, resample, observed, used, image, row_off, col_off, sun, gain):
-    count = tiles.shape[0]
+def run_tiles(arrays, pieces, resample, observed, plan, sun, gain):
+    used, image, row_off, col_off = plan
+    count = len(pieces)
+    tile_specs = [pl.BlockSpec(v.shape, lambda i, *s: (0, 0, 0)) for v in arrays]
     grid_spec = pltpu.PrefetchScalarGridSpec(
         num_scalar_prefetch=6,
         grid=(2 * count,),
-        in_specs=[
-            pl.BlockSpec((1, T + EXTRA, T), lambda i, *s: (i // 2, 0, 0)),
+        in_specs=tile_specs
+        + [
             pl.BlockSpec((1, 2, C, C), lambda i, u, m, *s: (m[i], 0, 0, 0)),
             pl.BlockSpec((1, C, C), lambda i, u, m, *s: (m[i], 0, 0)),
         ],
         out_specs=[
-            pl.BlockSpec((1, T + SPILL, T), lambda i, *s: (i // 2, 0, 0)),
+            pl.BlockSpec((1, 2, BACK, T), lambda i, *s: (i // 2, 0, 0, 0)),
             pl.BlockSpec((16, 5, 8, C), lambda i, *s: (0, 0, 0, 0)),
         ],
         scratch_shapes=SCRATCH,
     )
     return pl.pallas_call(
-        tile_kernel,
+        functools.partial(tile_kernel, pieces, len(arrays)),
         grid_spec=grid_spec,
         out_shape=[
-            jax.ShapeDtypeStruct((count, T + SPILL, T), BF16),
+            jax.ShapeDtypeStruct((count, 2, BACK, T), BF16),
             jax.ShapeDtypeStruct((16, 5, 8, C), F32),
         ],
         compiler_params=pltpu.CompilerParams(dimension_semantics=("arbitrary",)),
-        name="tiles",
-    )(used, image, row_off, col_off, sun, gain, tiles, resample, observed)
+        cost_estimate=pl.CostEstimate(
+            flops=count * 8 * C * C * C, bytes_accessed=count * 8_000_000, transcendentals=0
+        ),
+    )(used, image, row_off, col_off, sun, gain, *arrays, resample, observed)
+
+
+def around(step_x, step_y):
+    return [
+        (4 * y + x, 4 * ((y + step_y) % 4) + (x + step_x) % 4) for y in range(4) for x in range(4)
+    ]
+
+
+STEPS = {"x+": around(1, 0), "x-": around(-1, 0), "y+": around(0, 1), "y-": around(0, -1)}
+NEAR = [(0, 0), (-1, 0), (1, 0), (0, -1), (0, 1)]
+MIDDLE = [(-1, -1), (-1, 1), (1, -1), (1, 1), (2, 0), (0, 2)]
+FAR = [(2, -1), (2, 1), (-1, 2), (1, 2)]
+LAST = [(2, 2)]
+
+
+def send(messages):
+    return {way: lax.ppermute(v, "dy", STEPS[way]) for way, v in messages.items()}
+
+
+def send_middle(near):
+    a = {k: v[0] for k, v in near.items()}
+    b = {k: v[1] for k, v in near.items()}
+    return send(
+        {
+            "x+": jnp.stack([a["x+"], b["y+"], b["y-"]]),
+            "x-": jnp.stack([b["x-"], b["y+"], b["y-"]]),
+            "y+": jnp.stack([a["y+"], a["x+"], a["x-"]]),
+            "y-": jnp.stack([b["y-"], a["x+"], a["x-"]]),
+        }
+    )
+
+
+def send_far(middle):
+    return send(
+        {
+            "x+": jnp.stack([middle["y+"][1], middle["y-"][1]]),
+            "x-": middle["x-"][1:3],
+            "y+": middle["y+"][1:3],
+            "y-": jnp.stack([middle["x+"][2], middle["x-"][2]]),
+        }
+    )
+
+
+def send_last(far, cut):
+    got = send(
+        {
+            "x+": far["y+"][0, :cut],
+            "x-": far["y+"][1, cut:],
+            "y+": far["x-"][0, :cut],
+            "y-": far["x-"][1, cut:],
+        }
+    )
+    return jnp.stack(
+        [
+            jnp.concatenate([got["x+"], got["x-"]]),
+            jnp.concatenate([got["y+"], got["y-"]]),
+        ]
+    )
+
+
+def return_sums(near, middle, far, last, cut):
+    def wide(v):
+        return v.astype(F32)
+
+    def slim(v):
+        return v.astype(BF16)
+
+    got = send(
+        {
+            "x-": last[0, 0, :cut],
+            "x+": last[0, 0, cut:],
+            "y-": last[0, 1, :cut],
+            "y+": last[0, 1, cut:],
+        }
+    )
+
+    def top_added(v, extra):
+        return jnp.concatenate([slim(wide(v[:cut]) + wide(extra)), v[cut:]])
+
+    def low_added(v, extra):
+        return jnp.concatenate([v[:cut], slim(wide(v[cut:]) + wide(extra))])
+
+    got = send(
+        {
+            "x-": far[0:2, 0],
+            "x+": jnp.stack([top_added(far[0, 1], got["y-"]), low_added(far[1, 1], got["y+"])]),
+            "y-": jnp.stack([top_added(far[2, 0], got["x-"]), low_added(far[3, 0], got["x+"])]),
+            "y+": far[2:4, 1],
+        }
+    )
+    a_mm = slim(wide(middle[0, 0]) + wide(got["x-"][0]) + wide(got["y-"][0]))
+    a_mp = slim(wide(middle[1, 0]) + wide(got["x-"][1]))
+    b_mp = slim(wide(middle[1, 1]) + wide(got["y+"][0]))
+    a_pm = slim(wide(middle[2, 0]) + wide(got["y-"][1]))
+    b_pm = slim(wide(middle[2, 1]) + wide(got["x+"][0]))
+    b_pp = slim(wide(middle[3, 1]) + wide(got["x+"][1]) + wide(got["y+"][1]))
+    got = send(
+        {
+            "x-": jnp.stack([middle[4, 0], middle[0, 1], b_mp]),
+            "x+": jnp.stack([middle[4, 1], b_pm, b_pp]),
+            "y-": jnp.stack([middle[5, 0], a_mm, a_pm]),
+            "y+": jnp.stack([middle[5, 1], a_mp, middle[3, 0]]),
+        }
+    )
+    xm, xp, ym, yp = (wide(got[k]) for k in ("x-", "x+", "y-", "y+"))
+    mine = wide(near)
+    got = send(
+        {
+            "x-": slim(jnp.stack([mine[1, 0] + xm[0] + ym[1] + yp[1], mine[1, 1]])),
+            "x+": slim(jnp.stack([mine[2, 0] + ym[2] + yp[2], mine[2, 1] + xp[0]])),
+            "y-": slim(jnp.stack([mine[3, 0] + ym[0], mine[3, 1] + xm[1] + xp[1]])),
+            "y+": slim(jnp.stack([mine[4, 0], mine[4, 1] + xm[2] + xp[2] + yp[0]])),
+        }
+    )
+    return mine[0] + wide(got["x-"]) + wide(got["x+"]) + wide(got["y-"]) + wide(got["y+"])
 
 
 def next_images(used, image):
@@ -398,7 +541,19 @@
     match = recv_plan[0, 0][None, :] == slots[:, None]
     used = jnp.any(match, axis=1).astype(I32)
     image = jnp.sum(jnp.where(match, jnp.arange(16, dtype=I32)[None, :], 0), axis=1)
-    image = next_images(used, image)
+    table = jnp.stack([used, image, row_off, col_off])
+    relative = jnp.array(NEAR + MIDDLE + FAR + LAST, I32)
+    place = lax.axis_index("dy")
+    tile_ids = ((place // 4 + relative[:, 1]) % 4) * 4 + (place % 4 + relative[:, 0]) % 4
+    slot_ids = (2 * tile_ids[:, None] + jnp.arange(2, dtype=I32)[None, :]).reshape(-1)
+    table = jnp.sum(
+        jnp.where(slot_ids[None, :, None] == slots[None, None, :], table[:, None, :], 0), axis=2
+    )
+
+    def plan_of(first, count):
+        part = table[:, 2 * first : 2 * (first + count)]
+        return part[0], next_images(part[0], part[1]), part[2], part[3]
+
     sun = sun_vectors(sun_azimuth[0], sun_elevation[0]).reshape(-1)
     gain = jnp.exp(exposure[0])
 
@@ -406,31 +561,57 @@
     bottom = shifted(heights[:2], "dy", False)
     left = shifted(heights[:, -1], "dx", True)
     right = shifted(heights[:, 0], "dx", False)
-    rims = jnp.stack(
+    sides = pack(quantize(left), quantize(right)).reshape(2, 1, HALF)
+    sides = jnp.concatenate([sides, jnp.zeros((2, 1, T - HALF), I32)], axis=2)
+    ends = pack(quantize(jnp.stack([top[1:2], bottom[0:1]])), 0)
+    words = pack(quantize(heights), jnp.round((albedo - 1.0) * A_SCALE).astype(I32))
+    words = jnp.concatenate(
+        [words.reshape(2, HALF, T), sides, ends, jnp.zeros((2, PIECE - HALF - 2, T), I32)], axis=1
+    )
+    near = send({way: words for way in STEPS})
+    middle = send_middle(near)
+    far = send_far(middle)
+    last = send_last(far, 136)
+    order = ["x+", "x-", "y+", "y-"]
+    whole = ((0, 0), (0, 1))
+    out_near, parts = run_tiles(
+        [words] + [near[k] for k in order],
+        [((n, 0), (n, 1)) for n in range(5)],
+        resample, observed, plan_of(0, 5), sun, gain,
+    )
+    out_middle, more = run_tiles(
+        [middle[k] for k in order],
         [
-            pack(quantize(left), quantize(right)),
-            pack(quantize(top[1]), jnp.zeros_like(quantize(top[1]))),
-            pack(quantize(bottom[0]), jnp.zeros_like(quantize(bottom[0]))),
-        ]
-    )
-    words = pack(quantize(heights), jnp.round((albedo - 1.0) * A_SCALE).astype(I32))
-    words = jnp.concatenate([words, rims, jnp.zeros((EXTRA - 3, T), I32)], axis=0)
-    tiles = lax.all_gather(words, "dy", axis=0)
+            ((2, 1), (0, 1)),
+            ((3, 1), (0, 2)),
+            ((2, 2), (1, 1)),
+            ((3, 2), (1, 2)),
+            ((0, 0), (1, 0)),
+            ((2, 0), (3, 0)),
+        ],
+        resample, observed, plan_of(5, 6), sun, gain,
+    )
+    parts = parts + more
+    out_far, more = run_tiles(
+        [far[k] for k in order],
+        [((0, 0), (1, 0)), ((0, 1), (1, 1)), ((2, 0), (3, 0)), ((2, 1), (3, 1))],
+        resample, observed, plan_of(11, 4), sun, gain,
+    )
+    parts = parts + more
+    out_last, more = run_tiles([last], [whole], resample, observed, plan_of(15, 1), sun, gain)
+    parts = parts + more
     smooth = smoothness(heights, top, bottom)
-    outs, parts = run_tiles(
-        tiles, resample, observed, used, image, row_off, col_off, sun, gain
-    )
     crop_sums = finish_sums(parts)
     arrived = lax.all_to_all(crop_sums[:, None], "dy", split_axis=0, concat_axis=0, tiled=True)
     camera = arrived.sum(axis=0)
-    own = lax.psum_scatter(outs, "dy", scatter_dimension=0).astype(F32)
-    from_below = shifted(own[T], "dy", False)
-    from_above = shifted(own[T + 1], "dy", True)
-    from_right = shifted(own[T + 2], "dx", False)
-    from_left = shifted(own[T + 3], "dx", True)
+    own = return_sums(out_near, out_middle, out_far, out_last, 144)
+    from_below = shifted(own[0, HALF], "dy", False)
+    from_above = shifted(own[1, HALF], "dy", True)
+    from_right = shifted(own[:, HALF + 1, :HALF].reshape(-1), "dx", False)
+    from_left = shifted(own[:, HALF + 2, :HALF].reshape(-1), "dx", True)
     row_ids = lax.broadcasted_iota(I32, (T, T), 0)
     col_ids = lax.broadcasted_iota(I32, (T, T), 1)
-    data = own[:T]
+    data = own[:, :HALF].reshape(T, T)
     data = data + jnp.where(row_ids == T - 1, from_below[None, :], 0.0)
     data = data + jnp.where(row_ids == 0, from_above[None, :], 0.0)
     data = data + jnp.where(col_ids == T - 1, from_right[:, None], 0.0)
@@ -450,6 +631,7 @@
         P("dy", "dx", None, None),
         P("dy", "dx", None),
     )
+
     return jax.shard_map(
         per_device,
         mesh=mesh,

time: 339 us -> 366 us (1.080)
  waiting for transfers between devices: 171 us -> 90.9 us
  starting transfers between devices: 49.6 us -> 93.6 us
  other arithmetic: 13.8 us -> 46.9 us
  local copies, waits for them, and re-layouts: 10.1 us -> 33.5 us
  Pallas kernels: 78.4 us -> 95 us
  between operations: 15 us -> 4.11 us
    all_gather x1 -> x0, waiting for transfers between devices: 100 us -> none  [per_device(): tiles = lax.all_gather(words, 'dy', axis=0)]
    ppermute x0 -> x32, waiting for transfers between devices: none -> 82.3 us  [send(): lax.ppermute(v, 'dy', STEPS[way])]
    unnamed x3 -> x0, waiting for transfers between devices: 62.9 us -> none
    ppermute x0 -> x32, starting transfers between devices: none -> 48.3 us  [send(): lax.ppermute(v, 'dy', STEPS[way])]
    pallas_call x1 -> x4, Pallas kernels: 78.4 us -> 95 us  [run_tiles(): pl.pallas_call(functools.partial(tile_kernel, pieces, len(arrays)), grid_...]
    another operation x0 -> x20, other arithmetic: none -> 14.4 us  [the longest x1 3.08 us: send_middle(): jnp.stack([b['y-'], a['x+'], a['x-']])]
    convert_element_type x1 -> x9, other arithmetic: 0.13 us -> 12.9 us  [the longest x5 8.69 us: wide(): return v.astype(F32)]
    slice x2 -> x17, local copies, waits for them, and re-layouts: 0.9 us -> 12 us  [the longest x3 2.44 us: send_middle(): a = {k: v[0] for k, v in near.items()}]
  transfers between devices with their start and end apart: 14 -> 44, of which waited for: 6 -> 18; matrix products, arithmetic and copies ran while one was open for 5% -> 17% of each run, Pallas kernels for 0% -> 19%
where the time goes in v3:
time: 366 us; the launch traced here: 364 us
  Pallas kernels  95 us (26%)
  starting transfers between devices  93.6 us (26%)
  waiting for transfers between devices  90.9 us (25%)
  other arithmetic  46.9 us (13%)
  local copies, waits for them, and re-layouts  33.5 us (9%)
  between operations  4.11 us (1%)
    pallas_call x4, Pallas kernels, run_tiles(): pl.pallas_call(functools.partial(tile_kernel, pieces, len(arrays)), grid_...  95 us
    ppermute x32, waiting for transfers between devices, send(): lax.ppermute(v, 'dy', STEPS[way])  82.3 us
    ppermute x32, starting transfers between devices, send(): lax.ppermute(v, 'dy', STEPS[way])  48.3 us
    ppermute x10, starting transfers between devices, shifted(): lax.ppermute(value, axis, pairs if up else [(b, a) for a, b in pairs])  33.7 us
    convert_element_type x5, other arithmetic, wide(): return v.astype(F32)  8.69 us
    ppermute x10, waiting for transfers between devices, shifted(): lax.ppermute(value, axis, pairs if up else [(b, a) for a, b in pairs])  8.6 us
  transfers between devices with their start and end apart: 44, of which 18 were waited for; matrix products, arithmetic and copies ran while one was open for 17% of the time, Pallas kernels for 19%

profile of v3, /device:TPU:7, one launch (start us, length us, event | category | flops | bytes accessed | tf_op | source)
XLA Modules:
  0.0 364.1 jit_solution(7681200630241090963)
XLA Ops:
  1.4 2.4 collective-permute-start.3
  3.8 4.9 %collective-permute-start.2 = (f32[2,512]{1,0:T(2,128)S(1)}, f32[2,512]{1,0:T(2,128)S(1)}, u32[]{:S(2)}, u32[]{:S(2)}) collective-permute-start(f32[2,512]{1,0:T(2,128)S(1)} %get-tuple-element.77), channel_id=1, source_target_pairs={{0,8},{8,16},{16,24},{24,32},{32,40},{40,48},{48,56},{56,64},{64,7... | collective-permute-start | bytes 12296 | tf_op jit(solution)/shard_map/ppermute | solution.py:481
  10.1 4.7 %collective-permute-start = (f32[512]{0:T(512)S(1)}, f32[512]{0:T(512)S(1)}, u32[]{:S(2)}, u32[]{:S(2)}) collective-permute-start(f32[512]{0:T(512)S(1)} %get-tuple-element.18), channel_id=1, source_target_pairs={{0,1},{1,2},{2,3},{3,4},{4,5},{5,6},{6,7},{8,9},{9,10},{10,11},{11... | collective-permute-start | bytes 6152 | tf_op jit(solution)/shard_map/ppermute | solution.py:481
  14.8 1.9 collective-permute-start.1
  18.1 6.6 %all-to-all-start = ((s32[16,2,2]{2,1,0:T(2,128)}), s32[16,2,2]{2,1,0:T(2,128)S(1)}, u32[]{:S(2)}, u32[]{:S(2)}) async-start(s32[16,2,2]{2,1,0:T(2,128)} %copy.32), calls=%async_computation | async-start | bytes 32768 | tf_op jit(solution)/shard_map/all_to_all | solution.py:537
  26.3 1.8 and_or_fusion
  35.7 1.6 collective-permute-start.7
  38.0 19.8 %collective-permute-done.4.refs_7_ = s32[2,264,512]{2,1,0:T(8,128)} collective-permute-done((s32[2,264,512]{2,1,0:T(8,128)S(1)}, s32[2,264,512]{2,1,0:T(8,128)}, u32[]{:S(2)}, u32[]{:S(2)}) %collective-permute-start.4) | collective-permute-done | bytes 1081376 | tf_op jit(solution)/shard_map/ppermute | solution.py:345
  62.9 3.1 pad_add_fusion.4
  66.6 2.3 collective-permute-start.8
  69.6 2.4 collective-permute-start.11
  76.1 28.1 %collective-permute-done.10.refs_8_ = s32[3,264,512]{2,1,0:T(8,128)S(1)} collective-permute-done((s32[3,264,512]{2,1,0:T(8,128)}, s32[3,264,512]{2,1,0:T(8,128)S(1)}, u32[]{:S(2)}, u32[]{:S(2)}) %collective-permute-start.10) | collective-permute-done | bytes 1622048 | tf_op jit(solution)/shard_map/ppermute | solution.py:345
  105.3 2.3 slice.554
  111.1 2.4 collective-permute-start.15
  114.8 2.7 collective-permute-start.12
  119.7 4.5 %collective-permute-start.40 = (f32[516,2]{1,0:T(8,128)S(1)}, f32[516,2]{1,0:T(8,128)S(1)}, u32[]{:S(2)}, u32[]{:S(2)}) collective-permute-start(f32[516,2]{1,0:T(8,128)S(1)} %get-tuple-element.75), channel_id=1, source_target_pairs={{0,1},{1,2},{2,3},{3,4},{4,5},{5,6},{6,7},{8,9},{9,10},{10,11},{11... | collective-permute-start | bytes 12392 | tf_op jit(solution)/shard_map/ppermute | solution.py:481
  125.0 2.6 collective-permute-done.40
  127.6 2.1 collective-permute-start.41
  130.4 6.0 %collective-permute-done.41 = f32[516,2]{1,0:T(8,128)S(1)} collective-permute-done((f32[516,2]{1,0:T(8,128)S(1)}, f32[516,2]{1,0:T(8,128)S(1)}, u32[]{:S(2)}, u32[]{:S(2)}) %collective-permute-start.41) | collective-permute-done | bytes 4160 | tf_op jit(solution)/shard_map/ppermute | solution.py:481
  136.4 1.6 pad_maximum_fusion.6
  138.0 28.1 %shard_map.113 = (bf16[5,2,272,512]{3,2,1,0:T(8,128)(2,1)}, f32[16,5,8,384]{3,2,1,0:T(8,128)}) custom-call(s32[10]{0:T(128)} %get-tuple-element.98.refs_0_, s32[10]{0:T(128)} %select_reduce_fusion.3.refs_1_, s32[10]{0:T(128)} %get-tuple-element.96.refs_2_, s32[10]{0:T(128)} %get-tuple-element.95.refs_3_, f32[48]{0:T(128)} %reshape.312.refs_4_, ...), custom_call_target="tpu_custom_call" | custom-call | flops 2264924160 | bytes 40000000 | tf_op jit(solution)/shard_map/pallas_call | solution.py:317
  167.2 24.4 %shard_map.115 = (bf16[4,2,272,512]{3,2,1,0:T(8,128)(2,1)}, f32[16,5,8,384]{3,2,1,0:T(8,128)}) custom-call(s32[8]{0:T(128)} %get-tuple-element.90.refs_0_, s32[8]{0:T(128)} %select_reduce_fusion.6.refs_1_, s32[8]{0:T(128)} %get-tuple-element.88.refs_2_, s32[8]{0:T(128)} %get-tuple-element.87.refs_3_, f32[48]{0:T(128)} %reshape.312.refs_4_, ...), custom_call_target="tpu_custom_call" | custom-call | flops 1811939328 | bytes 32000000 | tf_op jit(solution)/shard_map/pallas_call | solution.py:317
  195.9 1.5 collective-permute-start.20
  198.4 1.6 collective-permute-start.21
  202.2 4.2 %collective-permute-start.16 = (bf16[2,272,512]{2,1,0:T(8,128)(2,1)S(1)}, bf16[2,272,512]{2,1,0:T(8,128)(2,1)}, u32[]{:S(2)}, u32[]{:S(2)}) collective-permute-start(bf16[2,272,512]{2,1,0:T(8,128)(2,1)S(1)} %get-tuple-element.61), channel_id=1, source_target_pairs={{0,32},{8,40},{16,48},{24,56},{32,64},{40,72},{48,80},{56,88},{64,... | collective-permute-start | bytes 1671176 | tf_op jit(solution)/shard_map/ppermute | solution.py:345
  207.4 9.2 %collective-permute-done.20 = s32[128,512]{1,0:T(8,128)S(1)} collective-permute-done((s32[128,512]{1,0:T(8,128)S(1)}, s32[128,512]{1,0:T(8,128)S(1)}, u32[]{:S(2)}, u32[]{:S(2)}) %collective-permute-start.20) | collective-permute-done | bytes 262176 | tf_op jit(solution)/shard_map/ppermute | solution.py:345
  217.8 9.0 %shard_map.116 = (bf16[1,2,272,512]{3,2,1,0:T(8,128)(2,1)}, f32[16,5,8,384]{3,2,1,0:T(8,128)}) custom-call(s32[2]{0:T(128)} %get-tuple-element.86.refs_0_, s32[2]{0:T(128)} %fusion.61.refs_1_, s32[2]{0:T(128)} %get-tuple-element.84.refs_2_, s32[2]{0:T(128)} %get-tuple-element.83.refs_3_, f32[48]{0:T(128)} %reshape.312.refs_4_, ...), custom_call_target="tpu_custom_call" | custom-call | flops 452984832 | bytes 8000000 | tf_op jit(solution)/shard_map/pallas_call | solution.py:317
  227.8 5.1 %collective-permute-start.24 = (bf16[128,512]{1,0:T(8,128)(2,1)S(1)}, bf16[128,512]{1,0:T(8,128)(2,1)S(1)}, u32[]{:S(2)}, u32[]{:S(2)}) collective-permute-start(bf16[128,512]{1,0:T(8,128)(2,1)S(1)} %get-tuple-element.81), channel_id=1, source_target_pairs={{0,8},{8,16},{16,24},{24,0},{32,40},{40,48},{48,56},{56,32},{64,72... | collective-permute-start | bytes 393224 | tf_op jit(solution)/shard_map/ppermute | solution.py:345
  234.8 1.9 collective-permute-start.29
  240.4 4.5 %collective-permute-start.31 = (bf16[2,272,512]{2,1,0:T(8,128)(2,1)S(1)}, bf16[2,272,512]{2,1,0:T(8,128)(2,1)}, u32[]{:S(2)}, u32[]{:S(2)}) collective-permute-start(bf16[2,272,512]{2,1,0:T(8,128)(2,1)S(1)} %pad_maximum_fusion.13), channel_id=1, source_target_pairs={{0,8},{8,16},{16,24},{24,0},{32,40},{40,48},{48,56},{56,32},{64,72... | collective-permute-start | bytes 1671176 | tf_op jit(solution)/shard_map/ppermute | solution.py:345
  247.9 3.2 convert_element_type.256
  251.1 33.4 %shard_map.114 = (bf16[6,2,272,512]{3,2,1,0:T(8,128)(2,1)}, f32[16,5,8,384]{3,2,1,0:T(8,128)}) custom-call(s32[12]{0:T(128)} %get-tuple-element.94.refs_0_, s32[12]{0:T(128)} %select_reduce_fusion.1.refs_1_, s32[12]{0:T(128)} %get-tuple-element.92.refs_2_, s32[12]{0:T(128)} %get-tuple-element.91.refs_3_, f32[48]{0:T(128)} %reshape.312.refs_4_, ...), custom_call_target="tpu_custom_call" | custom-call | flops 2717908992 | bytes 48000000 | tf_op jit(solution)/shard_map/pallas_call | solution.py:317
  284.6 1.6 slice_bitcast_fusion.16
  287.0 2.1 fusion.28
  290.1 6.2 %collective-permute-start.32 = (bf16[3,272,512]{2,1,0:T(8,128)(2,1)}, bf16[3,272,512]{2,1,0:T(8,128)(2,1)}, u32[]{:S(2)}, u32[]{:S(2)}) collective-permute-start(bf16[3,272,512]{2,1,0:T(8,128)(2,1)} %pad_maximum_fusion.10), channel_id=1, source_target_pairs={{0,8},{8,16},{16,24},{24,0},{32,40},{40,48},{48,56},{56,32},{64,72... | collective-permute-start | bytes 2506760 | tf_op jit(solution)/shard_map/ppermute | solution.py:345
  301.8 11.6 %collective-permute-done.32 = bf16[3,272,512]{2,1,0:T(8,128)(2,1)} collective-permute-done((bf16[3,272,512]{2,1,0:T(8,128)(2,1)}, bf16[3,272,512]{2,1,0:T(8,128)(2,1)}, u32[]{:S(2)}, u32[]{:S(2)}) %collective-permute-start.32) | collective-permute-done | bytes 835616 | tf_op jit(solution)/shard_map/ppermute | solution.py:345
  323.1 2.7 collective-permute-start.33
  329.6 5.0 %all-to-all-start.1 = ((f32[16,1,7]{2,1,0:T(1,128)}), f32[16,1,7]{2,1,0:T(1,128)S(1)}, u32[]{:S(2)}, u32[]{:S(2)}) async-start(f32[16,1,7]{2,1,0:T(1,128)} %copy.39), calls=%async_computation.1 | async-start | bytes 16384 | tf_op jit(solution)/shard_map/all_to_all | solution.py:605
  334.7 2.0 collective-permute-done.28
  337.5 3.2 collective-permute-done.34
  341.5 2.0 collective-permute-done.35
  343.5 1.9 fusion.7
  346.0 1.9 collective-permute-start.36
  347.9 5.5 %collective-permute-start.37 = (f32[512]{0:T(512)S(1)}, f32[512]{0:T(512)S(1)}, u32[]{:S(2)}, u32[]{:S(2)}) collective-permute-start(f32[512]{0:T(512)S(1)} %bitcast.269), channel_id=1, source_target_pairs={{0,8},{8,16},{16,24},{24,32},{32,40},{40,48},{48,56},{56,64},{64,7... | collective-permute-start | bytes 6152 | tf_op jit(solution)/shard_map/ppermute | solution.py:481
  353.4 2.9 collective-permute-start.38
  356.3 3.0 collective-permute-start.39
  359.3 1.7 fusion.1
  361.6 2.4 fusion.12
  (228 shorter events, 74.3 us)
Async XLA Ops:
  1.4 30.5 %collective-permute-start.3 = (f32[2,512]{1,0:T(2,128)S(1)}, f32[2,512]{1,0:T(2,128)S(1)}, u32[]{:S(2)}, u32[]{:S(2)}) collective-permute-start(f32[2,512]{1,0:T(2,128)S(1)} %get-tuple-element.78), channel_id=1, source_target_pairs={{8,0},{16,8},{24,16},{32,24},{40,32},{48,40},{56,48},{64,56},{72,6... | collective-permute-start | bytes 12296 | tf_op jit(solution)/shard_map/ppermute | solution.py:481
  3.8 28.1 %collective-permute-start.2 = (f32[2,512]{1,0:T(2,128)S(1)}, f32[2,512]{1,0:T(2,128)S(1)}, u32[]{:S(2)}, u32[]{:S(2)}) collective-permute-start(f32[2,512]{1,0:T(2,128)S(1)} %get-tuple-element.77), channel_id=1, source_target_pairs={{0,8},{8,16},{16,24},{24,32},{32,40},{40,48},{48,56},{56,64},{64,7... | collective-permute-start | bytes 12296 | tf_op jit(solution)/shard_map/ppermute | solution.py:481
  10.1 21.8 %collective-permute-start = (f32[512]{0:T(512)S(1)}, f32[512]{0:T(512)S(1)}, u32[]{:S(2)}, u32[]{:S(2)}) collective-permute-start(f32[512]{0:T(512)S(1)} %get-tuple-element.18), channel_id=1, source_target_pairs={{0,1},{1,2},{2,3},{3,4},{4,5},{5,6},{6,7},{8,9},{9,10},{10,11},{11... | collective-permute-start | bytes 6152 | tf_op jit(solution)/shard_map/ppermute | solution.py:481
  14.8 17.1 %collective-permute-start.1 = (f32[512]{0:T(512)S(1)}, f32[512]{0:T(512)S(1)}, u32[]{:S(2)}, u32[]{:S(2)}) collective-permute-start(f32[512]{0:T(512)S(1)} %get-tuple-element.19), channel_id=1, source_target_pairs={{1,0},{2,1},{3,2},{4,3},{5,4},{6,5},{7,6},{9,8},{10,9},{11,10},{12... | collective-permute-start | bytes 6152 | tf_op jit(solution)/shard_map/ppermute | solution.py:481
  18.1 11.7 %all-to-all-start = ((s32[16,2,2]{2,1,0:T(2,128)}), s32[16,2,2]{2,1,0:T(2,128)S(1)}, u32[]{:S(2)}, u32[]{:S(2)}) async-start(s32[16,2,2]{2,1,0:T(2,128)} %copy.32), calls=%async_computation | async-start | bytes 32768 | tf_op jit(solution)/shard_map/all_to_all | solution.py:537
  32.1 27.0 %copy-start.3 = (s32[2,264,512]{2,1,0:T(8,128)}, s32[2,264,512]{2,1,0:T(8,128)S(1)}, u32[]{:S(2)}) copy-start(s32[2,264,512]{2,1,0:T(8,128)S(1)} %fusion.9.refs_6_) | copy-start | bytes 3244036
  32.1 26.9 %collective-permute-start.6 = (s32[2,264,512]{2,1,0:T(8,128)S(1)}, s32[2,264,512]{2,1,0:T(8,128)S(1)}, u32[]{:S(2)}, u32[]{:S(2)}) collective-permute-start(s32[2,264,512]{2,1,0:T(8,128)S(1)} %fusion.9.refs_6_), channel_id=1, source_target_pairs={{0,32},{8,40},{16,48},{24,56},{32,64},{40,72},{48,80},{56,88},{64,... | collective-permute-start | bytes 3244040 | tf_op jit(solution)/shard_map/ppermute | solution.py:345
  33.4 24.5 %collective-permute-start.4 = (s32[2,264,512]{2,1,0:T(8,128)S(1)}, s32[2,264,512]{2,1,0:T(8,128)}, u32[]{:S(2)}, u32[]{:S(2)}) collective-permute-start(s32[2,264,512]{2,1,0:T(8,128)S(1)} %fusion.9.refs_6_), channel_id=1, source_target_pairs={{0,8},{8,16},{16,24},{24,0},{32,40},{40,48},{48,56},{56,32},{64,72... | collective-permute-start | bytes 3244040 | tf_op jit(solution)/shard_map/ppermute | solution.py:345
  33.9 26.6 %collective-permute-start.5 = (s32[2,264,512]{2,1,0:T(8,128)S(1)}, s32[2,264,512]{2,1,0:T(8,128)}, u32[]{:S(2)}, u32[]{:S(2)}) collective-permute-start(s32[2,264,512]{2,1,0:T(8,128)S(1)} %fusion.9.refs_6_), channel_id=1, source_target_pairs={{0,24},{8,0},{16,8},{24,16},{32,56},{40,32},{48,40},{56,48},{64,88... | collective-permute-start | bytes 3244040 | tf_op jit(solution)/shard_map/ppermute | solution.py:345
  35.7 26.1 %collective-permute-start.7 = (s32[2,264,512]{2,1,0:T(8,128)S(1)}, s32[2,264,512]{2,1,0:T(8,128)S(1)}, u32[]{:S(2)}, u32[]{:S(2)}) collective-permute-start(s32[2,264,512]{2,1,0:T(8,128)S(1)} %fusion.9.refs_6_), channel_id=1, source_target_pairs={{0,96},{8,104},{16,112},{24,120},{32,0},{40,8},{48,16},{56,24},{64... | collective-permute-start | bytes 3244040 | tf_op jit(solution)/shard_map/ppermute | solution.py:345
  66.0 38.2 %collective-permute-start.10 = (s32[3,264,512]{2,1,0:T(8,128)}, s32[3,264,512]{2,1,0:T(8,128)S(1)}, u32[]{:S(2)}, u32[]{:S(2)}) collective-permute-start(s32[3,264,512]{2,1,0:T(8,128)} %get-tuple-element.70), channel_id=1, source_target_pairs={{0,32},{8,40},{16,48},{24,56},{32,64},{40,72},{48,80},{56,88},{64,... | collective-permute-start | bytes 4866056 | tf_op jit(solution)/shard_map/ppermute | solution.py:345
  66.3 39.0 %collective-permute-start.9 = (s32[3,264,512]{2,1,0:T(8,128)}, s32[3,264,512]{2,1,0:T(8,128)}, u32[]{:S(2)}, u32[]{:S(2)}) collective-permute-start(s32[3,264,512]{2,1,0:T(8,128)} %get-tuple-element.69), channel_id=1, source_target_pairs={{0,24},{8,0},{16,8},{24,16},{32,56},{40,32},{48,40},{56,48},{64,88... | collective-permute-start | bytes 4866056 | tf_op jit(solution)/shard_map/ppermute | solution.py:345
  66.6 42.3 %collective-permute-start.8 = (s32[3,264,512]{2,1,0:T(8,128)}, s32[3,264,512]{2,1,0:T(8,128)}, u32[]{:S(2)}, u32[]{:S(2)}) collective-permute-start(s32[3,264,512]{2,1,0:T(8,128)} %get-tuple-element.68), channel_id=1, source_target_pairs={{0,8},{8,16},{16,24},{24,0},{32,40},{40,48},{48,56},{56,32},{64,72... | collective-permute-start | bytes 4866056 | tf_op jit(solution)/shard_map/ppermute | solution.py:345
  69.6 44.0 %collective-permute-start.11 = (s32[3,264,512]{2,1,0:T(8,128)}, s32[3,264,512]{2,1,0:T(8,128)}, u32[]{:S(2)}, u32[]{:S(2)}) collective-permute-start(s32[3,264,512]{2,1,0:T(8,128)} %get-tuple-element.67), channel_id=1, source_target_pairs={{0,96},{8,104},{16,112},{24,120},{32,0},{40,8},{48,16},{56,24},{64... | collective-permute-start | bytes 4866056 | tf_op jit(solution)/shard_map/ppermute | solution.py:345
  105.3 60.9 %collective-permute-start.14 = (s32[2,264,512]{2,1,0:T(8,128)}, s32[2,264,512]{2,1,0:T(8,128)}, u32[]{:S(2)}, u32[]{:S(2)}) collective-permute-start(s32[2,264,512]{2,1,0:T(8,128)} %slice.555), channel_id=1, source_target_pairs={{0,32},{8,40},{16,48},{24,56},{32,64},{40,72},{48,80},{56,88},{64,... | collective-permute-start | bytes 3244040 | tf_op jit(solution)/shard_map/ppermute | solution.py:345
  107.6 58.5 %collective-permute-start.13 = (s32[2,264,512]{2,1,0:T(8,128)}, s32[2,264,512]{2,1,0:T(8,128)}, u32[]{:S(2)}, u32[]{:S(2)}) collective-permute-start(s32[2,264,512]{2,1,0:T(8,128)} %slice.554), channel_id=1, source_target_pairs={{0,24},{8,0},{16,8},{24,16},{32,56},{40,32},{48,40},{56,48},{64,88... | collective-permute-start | bytes 3244040 | tf_op jit(solution)/shard_map/ppermute | solution.py:345
  111.1 55.1 %collective-permute-start.15 = (s32[2,264,512]{2,1,0:T(8,128)}, s32[2,264,512]{2,1,0:T(8,128)}, u32[]{:S(2)}, u32[]{:S(2)}) collective-permute-start(s32[2,264,512]{2,1,0:T(8,128)} %pad_add_fusion.10), channel_id=1, source_target_pairs={{0,96},{8,104},{16,112},{24,120},{32,0},{40,8},{48,16},{56,24},{64... | collective-permute-start | bytes 3244040 | tf_op jit(solution)/shard_map/ppermute | solution.py:345
  114.8 51.3 %collective-permute-start.12 = (s32[2,264,512]{2,1,0:T(8,128)S(1)}, s32[2,264,512]{2,1,0:T(8,128)S(1)}, u32[]{:S(2)}, u32[]{:S(2)}) collective-permute-start(s32[2,264,512]{2,1,0:T(8,128)S(1)} %pad_add_fusion.9), channel_id=1, source_target_pairs={{0,8},{8,16},{16,24},{24,0},{32,40},{40,48},{48,56},{56,32},{64,72... | collective-permute-start | bytes 3244040 | tf_op jit(solution)/shard_map/ppermute | solution.py:345
  119.7 7.8 %collective-permute-start.40 = (f32[516,2]{1,0:T(8,128)S(1)}, f32[516,2]{1,0:T(8,128)S(1)}, u32[]{:S(2)}, u32[]{:S(2)}) collective-permute-start(f32[516,2]{1,0:T(8,128)S(1)} %get-tuple-element.75), channel_id=1, source_target_pairs={{0,1},{1,2},{2,3},{3,4},{4,5},{5,6},{6,7},{8,9},{9,10},{10,11},{11... | collective-permute-start | bytes 12392 | tf_op jit(solution)/shard_map/ppermute | solution.py:481
  127.6 8.9 %collective-permute-start.41 = (f32[516,2]{1,0:T(8,128)S(1)}, f32[516,2]{1,0:T(8,128)S(1)}, u32[]{:S(2)}, u32[]{:S(2)}) collective-permute-start(f32[516,2]{1,0:T(8,128)S(1)} %get-tuple-element.76), channel_id=1, source_target_pairs={{1,0},{2,1},{3,2},{4,3},{5,4},{6,5},{7,6},{9,8},{10,9},{11,10},{12... | collective-permute-start | bytes 12392 | tf_op jit(solution)/shard_map/ppermute | solution.py:481
  194.9 21.7 %collective-permute-start.19 = (s32[136,512]{1,0:T(8,128)S(1)}, s32[136,512]{1,0:T(8,128)S(1)}, u32[]{:S(2)}, u32[]{:S(2)}) collective-permute-start(s32[136,512]{1,0:T(8,128)S(1)} %slice_bitcast_fusion.10), channel_id=1, source_target_pairs={{0,8},{8,16},{16,24},{24,0},{32,40},{40,48},{48,56},{56,32},{64,72... | collective-permute-start | bytes 835592 | tf_op jit(solution)/shard_map/ppermute | solution.py:345
  195.9 20.6 %collective-permute-start.20 = (s32[128,512]{1,0:T(8,128)S(1)}, s32[128,512]{1,0:T(8,128)S(1)}, u32[]{:S(2)}, u32[]{:S(2)}) collective-permute-start(s32[128,512]{1,0:T(8,128)S(1)} %slice_bitcast_fusion.20), channel_id=1, source_target_pairs={{0,24},{8,0},{16,8},{24,16},{32,56},{40,32},{48,40},{56,48},{64,88... | collective-permute-start | bytes 786440 | tf_op jit(solution)/shard_map/ppermute | solution.py:345
  198.4 18.2 %collective-permute-start.21 = (s32[136,512]{1,0:T(8,128)S(1)}, s32[136,512]{1,0:T(8,128)S(1)}, u32[]{:S(2)}, u32[]{:S(2)}) collective-permute-start(s32[136,512]{1,0:T(8,128)S(1)} %slice_bitcast_fusion.9), channel_id=1, source_target_pairs={{0,32},{8,40},{16,48},{24,56},{32,64},{40,72},{48,80},{56,88},{64,... | collective-permute-start | bytes 835592 | tf_op jit(solution)/shard_map/ppermute | solution.py:345
  201.0 15.6 %collective-permute-start.22 = (s32[128,512]{1,0:T(8,128)S(1)}, s32[128,512]{1,0:T(8,128)S(1)}, u32[]{:S(2)}, u32[]{:S(2)}) collective-permute-start(s32[128,512]{1,0:T(8,128)S(1)} %slice_bitcast_fusion.19), channel_id=1, source_target_pairs={{0,96},{8,104},{16,112},{24,120},{32,0},{40,8},{48,16},{56,24},{64... | collective-permute-start | bytes 786440 | tf_op jit(solution)/shard_map/ppermute | solution.py:345
  202.2 84.0 %collective-permute-start.16 = (bf16[2,272,512]{2,1,0:T(8,128)(2,1)S(1)}, bf16[2,272,512]{2,1,0:T(8,128)(2,1)}, u32[]{:S(2)}, u32[]{:S(2)}) collective-permute-start(bf16[2,272,512]{2,1,0:T(8,128)(2,1)S(1)} %get-tuple-element.61), channel_id=1, source_target_pairs={{0,32},{8,40},{16,48},{24,56},{32,64},{40,72},{48,80},{56,88},{64,... | collective-permute-start | bytes 1671176 | tf_op jit(solution)/shard_map/ppermute | solution.py:345
  216.6 69.7 %collective-permute-start.18 = (bf16[2,272,512]{2,1,0:T(8,128)(2,1)S(1)}, bf16[2,272,512]{2,1,0:T(8,128)(2,1)}, u32[]{:S(2)}, u32[]{:S(2)}) collective-permute-start(bf16[2,272,512]{2,1,0:T(8,128)(2,1)S(1)} %get-tuple-element.62), channel_id=1, source_target_pairs={{0,24},{8,0},{16,8},{24,16},{32,56},{40,32},{48,40},{56,48},{64,88... | collective-permute-start | bytes 1671176 | tf_op jit(solution)/shard_map/ppermute | solution.py:345
  227.8 7.0 %collective-permute-start.24 = (bf16[128,512]{1,0:T(8,128)(2,1)S(1)}, bf16[128,512]{1,0:T(8,128)(2,1)S(1)}, u32[]{:S(2)}, u32[]{:S(2)}) collective-permute-start(bf16[128,512]{1,0:T(8,128)(2,1)S(1)} %get-tuple-element.81), channel_id=1, source_target_pairs={{0,8},{8,16},{16,24},{24,0},{32,40},{40,48},{48,56},{56,32},{64,72... | collective-permute-start | bytes 393224 | tf_op jit(solution)/shard_map/ppermute | solution.py:345
  232.9 5.0 %collective-permute-start.30 = (bf16[128,512]{1,0:T(8,128)(2,1)S(1)}, bf16[128,512]{1,0:T(8,128)(2,1)S(1)}, u32[]{:S(2)}, u32[]{:S(2)}) collective-permute-start(bf16[128,512]{1,0:T(8,128)(2,1)S(1)} %get-tuple-element.82), channel_id=1, source_target_pairs={{0,32},{8,40},{16,48},{24,56},{32,64},{40,72},{48,80},{56,88},{64,... | collective-permute-start | bytes 393224 | tf_op jit(solution)/shard_map/ppermute | solution.py:345
  233.9 5.3 %collective-permute-start.23 = (bf16[144,512]{1,0:T(8,128)(2,1)S(1)}, bf16[144,512]{1,0:T(8,128)(2,1)S(1)}, u32[]{:S(2)}, u32[]{:S(2)}) collective-permute-start(bf16[144,512]{1,0:T(8,128)(2,1)S(1)} %get-tuple-element.79), channel_id=1, source_target_pairs={{0,24},{8,0},{16,8},{24,16},{32,56},{40,32},{48,40},{56,48},{64,88... | collective-permute-start | bytes 442376 | tf_op jit(solution)/shard_map/ppermute | solution.py:345
  234.8 4.4 %collective-permute-start.29 = (bf16[144,512]{1,0:T(8,128)(2,1)S(1)}, bf16[144,512]{1,0:T(8,128)(2,1)S(1)}, u32[]{:S(2)}, u32[]{:S(2)}) collective-permute-start(bf16[144,512]{1,0:T(8,128)(2,1)S(1)} %get-tuple-element.80), channel_id=1, source_target_pairs={{0,96},{8,104},{16,112},{24,120},{32,0},{40,8},{48,16},{56,24},{64... | collective-permute-start | bytes 442376 | tf_op jit(solution)/shard_map/ppermute | solution.py:345
  240.4 45.9 %collective-permute-start.31 = (bf16[2,272,512]{2,1,0:T(8,128)(2,1)S(1)}, bf16[2,272,512]{2,1,0:T(8,128)(2,1)}, u32[]{:S(2)}, u32[]{:S(2)}) collective-permute-start(bf16[2,272,512]{2,1,0:T(8,128)(2,1)S(1)} %pad_maximum_fusion.13), channel_id=1, source_target_pairs={{0,8},{8,16},{16,24},{24,0},{32,40},{40,48},{48,56},{56,32},{64,72... | collective-permute-start | bytes 1671176 | tf_op jit(solution)/shard_map/ppermute | solution.py:345
  245.8 40.4 %collective-permute-start.25 = (bf16[2,272,512]{2,1,0:T(8,128)(2,1)}, bf16[2,272,512]{2,1,0:T(8,128)(2,1)}, u32[]{:S(2)}, u32[]{:S(2)}) collective-permute-start(bf16[2,272,512]{2,1,0:T(8,128)(2,1)} %pad_maximum_fusion.11), channel_id=1, source_target_pairs={{0,96},{8,104},{16,112},{24,120},{32,0},{40,8},{48,16},{56,24},{64... | collective-permute-start | bytes 1671176 | tf_op jit(solution)/shard_map/ppermute | solution.py:345
  290.1 23.2 %collective-permute-start.32 = (bf16[3,272,512]{2,1,0:T(8,128)(2,1)}, bf16[3,272,512]{2,1,0:T(8,128)(2,1)}, u32[]{:S(2)}, u32[]{:S(2)}) collective-permute-start(bf16[3,272,512]{2,1,0:T(8,128)(2,1)} %pad_maximum_fusion.10), channel_id=1, source_target_pairs={{0,8},{8,16},{16,24},{24,0},{32,40},{40,48},{48,56},{56,32},{64,72... | collective-permute-start | bytes 2506760 | tf_op jit(solution)/shard_map/ppermute | solution.py:345
  297.3 18.0 %collective-permute-start.17 = (bf16[3,272,512]{2,1,0:T(8,128)(2,1)}, bf16[3,272,512]{2,1,0:T(8,128)(2,1)}, u32[]{:S(2)}, u32[]{:S(2)}) collective-permute-start(bf16[3,272,512]{2,1,0:T(8,128)(2,1)} %pad_maximum_fusion.7), channel_id=1, source_target_pairs={{0,24},{8,0},{16,8},{24,16},{32,56},{40,32},{48,40},{56,48},{64,88... | collective-permute-start | bytes 2506760 | tf_op jit(solution)/shard_map/ppermute | solution.py:345
  298.3 18.8 %collective-permute-start.26 = (bf16[3,272,512]{2,1,0:T(8,128)(2,1)}, bf16[3,272,512]{2,1,0:T(8,128)(2,1)}, u32[]{:S(2)}, u32[]{:S(2)}) collective-permute-start(bf16[3,272,512]{2,1,0:T(8,128)(2,1)} %pad_maximum_fusion.8), channel_id=1, source_target_pairs={{0,96},{8,104},{16,112},{24,120},{32,0},{40,8},{48,16},{56,24},{64... | collective-permute-start | bytes 2506760 | tf_op jit(solution)/shard_map/ppermute | solution.py:345
  299.4 20.0 %collective-permute-start.27 = (bf16[3,272,512]{2,1,0:T(8,128)(2,1)}, bf16[3,272,512]{2,1,0:T(8,128)(2,1)}, u32[]{:S(2)}, u32[]{:S(2)}) collective-permute-start(bf16[3,272,512]{2,1,0:T(8,128)(2,1)} %pad_maximum_fusion.9), channel_id=1, source_target_pairs={{0,32},{8,40},{16,48},{24,56},{32,64},{40,72},{48,80},{56,88},{64,... | collective-permute-start | bytes 2506760 | tf_op jit(solution)/shard_map/ppermute | solution.py:345
  322.2 14.5 %collective-permute-start.28 = (bf16[2,272,512]{2,1,0:T(8,128)(2,1)S(1)}, bf16[2,272,512]{2,1,0:T(8,128)(2,1)S(1)}, u32[]{:S(2)}, u32[]{:S(2)}) collective-permute-start(bf16[2,272,512]{2,1,0:T(8,128)(2,1)S(1)} %pad_maximum_fusion.12), channel_id=1, source_target_pairs={{0,24},{8,0},{16,8},{24,16},{32,56},{40,32},{48,40},{56,48},{64,88... | collective-permute-start | bytes 1671176 | tf_op jit(solution)/shard_map/ppermute | solution.py:345
  323.1 14.4 %collective-permute-start.33 = (bf16[2,272,512]{2,1,0:T(8,128)(2,1)}, bf16[2,272,512]{2,1,0:T(8,128)(2,1)S(1)}, u32[]{:S(2)}, u32[]{:S(2)}) collective-permute-start(bf16[2,272,512]{2,1,0:T(8,128)(2,1)} %pad_maximum_fusion.14), channel_id=1, source_target_pairs={{0,8},{8,16},{16,24},{24,0},{32,40},{40,48},{48,56},{56,32},{64,72... | collective-permute-start | bytes 1671176 | tf_op jit(solution)/shard_map/ppermute | solution.py:345
  326.6 14.0 %collective-permute-start.34 = (bf16[2,272,512]{2,1,0:T(8,128)(2,1)}, bf16[2,272,512]{2,1,0:T(8,128)(2,1)S(1)}, u32[]{:S(2)}, u32[]{:S(2)}) collective-permute-start(bf16[2,272,512]{2,1,0:T(8,128)(2,1)} %pad_maximum_fusion.15), channel_id=1, source_target_pairs={{0,96},{8,104},{16,112},{24,120},{32,0},{40,8},{48,16},{56,24},{64... | collective-permute-start | bytes 1671176 | tf_op jit(solution)/shard_map/ppermute | solution.py:345
  327.6 15.9 %collective-permute-start.35 = (bf16[2,272,512]{2,1,0:T(8,128)(2,1)}, bf16[2,272,512]{2,1,0:T(8,128)(2,1)}, u32[]{:S(2)}, u32[]{:S(2)}) collective-permute-start(bf16[2,272,512]{2,1,0:T(8,128)(2,1)} %pad_maximum_fusion.16), channel_id=1, source_target_pairs={{0,32},{8,40},{16,48},{24,56},{32,64},{40,72},{48,80},{56,88},{64,... | collective-permute-start | bytes 1671176 | tf_op jit(solution)/shard_map/ppermute | solution.py:345
  329.6 31.3 %all-to-all-start.1 = ((f32[16,1,7]{2,1,0:T(1,128)}), f32[16,1,7]{2,1,0:T(1,128)S(1)}, u32[]{:S(2)}, u32[]{:S(2)}) async-start(f32[16,1,7]{2,1,0:T(1,128)} %copy.39), calls=%async_computation.1 | async-start | bytes 16384 | tf_op jit(solution)/shard_map/all_to_all | solution.py:605
  334.6 24.6 %copy-start.1 = (f32[516,516]{1,0:T(8,128)S(1)}, f32[516,516]{1,0:T(8,128)}, u32[]{:S(2)}) copy-start(f32[516,516]{1,0:T(8,128)} %pad_maximum_fusion.6) | copy-start | bytes 3195076
  334.6 24.6 %copy-start.12 = (f32[516,2]{1,0:T(8,128)S(1)}, f32[516,2]{1,0:T(8,128)}, u32[]{:S(2)}) copy-start(f32[516,2]{1,0:T(8,128)} %copy-done.11) | copy-start | bytes 12388
  334.6 24.6 %copy-start.14 = (f32[516,2]{1,0:T(8,128)S(1)}, f32[516,2]{1,0:T(8,128)}, u32[]{:S(2)}) copy-start(f32[516,2]{1,0:T(8,128)} %copy-done.13) | copy-start | bytes 12388
  346.0 15.6 %collective-permute-start.36 = (f32[512]{0:T(512)}, f32[512]{0:T(512)S(1)}, u32[]{:S(2)}, u32[]{:S(2)}) collective-permute-start(f32[512]{0:T(512)} %bitcast.76), channel_id=1, source_target_pairs={{8,0},{16,8},{24,16},{32,24},{40,32},{48,40},{56,48},{64,56},{72,6... | collective-permute-start | bytes 6152 | tf_op jit(solution)/shard_map/ppermute | solution.py:481
  347.9 13.7 %collective-permute-start.37 = (f32[512]{0:T(512)S(1)}, f32[512]{0:T(512)S(1)}, u32[]{:S(2)}, u32[]{:S(2)}) collective-permute-start(f32[512]{0:T(512)S(1)} %bitcast.269), channel_id=1, source_target_pairs={{0,8},{8,16},{16,24},{24,32},{32,40},{40,48},{48,56},{56,64},{64,7... | collective-permute-start | bytes 6152 | tf_op jit(solution)/shard_map/ppermute | solution.py:481
  353.4 8.2 %collective-permute-start.38 = (f32[512]{0:T(512)S(1)}, f32[512]{0:T(512)S(1)}, u32[]{:S(2)}, u32[]{:S(2)}) collective-permute-start(f32[512]{0:T(512)S(1)} %bitcast.268), channel_id=1, source_target_pairs={{1,0},{2,1},{3,2},{4,3},{5,4},{6,5},{7,6},{9,8},{10,9},{11,10},{12... | collective-permute-start | bytes 6152 | tf_op jit(solution)/shard_map/ppermute | solution.py:481
  356.3 5.4 %collective-permute-start.39 = (f32[512]{0:T(512)S(1)}, f32[512]{0:T(512)S(1)}, u32[]{:S(2)}, u32[]{:S(2)}) collective-permute-start(f32[512]{0:T(512)S(1)} %bitcast.267), channel_id=1, source_target_pairs={{0,1},{1,2},{2,3},{3,4},{4,5},{5,6},{6,7},{8,9},{9,10},{10,11},{11... | collective-permute-start | bytes 6152 | tf_op jit(solution)/shard_map/ppermute | solution.py:481
  (24 other events, 113.2 us)

commit v4 on v3

--- a/solution.py
+++ b/solution.py
@@ -335,10 +335,12 @@
 
 
 STEPS = {"x+": around(1, 0), "x-": around(-1, 0), "y+": around(0, 1), "y-": around(0, -1)}
+STEPS["x2"] = around(2, 0)
+STEPS["y2"] = around(0, 2)
+WAYS = ("x+", "x-", "y+", "y-")
 NEAR = [(0, 0), (-1, 0), (1, 0), (0, -1), (0, 1)]
 MIDDLE = [(-1, -1), (-1, 1), (1, -1), (1, 1), (2, 0), (0, 2)]
-FAR = [(2, -1), (2, 1), (-1, 2), (1, 2)]
-LAST = [(2, 2)]
+FAR = [(2, -1), (2, 1), (-1, 2), (1, 2), (2, 2)]
 
 
 def send(messages):
@@ -365,57 +367,31 @@
             "x-": middle["x-"][1:3],
             "y+": middle["y+"][1:3],
             "y-": jnp.stack([middle["x+"][2], middle["x-"][2]]),
+            "x2": middle["y+"][0:1],
+            "y2": middle["x-"][0:1],
         }
     )
 
 
-def send_last(far, cut):
-    got = send(
-        {
-            "x+": far["y+"][0, :cut],
-            "x-": far["y+"][1, cut:],
-            "y+": far["x-"][0, :cut],
-            "y-": far["x-"][1, cut:],
-        }
-    )
-    return jnp.stack(
-        [
-            jnp.concatenate([got["x+"], got["x-"]]),
-            jnp.concatenate([got["y+"], got["y-"]]),
-        ]
-    )
-
-
-def return_sums(near, middle, far, last, cut):
+def return_sums(near, middle, far):
     def wide(v):
         return v.astype(F32)
 
     def slim(v):
         return v.astype(BF16)
-
-    got = send(
-        {
-            "x-": last[0, 0, :cut],
-            "x+": last[0, 0, cut:],
-            "y-": last[0, 1, :cut],
-            "y+": last[0, 1, cut:],
-        }
-    )
-
-    def top_added(v, extra):
-        return jnp.concatenate([slim(wide(v[:cut]) + wide(extra)), v[cut:]])
-
-    def low_added(v, extra):
-        return jnp.concatenate([v[:cut], slim(wide(v[cut:]) + wide(extra))])
 
     got = send(
         {
             "x-": far[0:2, 0],
-            "x+": jnp.stack([top_added(far[0, 1], got["y-"]), low_added(far[1, 1], got["y+"])]),
-            "y-": jnp.stack([top_added(far[2, 0], got["x-"]), low_added(far[3, 0], got["x+"])]),
+            "x+": far[0:2, 1],
+            "y-": far[2:4, 0],
             "y+": far[2:4, 1],
+            "x2": far[4, 0],
+            "y2": far[4, 1],
         }
     )
+    b_20 = slim(wide(middle[4, 1]) + wide(got["y2"]))
+    a_02 = slim(wide(middle[5, 0]) + wide(got["x2"]))
     a_mm = slim(wide(middle[0, 0]) + wide(got["x-"][0]) + wide(got["y-"][0]))
     a_mp = slim(wide(middle[1, 0]) + wide(got["x-"][1]))
     b_mp = slim(wide(middle[1, 1]) + wide(got["y+"][0]))
@@ -425,8 +401,8 @@
     got = send(
         {
             "x-": jnp.stack([middle[4, 0], middle[0, 1], b_mp]),
-            "x+": jnp.stack([middle[4, 1], b_pm, b_pp]),
-            "y-": jnp.stack([middle[5, 0], a_mm, a_pm]),
+            "x+": jnp.stack([b_20, b_pm, b_pp]),
+            "y-": jnp.stack([a_02, a_mm, a_pm]),
             "y+": jnp.stack([middle[5, 1], a_mp, middle[3, 0]]),
         }
     )
@@ -542,7 +518,7 @@
     used = jnp.any(match, axis=1).astype(I32)
     image = jnp.sum(jnp.where(match, jnp.arange(16, dtype=I32)[None, :], 0), axis=1)
     table = jnp.stack([used, image, row_off, col_off])
-    relative = jnp.array(NEAR + MIDDLE + FAR + LAST, I32)
+    relative = jnp.array(NEAR + MIDDLE + FAR, I32)
     place = lax.axis_index("dy")
     tile_ids = ((place // 4 + relative[:, 1]) % 4) * 4 + (place % 4 + relative[:, 0]) % 4
     slot_ids = (2 * tile_ids[:, None] + jnp.arange(2, dtype=I32)[None, :]).reshape(-1)
@@ -568,12 +544,10 @@
     words = jnp.concatenate(
         [words.reshape(2, HALF, T), sides, ends, jnp.zeros((2, PIECE - HALF - 2, T), I32)], axis=1
     )
-    near = send({way: words for way in STEPS})
+    near = send({way: words for way in WAYS})
     middle = send_middle(near)
     far = send_far(middle)
-    last = send_last(far, 136)
-    order = ["x+", "x-", "y+", "y-"]
-    whole = ((0, 0), (0, 1))
+    order = WAYS
     out_near, parts = run_tiles(
         [words] + [near[k] for k in order],
         [((n, 0), (n, 1)) for n in range(5)],
@@ -593,18 +567,22 @@
     )
     parts = parts + more
     out_far, more = run_tiles(
-        [far[k] for k in order],
-        [((0, 0), (1, 0)), ((0, 1), (1, 1)), ((2, 0), (3, 0)), ((2, 1), (3, 1))],
-        resample, observed, plan_of(11, 4), sun, gain,
-    )
-    parts = parts + more
-    out_last, more = run_tiles([last], [whole], resample, observed, plan_of(15, 1), sun, gain)
+        [far[k] for k in order] + [far["x2"], far["y2"]],
+        [
+            ((0, 0), (1, 0)),
+            ((0, 1), (1, 1)),
+            ((2, 0), (3, 0)),
+            ((2, 1), (3, 1)),
+            ((4, 0), (5, 0)),
+        ],
+        resample, observed, plan_of(11, 5), sun, gain,
+    )
     parts = parts + more
     smooth = smoothness(heights, top, bottom)
     crop_sums = finish_sums(parts)
     arrived = lax.all_to_all(crop_sums[:, None], "dy", split_axis=0, concat_axis=0, tiled=True)
     camera = arrived.sum(axis=0)
-    own = return_sums(out_near, out_middle, out_far, out_last, 144)
+    own = return_sums(out_near, out_middle, out_far)
     from_below = shifted(own[0, HALF], "dy", False)
     from_above = shifted(own[1, HALF], "dy", True)
     from_right = shifted(own[:, HALF + 1, :HALF].reshape(-1), "dx", False)

time: 366 us -> 343 us (0.937)
  waiting for transfers between devices: 90.9 us -> 70.5 us
  starting transfers between devices: 93.6 us -> 102 us
  other arithmetic: 46.9 us -> 42.3 us
    ppermute x32 -> x28, waiting for transfers between devices: 82.3 us -> 70.5 us  [send(): lax.ppermute(v, 'dy', STEPS[way])]
    ppermute x10, waiting for transfers between devices: 8.6 us -> 0.03 us  [shifted(): lax.ppermute(value, axis, pairs if up else [(b, a) for a, b in pairs])]
    ppermute x10, starting transfers between devices: 33.7 us -> 38.5 us  [shifted(): lax.ppermute(value, axis, pairs if up else [(b, a) for a, b in pairs])]
    ppermute x32 -> x28, starting transfers between devices: 48.3 us -> 51.3 us  [send(): lax.ppermute(v, 'dy', STEPS[way])]
    pallas_call x4 -> x3, Pallas kernels: 95 us -> 92 us  [run_tiles(): pl.pallas_call(functools.partial(tile_kernel, pieces, len(arrays)), grid_...]
  transfers between devices with their start and end apart: 44 -> 40, of which waited for: 18 -> 12; matrix products, arithmetic and copies ran while one was open for 17% -> 16% of each run, Pallas kernels for 19% -> 18%
where the time goes in v4:
time: 343 us; the launch traced here: 341 us
  starting transfers between devices  102 us (30%)
  Pallas kernels  92 us (27%)
  waiting for transfers between devices  70.5 us (21%)
  other arithmetic  42.3 us (12%)
  local copies, waits for them, and re-layouts  31 us (9%)
    pallas_call x3, Pallas kernels, run_tiles(): pl.pallas_call(functools.partial(tile_kernel, pieces, len(arrays)), grid_...  92 us
    ppermute x28, waiting for transfers between devices, send(): lax.ppermute(v, 'dy', STEPS[way])  70.5 us
    ppermute x28, starting transfers between devices, send(): lax.ppermute(v, 'dy', STEPS[way])  51.3 us
    ppermute x10, starting transfers between devices, shifted(): lax.ppermute(value, axis, pairs if up else [(b, a) for a, b in pairs])  38.5 us
    convert_element_type x5, other arithmetic, wide(): return v.astype(F32)  10.4 us
    all_to_all x1, starting transfers between devices, per_device(): lax.all_to_all(offsets, 'dy', split_axis=0, concat_axis=0, tiled=True)  6.86 us
  transfers between devices with their start and end apart: 40, of which 12 were waited for; matrix products, arithmetic and copies ran while one was open for 16% of the time, Pallas kernels for 18%

profile of v4, /device:TPU:7, one launch (start us, length us, event | category | flops | bytes accessed | tf_op | source)
XLA Modules:
  0.0 341.5 jit_solution(5635721339059587912)
XLA Ops:
  2.0 6.9 %all-to-all-start = ((s32[16,2,2]{2,1,0:T(2,128)}), s32[16,2,2]{2,1,0:T(2,128)S(1)}, u32[]{:S(2)}, u32[]{:S(2)}) async-start(s32[16,2,2]{2,1,0:T(2,128)} %copy.35), calls=%async_computation | async-start | bytes 32768 | tf_op jit(solution)/shard_map/all_to_all | solution.py:513
  9.6 2.5 collective-permute-start.3
  12.1 4.9 %collective-permute-start.2 = (f32[2,512]{1,0:T(2,128)S(1)}, f32[2,512]{1,0:T(2,128)S(1)}, u32[]{:S(2)}, u32[]{:S(2)}) collective-permute-start(f32[2,512]{1,0:T(2,128)S(1)} %get-tuple-element.74), channel_id=1, source_target_pairs={{0,8},{8,16},{16,24},{24,32},{32,40},{40,48},{48,56},{56,64},{64,7... | collective-permute-start | bytes 12296 | tf_op jit(solution)/shard_map/ppermute | solution.py:457
  18.4 5.2 %collective-permute-start = (f32[512]{0:T(512)S(1)}, f32[512]{0:T(512)S(1)}, u32[]{:S(2)}, u32[]{:S(2)}) collective-permute-start(f32[512]{0:T(512)S(1)} %get-tuple-element.14), channel_id=1, source_target_pairs={{0,1},{1,2},{2,3},{3,4},{4,5},{5,6},{6,7},{8,9},{9,10},{10,11},{11... | collective-permute-start | bytes 6152 | tf_op jit(solution)/shard_map/ppermute | solution.py:457
  23.6 1.9 collective-permute-start.1
  28.1 1.8 and_or_fusion
  33.0 1.5 collective-permute-start.5
  34.8 1.5 collective-permute-start.7
  37.3 19.3 %collective-permute-done.4.refs_7_ = s32[2,264,512]{2,1,0:T(8,128)} collective-permute-done((s32[2,264,512]{2,1,0:T(8,128)S(1)}, s32[2,264,512]{2,1,0:T(8,128)}, u32[]{:S(2)}, u32[]{:S(2)}) %collective-permute-start.4) | collective-permute-done | bytes 1081376 | tf_op jit(solution)/shard_map/ppermute | solution.py:347
  59.9 3.1 pad_add_fusion.4
  66.9 2.7 collective-permute-start.8
  69.6 1.5 collective-permute-start.11
  74.7 6.9 %collective-permute-start.36 = (f32[516,2]{1,0:T(8,128)S(1)}, f32[516,2]{1,0:T(8,128)S(1)}, u32[]{:S(2)}, u32[]{:S(2)}) collective-permute-start(f32[516,2]{1,0:T(8,128)S(1)} %get-tuple-element.72), channel_id=1, source_target_pairs={{0,1},{1,2},{2,3},{3,4},{4,5},{5,6},{6,7},{8,9},{9,10},{10,11},{11... | collective-permute-start | bytes 12392 | tf_op jit(solution)/shard_map/ppermute | solution.py:457
  81.6 20.1 %collective-permute-done.10.refs_8_ = s32[3,264,512]{2,1,0:T(8,128)S(1)} collective-permute-done((s32[3,264,512]{2,1,0:T(8,128)}, s32[3,264,512]{2,1,0:T(8,128)S(1)}, u32[]{:S(2)}, u32[]{:S(2)}) %collective-permute-start.10) | collective-permute-done | bytes 1622048 | tf_op jit(solution)/shard_map/ppermute | solution.py:347
  101.7 1.9 collective-permute-start.37
  104.9 2.1 collective-permute-start.16
  108.1 2.1 fusion.70
  111.3 1.5 collective-permute-start.15
  116.3 2.3 slice.460
  120.3 1.6 pad_maximum_fusion.6
  122.0 28.1 %shard_map.113 = (bf16[5,2,272,512]{3,2,1,0:T(8,128)(2,1)}, f32[16,5,8,384]{3,2,1,0:T(8,128)}) custom-call(s32[10]{0:T(128)} %get-tuple-element.83.refs_0_, s32[10]{0:T(128)} %select_reduce_fusion.5.refs_1_, s32[10]{0:T(128)} %get-tuple-element.81.refs_2_, s32[10]{0:T(128)} %get-tuple-element.80.refs_3_, f32[48]{0:T(128)} %reshape.296.refs_4_, ...), custom_call_target="tpu_custom_call" | custom-call | flops 2264924160 | bytes 40000000 | tf_op jit(solution)/shard_map/pallas_call | solution.py:317
  150.0 12.4 %collective-permute-start.17 = (s32[1,264,512]{2,1,0:T(8,128)}, s32[1,264,512]{2,1,0:T(8,128)}, u32[]{:S(2)}, u32[]{:S(2)}) collective-permute-start(s32[1,264,512]{2,1,0:T(8,128)} %get-tuple-element.56), channel_id=1, source_target_pairs={{0,64},{8,72},{16,80},{24,88},{32,96},{40,104},{48,112},{56,120},{... | collective-permute-start | bytes 1622024 | tf_op jit(solution)/shard_map/ppermute | solution.py:347
  162.4 1.9 slice_bitcast_fusion.13
  164.4 4.9 %convert_element_type.232 = f32[5,2,272,512]{3,2,1,0:T(8,128)} convert(bf16[5,2,272,512]{3,2,1,0:T(8,128)(2,1)} %get-tuple-element.8) | non-fusion elementwise | flops 1392640 | bytes 8355840 | tf_op jit(solution)/shard_map/convert_element_type | solution.py:378
  169.3 33.5 %shard_map.114 = (bf16[6,2,272,512]{3,2,1,0:T(8,128)(2,1)}, f32[16,5,8,384]{3,2,1,0:T(8,128)}) custom-call(s32[12]{0:T(128)} %get-tuple-element.89.refs_0_, s32[12]{0:T(128)} %select_reduce_fusion.3.refs_1_, s32[12]{0:T(128)} %get-tuple-element.87.refs_2_, s32[12]{0:T(128)} %get-tuple-element.86.refs_3_, f32[48]{0:T(128)} %reshape.296.refs_4_, ...), custom_call_target="tpu_custom_call" | custom-call | flops 2717908992 | bytes 48000000 | tf_op jit(solution)/shard_map/pallas_call | solution.py:317
  202.7 2.2 slice_bitcast_fusion.18
  206.3 30.5 %shard_map.115 = (bf16[5,2,272,512]{3,2,1,0:T(8,128)(2,1)}, f32[16,5,8,384]{3,2,1,0:T(8,128)}) custom-call(s32[10]{0:T(128)} %get-tuple-element.79.refs_0_, s32[10]{0:T(128)} %select_reduce_fusion.1.refs_1_, s32[10]{0:T(128)} %get-tuple-element.77.refs_2_, s32[10]{0:T(128)} %get-tuple-element.76.refs_3_, f32[48]{0:T(128)} %reshape.296.refs_4_, ...), custom_call_target="tpu_custom_call" | custom-call | flops 2264924160 | bytes 40000000 | tf_op jit(solution)/shard_map/pallas_call | solution.py:317
  238.1 1.6 slice_bitcast_fusion.6
  239.7 9.8 %collective-permute-start.26 = (bf16[272,512]{1,0:T(8,128)(2,1)S(1)}, bf16[272,512]{1,0:T(8,128)(2,1)S(1)}, u32[]{:S(2)}, u32[]{:S(2)}) collective-permute-start(bf16[272,512]{1,0:T(8,128)(2,1)S(1)} %get-tuple-element.52), channel_id=1, source_target_pairs={{0,64},{8,72},{16,80},{24,88},{32,96},{40,104},{48,112},{56,120},{... | collective-permute-start | bytes 835592 | tf_op jit(solution)/shard_map/ppermute | solution.py:347
  249.5 2.7 collective-permute-start.22
  253.3 2.7 collective-permute-start.27
  256.5 1.5 copy-done.6
  258.1 6.4 %collective-permute-done.18 = bf16[2,272,512]{2,1,0:T(8,128)(2,1)S(1)} collective-permute-done((bf16[2,272,512]{2,1,0:T(8,128)(2,1)S(1)}, bf16[2,272,512]{2,1,0:T(8,128)(2,1)S(1)}, u32[]{:S(2)}, u32[]{:S(2)}) %collective-permute-start.18) | collective-permute-done | bytes 557088 | tf_op jit(solution)/shard_map/ppermute | solution.py:347
  270.4 2.1 collective-permute-start.23
  273.9 12.7 %collective-permute-done.28 = bf16[3,272,512]{2,1,0:T(8,128)(2,1)} collective-permute-done((bf16[3,272,512]{2,1,0:T(8,128)(2,1)}, bf16[3,272,512]{2,1,0:T(8,128)(2,1)}, u32[]{:S(2)}, u32[]{:S(2)}) %collective-permute-start.28) | collective-permute-done | bytes 835616 | tf_op jit(solution)/shard_map/ppermute | solution.py:347
  287.9 2.8 collective-permute-done.19
  298.5 3.3 collective-permute-start.29
  305.7 5.6 %all-to-all-start.1 = ((f32[16,1,7]{2,1,0:T(1,128)}), f32[16,1,7]{2,1,0:T(1,128)S(1)}, u32[]{:S(2)}, u32[]{:S(2)}) async-start(f32[16,1,7]{2,1,0:T(1,128)} %copy.43), calls=%async_computation.1 | async-start | bytes 16384 | tf_op jit(solution)/shard_map/all_to_all | solution.py:583
  311.3 1.7 collective-permute-done.25
  313.1 2.9 collective-permute-done.30
  316.9 2.0 collective-permute-done.31
  318.9 1.9 fusion.7
  321.4 1.9 collective-permute-start.32
  323.3 5.5 %collective-permute-start.33 = (f32[512]{0:T(512)S(1)}, f32[512]{0:T(512)S(1)}, u32[]{:S(2)}, u32[]{:S(2)}) collective-permute-start(f32[512]{0:T(512)S(1)} %bitcast.223), channel_id=1, source_target_pairs={{0,8},{8,16},{16,24},{24,32},{32,40},{40,48},{48,56},{56,64},{64,7... | collective-permute-start | bytes 6152 | tf_op jit(solution)/shard_map/ppermute | solution.py:457
  328.8 4.5 %collective-permute-start.34 = (f32[512]{0:T(512)S(1)}, f32[512]{0:T(512)S(1)}, u32[]{:S(2)}, u32[]{:S(2)}) collective-permute-start(f32[512]{0:T(512)S(1)} %bitcast.222), channel_id=1, source_target_pairs={{1,0},{2,1},{3,2},{4,3},{5,4},{6,5},{7,6},{9,8},{10,9},{11,10},{12... | collective-permute-start | bytes 6152 | tf_op jit(solution)/shard_map/ppermute | solution.py:457
  333.3 3.3 collective-permute-start.35
  336.6 1.7 fusion.1
  339.0 2.4 fusion.12
  (198 shorter events, 54.1 us)
Async XLA Ops:
  2.0 30.8 %all-to-all-start = ((s32[16,2,2]{2,1,0:T(2,128)}), s32[16,2,2]{2,1,0:T(2,128)S(1)}, u32[]{:S(2)}, u32[]{:S(2)}) async-start(s32[16,2,2]{2,1,0:T(2,128)} %copy.35), calls=%async_computation | async-start | bytes 32768 | tf_op jit(solution)/shard_map/all_to_all | solution.py:513
  9.6 21.7 %collective-permute-start.3 = (f32[2,512]{1,0:T(2,128)S(1)}, f32[2,512]{1,0:T(2,128)S(1)}, u32[]{:S(2)}, u32[]{:S(2)}) collective-permute-start(f32[2,512]{1,0:T(2,128)S(1)} %get-tuple-element.75), channel_id=1, source_target_pairs={{8,0},{16,8},{24,16},{32,24},{40,32},{48,40},{56,48},{64,56},{72,6... | collective-permute-start | bytes 12296 | tf_op jit(solution)/shard_map/ppermute | solution.py:457
  12.1 19.2 %collective-permute-start.2 = (f32[2,512]{1,0:T(2,128)S(1)}, f32[2,512]{1,0:T(2,128)S(1)}, u32[]{:S(2)}, u32[]{:S(2)}) collective-permute-start(f32[2,512]{1,0:T(2,128)S(1)} %get-tuple-element.74), channel_id=1, source_target_pairs={{0,8},{8,16},{16,24},{24,32},{32,40},{40,48},{48,56},{56,64},{64,7... | collective-permute-start | bytes 12296 | tf_op jit(solution)/shard_map/ppermute | solution.py:457
  18.4 13.0 %collective-permute-start = (f32[512]{0:T(512)S(1)}, f32[512]{0:T(512)S(1)}, u32[]{:S(2)}, u32[]{:S(2)}) collective-permute-start(f32[512]{0:T(512)S(1)} %get-tuple-element.14), channel_id=1, source_target_pairs={{0,1},{1,2},{2,3},{3,4},{4,5},{5,6},{6,7},{8,9},{9,10},{10,11},{11... | collective-permute-start | bytes 6152 | tf_op jit(solution)/shard_map/ppermute | solution.py:457
  23.6 7.7 %collective-permute-start.1 = (f32[512]{0:T(512)S(1)}, f32[512]{0:T(512)S(1)}, u32[]{:S(2)}, u32[]{:S(2)}) collective-permute-start(f32[512]{0:T(512)S(1)} %get-tuple-element.15), channel_id=1, source_target_pairs={{1,0},{2,1},{3,2},{4,3},{5,4},{6,5},{7,6},{9,8},{10,9},{11,10},{12... | collective-permute-start | bytes 6152 | tf_op jit(solution)/shard_map/ppermute | solution.py:457
  31.5 26.3 %copy-start.3 = (s32[2,264,512]{2,1,0:T(8,128)}, s32[2,264,512]{2,1,0:T(8,128)S(1)}, u32[]{:S(2)}) copy-start(s32[2,264,512]{2,1,0:T(8,128)S(1)} %fusion.9.refs_6_) | copy-start | bytes 3244036
  31.5 26.2 %collective-permute-start.6 = (s32[2,264,512]{2,1,0:T(8,128)S(1)}, s32[2,264,512]{2,1,0:T(8,128)S(1)}, u32[]{:S(2)}, u32[]{:S(2)}) collective-permute-start(s32[2,264,512]{2,1,0:T(8,128)S(1)} %fusion.9.refs_6_), channel_id=1, source_target_pairs={{0,32},{8,40},{16,48},{24,56},{32,64},{40,72},{48,80},{56,88},{64,... | collective-permute-start | bytes 3244040 | tf_op jit(solution)/shard_map/ppermute | solution.py:347
  32.8 23.9 %collective-permute-start.4 = (s32[2,264,512]{2,1,0:T(8,128)S(1)}, s32[2,264,512]{2,1,0:T(8,128)}, u32[]{:S(2)}, u32[]{:S(2)}) collective-permute-start(s32[2,264,512]{2,1,0:T(8,128)S(1)} %fusion.9.refs_6_), channel_id=1, source_target_pairs={{0,8},{8,16},{16,24},{24,0},{32,40},{40,48},{48,56},{56,32},{64,72... | collective-permute-start | bytes 3244040 | tf_op jit(solution)/shard_map/ppermute | solution.py:347
  33.0 24.8 %collective-permute-start.5 = (s32[2,264,512]{2,1,0:T(8,128)S(1)}, s32[2,264,512]{2,1,0:T(8,128)S(1)}, u32[]{:S(2)}, u32[]{:S(2)}) collective-permute-start(s32[2,264,512]{2,1,0:T(8,128)S(1)} %fusion.9.refs_6_), channel_id=1, source_target_pairs={{0,24},{8,0},{16,8},{24,16},{32,56},{40,32},{48,40},{56,48},{64,88... | collective-permute-start | bytes 3244040 | tf_op jit(solution)/shard_map/ppermute | solution.py:347
  34.8 24.1 %collective-permute-start.7 = (s32[2,264,512]{2,1,0:T(8,128)S(1)}, s32[2,264,512]{2,1,0:T(8,128)S(1)}, u32[]{:S(2)}, u32[]{:S(2)}) collective-permute-start(s32[2,264,512]{2,1,0:T(8,128)S(1)} %fusion.9.refs_6_), channel_id=1, source_target_pairs={{0,96},{8,104},{16,112},{24,120},{32,0},{40,8},{48,16},{56,24},{64... | collective-permute-start | bytes 3244040 | tf_op jit(solution)/shard_map/ppermute | solution.py:347
  63.0 38.7 %collective-permute-start.10 = (s32[3,264,512]{2,1,0:T(8,128)}, s32[3,264,512]{2,1,0:T(8,128)S(1)}, u32[]{:S(2)}, u32[]{:S(2)}) collective-permute-start(s32[3,264,512]{2,1,0:T(8,128)} %get-tuple-element.67), channel_id=1, source_target_pairs={{0,32},{8,40},{16,48},{24,56},{32,64},{40,72},{48,80},{56,88},{64,... | collective-permute-start | bytes 4866056 | tf_op jit(solution)/shard_map/ppermute | solution.py:347
  66.9 41.2 %collective-permute-start.9 = (s32[3,264,512]{2,1,0:T(8,128)}, s32[3,264,512]{2,1,0:T(8,128)}, u32[]{:S(2)}, u32[]{:S(2)}) collective-permute-start(s32[3,264,512]{2,1,0:T(8,128)} %get-tuple-element.66), channel_id=1, source_target_pairs={{0,24},{8,0},{16,8},{24,16},{32,56},{40,32},{48,40},{56,48},{64,88... | collective-permute-start | bytes 4866056 | tf_op jit(solution)/shard_map/ppermute | solution.py:347
  66.9 38.0 %collective-permute-start.8 = (s32[3,264,512]{2,1,0:T(8,128)}, s32[3,264,512]{2,1,0:T(8,128)}, u32[]{:S(2)}, u32[]{:S(2)}) collective-permute-start(s32[3,264,512]{2,1,0:T(8,128)} %get-tuple-element.65), channel_id=1, source_target_pairs={{0,8},{8,16},{16,24},{24,0},{32,40},{40,48},{48,56},{56,32},{64,72... | collective-permute-start | bytes 4866056 | tf_op jit(solution)/shard_map/ppermute | solution.py:347
  69.6 43.3 %collective-permute-start.11 = (s32[3,264,512]{2,1,0:T(8,128)}, s32[3,264,512]{2,1,0:T(8,128)}, u32[]{:S(2)}, u32[]{:S(2)}) collective-permute-start(s32[3,264,512]{2,1,0:T(8,128)} %get-tuple-element.64), channel_id=1, source_target_pairs={{0,96},{8,104},{16,112},{24,120},{32,0},{40,8},{48,16},{56,24},{64... | collective-permute-start | bytes 4866056 | tf_op jit(solution)/shard_map/ppermute | solution.py:347
  74.7 45.1 %collective-permute-start.36 = (f32[516,2]{1,0:T(8,128)S(1)}, f32[516,2]{1,0:T(8,128)S(1)}, u32[]{:S(2)}, u32[]{:S(2)}) collective-permute-start(f32[516,2]{1,0:T(8,128)S(1)} %get-tuple-element.72), channel_id=1, source_target_pairs={{0,1},{1,2},{2,3},{3,4},{4,5},{5,6},{6,7},{8,9},{9,10},{10,11},{11... | collective-permute-start | bytes 12392 | tf_op jit(solution)/shard_map/ppermute | solution.py:457
  101.7 18.7 %collective-permute-start.37 = (f32[516,2]{1,0:T(8,128)S(1)}, f32[516,2]{1,0:T(8,128)S(1)}, u32[]{:S(2)}, u32[]{:S(2)}) collective-permute-start(f32[516,2]{1,0:T(8,128)S(1)} %get-tuple-element.73), channel_id=1, source_target_pairs={{1,0},{2,1},{3,2},{4,3},{5,4},{6,5},{7,6},{9,8},{10,9},{11,10},{12... | collective-permute-start | bytes 12392 | tf_op jit(solution)/shard_map/ppermute | solution.py:457
  104.9 45.1 %collective-permute-start.16 = (s32[1,264,512]{2,1,0:T(8,128)}, s32[1,264,512]{2,1,0:T(8,128)}, u32[]{:S(2)}, u32[]{:S(2)}) collective-permute-start(s32[1,264,512]{2,1,0:T(8,128)} %get-tuple-element.58), channel_id=1, source_target_pairs={{0,16},{8,24},{16,0},{24,8},{32,48},{40,56},{48,32},{56,40},{64,80... | collective-permute-start | bytes 1622024 | tf_op jit(solution)/shard_map/ppermute | solution.py:347
  111.3 93.7 %collective-permute-start.15 = (s32[2,264,512]{2,1,0:T(8,128)}, s32[2,264,512]{2,1,0:T(8,128)}, u32[]{:S(2)}, u32[]{:S(2)}) collective-permute-start(s32[2,264,512]{2,1,0:T(8,128)} %pad_add_fusion.10), channel_id=1, source_target_pairs={{0,96},{8,104},{16,112},{24,120},{32,0},{40,8},{48,16},{56,24},{64... | collective-permute-start | bytes 3244040 | tf_op jit(solution)/shard_map/ppermute | solution.py:347
  115.0 90.0 %collective-permute-start.12 = (s32[2,264,512]{2,1,0:T(8,128)}, s32[2,264,512]{2,1,0:T(8,128)}, u32[]{:S(2)}, u32[]{:S(2)}) collective-permute-start(s32[2,264,512]{2,1,0:T(8,128)} %pad_add_fusion.9), channel_id=1, source_target_pairs={{0,8},{8,16},{16,24},{24,0},{32,40},{40,48},{48,56},{56,32},{64,72... | collective-permute-start | bytes 3244040 | tf_op jit(solution)/shard_map/ppermute | solution.py:347
  119.8 85.2 %collective-permute-start.13 = (s32[2,264,512]{2,1,0:T(8,128)}, s32[2,264,512]{2,1,0:T(8,128)S(1)}, u32[]{:S(2)}, u32[]{:S(2)}) collective-permute-start(s32[2,264,512]{2,1,0:T(8,128)} %slice.460), channel_id=1, source_target_pairs={{0,24},{8,0},{16,8},{24,16},{32,56},{40,32},{48,40},{56,48},{64,88... | collective-permute-start | bytes 3244040 | tf_op jit(solution)/shard_map/ppermute | solution.py:347
  120.3 84.7 %collective-permute-start.14 = (s32[2,264,512]{2,1,0:T(8,128)}, s32[2,264,512]{2,1,0:T(8,128)S(1)}, u32[]{:S(2)}, u32[]{:S(2)}) collective-permute-start(s32[2,264,512]{2,1,0:T(8,128)} %slice.461), channel_id=1, source_target_pairs={{0,32},{8,40},{16,48},{24,56},{32,64},{40,72},{48,80},{56,88},{64,... | collective-permute-start | bytes 3244040 | tf_op jit(solution)/shard_map/ppermute | solution.py:347
  150.0 54.9 %collective-permute-start.17 = (s32[1,264,512]{2,1,0:T(8,128)}, s32[1,264,512]{2,1,0:T(8,128)}, u32[]{:S(2)}, u32[]{:S(2)}) collective-permute-start(s32[1,264,512]{2,1,0:T(8,128)} %get-tuple-element.56), channel_id=1, source_target_pairs={{0,64},{8,72},{16,80},{24,88},{32,96},{40,104},{48,112},{56,120},{... | collective-permute-start | bytes 1622024 | tf_op jit(solution)/shard_map/ppermute | solution.py:347
  237.9 15.3 %collective-permute-start.20 = (bf16[272,512]{1,0:T(8,128)(2,1)S(1)}, bf16[272,512]{1,0:T(8,128)(2,1)S(1)}, u32[]{:S(2)}, u32[]{:S(2)}) collective-permute-start(bf16[272,512]{1,0:T(8,128)(2,1)S(1)} %get-tuple-element.51), channel_id=1, source_target_pairs={{0,16},{8,24},{16,0},{24,8},{32,48},{40,56},{48,32},{56,40},{64,80... | collective-permute-start | bytes 835592 | tf_op jit(solution)/shard_map/ppermute | solution.py:347
  238.0 18.0 %copy-start.21 = (f32[16,5,8,384]{3,2,1,0:T(8,128)S(1)}, f32[16,5,8,384]{3,2,1,0:T(8,128)}, u32[]{:S(2)}) copy-start(f32[16,5,8,384]{3,2,1,0:T(8,128)} %get-tuple-element.12) | copy-start | bytes 2949124
  238.1 18.0 %copy-start.22 = (f32[16,5,8,384]{3,2,1,0:T(8,128)S(1)}, f32[16,5,8,384]{3,2,1,0:T(8,128)}, u32[]{:S(2)}) copy-start(f32[16,5,8,384]{3,2,1,0:T(8,128)} %get-tuple-element.13) | copy-start | bytes 2949124
  239.7 16.8 %collective-permute-start.26 = (bf16[272,512]{1,0:T(8,128)(2,1)S(1)}, bf16[272,512]{1,0:T(8,128)(2,1)S(1)}, u32[]{:S(2)}, u32[]{:S(2)}) collective-permute-start(bf16[272,512]{1,0:T(8,128)(2,1)S(1)} %get-tuple-element.52), channel_id=1, source_target_pairs={{0,64},{8,72},{16,80},{24,88},{32,96},{40,104},{48,112},{56,120},{... | collective-permute-start | bytes 835592 | tf_op jit(solution)/shard_map/ppermute | solution.py:347
  249.5 15.0 %collective-permute-start.18 = (bf16[2,272,512]{2,1,0:T(8,128)(2,1)S(1)}, bf16[2,272,512]{2,1,0:T(8,128)(2,1)S(1)}, u32[]{:S(2)}, u32[]{:S(2)}) collective-permute-start(bf16[2,272,512]{2,1,0:T(8,128)(2,1)S(1)} %get-tuple-element.55), channel_id=1, source_target_pairs={{0,32},{8,40},{16,48},{24,56},{32,64},{40,72},{48,80},{56,88},{64,... | collective-permute-start | bytes 1671176 | tf_op jit(solution)/shard_map/ppermute | solution.py:347
  249.5 15.0 %collective-permute-start.21 = (bf16[2,272,512]{2,1,0:T(8,128)(2,1)S(1)}, bf16[2,272,512]{2,1,0:T(8,128)(2,1)S(1)}, u32[]{:S(2)}, u32[]{:S(2)}) collective-permute-start(bf16[2,272,512]{2,1,0:T(8,128)(2,1)S(1)} %get-tuple-element.54), channel_id=1, source_target_pairs={{0,24},{8,0},{16,8},{24,16},{32,56},{40,32},{48,40},{56,48},{64,88... | collective-permute-start | bytes 1671176 | tf_op jit(solution)/shard_map/ppermute | solution.py:347
  249.5 15.0 %collective-permute-start.22 = (bf16[2,272,512]{2,1,0:T(8,128)(2,1)S(1)}, bf16[2,272,512]{2,1,0:T(8,128)(2,1)S(1)}, u32[]{:S(2)}, u32[]{:S(2)}) collective-permute-start(bf16[2,272,512]{2,1,0:T(8,128)(2,1)S(1)} %get-tuple-element.53), channel_id=1, source_target_pairs={{0,96},{8,104},{16,112},{24,120},{32,0},{40,8},{48,16},{56,24},{64... | collective-permute-start | bytes 1671176 | tf_op jit(solution)/shard_map/ppermute | solution.py:347
  253.3 11.9 %collective-permute-start.27 = (bf16[2,272,512]{2,1,0:T(8,128)(2,1)S(1)}, bf16[2,272,512]{2,1,0:T(8,128)(2,1)S(1)}, u32[]{:S(2)}, u32[]{:S(2)}) collective-permute-start(bf16[2,272,512]{2,1,0:T(8,128)(2,1)S(1)} %slice_bitcast_fusion.10), channel_id=1, source_target_pairs={{0,8},{8,16},{16,24},{24,0},{32,40},{40,48},{48,56},{56,32},{64,72... | collective-permute-start | bytes 1671176 | tf_op jit(solution)/shard_map/ppermute | solution.py:347
  266.8 19.7 %collective-permute-start.28 = (bf16[3,272,512]{2,1,0:T(8,128)(2,1)}, bf16[3,272,512]{2,1,0:T(8,128)(2,1)}, u32[]{:S(2)}, u32[]{:S(2)}) collective-permute-start(bf16[3,272,512]{2,1,0:T(8,128)(2,1)} %pad_maximum_fusion.10), channel_id=1, source_target_pairs={{0,8},{8,16},{16,24},{24,0},{32,40},{40,48},{48,56},{56,32},{64,72... | collective-permute-start | bytes 2506760 | tf_op jit(solution)/shard_map/ppermute | solution.py:347
  268.0 28.1 %slice-start = ((s8[5570560]{0:T(1024)(128)(4,1)}), s8[1376256]{0:T(1024)(128)(4,1)S(1)}, s32[]{:S(2)}) async-start(s8[5570560]{0:T(1024)(128)(4,1)} %bitcast.213), calls=%async_computation.2 | async-start | bytes 2752512
  269.1 21.7 %collective-permute-start.19 = (bf16[3,272,512]{2,1,0:T(8,128)(2,1)}, bf16[3,272,512]{2,1,0:T(8,128)(2,1)}, u32[]{:S(2)}, u32[]{:S(2)}) collective-permute-start(bf16[3,272,512]{2,1,0:T(8,128)(2,1)} %pad_maximum_fusion.7), channel_id=1, source_target_pairs={{0,24},{8,0},{16,8},{24,16},{32,56},{40,32},{48,40},{56,48},{64,88... | collective-permute-start | bytes 2506760 | tf_op jit(solution)/shard_map/ppermute | solution.py:347
  270.4 21.8 %collective-permute-start.23 = (bf16[3,272,512]{2,1,0:T(8,128)(2,1)}, bf16[3,272,512]{2,1,0:T(8,128)(2,1)}, u32[]{:S(2)}, u32[]{:S(2)}) collective-permute-start(bf16[3,272,512]{2,1,0:T(8,128)(2,1)} %pad_maximum_fusion.8), channel_id=1, source_target_pairs={{0,96},{8,104},{16,112},{24,120},{32,0},{40,8},{48,16},{56,24},{64... | collective-permute-start | bytes 2506760 | tf_op jit(solution)/shard_map/ppermute | solution.py:347
  273.4 21.3 %collective-permute-start.24 = (bf16[3,272,512]{2,1,0:T(8,128)(2,1)}, bf16[3,272,512]{2,1,0:T(8,128)(2,1)}, u32[]{:S(2)}, u32[]{:S(2)}) collective-permute-start(bf16[3,272,512]{2,1,0:T(8,128)(2,1)} %pad_maximum_fusion.9), channel_id=1, source_target_pairs={{0,32},{8,40},{16,48},{24,56},{32,64},{40,72},{48,80},{56,88},{64,... | collective-permute-start | bytes 2506760 | tf_op jit(solution)/shard_map/ppermute | solution.py:347
  273.9 22.2 %slice-start.1 = ((s8[5570560]{0:T(1024)(128)(4,1)}), s8[4194304]{0:T(1024)(128)(4,1)S(1)}, s32[]{:S(2)}) async-start(s8[5570560]{0:T(1024)(128)(4,1)} %bitcast.213), calls=%async_computation.3 | async-start | bytes 8388608
  297.5 15.5 %collective-permute-start.25 = (bf16[2,272,512]{2,1,0:T(8,128)(2,1)S(1)}, bf16[2,272,512]{2,1,0:T(8,128)(2,1)S(1)}, u32[]{:S(2)}, u32[]{:S(2)}) collective-permute-start(bf16[2,272,512]{2,1,0:T(8,128)(2,1)S(1)} %pad_maximum_fusion.11), channel_id=1, source_target_pairs={{0,24},{8,0},{16,8},{24,16},{32,56},{40,32},{48,40},{56,48},{64,88... | collective-permute-start | bytes 1671176 | tf_op jit(solution)/shard_map/ppermute | solution.py:347
  298.5 14.6 %collective-permute-start.29 = (bf16[2,272,512]{2,1,0:T(8,128)(2,1)}, bf16[2,272,512]{2,1,0:T(8,128)(2,1)S(1)}, u32[]{:S(2)}, u32[]{:S(2)}) collective-permute-start(bf16[2,272,512]{2,1,0:T(8,128)(2,1)} %pad_maximum_fusion.12), channel_id=1, source_target_pairs={{0,8},{8,16},{16,24},{24,0},{32,40},{40,48},{48,56},{56,32},{64,72... | collective-permute-start | bytes 1671176 | tf_op jit(solution)/shard_map/ppermute | solution.py:347
  302.7 13.3 %collective-permute-start.30 = (bf16[2,272,512]{2,1,0:T(8,128)(2,1)}, bf16[2,272,512]{2,1,0:T(8,128)(2,1)S(1)}, u32[]{:S(2)}, u32[]{:S(2)}) collective-permute-start(bf16[2,272,512]{2,1,0:T(8,128)(2,1)} %pad_maximum_fusion.13), channel_id=1, source_target_pairs={{0,96},{8,104},{16,112},{24,120},{32,0},{40,8},{48,16},{56,24},{64... | collective-permute-start | bytes 1671176 | tf_op jit(solution)/shard_map/ppermute | solution.py:347
  304.3 14.6 %collective-permute-start.31 = (bf16[2,272,512]{2,1,0:T(8,128)(2,1)}, bf16[2,272,512]{2,1,0:T(8,128)(2,1)}, u32[]{:S(2)}, u32[]{:S(2)}) collective-permute-start(bf16[2,272,512]{2,1,0:T(8,128)(2,1)} %pad_maximum_fusion.14), channel_id=1, source_target_pairs={{0,32},{8,40},{16,48},{24,56},{32,64},{40,72},{48,80},{56,88},{64,... | collective-permute-start | bytes 1671176 | tf_op jit(solution)/shard_map/ppermute | solution.py:347
  305.7 32.6 %all-to-all-start.1 = ((f32[16,1,7]{2,1,0:T(1,128)}), f32[16,1,7]{2,1,0:T(1,128)S(1)}, u32[]{:S(2)}, u32[]{:S(2)}) async-start(f32[16,1,7]{2,1,0:T(1,128)} %copy.43), calls=%async_computation.1 | async-start | bytes 16384 | tf_op jit(solution)/shard_map/all_to_all | solution.py:583
  311.3 25.3 %copy-start.1 = (f32[516,516]{1,0:T(8,128)S(1)}, f32[516,516]{1,0:T(8,128)}, u32[]{:S(2)}) copy-start(f32[516,516]{1,0:T(8,128)} %pad_maximum_fusion.6) | copy-start | bytes 3195076
  311.3 25.3 %copy-start.17 = (f32[516,2]{1,0:T(8,128)S(1)}, f32[516,2]{1,0:T(8,128)}, u32[]{:S(2)}) copy-start(f32[516,2]{1,0:T(8,128)} %copy-done.16) | copy-start | bytes 12388
  311.3 25.3 %copy-start.19 = (f32[516,2]{1,0:T(8,128)S(1)}, f32[516,2]{1,0:T(8,128)}, u32[]{:S(2)}) copy-start(f32[516,2]{1,0:T(8,128)} %copy-done.18) | copy-start | bytes 12388
  321.4 17.6 %collective-permute-start.32 = (f32[512]{0:T(512)}, f32[512]{0:T(512)S(1)}, u32[]{:S(2)}, u32[]{:S(2)}) collective-permute-start(f32[512]{0:T(512)} %bitcast.55), channel_id=1, source_target_pairs={{8,0},{16,8},{24,16},{32,24},{40,32},{48,40},{56,48},{64,56},{72,6... | collective-permute-start | bytes 6152 | tf_op jit(solution)/shard_map/ppermute | solution.py:457
  323.3 15.7 %collective-permute-start.33 = (f32[512]{0:T(512)S(1)}, f32[512]{0:T(512)S(1)}, u32[]{:S(2)}, u32[]{:S(2)}) collective-permute-start(f32[512]{0:T(512)S(1)} %bitcast.223), channel_id=1, source_target_pairs={{0,8},{8,16},{16,24},{24,32},{32,40},{40,48},{48,56},{56,64},{64,7... | collective-permute-start | bytes 6152 | tf_op jit(solution)/shard_map/ppermute | solution.py:457
  328.8 10.2 %collective-permute-start.34 = (f32[512]{0:T(512)S(1)}, f32[512]{0:T(512)S(1)}, u32[]{:S(2)}, u32[]{:S(2)}) collective-permute-start(f32[512]{0:T(512)S(1)} %bitcast.222), channel_id=1, source_target_pairs={{1,0},{2,1},{3,2},{4,3},{5,4},{6,5},{7,6},{9,8},{10,9},{11,10},{12... | collective-permute-start | bytes 6152 | tf_op jit(solution)/shard_map/ppermute | solution.py:457
  333.3 5.7 %collective-permute-start.35 = (f32[512]{0:T(512)S(1)}, f32[512]{0:T(512)S(1)}, u32[]{:S(2)}, u32[]{:S(2)}) collective-permute-start(f32[512]{0:T(512)S(1)} %bitcast.221), channel_id=1, source_target_pairs={{0,1},{1,2},{2,3},{3,4},{4,5},{5,6},{6,7},{8,9},{9,10},{10,11},{11... | collective-permute-start | bytes 6152 | tf_op jit(solution)/shard_map/ppermute | solution.py:457
  (21 other events, 87.0 us)

commit v5 on v4

--- a/solution.py
+++ b/solution.py
@@ -135,7 +135,7 @@
                 gy_ref[b, pl.ds(base + 8, CH)] = jnp.zeros((CH, 128), F32)
             return 0
 
-        lax.fori_loop(0, T // CH, slope, 0, unroll=2)
+        lax.fori_loop(0, T // CH, slope, 0, unroll=4)
 
     @pl.when(mine)
     def _():
@@ -156,7 +156,7 @@
                 tbuf[b, pl.ds(base, CH)] = q * r2_ref[ob + b, rows]
             return 0
 
-        lax.fori_loop(0, C // CH, shade, 0, unroll=2)
+        lax.fori_loop(0, C // CH, shade, 0, unroll=4)
         row_mat = res_ref[0, 0]
         col_mat = res_ref[0, 1]
         first_pass = jnp.dot(row_mat, shaded[...], preferred_element_type=F32).astype(BF16)
@@ -229,7 +229,7 @@
                 )
             return 0
 
-        lax.fori_loop(0, C // CH, pull, 0, unroll=2)
+        lax.fori_loop(0, C // CH, pull, 0, unroll=4)
 
     @pl.when((slot_odd == 1) & any_used)
     def _():
@@ -253,7 +253,7 @@
                 out_ref[0, half, to, lanes(b)] = (0.5 * total).astype(BF16)
             return 0
 
-        lax.fori_loop(0, T // CH, stencil, 0, unroll=2)
+        lax.fori_loop(0, T // CH, stencil, 0, unroll=4)
         sub = lax.broadcasted_iota(I32, (16, 128), 0)
         lane16 = lax.broadcasted_iota(I32, (16, 128), 1)
         pick_low = jnp.where((sub == 1) & (lane16 == 0), -0.5, 0.0).astype(BF16)
@@ -338,6 +338,7 @@
 STEPS["x2"] = around(2, 0)
 STEPS["y2"] = around(0, 2)
 WAYS = ("x+", "x-", "y+", "y-")
+WAYS_BACK = ("x-", "x+", "y-", "y+")
 NEAR = [(0, 0), (-1, 0), (1, 0), (0, -1), (0, 1)]
 MIDDLE = [(-1, -1), (-1, 1), (1, -1), (1, 1), (2, 0), (0, 2)]
 FAR = [(2, -1), (2, 1), (-1, 2), (1, 2), (2, 2)]
@@ -380,43 +381,53 @@
     def slim(v):
         return v.astype(BF16)
 
+    flat = far.reshape((10,) + far.shape[2:])
     got = send(
         {
-            "x-": far[0:2, 0],
-            "x+": far[0:2, 1],
-            "y-": far[2:4, 0],
-            "y+": far[2:4, 1],
-            "x2": far[4, 0],
-            "y2": far[4, 1],
+            "x2": flat[8:9],
+            "y2": flat[9:10],
+            "x-": flat[0:3],
+            "y-": flat[4:7],
+            "x+": flat[3:4],
+            "y+": flat[7:8],
         }
     )
-    b_20 = slim(wide(middle[4, 1]) + wide(got["y2"]))
-    a_02 = slim(wide(middle[5, 0]) + wide(got["x2"]))
-    a_mm = slim(wide(middle[0, 0]) + wide(got["x-"][0]) + wide(got["y-"][0]))
-    a_mp = slim(wide(middle[1, 0]) + wide(got["x-"][1]))
-    b_mp = slim(wide(middle[1, 1]) + wide(got["y+"][0]))
-    a_pm = slim(wide(middle[2, 0]) + wide(got["y-"][1]))
-    b_pm = slim(wide(middle[2, 1]) + wide(got["x+"][0]))
-    b_pp = slim(wide(middle[3, 1]) + wide(got["x+"][1]) + wide(got["y+"][1]))
+    xm, xp, ym, yp = (got[k] for k in WAYS_BACK)
+    b_20 = slim(wide(middle[4, 1]) + wide(got["y2"][0]))
+    a_02 = slim(wide(middle[5, 0]) + wide(got["x2"][0]))
+    a_mm = slim(wide(middle[0, 0]) + wide(xm[0]) + wide(ym[0]))
+    b_mm = slim(wide(middle[0, 1]) + wide(xm[1]) + wide(ym[1]))
+    a_mp = slim(wide(middle[1, 0]) + wide(xm[2]))
+    a_pm = slim(wide(middle[2, 0]) + wide(ym[2]))
+    b_pp = slim(wide(middle[3, 1]) + wide(xp[0]) + wide(yp[0]))
     got = send(
         {
-            "x-": jnp.stack([middle[4, 0], middle[0, 1], b_mp]),
-            "x+": jnp.stack([b_20, b_pm, b_pp]),
+            "x-": jnp.stack([middle[4, 0], b_mm, middle[1, 1]]),
+            "x+": jnp.stack([b_20, middle[2, 1], b_pp]),
             "y-": jnp.stack([a_02, a_mm, a_pm]),
             "y+": jnp.stack([middle[5, 1], a_mp, middle[3, 0]]),
         }
     )
-    xm, xp, ym, yp = (wide(got[k]) for k in ("x-", "x+", "y-", "y+"))
-    mine = wide(near)
+    xm, xp, ym, yp = (got[k] for k in WAYS_BACK)
+
+    def total(*pieces):
+        result = wide(pieces[0])
+        for piece in pieces[1:]:
+            result = result + wide(piece)
+        return slim(result)
+
     got = send(
         {
-            "x-": slim(jnp.stack([mine[1, 0] + xm[0] + ym[1] + yp[1], mine[1, 1]])),
-            "x+": slim(jnp.stack([mine[2, 0] + ym[2] + yp[2], mine[2, 1] + xp[0]])),
-            "y-": slim(jnp.stack([mine[3, 0] + ym[0], mine[3, 1] + xm[1] + xp[1]])),
-            "y+": slim(jnp.stack([mine[4, 0], mine[4, 1] + xm[2] + xp[2] + yp[0]])),
+            "x-": jnp.stack([total(near[1, 0], xm[0], ym[1], yp[1]), near[1, 1]]),
+            "x+": jnp.stack([total(near[2, 0], ym[2], yp[2]), total(near[2, 1], xp[0])]),
+            "y-": jnp.stack([total(near[3, 0], ym[0]), total(near[3, 1], xm[1], xp[1])]),
+            "y+": jnp.stack([near[4, 0], total(near[4, 1], xm[2], xp[2], yp[0])]),
         }
     )
-    return mine[0] + wide(got["x-"]) + wide(got["x+"]) + wide(got["y-"]) + wide(got["y+"])
+    result = wide(near[0])
+    for way in WAYS_BACK:
+        result = result + wide(got[way])
+    return result
 
 
 def next_images(used, image):

time: 343 us -> 328 us (0.956)
  the two profiles are of different devices: /device:TPU:7 before, /device:TPU:57 now
where the time goes in v5:
time: 328 us; the launch traced here: 327 us
  starting transfers between devices  115 us (35%)
  Pallas kernels  87.4 us (27%)
  waiting for transfers between devices  60.3 us (18%)
  other arithmetic  34.5 us (11%)
  local copies, waits for them, and re-layouts  26.1 us (8%)
    pallas_call x3, Pallas kernels, run_tiles(): pl.pallas_call(functools.partial(tile_kernel, pieces, len(arrays)), grid_...  87.4 us
    ppermute x10, starting transfers between devices, shifted(): lax.ppermute(value, axis, pairs if up else [(b, a) for a, b in pairs])  63.4 us
    ppermute x28, waiting for transfers between devices, send(): lax.ppermute(v, 'dy', STEPS[way])  59.7 us
    ppermute x28, starting transfers between devices, send(): lax.ppermute(v, 'dy', STEPS[way])  41.2 us
  transfers between devices with their start and end apart: 40, of which 13 were waited for; matrix products, arithmetic and copies ran while one was open for 12% of the time, Pallas kernels for 19%

profile of v5, /device:TPU:57, one launch (start us, length us, event | category | flops | bytes accessed | tf_op | source)
XLA Modules:
  0.0 326.5 jit_solution(13778020616700396613)
XLA Ops:
  0.6 1.3 slice_reduce_fusion.1
  2.0 4.1 %collective-permute-start = (f32[512]{0:T(512)S(1)}, f32[512]{0:T(512)S(1)}, u32[]{:S(2)}, u32[]{:S(2)}) collective-permute-start(f32[512]{0:T(512)S(1)} %get-tuple-element.14), channel_id=1, source_target_pairs={{0,1},{1,2},{2,3},{3,4},{4,5},{5,6},{6,7},{8,9},{9,10},{10,11},{11... | collective-permute-start | bytes 6152 | tf_op jit(solution)/shard_map/ppermute | solution.py:468
  6.1 1.9 collective-permute-start.1
  8.8 3.1 collective-permute-start.2
  11.9 4.3 %collective-permute-start.3 = (f32[2,512]{1,0:T(2,128)S(1)}, f32[2,512]{1,0:T(2,128)S(1)}, u32[]{:S(2)}, u32[]{:S(2)}) collective-permute-start(f32[2,512]{1,0:T(2,128)S(1)} %get-tuple-element.77), channel_id=1, source_target_pairs={{8,0},{16,8},{24,16},{32,24},{40,32},{48,40},{56,48},{64,56},{72,6... | collective-permute-start | bytes 12296 | tf_op jit(solution)/shard_map/ppermute | solution.py:468
  17.5 4.5 %all-to-all-start = ((s32[16,2,2]{2,1,0:T(2,128)}), s32[16,2,2]{2,1,0:T(2,128)S(1)}, u32[]{:S(2)}, u32[]{:S(2)}) async-start(s32[16,2,2]{2,1,0:T(2,128)} %copy.26), calls=%async_computation | async-start | bytes 32768 | tf_op jit(solution)/shard_map/all_to_all | solution.py:524
  25.7 1.8 and_or_fusion
  28.6 2.1 collective-permute-start.6
  30.7 2.4 collective-permute-start.5
  34.3 19.1 %collective-permute-done.7.refs_10_ = s32[2,264,512]{2,1,0:T(8,128)} collective-permute-done((s32[2,264,512]{2,1,0:T(8,128)S(1)}, s32[2,264,512]{2,1,0:T(8,128)}, u32[]{:S(2)}, u32[]{:S(2)}) %collective-permute-start.7) | collective-permute-done | bytes 1081376 | tf_op jit(solution)/shard_map/ppermute | solution.py:348
  55.5 2.9 collective-permute-done.4.refs_7_
  59.5 3.2 pad_add_fusion.4
  64.2 1.5 collective-permute-start.8
  67.1 2.7 collective-permute-start.10
  71.5 7.3 %collective-permute-start.36 = (f32[516,2]{1,0:T(8,128)S(1)}, f32[516,2]{1,0:T(8,128)S(1)}, u32[]{:S(2)}, u32[]{:S(2)}) collective-permute-start(f32[516,2]{1,0:T(8,128)S(1)} %get-tuple-element.74), channel_id=1, source_target_pairs={{0,1},{1,2},{2,3},{3,4},{4,5},{5,6},{6,7},{8,9},{9,10},{10,11},{11... | collective-permute-start | bytes 12392 | tf_op jit(solution)/shard_map/ppermute | solution.py:468
  78.8 18.3 %collective-permute-done.9.refs_7_ = s32[3,264,512]{2,1,0:T(8,128)} collective-permute-done((s32[3,264,512]{2,1,0:T(8,128)}, s32[3,264,512]{2,1,0:T(8,128)}, u32[]{:S(2)}, u32[]{:S(2)}) %collective-permute-start.9) | collective-permute-done | bytes 1622048 | tf_op jit(solution)/shard_map/ppermute | solution.py:348
  97.0 5.8 %collective-permute-start.37 = (f32[516,2]{1,0:T(8,128)S(1)}, f32[516,2]{1,0:T(8,128)S(1)}, u32[]{:S(2)}, u32[]{:S(2)}) collective-permute-start(f32[516,2]{1,0:T(8,128)S(1)} %get-tuple-element.75), channel_id=1, source_target_pairs={{1,0},{2,1},{3,2},{4,3},{5,4},{6,5},{7,6},{9,8},{10,9},{11,10},{12... | collective-permute-start | bytes 12392 | tf_op jit(solution)/shard_map/ppermute | solution.py:468
  108.6 1.7 collective-permute-start.13
  113.4 1.7 collective-permute-start.14
  117.9 1.7 collective-permute-done.17.refs_11_
  119.8 1.6 pad_maximum_fusion.6
  121.4 25.4 %shard_map.113 = (bf16[5,2,272,512]{3,2,1,0:T(8,128)(2,1)}, f32[16,5,8,384]{3,2,1,0:T(8,128)}) custom-call(s32[10]{0:T(128)} %get-tuple-element.85.refs_0_, s32[10]{0:T(128)} %select_reduce_fusion.5.refs_1_, s32[10]{0:T(128)} %get-tuple-element.83.refs_2_, s32[10]{0:T(128)} %get-tuple-element.78.refs_3_, f32[48]{0:T(128)} %reshape.375.refs_4_, ...), custom_call_target="tpu_custom_call" | custom-call | flops 2264924160 | bytes 40000000 | tf_op jit(solution)/shard_map/pallas_call | solution.py:317
  149.9 25.9 %shard_map.115 = (bf16[5,2,272,512]{3,2,1,0:T(8,128)(2,1)}, f32[16,5,8,384]{3,2,1,0:T(8,128)}) custom-call(s32[10]{0:T(128)} %get-tuple-element.82.refs_0_, s32[10]{0:T(128)} %select_reduce_fusion.1.refs_1_, s32[10]{0:T(128)} %get-tuple-element.80.refs_2_, s32[10]{0:T(128)} %get-tuple-element.79.refs_3_, f32[48]{0:T(128)} %reshape.375.refs_4_, ...), custom_call_target="tpu_custom_call" | custom-call | flops 2264924160 | bytes 40000000 | tf_op jit(solution)/shard_map/pallas_call | solution.py:317
  175.8 2.0 fusion.73
  177.8 2.8 fusion.74
  180.6 8.7 %collective-permute-start.21 = (bf16[1,272,512]{2,1,0:T(8,128)(2,1)S(1)}, bf16[1,272,512]{2,1,0:T(8,128)(2,1)S(1)}, u32[]{:S(2)}, u32[]{:S(2)}) collective-permute-start(bf16[1,272,512]{2,1,0:T(8,128)(2,1)S(1)} %get-tuple-element.52), channel_id=1, source_target_pairs={{0,16},{8,24},{16,0},{24,8},{32,48},{40,56},{48,32},{56,40},{64,80... | collective-permute-start | bytes 835592 | tf_op jit(solution)/shard_map/ppermute | solution.py:348
  189.3 36.0 %shard_map.114 = (bf16[6,2,272,512]{3,2,1,0:T(8,128)(2,1)}, f32[16,5,8,384]{3,2,1,0:T(8,128)}) custom-call(s32[12]{0:T(128)} %get-tuple-element.91.refs_0_, s32[12]{0:T(128)} %select_reduce_fusion.3.refs_1_, s32[12]{0:T(128)} %get-tuple-element.89.refs_2_, s32[12]{0:T(128)} %get-tuple-element.88.refs_3_, f32[48]{0:T(128)} %reshape.375.refs_4_, ...), custom_call_target="tpu_custom_call" | custom-call | flops 2717908992 | bytes 48000000 | tf_op jit(solution)/shard_map/pallas_call | solution.py:317
  225.3 1.5 slice_bitcast_fusion.6
  226.9 4.8 %collective-permute-start.27 = (bf16[1,272,512]{2,1,0:T(8,128)(2,1)}, bf16[1,272,512]{2,1,0:T(8,128)(2,1)S(1)}, u32[]{:S(2)}, u32[]{:S(2)}) collective-permute-start(bf16[1,272,512]{2,1,0:T(8,128)(2,1)} %get-tuple-element.53), channel_id=1, source_target_pairs={{0,32},{8,40},{16,48},{24,56},{32,64},{40,72},{48,80},{56,88},{64,... | collective-permute-start | bytes 835592 | tf_op jit(solution)/shard_map/ppermute | solution.py:348
  231.7 1.6 add_add_fusion
  233.6 4.9 %collective-permute-done.27 = bf16[1,272,512]{2,1,0:T(8,128)(2,1)S(1)} collective-permute-done((bf16[1,272,512]{2,1,0:T(8,128)(2,1)}, bf16[1,272,512]{2,1,0:T(8,128)(2,1)S(1)}, u32[]{:S(2)}, u32[]{:S(2)}) %collective-permute-start.27) | collective-permute-done | bytes 278560 | tf_op jit(solution)/shard_map/ppermute | solution.py:348
  238.6 2.1 fusion.31
  241.7 3.9 %collective-permute-start.28 = (bf16[3,272,512]{2,1,0:T(8,128)(2,1)}, bf16[3,272,512]{2,1,0:T(8,128)(2,1)}, u32[]{:S(2)}, u32[]{:S(2)}) collective-permute-start(bf16[3,272,512]{2,1,0:T(8,128)(2,1)} %pad_maximum_fusion.10), channel_id=1, source_target_pairs={{0,8},{8,16},{16,24},{24,0},{32,40},{40,48},{48,56},{56,32},{64,72... | collective-permute-start | bytes 2506760 | tf_op jit(solution)/shard_map/ppermute | solution.py:348
  247.6 3.2 collective-permute-start.23
  253.5 3.5 %collective-permute-done.28 = bf16[3,272,512]{2,1,0:T(8,128)(2,1)} collective-permute-done((bf16[3,272,512]{2,1,0:T(8,128)(2,1)}, bf16[3,272,512]{2,1,0:T(8,128)(2,1)}, u32[]{:S(2)}, u32[]{:S(2)}) %collective-permute-start.28) | collective-permute-done | bytes 835616 | tf_op jit(solution)/shard_map/ppermute | solution.py:348
  258.3 4.3 %collective-permute-done.23 = bf16[3,272,512]{2,1,0:T(8,128)(2,1)} collective-permute-done((bf16[3,272,512]{2,1,0:T(8,128)(2,1)}, bf16[3,272,512]{2,1,0:T(8,128)(2,1)}, u32[]{:S(2)}, u32[]{:S(2)}) %collective-permute-start.23) | collective-permute-done | bytes 835616 | tf_op jit(solution)/shard_map/ppermute | solution.py:348
  262.6 2.4 collective-permute-done.22
  265.0 3.1 fusion.36
  268.2 2.1 collective-permute-start.30
  272.0 2.7 collective-permute-start.24
  275.3 5.9 %all-to-all-start.1 = ((f32[16,1,7]{2,1,0:T(1,128)}), f32[16,1,7]{2,1,0:T(1,128)S(1)}, u32[]{:S(2)}, u32[]{:S(2)}) async-start(f32[16,1,7]{2,1,0:T(1,128)} %copy.31), calls=%async_computation.1 | async-start | bytes 16384 | tf_op jit(solution)/shard_map/all_to_all | solution.py:594
  281.4 2.2 fusion.6
  284.2 3.0 collective-permute-start.33
  287.2 4.6 %collective-permute-start.32 = (f32[512]{0:T(512)S(1)}, f32[512]{0:T(512)S(1)}, u32[]{:S(2)}, u32[]{:S(2)}) collective-permute-start(f32[512]{0:T(512)S(1)} %bitcast.194), channel_id=1, source_target_pairs={{8,0},{16,8},{24,16},{32,24},{40,32},{48,40},{56,48},{64,56},{72,6... | collective-permute-start | bytes 6152 | tf_op jit(solution)/shard_map/ppermute | solution.py:468
  291.8 27.4 %collective-permute-start.35 = (f32[512]{0:T(512)S(1)}, f32[512]{0:T(512)S(1)}, u32[]{:S(2)}, u32[]{:S(2)}) collective-permute-start(f32[512]{0:T(512)S(1)} %bitcast.193), channel_id=1, source_target_pairs={{0,1},{1,2},{2,3},{3,4},{4,5},{5,6},{6,7},{8,9},{9,10},{10,11},{11... | collective-permute-start | bytes 6152 | tf_op jit(solution)/shard_map/ppermute | solution.py:468
  319.2 1.9 collective-permute-start.34
  321.1 1.7 fusion.1
  324.1 2.4 fusion.11
  (166 shorter events, 40.4 us)
Async XLA Ops:
  2.0 25.8 %collective-permute-start = (f32[512]{0:T(512)S(1)}, f32[512]{0:T(512)S(1)}, u32[]{:S(2)}, u32[]{:S(2)}) collective-permute-start(f32[512]{0:T(512)S(1)} %get-tuple-element.14), channel_id=1, source_target_pairs={{0,1},{1,2},{2,3},{3,4},{4,5},{5,6},{6,7},{8,9},{9,10},{10,11},{11... | collective-permute-start | bytes 6152 | tf_op jit(solution)/shard_map/ppermute | solution.py:468
  6.1 21.6 %collective-permute-start.1 = (f32[512]{0:T(512)S(1)}, f32[512]{0:T(512)S(1)}, u32[]{:S(2)}, u32[]{:S(2)}) collective-permute-start(f32[512]{0:T(512)S(1)} %get-tuple-element.15), channel_id=1, source_target_pairs={{1,0},{2,1},{3,2},{4,3},{5,4},{6,5},{7,6},{9,8},{10,9},{11,10},{12... | collective-permute-start | bytes 6152 | tf_op jit(solution)/shard_map/ppermute | solution.py:468
  8.8 19.0 %collective-permute-start.2 = (f32[2,512]{1,0:T(2,128)S(1)}, f32[2,512]{1,0:T(2,128)S(1)}, u32[]{:S(2)}, u32[]{:S(2)}) collective-permute-start(f32[2,512]{1,0:T(2,128)S(1)} %get-tuple-element.76), channel_id=1, source_target_pairs={{0,8},{8,16},{16,24},{24,32},{32,40},{40,48},{48,56},{56,64},{64,7... | collective-permute-start | bytes 12296 | tf_op jit(solution)/shard_map/ppermute | solution.py:468
  11.9 15.9 %collective-permute-start.3 = (f32[2,512]{1,0:T(2,128)S(1)}, f32[2,512]{1,0:T(2,128)S(1)}, u32[]{:S(2)}, u32[]{:S(2)}) collective-permute-start(f32[2,512]{1,0:T(2,128)S(1)} %get-tuple-element.77), channel_id=1, source_target_pairs={{8,0},{16,8},{24,16},{32,24},{40,32},{48,40},{56,48},{64,56},{72,6... | collective-permute-start | bytes 12296 | tf_op jit(solution)/shard_map/ppermute | solution.py:468
  17.5 16.3 %all-to-all-start = ((s32[16,2,2]{2,1,0:T(2,128)}), s32[16,2,2]{2,1,0:T(2,128)S(1)}, u32[]{:S(2)}, u32[]{:S(2)}) async-start(s32[16,2,2]{2,1,0:T(2,128)} %copy.26), calls=%async_computation | async-start | bytes 32768 | tf_op jit(solution)/shard_map/all_to_all | solution.py:524
  27.9 26.7 %copy-start.3 = (s32[2,264,512]{2,1,0:T(8,128)}, s32[2,264,512]{2,1,0:T(8,128)S(1)}, u32[]{:S(2)}) copy-start(s32[2,264,512]{2,1,0:T(8,128)S(1)} %fusion.8.refs_6_) | copy-start | bytes 3244036
  28.0 25.5 %collective-permute-start.7 = (s32[2,264,512]{2,1,0:T(8,128)S(1)}, s32[2,264,512]{2,1,0:T(8,128)}, u32[]{:S(2)}, u32[]{:S(2)}) collective-permute-start(s32[2,264,512]{2,1,0:T(8,128)S(1)} %fusion.8.refs_6_), channel_id=1, source_target_pairs={{0,96},{8,104},{16,112},{24,120},{32,0},{40,8},{48,16},{56,24},{64... | collective-permute-start | bytes 3244040 | tf_op jit(solution)/shard_map/ppermute | solution.py:348
  28.6 25.9 %collective-permute-start.6 = (s32[2,264,512]{2,1,0:T(8,128)S(1)}, s32[2,264,512]{2,1,0:T(8,128)S(1)}, u32[]{:S(2)}, u32[]{:S(2)}) collective-permute-start(s32[2,264,512]{2,1,0:T(8,128)S(1)} %fusion.8.refs_6_), channel_id=1, source_target_pairs={{0,32},{8,40},{16,48},{24,56},{32,64},{40,72},{48,80},{56,88},{64,... | collective-permute-start | bytes 3244040 | tf_op jit(solution)/shard_map/ppermute | solution.py:348
  30.7 23.9 %collective-permute-start.5 = (s32[2,264,512]{2,1,0:T(8,128)S(1)}, s32[2,264,512]{2,1,0:T(8,128)S(1)}, u32[]{:S(2)}, u32[]{:S(2)}) collective-permute-start(s32[2,264,512]{2,1,0:T(8,128)S(1)} %fusion.8.refs_6_), channel_id=1, source_target_pairs={{0,24},{8,0},{16,8},{24,16},{32,56},{40,32},{48,40},{56,48},{64,88... | collective-permute-start | bytes 3244040 | tf_op jit(solution)/shard_map/ppermute | solution.py:348
  33.9 24.6 %collective-permute-start.4 = (s32[2,264,512]{2,1,0:T(8,128)S(1)}, s32[2,264,512]{2,1,0:T(8,128)}, u32[]{:S(2)}, u32[]{:S(2)}) collective-permute-start(s32[2,264,512]{2,1,0:T(8,128)S(1)} %fusion.8.refs_6_), channel_id=1, source_target_pairs={{0,8},{8,16},{16,24},{24,0},{32,40},{40,48},{48,56},{56,32},{64,72... | collective-permute-start | bytes 3244040 | tf_op jit(solution)/shard_map/ppermute | solution.py:348
  59.5 11.8 %copy-start = (f32[512,512]{1,0:T(8,128)S(1)}, f32[512,512]{1,0:T(8,128)}, u32[]{:S(2)}) copy-start(f32[512,512]{1,0:T(8,128)} %param.10) | copy-start | bytes 3145732
  62.7 34.3 %collective-permute-start.9 = (s32[3,264,512]{2,1,0:T(8,128)}, s32[3,264,512]{2,1,0:T(8,128)}, u32[]{:S(2)}, u32[]{:S(2)}) collective-permute-start(s32[3,264,512]{2,1,0:T(8,128)} %get-tuple-element.68), channel_id=1, source_target_pairs={{0,24},{8,0},{16,8},{24,16},{32,56},{40,32},{48,40},{56,48},{64,88... | collective-permute-start | bytes 4866056 | tf_op jit(solution)/shard_map/ppermute | solution.py:348
  64.2 41.3 %collective-permute-start.8 = (s32[3,264,512]{2,1,0:T(8,128)}, s32[3,264,512]{2,1,0:T(8,128)}, u32[]{:S(2)}, u32[]{:S(2)}) collective-permute-start(s32[3,264,512]{2,1,0:T(8,128)} %get-tuple-element.67), channel_id=1, source_target_pairs={{0,8},{8,16},{16,24},{24,0},{32,40},{40,48},{48,56},{56,32},{64,72... | collective-permute-start | bytes 4866056 | tf_op jit(solution)/shard_map/ppermute | solution.py:348
  67.0 40.7 %collective-permute-start.11 = (s32[3,264,512]{2,1,0:T(8,128)}, s32[3,264,512]{2,1,0:T(8,128)S(1)}, u32[]{:S(2)}, u32[]{:S(2)}) collective-permute-start(s32[3,264,512]{2,1,0:T(8,128)} %get-tuple-element.66), channel_id=1, source_target_pairs={{0,96},{8,104},{16,112},{24,120},{32,0},{40,8},{48,16},{56,24},{64... | collective-permute-start | bytes 4866056 | tf_op jit(solution)/shard_map/ppermute | solution.py:348
  67.1 41.5 %collective-permute-start.10 = (s32[3,264,512]{2,1,0:T(8,128)}, s32[3,264,512]{2,1,0:T(8,128)S(1)}, u32[]{:S(2)}, u32[]{:S(2)}) collective-permute-start(s32[3,264,512]{2,1,0:T(8,128)} %get-tuple-element.69), channel_id=1, source_target_pairs={{0,32},{8,40},{16,48},{24,56},{32,64},{40,72},{48,80},{56,88},{64,... | collective-permute-start | bytes 4866056 | tf_op jit(solution)/shard_map/ppermute | solution.py:348
  71.5 41.9 %collective-permute-start.36 = (f32[516,2]{1,0:T(8,128)S(1)}, f32[516,2]{1,0:T(8,128)S(1)}, u32[]{:S(2)}, u32[]{:S(2)}) collective-permute-start(f32[516,2]{1,0:T(8,128)S(1)} %get-tuple-element.74), channel_id=1, source_target_pairs={{0,1},{1,2},{2,3},{3,4},{4,5},{5,6},{6,7},{8,9},{9,10},{10,11},{11... | collective-permute-start | bytes 12392 | tf_op jit(solution)/shard_map/ppermute | solution.py:468
  97.0 16.3 %collective-permute-start.37 = (f32[516,2]{1,0:T(8,128)S(1)}, f32[516,2]{1,0:T(8,128)S(1)}, u32[]{:S(2)}, u32[]{:S(2)}) collective-permute-start(f32[516,2]{1,0:T(8,128)S(1)} %get-tuple-element.75), channel_id=1, source_target_pairs={{1,0},{2,1},{3,2},{4,3},{5,4},{6,5},{7,6},{9,8},{10,9},{11,10},{12... | collective-permute-start | bytes 12392 | tf_op jit(solution)/shard_map/ppermute | solution.py:468
  105.4 14.2 %collective-permute-start.17 = (s32[1,264,512]{2,1,0:T(8,128)S(1)}, s32[1,264,512]{2,1,0:T(8,128)}, u32[]{:S(2)}, u32[]{:S(2)}) collective-permute-start(s32[1,264,512]{2,1,0:T(8,128)S(1)} %get-tuple-element.58), channel_id=1, source_target_pairs={{0,64},{8,72},{16,80},{24,88},{32,96},{40,104},{48,112},{56,120},{... | collective-permute-start | bytes 1622024 | tf_op jit(solution)/shard_map/ppermute | solution.py:348
  107.7 41.4 %collective-permute-start.15 = (s32[2,264,512]{2,1,0:T(8,128)}, s32[2,264,512]{2,1,0:T(8,128)}, u32[]{:S(2)}, u32[]{:S(2)}) collective-permute-start(s32[2,264,512]{2,1,0:T(8,128)} %pad_add_fusion.10), channel_id=1, source_target_pairs={{0,96},{8,104},{16,112},{24,120},{32,0},{40,8},{48,16},{56,24},{64... | collective-permute-start | bytes 3244040 | tf_op jit(solution)/shard_map/ppermute | solution.py:348
  108.6 40.5 %collective-permute-start.13 = (s32[2,264,512]{2,1,0:T(8,128)S(1)}, s32[2,264,512]{2,1,0:T(8,128)}, u32[]{:S(2)}, u32[]{:S(2)}) collective-permute-start(s32[2,264,512]{2,1,0:T(8,128)S(1)} %slice.448), channel_id=1, source_target_pairs={{0,24},{8,0},{16,8},{24,16},{32,56},{40,32},{48,40},{56,48},{64,88... | collective-permute-start | bytes 3244040 | tf_op jit(solution)/shard_map/ppermute | solution.py:348
  113.4 8.0 %copy-start.8 = (f32[516,2]{1,0:T(8,128)}, f32[516,2]{1,0:T(8,128)S(1)}, u32[]{:S(2)}) copy-start(f32[516,2]{1,0:T(8,128)S(1)} %collective-permute-done.36) | copy-start | bytes 12388
  113.4 35.7 %collective-permute-start.12 = (s32[2,264,512]{2,1,0:T(8,128)}, s32[2,264,512]{2,1,0:T(8,128)}, u32[]{:S(2)}, u32[]{:S(2)}) collective-permute-start(s32[2,264,512]{2,1,0:T(8,128)} %pad_add_fusion.9), channel_id=1, source_target_pairs={{0,8},{8,16},{16,24},{24,0},{32,40},{40,48},{48,56},{56,32},{64,72... | collective-permute-start | bytes 3244040 | tf_op jit(solution)/shard_map/ppermute | solution.py:348
  113.4 8.0 %copy-start.10 = (f32[516,2]{1,0:T(8,128)}, f32[516,2]{1,0:T(8,128)S(1)}, u32[]{:S(2)}) copy-start(f32[516,2]{1,0:T(8,128)S(1)} %collective-permute-done.37) | copy-start | bytes 12388
  113.4 35.7 %collective-permute-start.14 = (s32[2,264,512]{2,1,0:T(8,128)}, s32[2,264,512]{2,1,0:T(8,128)}, u32[]{:S(2)}, u32[]{:S(2)}) collective-permute-start(s32[2,264,512]{2,1,0:T(8,128)} %slice.449), channel_id=1, source_target_pairs={{0,32},{8,40},{16,48},{24,56},{32,64},{40,72},{48,80},{56,88},{64,... | collective-permute-start | bytes 3244040 | tf_op jit(solution)/shard_map/ppermute | solution.py:348
  119.6 29.5 %collective-permute-start.16 = (s32[1,264,512]{2,1,0:T(8,128)}, s32[1,264,512]{2,1,0:T(8,128)S(1)}, u32[]{:S(2)}, u32[]{:S(2)}) collective-permute-start(s32[1,264,512]{2,1,0:T(8,128)} %get-tuple-element.60), channel_id=1, source_target_pairs={{0,16},{8,24},{16,0},{24,8},{32,48},{40,56},{48,32},{56,40},{64,80... | collective-permute-start | bytes 1622024 | tf_op jit(solution)/shard_map/ppermute | solution.py:348
  180.6 51.1 %collective-permute-start.21 = (bf16[1,272,512]{2,1,0:T(8,128)(2,1)S(1)}, bf16[1,272,512]{2,1,0:T(8,128)(2,1)S(1)}, u32[]{:S(2)}, u32[]{:S(2)}) collective-permute-start(bf16[1,272,512]{2,1,0:T(8,128)(2,1)S(1)} %get-tuple-element.52), channel_id=1, source_target_pairs={{0,16},{8,24},{16,0},{24,8},{32,48},{40,56},{48,32},{56,40},{64,80... | collective-permute-start | bytes 835592 | tf_op jit(solution)/shard_map/ppermute | solution.py:348
  189.3 49.2 %collective-permute-start.19 = (bf16[3,272,512]{2,1,0:T(8,128)(2,1)}, bf16[3,272,512]{2,1,0:T(8,128)(2,1)}, u32[]{:S(2)}, u32[]{:S(2)}) collective-permute-start(bf16[3,272,512]{2,1,0:T(8,128)(2,1)} %get-tuple-element.56), channel_id=1, source_target_pairs={{0,96},{8,104},{16,112},{24,120},{32,0},{40,8},{48,16},{56,24},{64... | collective-permute-start | bytes 2506760 | tf_op jit(solution)/shard_map/ppermute | solution.py:348
  189.3 49.2 %collective-permute-start.18 = (bf16[3,272,512]{2,1,0:T(8,128)(2,1)}, bf16[3,272,512]{2,1,0:T(8,128)(2,1)}, u32[]{:S(2)}, u32[]{:S(2)}) collective-permute-start(bf16[3,272,512]{2,1,0:T(8,128)(2,1)} %get-tuple-element.57), channel_id=1, source_target_pairs={{0,24},{8,0},{16,8},{24,16},{32,56},{40,32},{48,40},{56,48},{64,88... | collective-permute-start | bytes 2506760 | tf_op jit(solution)/shard_map/ppermute | solution.py:348
  226.9 11.6 %collective-permute-start.27 = (bf16[1,272,512]{2,1,0:T(8,128)(2,1)}, bf16[1,272,512]{2,1,0:T(8,128)(2,1)S(1)}, u32[]{:S(2)}, u32[]{:S(2)}) collective-permute-start(bf16[1,272,512]{2,1,0:T(8,128)(2,1)} %get-tuple-element.53), channel_id=1, source_target_pairs={{0,32},{8,40},{16,48},{24,56},{32,64},{40,72},{48,80},{56,88},{64,... | collective-permute-start | bytes 835592 | tf_op jit(solution)/shard_map/ppermute | solution.py:348
  231.6 6.8 %collective-permute-start.26 = (bf16[1,272,512]{2,1,0:T(8,128)(2,1)S(1)}, bf16[1,272,512]{2,1,0:T(8,128)(2,1)S(1)}, u32[]{:S(2)}, u32[]{:S(2)}) collective-permute-start(bf16[1,272,512]{2,1,0:T(8,128)(2,1)S(1)} %get-tuple-element.54), channel_id=1, source_target_pairs={{0,8},{8,16},{16,24},{24,0},{32,40},{40,48},{48,56},{56,32},{64,72... | collective-permute-start | bytes 835592 | tf_op jit(solution)/shard_map/ppermute | solution.py:348
  231.6 6.9 %collective-permute-start.25 = (bf16[1,272,512]{2,1,0:T(8,128)(2,1)S(1)}, bf16[1,272,512]{2,1,0:T(8,128)(2,1)S(1)}, u32[]{:S(2)}, u32[]{:S(2)}) collective-permute-start(bf16[1,272,512]{2,1,0:T(8,128)(2,1)S(1)} %get-tuple-element.55), channel_id=1, source_target_pairs={{0,64},{8,72},{16,80},{24,88},{32,96},{40,104},{48,112},{56,120},{... | collective-permute-start | bytes 835592 | tf_op jit(solution)/shard_map/ppermute | solution.py:348
  231.7 6.9 %copy-start.6 = (bf16[6,2,272,512]{3,2,1,0:T(8,128)(2,1)S(1)}, bf16[6,2,272,512]{3,2,1,0:T(8,128)(2,1)}, u32[]{:S(2)}) copy-start(bf16[6,2,272,512]{3,2,1,0:T(8,128)(2,1)} %get-tuple-element.9) | copy-start | bytes 10027012
  241.7 15.3 %collective-permute-start.28 = (bf16[3,272,512]{2,1,0:T(8,128)(2,1)}, bf16[3,272,512]{2,1,0:T(8,128)(2,1)}, u32[]{:S(2)}, u32[]{:S(2)}) collective-permute-start(bf16[3,272,512]{2,1,0:T(8,128)(2,1)} %pad_maximum_fusion.10), channel_id=1, source_target_pairs={{0,8},{8,16},{16,24},{24,0},{32,40},{40,48},{48,56},{56,32},{64,72... | collective-permute-start | bytes 2506760 | tf_op jit(solution)/shard_map/ppermute | solution.py:348
  246.6 11.7 %collective-permute-start.20 = (bf16[3,272,512]{2,1,0:T(8,128)(2,1)}, bf16[3,272,512]{2,1,0:T(8,128)(2,1)}, u32[]{:S(2)}, u32[]{:S(2)}) collective-permute-start(bf16[3,272,512]{2,1,0:T(8,128)(2,1)} %pad_maximum_fusion.7), channel_id=1, source_target_pairs={{0,24},{8,0},{16,8},{24,16},{32,56},{40,32},{48,40},{56,48},{64,88... | collective-permute-start | bytes 2506760 | tf_op jit(solution)/shard_map/ppermute | solution.py:348
  247.6 15.0 %collective-permute-start.23 = (bf16[3,272,512]{2,1,0:T(8,128)(2,1)}, bf16[3,272,512]{2,1,0:T(8,128)(2,1)}, u32[]{:S(2)}, u32[]{:S(2)}) collective-permute-start(bf16[3,272,512]{2,1,0:T(8,128)(2,1)} %pad_maximum_fusion.9), channel_id=1, source_target_pairs={{0,32},{8,40},{16,48},{24,56},{32,64},{40,72},{48,80},{56,88},{64,... | collective-permute-start | bytes 2506760 | tf_op jit(solution)/shard_map/ppermute | solution.py:348
  251.8 13.2 %collective-permute-start.22 = (bf16[3,272,512]{2,1,0:T(8,128)(2,1)}, bf16[3,272,512]{2,1,0:T(8,128)(2,1)}, u32[]{:S(2)}, u32[]{:S(2)}) collective-permute-start(bf16[3,272,512]{2,1,0:T(8,128)(2,1)} %pad_maximum_fusion.8), channel_id=1, source_target_pairs={{0,96},{8,104},{16,112},{24,120},{32,0},{40,8},{48,16},{56,24},{64... | collective-permute-start | bytes 2506760 | tf_op jit(solution)/shard_map/ppermute | solution.py:348
  268.1 13.1 %collective-permute-start.29 = (bf16[2,272,512]{2,1,0:T(8,128)(2,1)S(1)}, bf16[2,272,512]{2,1,0:T(8,128)(2,1)}, u32[]{:S(2)}, u32[]{:S(2)}) collective-permute-start(bf16[2,272,512]{2,1,0:T(8,128)(2,1)S(1)} %pad_maximum_fusion.12), channel_id=1, source_target_pairs={{0,8},{8,16},{16,24},{24,0},{32,40},{40,48},{48,56},{56,32},{64,72... | collective-permute-start | bytes 1671176 | tf_op jit(solution)/shard_map/ppermute | solution.py:348
  268.2 13.0 %collective-permute-start.30 = (bf16[2,272,512]{2,1,0:T(8,128)(2,1)S(1)}, bf16[2,272,512]{2,1,0:T(8,128)(2,1)}, u32[]{:S(2)}, u32[]{:S(2)}) collective-permute-start(bf16[2,272,512]{2,1,0:T(8,128)(2,1)S(1)} %pad_maximum_fusion.13), channel_id=1, source_target_pairs={{0,96},{8,104},{16,112},{24,120},{32,0},{40,8},{48,16},{56,24},{64... | collective-permute-start | bytes 1671176 | tf_op jit(solution)/shard_map/ppermute | solution.py:348
  270.4 10.8 %collective-permute-start.31 = (bf16[2,272,512]{2,1,0:T(8,128)(2,1)S(1)}, bf16[2,272,512]{2,1,0:T(8,128)(2,1)}, u32[]{:S(2)}, u32[]{:S(2)}) collective-permute-start(bf16[2,272,512]{2,1,0:T(8,128)(2,1)S(1)} %pad_maximum_fusion.14), channel_id=1, source_target_pairs={{0,32},{8,40},{16,48},{24,56},{32,64},{40,72},{48,80},{56,88},{64,... | collective-permute-start | bytes 1671176 | tf_op jit(solution)/shard_map/ppermute | solution.py:348
  272.0 9.4 %collective-permute-start.24 = (bf16[2,272,512]{2,1,0:T(8,128)(2,1)}, bf16[2,272,512]{2,1,0:T(8,128)(2,1)}, u32[]{:S(2)}, u32[]{:S(2)}) collective-permute-start(bf16[2,272,512]{2,1,0:T(8,128)(2,1)} %pad_maximum_fusion.11), channel_id=1, source_target_pairs={{0,24},{8,0},{16,8},{24,16},{32,56},{40,32},{48,40},{56,48},{64,88... | collective-permute-start | bytes 1671176 | tf_op jit(solution)/shard_map/ppermute | solution.py:348
  275.3 47.5 %all-to-all-start.1 = ((f32[16,1,7]{2,1,0:T(1,128)}), f32[16,1,7]{2,1,0:T(1,128)S(1)}, u32[]{:S(2)}, u32[]{:S(2)}) async-start(f32[16,1,7]{2,1,0:T(1,128)} %copy.31), calls=%async_computation.1 | async-start | bytes 16384 | tf_op jit(solution)/shard_map/all_to_all | solution.py:594
  281.2 39.9 %copy-start.1 = (f32[516,516]{1,0:T(8,128)S(1)}, f32[516,516]{1,0:T(8,128)}, u32[]{:S(2)}) copy-start(f32[516,516]{1,0:T(8,128)} %pad_maximum_fusion.6) | copy-start | bytes 3195076
  281.2 39.9 %copy-start.9 = (f32[516,2]{1,0:T(8,128)S(1)}, f32[516,2]{1,0:T(8,128)}, u32[]{:S(2)}) copy-start(f32[516,2]{1,0:T(8,128)} %copy-done.8) | copy-start | bytes 12388
  281.2 39.9 %copy-start.11 = (f32[516,2]{1,0:T(8,128)S(1)}, f32[516,2]{1,0:T(8,128)}, u32[]{:S(2)}) copy-start(f32[516,2]{1,0:T(8,128)} %copy-done.10) | copy-start | bytes 12388
  284.2 39.3 %collective-permute-start.33 = (f32[512]{0:T(512)}, f32[512]{0:T(512)S(1)}, u32[]{:S(2)}, u32[]{:S(2)}) collective-permute-start(f32[512]{0:T(512)} %bitcast.49), channel_id=1, source_target_pairs={{0,8},{8,16},{16,24},{24,32},{32,40},{40,48},{48,56},{56,64},{64,7... | collective-permute-start | bytes 6152 | tf_op jit(solution)/shard_map/ppermute | solution.py:468
  287.2 36.3 %collective-permute-start.32 = (f32[512]{0:T(512)S(1)}, f32[512]{0:T(512)S(1)}, u32[]{:S(2)}, u32[]{:S(2)}) collective-permute-start(f32[512]{0:T(512)S(1)} %bitcast.194), channel_id=1, source_target_pairs={{8,0},{16,8},{24,16},{32,24},{40,32},{48,40},{56,48},{64,56},{72,6... | collective-permute-start | bytes 6152 | tf_op jit(solution)/shard_map/ppermute | solution.py:468
  291.8 31.7 %collective-permute-start.35 = (f32[512]{0:T(512)S(1)}, f32[512]{0:T(512)S(1)}, u32[]{:S(2)}, u32[]{:S(2)}) collective-permute-start(f32[512]{0:T(512)S(1)} %bitcast.193), channel_id=1, source_target_pairs={{0,1},{1,2},{2,3},{3,4},{4,5},{5,6},{6,7},{8,9},{9,10},{10,11},{11... | collective-permute-start | bytes 6152 | tf_op jit(solution)/shard_map/ppermute | solution.py:468
  319.2 4.9 %collective-permute-start.34 = (f32[512]{0:T(512)S(1)}, f32[512]{0:T(512)S(1)}, u32[]{:S(2)}, u32[]{:S(2)}) collective-permute-start(f32[512]{0:T(512)S(1)} %bitcast.192), channel_id=1, source_target_pairs={{1,0},{2,1},{3,2},{4,3},{5,4},{6,5},{7,6},{9,8},{10,9},{11,10},{12... | collective-permute-start | bytes 6152 | tf_op jit(solution)/shard_map/ppermute | solution.py:468
  (9 other events, 33.8 us)

commit v6 on v5

--- a/solution.py
+++ b/solution.py
@@ -40,7 +40,7 @@
     (
         res_ref, obs_ref,
         out_ref, sums_ref,
-        rim, hbuf, hcol, sx_ref, sy_ref, w_ref, r2_ref, gx_ref, gy_ref,
+        rim, words_ref, hbuf, hcol, sx_ref, sy_ref, w_ref, r2_ref, gx_ref, gy_ref,
         shaded, tbuf, pbuf, weighted, grad,
     ) = refs[6 + operands :]
     step = pl.program_id(0)
@@ -48,6 +48,16 @@
     slot_odd = step % 2
     mine = used[step] == 1
     any_used = used[first] + used[first + 1] > 0
+    low_row = jnp.minimum(
+        jnp.where(used[first] == 1, row_off[first], 128),
+        jnp.where(used[first + 1] == 1, row_off[first + 1], 128),
+    )
+    high_row = C + jnp.maximum(
+        jnp.where(used[first] == 1, row_off[first], 0),
+        jnp.where(used[first + 1] == 1, row_off[first + 1], 0),
+    )
+    low_block = low_row // 128
+    high_block = high_row // 128
     lane = lax.broadcasted_iota(I32, (CH, 128), 1)
     at_first = lane == 0
     at_last = lane == 127
@@ -68,15 +78,18 @@
                 rim[half] = ref[at, HALF:PIECE]
 
                 def unpack(k, _, ref=ref, at=at, half=half):
-                    base = pl.multiple_of(k * CH, CH)
-                    to = pl.multiple_of(base + HALF * half, CH)
+                    base = pl.multiple_of(k * 64, 64)
+                    to = pl.multiple_of(base + HALF * half, 64)
                     for b in range(4):
-                        words = ref[at, pl.ds(base, CH), lanes(b)]
-                        hbuf[b, pl.ds(to + 8, CH)] = high_of(words)
-                        w_ref[b, pl.ds(to, CH)] = low_of(words) * (1.0 / A_SCALE) + 1.0
+                        words = ref[at, pl.ds(base, 64), lanes(b)]
+                        hbuf[b, pl.ds(to + 8, 64)] = high_of(words)
+                        words_ref[b, pl.ds(to, 64)] = words
                     return 0
 
-                lax.fori_loop(0, HALF // CH, unpack, 0)
+                if half:
+                    lax.fori_loop(0, high_block, unpack, 0)
+                else:
+                    lax.fori_loop(low_block, 4, unpack, 0)
 
     @pl.when((slot_odd == 0) & any_used)
     def _():
@@ -108,10 +121,13 @@
         for b in range(4):
             hbuf[b, 7:8] = top[1:2, lanes(b)]
             hbuf[b, T + 8 : T + 9] = bottom[1:2, lanes(b)]
-            gy_ref[b, 0:8] = jnp.zeros((8, 128), F32)
-            gy_ref[b, T + 8 : T + 16] = jnp.zeros((8, 128), F32)
-
-        def slope(k, _):
+            for at in (0, 8, 128, C + 8, T, T + 8):
+                gy_ref[b, at : at + 8] = jnp.zeros((8, 128), F32)
+        for b in (0, 3):
+            gx_ref[b, 0:128] = jnp.zeros((128, 128), F32)
+            gx_ref[b, C:T] = jnp.zeros((128, 128), F32)
+
+        def slope(k):
             base = pl.multiple_of(k * CH, CH)
             rows = pl.ds(base, CH)
             here = [hbuf[b, pl.ds(base + 8, CH)] for b in range(4)]
@@ -126,16 +142,21 @@
                 sy = (hbuf[b, pl.ds(base + 9, CH)] - hbuf[b, pl.ds(base + 7, CH)]) * (
                     0.5 / H_SCALE
                 )
+                albedo = low_of(words_ref[b, rows]) * (1.0 / A_SCALE) + 1.0
                 r = lax.rsqrt(1.0 + sx * sx + sy * sy)
                 sx_ref[b, rows] = sx
                 sy_ref[b, rows] = sy
-                w_ref[b, rows] = w_ref[b, rows] * r
+                w_ref[b, rows] = albedo * r
                 r2_ref[b, rows] = r * r
                 gx_ref[b, rows] = jnp.zeros((CH, 128), F32)
                 gy_ref[b, pl.ds(base + 8, CH)] = jnp.zeros((CH, 128), F32)
+
+        def slope_block(k, _):
+            for n in range(4):
+                slope(4 * k + n)
             return 0
 
-        lax.fori_loop(0, T // CH, slope, 0, unroll=4)
+        lax.fori_loop(low_block, high_block, slope_block, 0)
 
     @pl.when(mine)
     def _():
@@ -147,26 +168,36 @@
         s3 = sun[32 + m]
         e = gain[m]
 
-        def shade(k, _):
-            base = pl.multiple_of(k * CH, CH)
+        def shade(k):
+            base = k * CH
             rows = pl.ds(pl.multiple_of(oy + base, CH), CH)
             for b in range(3):
                 q = s3 - s1 * sx_ref[ob + b, rows] - s2 * sy_ref[ob + b, rows]
                 shaded[pl.ds(base, CH), lanes(b)] = (w_ref[ob + b, rows] * q).astype(BF16)
                 tbuf[b, pl.ds(base, CH)] = q * r2_ref[ob + b, rows]
-            return 0
-
-        lax.fori_loop(0, C // CH, shade, 0, unroll=4)
+
+        for k in range(C // CH):
+            shade(k)
         row_mat = res_ref[0, 0]
         col_mat = res_ref[0, 1]
         first_pass = jnp.dot(row_mat, shaded[...], preferred_element_type=F32).astype(BF16)
-        predicted = e * lax.dot_general(
-            first_pass, col_mat, (((1,), (1,)), ((), ())), preferred_element_type=F32
-        )
-        for b in range(3):
-            pbuf[b, 8 : 8 + C] = predicted[:, lanes(b)]
-            pbuf[b, 7:8] = 2.0 * pbuf[b, 8:9] - pbuf[b, 9:10]
-            pbuf[b, C + 8 : C + 9] = 2.0 * pbuf[b, C + 7 : C + 8] - pbuf[b, C + 6 : C + 7]
+
+        def predict(low, high):
+            block = e * lax.dot_general(
+                first_pass[low:high],
+                col_mat,
+                (((1,), (1,)), ((), ())),
+                preferred_element_type=F32,
+            )
+            for b in range(3):
+                pbuf[b, 8 + low : 8 + high] = block[:, lanes(b)]
+                if low == 0:
+                    pbuf[b, 7:8] = 2.0 * block[0:1, lanes(b)] - block[1:2, lanes(b)]
+                if high == C:
+                    end = high - low
+                    pbuf[b, C + 8 : C + 9] = (
+                        2.0 * block[end - 1 : end, lanes(b)] - block[end - 2 : end - 1, lanes(b)]
+                    )
 
         def add_up(v, base, total, by_row):
             groups = [v[8 * g : 8 * g + 8] for g in range(CH // 8)]
@@ -179,8 +210,8 @@
             return total + tail, by_row + lead * 8.0 + tail * base
 
         def terms(k, carry):
-            base = pl.multiple_of(k * CH, CH)
-            at = base.astype(F32)
+            base = k * CH
+            at = float(base)
             rows = pl.ds(base, CH)
             here = [pbuf[b, pl.ds(base + 8, CH)] for b in range(3)]
             right_turn = [pltpu.roll(p, 1, 1) for p in here]
@@ -205,19 +236,22 @@
             return tuple(result)
 
         zero = jnp.zeros((8, 128), F32)
-        parts = lax.fori_loop(0, C // CH, terms, ((zero,) * 5,) * 3, unroll=3)
+        parts = ((zero,) * 5,) * 3
+        predict(0, 256)
+        for k in range(0, 7):
+            parts = terms(k, parts)
+        predict(256, 384)
+        tall = (((0,), (0,)), ((), ()))
+        for k in range(7, 12):
+            parts = terms(k, parts)
+        back = lax.dot_general(row_mat, weighted[...], tall, preferred_element_type=F32)
         for b in range(3):
             for n in range(5):
                 sums_ref[m, n, :, lanes(b)] = parts[b][n]
-        back_pass = lax.dot_general(
-            row_mat, weighted[...], (((0,), (0,)), ((), ())), preferred_element_type=F32
-        ).astype(BF16)
-        crop_grad = jnp.dot(back_pass, col_mat, preferred_element_type=F32)
-        for b in range(3):
-            grad[b] = crop_grad[:, lanes(b)]
-
-        def pull(k, _):
-            base = pl.multiple_of(k * CH, CH)
+        back_pass = back.astype(BF16)
+
+        def pull(k):
+            base = k * CH
             rows = pl.ds(pl.multiple_of(oy + base, CH), CH)
             rows_y = pl.ds(pl.multiple_of(oy + base + 8, 8), CH)
             for b in range(3):
@@ -227,16 +261,19 @@
                 gy_ref[ob + b, rows_y] = gy_ref[ob + b, rows_y] - wg * (
                     s2 + t * sy_ref[ob + b, rows]
                 )
-            return 0
-
-        lax.fori_loop(0, C // CH, pull, 0, unroll=4)
+
+        for low, high in ((0, 256), (256, C)):
+            block = jnp.dot(back_pass[low:high], col_mat, preferred_element_type=F32)
+            for b in range(3):
+                grad[b, low:high] = block[:, lanes(b)]
+            for k in range(low // CH, high // CH):
+                pull(k)
 
     @pl.when((slot_odd == 1) & any_used)
     def _():
-        def stencil(k, _):
+        def stencil(k, half):
             base = pl.multiple_of(k * CH, CH)
             rows = pl.ds(base, CH)
-            half = k // (HALF // CH)
             to = pl.ds(pl.multiple_of(base - half * HALF, CH), CH)
             here = [gx_ref[b, rows] for b in range(4)]
             right_turn = [pltpu.roll(g, 1, 1) for g in here]
@@ -251,11 +288,30 @@
                 down = gy_ref[b, pl.ds(base + 9, CH)]
                 total = (left - right) + (up - down)
                 out_ref[0, half, to, lanes(b)] = (0.5 * total).astype(BF16)
+
+        def stencil_block(k, _):
+            for n in range(4):
+                stencil(4 * k + n, k // 2)
             return 0
 
-        lax.fori_loop(0, T // CH, stencil, 0, unroll=4)
+        lax.fori_loop(low_block, high_block, stencil_block, 0)
         sub = lax.broadcasted_iota(I32, (16, 128), 0)
         lane16 = lax.broadcasted_iota(I32, (16, 128), 1)
+
+        @pl.when(low_block == 1)
+        def _():
+            for b in range(4):
+                out_ref[0, 0, 0:112, lanes(b)] = jnp.zeros((112, 128), BF16)
+                edge = jnp.where(sub == 15, -0.5 * gy_ref[b, 136:137], 0.0)
+                out_ref[0, 0, 112:128, lanes(b)] = edge.astype(BF16)
+
+        @pl.when(high_block == 3)
+        def _():
+            for b in range(4):
+                edge = jnp.where(sub == 0, 0.5 * gy_ref[b, C + 7 : C + 8], 0.0)
+                out_ref[0, 1, 128:144, lanes(b)] = edge.astype(BF16)
+                out_ref[0, 1, 144:256, lanes(b)] = jnp.zeros((112, 128), BF16)
+
         pick_low = jnp.where((sub == 1) & (lane16 == 0), -0.5, 0.0).astype(BF16)
         pick_high = jnp.where((sub == 2) & (lane16 == 127), 0.5, 0.0).astype(BF16)
         cross = (((1,), (1,)), ((), ()))
@@ -280,6 +336,7 @@
 
 SCRATCH = [
     pltpu.VMEM((2, PIECE - HALF, T), I32),
+    pltpu.VMEM((4, T, 128), I32),
     pltpu.VMEM((4, T + 16, 128), F32),
     pltpu.VMEM((2, T, 128), F32),
     pltpu.VMEM((4, T, 128), F32),

time: 328 us -> 304 us (0.927)
  the two profiles are of different devices: /device:TPU:57 before, /device:TPU:7 now
where the time goes in v6:
time: 304 us; the launch traced here: 300 us
  starting transfers between devices  89.4 us (29%)
  waiting for transfers between devices  78.9 us (26%)
  Pallas kernels  68.8 us (23%)
  other arithmetic  34.4 us (11%)
  local copies, waits for them, and re-layouts  25.5 us (8%)
  between operations  3.19 us (1%)
    ppermute x28, waiting for transfers between devices, send(): lax.ppermute(v, 'dy', STEPS[way])  78.9 us
    pallas_call x3, Pallas kernels, run_tiles(): pl.pallas_call(functools.partial(tile_kernel, pieces, len(arrays)), grid_...  68.8 us
    ppermute x28, starting transfers between devices, send(): lax.ppermute(v, 'dy', STEPS[way])  43.4 us
    ppermute x10, starting transfers between devices, shifted(): lax.ppermute(value, axis, pairs if up else [(b, a) for a, b in pairs])  32.5 us
    all_to_all x1, starting transfers between devices, per_device(): lax.all_to_all(offsets, 'dy', split_axis=0, concat_axis=0, tiled=True)  6.86 us
    all_to_all x1, starting transfers between devices, per_device(): lax.all_to_all(crop_sums[:, None], 'dy', split_axis=0, concat_axis=0, til...  6.62 us
  transfers between devices with their start and end apart: 40, of which 15 were waited for; matrix products, arithmetic and copies ran while one was open for 13% of the time, Pallas kernels for 15%

profile of v6, /device:TPU:7, one launch (start us, length us, event | category | flops | bytes accessed | tf_op | source)
XLA Modules:
  0.0 300.1 jit_solution(6859408080255546196)
XLA Ops:
  2.0 4.1 %collective-permute-start = (f32[512]{0:T(512)S(1)}, f32[512]{0:T(512)S(1)}, u32[]{:S(2)}, u32[]{:S(2)}) collective-permute-start(f32[512]{0:T(512)S(1)} %get-tuple-element.14), channel_id=1, source_target_pairs={{0,1},{1,2},{2,3},{3,4},{4,5},{5,6},{6,7},{8,9},{9,10},{10,11},{11... | collective-permute-start | bytes 6152 | tf_op jit(solution)/shard_map/ppermute | solution.py:525
  6.1 1.9 collective-permute-start.1
  8.8 3.1 %collective-permute-start.2 = (f32[2,512]{1,0:T(2,128)S(1)}, f32[2,512]{1,0:T(2,128)S(1)}, u32[]{:S(2)}, u32[]{:S(2)}) collective-permute-start(f32[2,512]{1,0:T(2,128)S(1)} %get-tuple-element.76), channel_id=1, source_target_pairs={{0,8},{8,16},{16,24},{24,32},{32,40},{40,48},{48,56},{56,64},{64,7... | collective-permute-start | bytes 12296 | tf_op jit(solution)/shard_map/ppermute | solution.py:525
  11.9 2.2 collective-permute-start.3
  15.4 6.9 %all-to-all-start = ((s32[16,2,2]{2,1,0:T(2,128)}), s32[16,2,2]{2,1,0:T(2,128)S(1)}, u32[]{:S(2)}, u32[]{:S(2)}) async-start(s32[16,2,2]{2,1,0:T(2,128)} %copy.26), calls=%async_computation | async-start | bytes 32768 | tf_op jit(solution)/shard_map/all_to_all | solution.py:581
  26.0 1.8 and_or_fusion
  28.2 2.5 collective-permute-start.7
  32.0 2.1 collective-permute-start.4
  34.6 19.0 %collective-permute-done.7.refs_10_ = s32[2,264,512]{2,1,0:T(8,128)} collective-permute-done((s32[2,264,512]{2,1,0:T(8,128)S(1)}, s32[2,264,512]{2,1,0:T(8,128)}, u32[]{:S(2)}, u32[]{:S(2)}) %collective-permute-start.7) | collective-permute-done | bytes 1081376 | tf_op jit(solution)/shard_map/ppermute | solution.py:405
  54.7 2.3 collective-permute-done.6.refs_9_
  59.1 3.2 %pad_add_fusion.4 = (s32[3,264,512]{2,1,0:T(8,128)}, s32[3,264,512]{2,1,0:T(8,128)}, s32[3,264,512]{2,1,0:T(8,128)}, s32[3,264,512]{2,1,0:T(8,128)}) fusion(s32[1,264,512]{2,1,0:T(8,128)S(1)} %get-tuple-element.72, s32[1,264,512]{2,1,0:T(8,128)S(1)} %slice.440, s32[1,264,512]{2,1,0:T(8,128)S(1)} %slice.442, s32[1,264,512]{2,1,0:T(8,128)S(1)} %get-tuple-element.71, ...), kind=kLoop, calls=%fused_computation.4 | loop fusion | flops 3244032 | bytes 9732096 | tf_op jit(solution)/shard_map/stack | solution.py:416
  64.3 2.4 collective-permute-start.8
  68.1 3.0 collective-permute-start.11
  72.8 4.5 %collective-permute-start.36 = (f32[516,2]{1,0:T(8,128)S(1)}, f32[516,2]{1,0:T(8,128)S(1)}, u32[]{:S(2)}, u32[]{:S(2)}) collective-permute-start(f32[516,2]{1,0:T(8,128)S(1)} %get-tuple-element.74), channel_id=1, source_target_pairs={{0,1},{1,2},{2,3},{3,4},{4,5},{5,6},{6,7},{8,9},{9,10},{10,11},{11... | collective-permute-start | bytes 12392 | tf_op jit(solution)/shard_map/ppermute | solution.py:525
  77.3 23.7 %collective-permute-done.9.refs_7_ = s32[3,264,512]{2,1,0:T(8,128)} collective-permute-done((s32[3,264,512]{2,1,0:T(8,128)}, s32[3,264,512]{2,1,0:T(8,128)}, u32[]{:S(2)}, u32[]{:S(2)}) %collective-permute-start.9) | collective-permute-done | bytes 1622048 | tf_op jit(solution)/shard_map/ppermute | solution.py:405
  101.0 2.9 collective-permute-start.37
  106.5 2.1 collective-permute-start.17
  115.1 2.6 collective-permute-start.12
  124.3 21.6 %shard_map.113 = (bf16[5,2,272,512]{3,2,1,0:T(8,128)(2,1)}, f32[16,5,8,384]{3,2,1,0:T(8,128)}) custom-call(s32[10]{0:T(128)} %get-tuple-element.85.refs_0_, s32[10]{0:T(128)} %select_reduce_fusion.5.refs_1_, s32[10]{0:T(128)} %get-tuple-element.83.refs_2_, s32[10]{0:T(128)} %get-tuple-element.78.refs_3_, f32[48]{0:T(128)} %reshape.375.refs_4_, ...), custom_call_target="tpu_custom_call" | custom-call | flops 2264924160 | bytes 40000000 | tf_op jit(solution)/shard_map/pallas_call | solution.py:374
  147.0 3.1 %collective-permute-done.16.refs_10_ = s32[1,264,512]{2,1,0:T(8,128)S(1)} collective-permute-done((s32[1,264,512]{2,1,0:T(8,128)}, s32[1,264,512]{2,1,0:T(8,128)S(1)}, u32[]{:S(2)}, u32[]{:S(2)}) %collective-permute-start.16) | collective-permute-done | bytes 540704 | tf_op jit(solution)/shard_map/ppermute | solution.py:405
  150.1 2.3 collective-permute-done.12.refs_6_
  152.4 22.5 %shard_map.115 = (bf16[5,2,272,512]{3,2,1,0:T(8,128)(2,1)}, f32[16,5,8,384]{3,2,1,0:T(8,128)}) custom-call(s32[10]{0:T(128)} %get-tuple-element.82.refs_0_, s32[10]{0:T(128)} %select_reduce_fusion.1.refs_1_, s32[10]{0:T(128)} %get-tuple-element.80.refs_2_, s32[10]{0:T(128)} %get-tuple-element.79.refs_3_, f32[48]{0:T(128)} %reshape.375.refs_4_, ...), custom_call_target="tpu_custom_call" | custom-call | flops 2264924160 | bytes 40000000 | tf_op jit(solution)/shard_map/pallas_call | solution.py:374
  174.9 2.0 fusion.73
  176.9 2.8 fusion.74
  179.7 2.1 collective-permute-start.21
  181.8 3.0 collective-permute-start.19
  184.7 2.3 collective-permute-start.18
  187.1 24.6 %shard_map.114 = (bf16[6,2,272,512]{3,2,1,0:T(8,128)(2,1)}, f32[16,5,8,384]{3,2,1,0:T(8,128)}) custom-call(s32[12]{0:T(128)} %get-tuple-element.91.refs_0_, s32[12]{0:T(128)} %select_reduce_fusion.3.refs_1_, s32[12]{0:T(128)} %get-tuple-element.89.refs_2_, s32[12]{0:T(128)} %get-tuple-element.88.refs_3_, f32[48]{0:T(128)} %reshape.375.refs_4_, ...), custom_call_target="tpu_custom_call" | custom-call | flops 2717908992 | bytes 48000000 | tf_op jit(solution)/shard_map/pallas_call | solution.py:374
  213.3 4.3 %collective-permute-start.26 = (bf16[1,272,512]{2,1,0:T(8,128)(2,1)S(1)}, bf16[1,272,512]{2,1,0:T(8,128)(2,1)S(1)}, u32[]{:S(2)}, u32[]{:S(2)}) collective-permute-start(bf16[1,272,512]{2,1,0:T(8,128)(2,1)S(1)} %get-tuple-element.54), channel_id=1, source_target_pairs={{0,8},{8,16},{16,24},{24,0},{32,40},{40,48},{48,56},{56,32},{64,72... | collective-permute-start | bytes 835592 | tf_op jit(solution)/shard_map/ppermute | solution.py:405
  217.7 2.1 collective-permute-start.25
  222.5 5.3 %collective-permute-done.25 = bf16[1,272,512]{2,1,0:T(8,128)(2,1)S(1)} collective-permute-done((bf16[1,272,512]{2,1,0:T(8,128)(2,1)S(1)}, bf16[1,272,512]{2,1,0:T(8,128)(2,1)S(1)}, u32[]{:S(2)}, u32[]{:S(2)}) %collective-permute-start.25) | collective-permute-done | bytes 278560 | tf_op jit(solution)/shard_map/ppermute | solution.py:405
  227.8 2.1 fusion.31
  231.0 3.9 %collective-permute-start.28 = (bf16[3,272,512]{2,1,0:T(8,128)(2,1)}, bf16[3,272,512]{2,1,0:T(8,128)(2,1)}, u32[]{:S(2)}, u32[]{:S(2)}) collective-permute-start(bf16[3,272,512]{2,1,0:T(8,128)(2,1)} %pad_maximum_fusion.10), channel_id=1, source_target_pairs={{0,8},{8,16},{16,24},{24,0},{32,40},{40,48},{48,56},{56,32},{64,72... | collective-permute-start | bytes 2506760 | tf_op jit(solution)/shard_map/ppermute | solution.py:405
  238.0 2.7 collective-permute-start.22
  241.1 10.5 %collective-permute-done.28 = bf16[3,272,512]{2,1,0:T(8,128)(2,1)} collective-permute-done((bf16[3,272,512]{2,1,0:T(8,128)(2,1)}, bf16[3,272,512]{2,1,0:T(8,128)(2,1)}, u32[]{:S(2)}, u32[]{:S(2)}) %collective-permute-start.28) | collective-permute-done | bytes 835616 | tf_op jit(solution)/shard_map/ppermute | solution.py:405
  251.6 4.1 %collective-permute-done.20 = bf16[3,272,512]{2,1,0:T(8,128)(2,1)} collective-permute-done((bf16[3,272,512]{2,1,0:T(8,128)(2,1)}, bf16[3,272,512]{2,1,0:T(8,128)(2,1)}, u32[]{:S(2)}, u32[]{:S(2)}) %collective-permute-start.20) | collective-permute-done | bytes 835616 | tf_op jit(solution)/shard_map/ppermute | solution.py:405
  257.6 3.1 %fusion.36 = (bf16[1,272,512]{2,1,0:T(8,128)(2,1)S(1)}, bf16[1,272,512]{2,1,0:T(8,128)(2,1)S(1)}, bf16[1,272,512]{2,1,0:T(8,128)(2,1)S(1)}, bf16[1,272,512]{2,1,...) fusion(bf16[3,272,512]{2,1,0:T(8,128)(2,1)} %collective-permute-done.23, ...), kind=kLoop, calls=%fused_computation.85 | loop fusion | flops 5013504 | bytes 6684672 | tf_op jit(solution)/shard_map/convert_element_type | solution.py:439
  260.8 2.9 collective-permute-start.29
  263.7 2.1 collective-permute-start.30
  267.5 6.6 %all-to-all-start.1 = ((f32[16,1,7]{2,1,0:T(1,128)}), f32[16,1,7]{2,1,0:T(1,128)S(1)}, u32[]{:S(2)}, u32[]{:S(2)}) async-start(f32[16,1,7]{2,1,0:T(1,128)} %copy.31), calls=%async_computation.1 | async-start | bytes 16384 | tf_op jit(solution)/shard_map/all_to_all | solution.py:651
  275.5 2.0 collective-permute-done.31
  278.7 2.1 fusion.6
  281.3 2.4 collective-permute-start.33
  283.7 2.9 collective-permute-start.32
  286.6 3.9 %collective-permute-start.35 = (f32[512]{0:T(512)S(1)}, f32[512]{0:T(512)S(1)}, u32[]{:S(2)}, u32[]{:S(2)}) collective-permute-start(f32[512]{0:T(512)S(1)} %bitcast.193), channel_id=1, source_target_pairs={{0,1},{1,2},{2,3},{3,4},{4,5},{5,6},{6,7},{8,9},{9,10},{10,11},{11... | collective-permute-start | bytes 6152 | tf_op jit(solution)/shard_map/ppermute | solution.py:525
  290.5 4.6 %collective-permute-start.34 = (f32[512]{0:T(512)S(1)}, f32[512]{0:T(512)S(1)}, u32[]{:S(2)}, u32[]{:S(2)}) collective-permute-start(f32[512]{0:T(512)S(1)} %bitcast.192), channel_id=1, source_target_pairs={{1,0},{2,1},{3,2},{4,3},{5,4},{6,5},{7,6},{9,8},{10,9},{11,10},{12... | collective-permute-start | bytes 6152 | tf_op jit(solution)/shard_map/ppermute | solution.py:525
  295.2 1.7 fusion.1
  297.6 2.5 fusion.11
  (166 shorter events, 48.5 us)
Async XLA Ops:
  2.0 26.0 %collective-permute-start = (f32[512]{0:T(512)S(1)}, f32[512]{0:T(512)S(1)}, u32[]{:S(2)}, u32[]{:S(2)}) collective-permute-start(f32[512]{0:T(512)S(1)} %get-tuple-element.14), channel_id=1, source_target_pairs={{0,1},{1,2},{2,3},{3,4},{4,5},{5,6},{6,7},{8,9},{9,10},{10,11},{11... | collective-permute-start | bytes 6152 | tf_op jit(solution)/shard_map/ppermute | solution.py:525
  6.1 21.9 %collective-permute-start.1 = (f32[512]{0:T(512)S(1)}, f32[512]{0:T(512)S(1)}, u32[]{:S(2)}, u32[]{:S(2)}) collective-permute-start(f32[512]{0:T(512)S(1)} %get-tuple-element.15), channel_id=1, source_target_pairs={{1,0},{2,1},{3,2},{4,3},{5,4},{6,5},{7,6},{9,8},{10,9},{11,10},{12... | collective-permute-start | bytes 6152 | tf_op jit(solution)/shard_map/ppermute | solution.py:525
  8.8 19.2 %collective-permute-start.2 = (f32[2,512]{1,0:T(2,128)S(1)}, f32[2,512]{1,0:T(2,128)S(1)}, u32[]{:S(2)}, u32[]{:S(2)}) collective-permute-start(f32[2,512]{1,0:T(2,128)S(1)} %get-tuple-element.76), channel_id=1, source_target_pairs={{0,8},{8,16},{16,24},{24,32},{32,40},{40,48},{48,56},{56,64},{64,7... | collective-permute-start | bytes 12296 | tf_op jit(solution)/shard_map/ppermute | solution.py:525
  11.9 16.1 %collective-permute-start.3 = (f32[2,512]{1,0:T(2,128)S(1)}, f32[2,512]{1,0:T(2,128)S(1)}, u32[]{:S(2)}, u32[]{:S(2)}) collective-permute-start(f32[2,512]{1,0:T(2,128)S(1)} %get-tuple-element.77), channel_id=1, source_target_pairs={{8,0},{16,8},{24,16},{32,24},{40,32},{48,40},{56,48},{64,56},{72,6... | collective-permute-start | bytes 12296 | tf_op jit(solution)/shard_map/ppermute | solution.py:525
  15.4 18.7 %all-to-all-start = ((s32[16,2,2]{2,1,0:T(2,128)}), s32[16,2,2]{2,1,0:T(2,128)S(1)}, u32[]{:S(2)}, u32[]{:S(2)}) async-start(s32[16,2,2]{2,1,0:T(2,128)} %copy.26), calls=%async_computation | async-start | bytes 32768 | tf_op jit(solution)/shard_map/all_to_all | solution.py:581
  28.2 28.9 %copy-start.3 = (s32[2,264,512]{2,1,0:T(8,128)}, s32[2,264,512]{2,1,0:T(8,128)S(1)}, u32[]{:S(2)}) copy-start(s32[2,264,512]{2,1,0:T(8,128)S(1)} %fusion.8.refs_6_) | copy-start | bytes 3244036
  28.2 25.4 %collective-permute-start.7 = (s32[2,264,512]{2,1,0:T(8,128)S(1)}, s32[2,264,512]{2,1,0:T(8,128)}, u32[]{:S(2)}, u32[]{:S(2)}) collective-permute-start(s32[2,264,512]{2,1,0:T(8,128)S(1)} %fusion.8.refs_6_), channel_id=1, source_target_pairs={{0,96},{8,104},{16,112},{24,120},{32,0},{40,8},{48,16},{56,24},{64... | collective-permute-start | bytes 3244040 | tf_op jit(solution)/shard_map/ppermute | solution.py:405
  30.7 26.3 %collective-permute-start.6 = (s32[2,264,512]{2,1,0:T(8,128)S(1)}, s32[2,264,512]{2,1,0:T(8,128)S(1)}, u32[]{:S(2)}, u32[]{:S(2)}) collective-permute-start(s32[2,264,512]{2,1,0:T(8,128)S(1)} %fusion.8.refs_6_), channel_id=1, source_target_pairs={{0,32},{8,40},{16,48},{24,56},{32,64},{40,72},{48,80},{56,88},{64,... | collective-permute-start | bytes 3244040 | tf_op jit(solution)/shard_map/ppermute | solution.py:405
  30.7 26.4 %collective-permute-start.5 = (s32[2,264,512]{2,1,0:T(8,128)S(1)}, s32[2,264,512]{2,1,0:T(8,128)S(1)}, u32[]{:S(2)}, u32[]{:S(2)}) collective-permute-start(s32[2,264,512]{2,1,0:T(8,128)S(1)} %fusion.8.refs_6_), channel_id=1, source_target_pairs={{0,24},{8,0},{16,8},{24,16},{32,56},{40,32},{48,40},{56,48},{64,88... | collective-permute-start | bytes 3244040 | tf_op jit(solution)/shard_map/ppermute | solution.py:405
  32.0 26.0 %collective-permute-start.4 = (s32[2,264,512]{2,1,0:T(8,128)S(1)}, s32[2,264,512]{2,1,0:T(8,128)}, u32[]{:S(2)}, u32[]{:S(2)}) collective-permute-start(s32[2,264,512]{2,1,0:T(8,128)S(1)} %fusion.8.refs_6_), channel_id=1, source_target_pairs={{0,8},{8,16},{16,24},{24,0},{32,40},{40,48},{48,56},{56,32},{64,72... | collective-permute-start | bytes 3244040 | tf_op jit(solution)/shard_map/ppermute | solution.py:405
  59.1 13.6 %copy-start = (f32[512,512]{1,0:T(8,128)S(1)}, f32[512,512]{1,0:T(8,128)}, u32[]{:S(2)}) copy-start(f32[512,512]{1,0:T(8,128)} %param.10) | copy-start | bytes 3145732
  62.3 38.7 %collective-permute-start.9 = (s32[3,264,512]{2,1,0:T(8,128)}, s32[3,264,512]{2,1,0:T(8,128)}, u32[]{:S(2)}, u32[]{:S(2)}) collective-permute-start(s32[3,264,512]{2,1,0:T(8,128)} %get-tuple-element.68), channel_id=1, source_target_pairs={{0,24},{8,0},{16,8},{24,16},{32,56},{40,32},{48,40},{56,48},{64,88... | collective-permute-start | bytes 4866056 | tf_op jit(solution)/shard_map/ppermute | solution.py:405
  64.3 42.2 %collective-permute-start.8 = (s32[3,264,512]{2,1,0:T(8,128)}, s32[3,264,512]{2,1,0:T(8,128)}, u32[]{:S(2)}, u32[]{:S(2)}) collective-permute-start(s32[3,264,512]{2,1,0:T(8,128)} %get-tuple-element.67), channel_id=1, source_target_pairs={{0,8},{8,16},{16,24},{24,0},{32,40},{40,48},{48,56},{56,32},{64,72... | collective-permute-start | bytes 4866056 | tf_op jit(solution)/shard_map/ppermute | solution.py:405
  68.1 42.7 %collective-permute-start.11 = (s32[3,264,512]{2,1,0:T(8,128)}, s32[3,264,512]{2,1,0:T(8,128)S(1)}, u32[]{:S(2)}, u32[]{:S(2)}) collective-permute-start(s32[3,264,512]{2,1,0:T(8,128)} %get-tuple-element.66), channel_id=1, source_target_pairs={{0,96},{8,104},{16,112},{24,120},{32,0},{40,8},{48,16},{56,24},{64... | collective-permute-start | bytes 4866056 | tf_op jit(solution)/shard_map/ppermute | solution.py:405
  71.1 40.6 %collective-permute-start.10 = (s32[3,264,512]{2,1,0:T(8,128)}, s32[3,264,512]{2,1,0:T(8,128)S(1)}, u32[]{:S(2)}, u32[]{:S(2)}) collective-permute-start(s32[3,264,512]{2,1,0:T(8,128)} %get-tuple-element.69), channel_id=1, source_target_pairs={{0,32},{8,40},{16,48},{24,56},{32,64},{40,72},{48,80},{56,88},{64,... | collective-permute-start | bytes 4866056 | tf_op jit(solution)/shard_map/ppermute | solution.py:405
  72.8 42.2 %collective-permute-start.36 = (f32[516,2]{1,0:T(8,128)S(1)}, f32[516,2]{1,0:T(8,128)S(1)}, u32[]{:S(2)}, u32[]{:S(2)}) collective-permute-start(f32[516,2]{1,0:T(8,128)S(1)} %get-tuple-element.74), channel_id=1, source_target_pairs={{0,1},{1,2},{2,3},{3,4},{4,5},{5,6},{6,7},{8,9},{9,10},{10,11},{11... | collective-permute-start | bytes 12392 | tf_op jit(solution)/shard_map/ppermute | solution.py:525
  101.0 16.6 %collective-permute-start.37 = (f32[516,2]{1,0:T(8,128)S(1)}, f32[516,2]{1,0:T(8,128)S(1)}, u32[]{:S(2)}, u32[]{:S(2)}) collective-permute-start(f32[516,2]{1,0:T(8,128)S(1)} %get-tuple-element.75), channel_id=1, source_target_pairs={{1,0},{2,1},{3,2},{4,3},{5,4},{6,5},{7,6},{9,8},{10,9},{11,10},{12... | collective-permute-start | bytes 12392 | tf_op jit(solution)/shard_map/ppermute | solution.py:525
  106.5 15.7 %collective-permute-start.17 = (s32[1,264,512]{2,1,0:T(8,128)S(1)}, s32[1,264,512]{2,1,0:T(8,128)}, u32[]{:S(2)}, u32[]{:S(2)}) collective-permute-start(s32[1,264,512]{2,1,0:T(8,128)S(1)} %get-tuple-element.58), channel_id=1, source_target_pairs={{0,64},{8,72},{16,80},{24,88},{32,96},{40,104},{48,112},{56,120},{... | collective-permute-start | bytes 1622024 | tf_op jit(solution)/shard_map/ppermute | solution.py:405
  110.8 39.4 %collective-permute-start.15 = (s32[2,264,512]{2,1,0:T(8,128)}, s32[2,264,512]{2,1,0:T(8,128)}, u32[]{:S(2)}, u32[]{:S(2)}) collective-permute-start(s32[2,264,512]{2,1,0:T(8,128)} %pad_add_fusion.10), channel_id=1, source_target_pairs={{0,96},{8,104},{16,112},{24,120},{32,0},{40,8},{48,16},{56,24},{64... | collective-permute-start | bytes 3244040 | tf_op jit(solution)/shard_map/ppermute | solution.py:405
  111.8 38.4 %collective-permute-start.13 = (s32[2,264,512]{2,1,0:T(8,128)S(1)}, s32[2,264,512]{2,1,0:T(8,128)}, u32[]{:S(2)}, u32[]{:S(2)}) collective-permute-start(s32[2,264,512]{2,1,0:T(8,128)S(1)} %slice.448), channel_id=1, source_target_pairs={{0,24},{8,0},{16,8},{24,16},{32,56},{40,32},{48,40},{56,48},{64,88... | collective-permute-start | bytes 3244040 | tf_op jit(solution)/shard_map/ppermute | solution.py:405
  115.1 9.3 %copy-start.8 = (f32[516,2]{1,0:T(8,128)}, f32[516,2]{1,0:T(8,128)S(1)}, u32[]{:S(2)}) copy-start(f32[516,2]{1,0:T(8,128)S(1)} %collective-permute-done.36) | copy-start | bytes 12388
  115.1 37.4 %collective-permute-start.12 = (s32[2,264,512]{2,1,0:T(8,128)}, s32[2,264,512]{2,1,0:T(8,128)}, u32[]{:S(2)}, u32[]{:S(2)}) collective-permute-start(s32[2,264,512]{2,1,0:T(8,128)} %pad_add_fusion.9), channel_id=1, source_target_pairs={{0,8},{8,16},{16,24},{24,0},{32,40},{40,48},{48,56},{56,32},{64,72... | collective-permute-start | bytes 3244040 | tf_op jit(solution)/shard_map/ppermute | solution.py:405
  117.6 34.8 %collective-permute-start.14 = (s32[2,264,512]{2,1,0:T(8,128)}, s32[2,264,512]{2,1,0:T(8,128)}, u32[]{:S(2)}, u32[]{:S(2)}) collective-permute-start(s32[2,264,512]{2,1,0:T(8,128)} %slice.449), channel_id=1, source_target_pairs={{0,32},{8,40},{16,48},{24,56},{32,64},{40,72},{48,80},{56,88},{64,... | collective-permute-start | bytes 3244040 | tf_op jit(solution)/shard_map/ppermute | solution.py:405
  122.2 27.9 %collective-permute-start.16 = (s32[1,264,512]{2,1,0:T(8,128)}, s32[1,264,512]{2,1,0:T(8,128)S(1)}, u32[]{:S(2)}, u32[]{:S(2)}) collective-permute-start(s32[1,264,512]{2,1,0:T(8,128)} %get-tuple-element.60), channel_id=1, source_target_pairs={{0,16},{8,24},{16,0},{24,8},{32,48},{40,56},{48,32},{56,40},{64,80... | collective-permute-start | bytes 1622024 | tf_op jit(solution)/shard_map/ppermute | solution.py:405
  179.7 38.0 %collective-permute-start.21 = (bf16[1,272,512]{2,1,0:T(8,128)(2,1)S(1)}, bf16[1,272,512]{2,1,0:T(8,128)(2,1)S(1)}, u32[]{:S(2)}, u32[]{:S(2)}) collective-permute-start(bf16[1,272,512]{2,1,0:T(8,128)(2,1)S(1)} %get-tuple-element.52), channel_id=1, source_target_pairs={{0,16},{8,24},{16,0},{24,8},{32,48},{40,56},{48,32},{56,40},{64,80... | collective-permute-start | bytes 835592 | tf_op jit(solution)/shard_map/ppermute | solution.py:405
  181.8 46.1 %collective-permute-start.19 = (bf16[3,272,512]{2,1,0:T(8,128)(2,1)}, bf16[3,272,512]{2,1,0:T(8,128)(2,1)}, u32[]{:S(2)}, u32[]{:S(2)}) collective-permute-start(bf16[3,272,512]{2,1,0:T(8,128)(2,1)} %get-tuple-element.56), channel_id=1, source_target_pairs={{0,96},{8,104},{16,112},{24,120},{32,0},{40,8},{48,16},{56,24},{64... | collective-permute-start | bytes 2506760 | tf_op jit(solution)/shard_map/ppermute | solution.py:405
  184.7 43.1 %collective-permute-start.18 = (bf16[3,272,512]{2,1,0:T(8,128)(2,1)}, bf16[3,272,512]{2,1,0:T(8,128)(2,1)}, u32[]{:S(2)}, u32[]{:S(2)}) collective-permute-start(bf16[3,272,512]{2,1,0:T(8,128)(2,1)} %get-tuple-element.57), channel_id=1, source_target_pairs={{0,24},{8,0},{16,8},{24,16},{32,56},{40,32},{48,40},{56,48},{64,88... | collective-permute-start | bytes 2506760 | tf_op jit(solution)/shard_map/ppermute | solution.py:405
  211.7 8.0 %copy-start.13 = (f32[16,5,8,384]{3,2,1,0:T(8,128)S(1)}, f32[16,5,8,384]{3,2,1,0:T(8,128)}, u32[]{:S(2)}) copy-start(f32[16,5,8,384]{3,2,1,0:T(8,128)} %get-tuple-element.13) | copy-start | bytes 2949124
  213.2 8.4 %collective-permute-start.27 = (bf16[1,272,512]{2,1,0:T(8,128)(2,1)}, bf16[1,272,512]{2,1,0:T(8,128)(2,1)S(1)}, u32[]{:S(2)}, u32[]{:S(2)}) collective-permute-start(bf16[1,272,512]{2,1,0:T(8,128)(2,1)} %get-tuple-element.53), channel_id=1, source_target_pairs={{0,32},{8,40},{16,48},{24,56},{32,64},{40,72},{48,80},{56,88},{64,... | collective-permute-start | bytes 835592 | tf_op jit(solution)/shard_map/ppermute | solution.py:405
  213.3 9.2 %collective-permute-start.26 = (bf16[1,272,512]{2,1,0:T(8,128)(2,1)S(1)}, bf16[1,272,512]{2,1,0:T(8,128)(2,1)S(1)}, u32[]{:S(2)}, u32[]{:S(2)}) collective-permute-start(bf16[1,272,512]{2,1,0:T(8,128)(2,1)S(1)} %get-tuple-element.54), channel_id=1, source_target_pairs={{0,8},{8,16},{16,24},{24,0},{32,40},{40,48},{48,56},{56,32},{64,72... | collective-permute-start | bytes 835592 | tf_op jit(solution)/shard_map/ppermute | solution.py:405
  217.7 10.2 %collective-permute-start.25 = (bf16[1,272,512]{2,1,0:T(8,128)(2,1)S(1)}, bf16[1,272,512]{2,1,0:T(8,128)(2,1)S(1)}, u32[]{:S(2)}, u32[]{:S(2)}) collective-permute-start(bf16[1,272,512]{2,1,0:T(8,128)(2,1)S(1)} %get-tuple-element.55), channel_id=1, source_target_pairs={{0,64},{8,72},{16,80},{24,88},{32,96},{40,104},{48,112},{56,120},{... | collective-permute-start | bytes 835592 | tf_op jit(solution)/shard_map/ppermute | solution.py:405
  219.7 8.1 %copy-start.6 = (bf16[6,2,272,512]{3,2,1,0:T(8,128)(2,1)S(1)}, bf16[6,2,272,512]{3,2,1,0:T(8,128)(2,1)}, u32[]{:S(2)}) copy-start(bf16[6,2,272,512]{3,2,1,0:T(8,128)(2,1)} %get-tuple-element.9) | copy-start | bytes 10027012
  231.0 20.6 %collective-permute-start.28 = (bf16[3,272,512]{2,1,0:T(8,128)(2,1)}, bf16[3,272,512]{2,1,0:T(8,128)(2,1)}, u32[]{:S(2)}, u32[]{:S(2)}) collective-permute-start(bf16[3,272,512]{2,1,0:T(8,128)(2,1)} %pad_maximum_fusion.10), channel_id=1, source_target_pairs={{0,8},{8,16},{16,24},{24,0},{32,40},{40,48},{48,56},{56,32},{64,72... | collective-permute-start | bytes 2506760 | tf_op jit(solution)/shard_map/ppermute | solution.py:405
  235.9 19.8 %collective-permute-start.20 = (bf16[3,272,512]{2,1,0:T(8,128)(2,1)}, bf16[3,272,512]{2,1,0:T(8,128)(2,1)}, u32[]{:S(2)}, u32[]{:S(2)}) collective-permute-start(bf16[3,272,512]{2,1,0:T(8,128)(2,1)} %pad_maximum_fusion.7), channel_id=1, source_target_pairs={{0,24},{8,0},{16,8},{24,16},{32,56},{40,32},{48,40},{56,48},{64,88... | collective-permute-start | bytes 2506760 | tf_op jit(solution)/shard_map/ppermute | solution.py:405
  236.9 19.3 %collective-permute-start.23 = (bf16[3,272,512]{2,1,0:T(8,128)(2,1)}, bf16[3,272,512]{2,1,0:T(8,128)(2,1)}, u32[]{:S(2)}, u32[]{:S(2)}) collective-permute-start(bf16[3,272,512]{2,1,0:T(8,128)(2,1)} %pad_maximum_fusion.9), channel_id=1, source_target_pairs={{0,32},{8,40},{16,48},{24,56},{32,64},{40,72},{48,80},{56,88},{64,... | collective-permute-start | bytes 2506760 | tf_op jit(solution)/shard_map/ppermute | solution.py:405
  238.0 19.7 %collective-permute-start.22 = (bf16[3,272,512]{2,1,0:T(8,128)(2,1)}, bf16[3,272,512]{2,1,0:T(8,128)(2,1)}, u32[]{:S(2)}, u32[]{:S(2)}) collective-permute-start(bf16[3,272,512]{2,1,0:T(8,128)(2,1)} %pad_maximum_fusion.8), channel_id=1, source_target_pairs={{0,96},{8,104},{16,112},{24,120},{32,0},{40,8},{48,16},{56,24},{64... | collective-permute-start | bytes 2506760 | tf_op jit(solution)/shard_map/ppermute | solution.py:405
  260.8 13.4 %collective-permute-start.29 = (bf16[2,272,512]{2,1,0:T(8,128)(2,1)S(1)}, bf16[2,272,512]{2,1,0:T(8,128)(2,1)}, u32[]{:S(2)}, u32[]{:S(2)}) collective-permute-start(bf16[2,272,512]{2,1,0:T(8,128)(2,1)S(1)} %pad_maximum_fusion.12), channel_id=1, source_target_pairs={{0,8},{8,16},{16,24},{24,0},{32,40},{40,48},{48,56},{56,32},{64,72... | collective-permute-start | bytes 1671176 | tf_op jit(solution)/shard_map/ppermute | solution.py:405
  263.7 11.8 %collective-permute-start.30 = (bf16[2,272,512]{2,1,0:T(8,128)(2,1)S(1)}, bf16[2,272,512]{2,1,0:T(8,128)(2,1)}, u32[]{:S(2)}, u32[]{:S(2)}) collective-permute-start(bf16[2,272,512]{2,1,0:T(8,128)(2,1)S(1)} %pad_maximum_fusion.13), channel_id=1, source_target_pairs={{0,96},{8,104},{16,112},{24,120},{32,0},{40,8},{48,16},{56,24},{64... | collective-permute-start | bytes 1671176 | tf_op jit(solution)/shard_map/ppermute | solution.py:405
  265.9 11.7 %collective-permute-start.31 = (bf16[2,272,512]{2,1,0:T(8,128)(2,1)S(1)}, bf16[2,272,512]{2,1,0:T(8,128)(2,1)}, u32[]{:S(2)}, u32[]{:S(2)}) collective-permute-start(bf16[2,272,512]{2,1,0:T(8,128)(2,1)S(1)} %pad_maximum_fusion.14), channel_id=1, source_target_pairs={{0,32},{8,40},{16,48},{24,56},{32,64},{40,72},{48,80},{56,88},{64,... | collective-permute-start | bytes 1671176 | tf_op jit(solution)/shard_map/ppermute | solution.py:405
  266.8 11.8 %collective-permute-start.24 = (bf16[2,272,512]{2,1,0:T(8,128)(2,1)}, bf16[2,272,512]{2,1,0:T(8,128)(2,1)}, u32[]{:S(2)}, u32[]{:S(2)}) collective-permute-start(bf16[2,272,512]{2,1,0:T(8,128)(2,1)} %pad_maximum_fusion.11), channel_id=1, source_target_pairs={{0,24},{8,0},{16,8},{24,16},{32,56},{40,32},{48,40},{56,48},{64,88... | collective-permute-start | bytes 1671176 | tf_op jit(solution)/shard_map/ppermute | solution.py:405
  267.5 29.4 %all-to-all-start.1 = ((f32[16,1,7]{2,1,0:T(1,128)}), f32[16,1,7]{2,1,0:T(1,128)S(1)}, u32[]{:S(2)}, u32[]{:S(2)}) async-start(f32[16,1,7]{2,1,0:T(1,128)} %copy.31), calls=%async_computation.1 | async-start | bytes 16384 | tf_op jit(solution)/shard_map/all_to_all | solution.py:651
  274.2 21.0 %copy-start.1 = (f32[516,516]{1,0:T(8,128)S(1)}, f32[516,516]{1,0:T(8,128)}, u32[]{:S(2)}) copy-start(f32[516,516]{1,0:T(8,128)} %pad_maximum_fusion.6) | copy-start | bytes 3195076
  274.2 21.0 %copy-start.9 = (f32[516,2]{1,0:T(8,128)S(1)}, f32[516,2]{1,0:T(8,128)}, u32[]{:S(2)}) copy-start(f32[516,2]{1,0:T(8,128)} %copy-done.8) | copy-start | bytes 12388
  274.2 21.0 %copy-start.11 = (f32[516,2]{1,0:T(8,128)S(1)}, f32[516,2]{1,0:T(8,128)}, u32[]{:S(2)}) copy-start(f32[516,2]{1,0:T(8,128)} %copy-done.10) | copy-start | bytes 12388
  281.3 16.2 %collective-permute-start.33 = (f32[512]{0:T(512)}, f32[512]{0:T(512)S(1)}, u32[]{:S(2)}, u32[]{:S(2)}) collective-permute-start(f32[512]{0:T(512)} %bitcast.49), channel_id=1, source_target_pairs={{0,8},{8,16},{16,24},{24,32},{32,40},{40,48},{48,56},{56,64},{64,7... | collective-permute-start | bytes 6152 | tf_op jit(solution)/shard_map/ppermute | solution.py:525
  283.7 13.9 %collective-permute-start.32 = (f32[512]{0:T(512)S(1)}, f32[512]{0:T(512)S(1)}, u32[]{:S(2)}, u32[]{:S(2)}) collective-permute-start(f32[512]{0:T(512)S(1)} %bitcast.194), channel_id=1, source_target_pairs={{8,0},{16,8},{24,16},{32,24},{40,32},{48,40},{56,48},{64,56},{72,6... | collective-permute-start | bytes 6152 | tf_op jit(solution)/shard_map/ppermute | solution.py:525
  286.6 11.0 %collective-permute-start.35 = (f32[512]{0:T(512)S(1)}, f32[512]{0:T(512)S(1)}, u32[]{:S(2)}, u32[]{:S(2)}) collective-permute-start(f32[512]{0:T(512)S(1)} %bitcast.193), channel_id=1, source_target_pairs={{0,1},{1,2},{2,3},{3,4},{4,5},{5,6},{6,7},{8,9},{9,10},{10,11},{11... | collective-permute-start | bytes 6152 | tf_op jit(solution)/shard_map/ppermute | solution.py:525
  290.5 7.1 %collective-permute-start.34 = (f32[512]{0:T(512)S(1)}, f32[512]{0:T(512)S(1)}, u32[]{:S(2)}, u32[]{:S(2)}) collective-permute-start(f32[512]{0:T(512)S(1)} %bitcast.192), channel_id=1, source_target_pairs={{1,0},{2,1},{3,2},{4,3},{5,4},{6,5},{7,6},{9,8},{10,9},{11,10},{12... | collective-permute-start | bytes 6152 | tf_op jit(solution)/shard_map/ppermute | solution.py:525
  (9 other events, 29.5 us)

commit v7 on v6

--- a/solution.py
+++ b/solution.py
@@ -405,30 +405,33 @@
     return {way: lax.ppermute(v, "dy", STEPS[way]) for way, v in messages.items()}
 
 
-def send_middle(near):
-    a = {k: v[0] for k, v in near.items()}
-    b = {k: v[1] for k, v in near.items()}
-    return send(
+def send_near(upper, lower):
+    return send({way: upper for way in WAYS}), send({way: lower for way in WAYS})
+
+
+def send_middle(upper, lower):
+    ahead = send(
+        {"x+": upper["x+"], "x-": lower["x-"], "y+": upper["y+"], "y-": lower["y-"]}
+    )
+    along_x = jnp.concatenate([lower["y+"], lower["y-"]])
+    along_y = jnp.concatenate([upper["x+"], upper["x-"]])
+    aside = send({"x+": along_x, "x-": along_x, "y+": along_y, "y-": along_y})
+    return ahead, aside
+
+
+def send_far(ahead, aside):
+    pairs = send({"x-": aside["x-"], "y-": aside["y-"]})
+    single = send(
         {
-            "x+": jnp.stack([a["x+"], b["y+"], b["y-"]]),
-            "x-": jnp.stack([b["x-"], b["y+"], b["y-"]]),
-            "y+": jnp.stack([a["y+"], a["x+"], a["x-"]]),
-            "y-": jnp.stack([b["y-"], a["x+"], a["x-"]]),
+            "x2": ahead["y+"],
+            "y2": ahead["x-"],
+            "x-": ahead["y-"],
+            "x+": ahead["y-"],
+            "y-": ahead["x+"],
+            "y+": ahead["x+"],
         }
     )
-
-
-def send_far(middle):
-    return send(
-        {
-            "x+": jnp.stack([middle["y+"][1], middle["y-"][1]]),
-            "x-": middle["x-"][1:3],
-            "y+": middle["y+"][1:3],
-            "y-": jnp.stack([middle["x+"][2], middle["x-"][2]]),
-            "x2": middle["y+"][0:1],
-            "y2": middle["x-"][0:1],
-        }
-    )
+    return pairs, single
 
 
 def return_sums(near, middle, far):
@@ -609,39 +612,40 @@
     sides = jnp.concatenate([sides, jnp.zeros((2, 1, T - HALF), I32)], axis=2)
     ends = pack(quantize(jnp.stack([top[1:2], bottom[0:1]])), 0)
     words = pack(quantize(heights), jnp.round((albedo - 1.0) * A_SCALE).astype(I32))
-    words = jnp.concatenate(
-        [words.reshape(2, HALF, T), sides, ends, jnp.zeros((2, PIECE - HALF - 2, T), I32)], axis=1
-    )
-    near = send({way: words for way in WAYS})
-    middle = send_middle(near)
-    far = send_far(middle)
-    order = WAYS
+    blank = jnp.zeros((PIECE - HALF - 2, T), I32)
+    upper, lower = (
+        jnp.concatenate([words[HALF * n : HALF * (n + 1)], sides[n], ends[n], blank])[None]
+        for n in range(2)
+    )
+    near_a, near_b = send_near(upper, lower)
+    ahead, aside = send_middle(near_a, near_b)
+    pairs, single = send_far(ahead, aside)
     out_near, parts = run_tiles(
-        [words] + [near[k] for k in order],
-        [((n, 0), (n, 1)) for n in range(5)],
+        [upper] + [near_a[k] for k in WAYS] + [lower] + [near_b[k] for k in WAYS],
+        [((n, 0), (n + 5, 0)) for n in range(5)],
         resample, observed, plan_of(0, 5), sun, gain,
     )
     out_middle, more = run_tiles(
-        [middle[k] for k in order],
+        [aside[k] for k in WAYS] + [ahead[k] for k in WAYS],
         [
-            ((2, 1), (0, 1)),
-            ((3, 1), (0, 2)),
-            ((2, 2), (1, 1)),
-            ((3, 2), (1, 2)),
-            ((0, 0), (1, 0)),
-            ((2, 0), (3, 0)),
+            ((2, 0), (0, 0)),
+            ((3, 0), (0, 1)),
+            ((2, 1), (1, 0)),
+            ((3, 1), (1, 1)),
+            ((4, 0), (5, 0)),
+            ((6, 0), (7, 0)),
         ],
         resample, observed, plan_of(5, 6), sun, gain,
     )
     parts = parts + more
     out_far, more = run_tiles(
-        [far[k] for k in order] + [far["x2"], far["y2"]],
+        [pairs["x-"], pairs["y-"]] + [single[k] for k in ("y+", "y-", "x+", "x-", "x2", "y2")],
         [
-            ((0, 0), (1, 0)),
-            ((0, 1), (1, 1)),
-            ((2, 0), (3, 0)),
-            ((2, 1), (3, 1)),
-            ((4, 0), (5, 0)),
+            ((2, 0), (0, 0)),
+            ((3, 0), (0, 1)),
+            ((1, 0), (4, 0)),
+            ((1, 1), (5, 0)),
+            ((6, 0), (7, 0)),
         ],
         resample, observed, plan_of(11, 5), sun, gain,
     )

time: 304 us -> 337 us (1.11)
  waiting for transfers between devices: 78.9 us -> 112 us
  other arithmetic: 34.4 us -> 29.9 us
    ppermute x28 -> x38, waiting for transfers between devices: 78.9 us -> 107 us  [send(): lax.ppermute(v, 'dy', STEPS[way])]
    slice x10 -> x1, local copies, waits for them, and re-layouts: 8.15 us -> 0.07 us  [per_device(): words[HALF * n:HALF * (n + 1)]]
    unnamed x34 -> x54, local copies, waits for them, and re-layouts: 0.86 us -> 6.53 us
    another operation x3 -> x0, other arithmetic: 5.35 us -> none  [the longest x1 3.2 us: send_middle(): jnp.stack([b['y-'], a['x+'], a['x-']])]
    ppermute x10, waiting for transfers between devices: 0.03 us -> 5.35 us  [shifted(): lax.ppermute(value, axis, pairs if up else [(b, a) for a, b in pairs])]
    ppermute x10, starting transfers between devices: 32.5 us -> 36.7 us  [shifted(): lax.ppermute(value, axis, pairs if up else [(b, a) for a, b in pairs])]
    ppermute x28 -> x38, starting transfers between devices: 43.4 us -> 43.8 us  [send(): lax.ppermute(v, 'dy', STEPS[way])]
  transfers between devices with their start and end apart: 40 -> 50, of which waited for: 15 -> 17; matrix products, arithmetic and copies ran while one was open for 13% -> 12% of each run, Pallas kernels for 15% -> 21%
where the time goes in v7:
time: 337 us; the launch traced here: 331 us
  waiting for transfers between devices  112 us (33%)
  starting transfers between devices  92.3 us (27%)
  Pallas kernels  68.8 us (20%)
  other arithmetic  29.9 us (9%)
  local copies, waits for them, and re-layouts  24.5 us (7%)
    ppermute x38, waiting for transfers between devices, send(): lax.ppermute(v, 'dy', STEPS[way])  107 us
    pallas_call x3, Pallas kernels, run_tiles(): pl.pallas_call(functools.partial(tile_kernel, pieces, len(arrays)), grid_...  68.8 us
    ppermute x38, starting transfers between devices, send(): lax.ppermute(v, 'dy', STEPS[way])  43.8 us
    ppermute x10, starting transfers between devices, shifted(): lax.ppermute(value, axis, pairs if up else [(b, a) for a, b in pairs])  36.7 us
    all_to_all x1, starting transfers between devices, per_device(): lax.all_to_all(offsets, 'dy', split_axis=0, concat_axis=0, tiled=True)  6.86 us
  transfers between devices with their start and end apart: 50, of which 17 were waited for; matrix products, arithmetic and copies ran while one was open for 12% of the time, Pallas kernels for 21%

profile of v7, /device:TPU:7, one launch (start us, length us, event | category | flops | bytes accessed | tf_op | source)
XLA Modules:
  0.0 330.8 jit_solution(6938050636816787513)
XLA Ops:
  2.0 6.9 %all-to-all-start = ((s32[16,2,2]{2,1,0:T(2,128)}), s32[16,2,2]{2,1,0:T(2,128)S(1)}, u32[]{:S(2)}, u32[]{:S(2)}) async-start(s32[16,2,2]{2,1,0:T(2,128)} %copy.26), calls=%async_computation | async-start | bytes 32768 | tf_op jit(solution)/shard_map/all_to_all | solution.py:584
  9.6 2.5 collective-permute-start.3
  12.1 4.9 %collective-permute-start.2 = (f32[2,512]{1,0:T(2,128)S(1)}, f32[2,512]{1,0:T(2,128)S(1)}, u32[]{:S(2)}, u32[]{:S(2)}) collective-permute-start(f32[2,512]{1,0:T(2,128)S(1)} %get-tuple-element.66), channel_id=1, source_target_pairs={{0,8},{8,16},{16,24},{24,32},{32,40},{40,48},{48,56},{56,64},{64,7... | collective-permute-start | bytes 12296 | tf_op jit(solution)/shard_map/ppermute | solution.py:528
  18.4 5.2 %collective-permute-start = (f32[512]{0:T(512)S(1)}, f32[512]{0:T(512)S(1)}, u32[]{:S(2)}, u32[]{:S(2)}) collective-permute-start(f32[512]{0:T(512)S(1)} %get-tuple-element.14), channel_id=1, source_target_pairs={{0,1},{1,2},{2,3},{3,4},{4,5},{5,6},{6,7},{8,9},{9,10},{10,11},{11... | collective-permute-start | bytes 6152 | tf_op jit(solution)/shard_map/ppermute | solution.py:528
  23.6 1.9 collective-permute-start.1
  28.0 1.8 and_or_fusion
  36.4 4.5 %collective-permute-start.46 = (f32[516,2]{1,0:T(8,128)}, f32[516,2]{1,0:T(8,128)S(1)}, u32[]{:S(2)}, u32[]{:S(2)}) collective-permute-start(f32[516,2]{1,0:T(8,128)} %get-tuple-element.62), channel_id=1, source_target_pairs={{0,1},{1,2},{2,3},{3,4},{4,5},{5,6},{6,7},{8,9},{9,10},{10,11},{11... | collective-permute-start | bytes 12392 | tf_op jit(solution)/shard_map/ppermute | solution.py:528
  46.4 3.2 collective-permute-done.10.refs_14_
  52.2 1.9 constant_dynamic-update-slice_fusion.1
  55.0 1.7 collective-permute-done.11.refs_15_
  56.7 1.9 collective-permute-start.47
  58.6 1.9 constant_dynamic-update-slice_fusion
  60.5 4.6 %collective-permute-done.47 = f32[516,2]{1,0:T(8,128)S(1)} collective-permute-done((f32[516,2]{1,0:T(8,128)S(1)}, f32[516,2]{1,0:T(8,128)S(1)}, u32[]{:S(2)}, u32[]{:S(2)}) %collective-permute-start.47) | collective-permute-done | bytes 4160 | tf_op jit(solution)/shard_map/ppermute | solution.py:528
  65.1 2.4 collective-permute-start.15
  67.6 2.7 collective-permute-start.16
  73.2 5.4 %collective-permute-done.16.refs_10_ = s32[1,264,512]{2,1,0:T(8,128)} collective-permute-done((s32[1,264,512]{2,1,0:T(8,128)S(1)}, s32[1,264,512]{2,1,0:T(8,128)}, u32[]{:S(2)}, u32[]{:S(2)}) %collective-permute-start.16) | collective-permute-done | bytes 540704 | tf_op jit(solution)/shard_map/ppermute | solution.py:405
  78.8 22.3 %collective-permute-done.19.refs_13_ = s32[1,264,512]{2,1,0:T(8,128)S(1)} collective-permute-done((s32[1,264,512]{2,1,0:T(8,128)}, s32[1,264,512]{2,1,0:T(8,128)S(1)}, u32[]{:S(2)}, u32[]{:S(2)}) %collective-permute-start.19) | collective-permute-done | bytes 540704 | tf_op jit(solution)/shard_map/ppermute | solution.py:405
  102.2 1.6 collective-permute-start.23
  108.1 8.3 %collective-permute-done.22.refs_8_ = s32[1,264,512]{2,1,0:T(8,128)S(1)} collective-permute-done((s32[1,264,512]{2,1,0:T(8,128)}, s32[1,264,512]{2,1,0:T(8,128)S(1)}, u32[]{:S(2)}, u32[]{:S(2)}) %collective-permute-start.22) | collective-permute-done | bytes 540704 | tf_op jit(solution)/shard_map/ppermute | solution.py:405
  116.9 2.2 collective-permute-start.26
  122.4 1.6 pad_maximum_fusion.6
  124.0 33.5 %collective-permute-done.25.refs_11_ = s32[1,264,512]{2,1,0:T(8,128)S(1)} collective-permute-done((s32[1,264,512]{2,1,0:T(8,128)S(1)}, s32[1,264,512]{2,1,0:T(8,128)S(1)}, u32[]{:S(2)}, u32[]{:S(2)}) %collective-permute-start.25) | collective-permute-done | bytes 540704 | tf_op jit(solution)/shard_map/ppermute | solution.py:405
  159.1 21.6 %shard_map.113 = (bf16[5,2,272,512]{3,2,1,0:T(8,128)(2,1)}, f32[16,5,8,384]{3,2,1,0:T(8,128)}) custom-call(s32[10]{0:T(128)} %get-tuple-element.77.refs_0_, s32[10]{0:T(128)} %select_reduce_fusion.5.refs_1_, s32[10]{0:T(128)} %get-tuple-element.75.refs_2_, s32[10]{0:T(128)} %get-tuple-element.70.refs_3_, f32[48]{0:T(128)} %reshape.372.refs_4_, ...), custom_call_target="tpu_custom_call" | custom-call | flops 2264924160 | bytes 40000000 | tf_op jit(solution)/shard_map/pallas_call | solution.py:374
  181.8 22.5 %shard_map.115 = (bf16[5,2,272,512]{3,2,1,0:T(8,128)(2,1)}, f32[16,5,8,384]{3,2,1,0:T(8,128)}) custom-call(s32[10]{0:T(128)} %get-tuple-element.74.refs_0_, s32[10]{0:T(128)} %select_reduce_fusion.1.refs_1_, s32[10]{0:T(128)} %get-tuple-element.72.refs_2_, s32[10]{0:T(128)} %get-tuple-element.71.refs_3_, f32[48]{0:T(128)} %reshape.372.refs_4_, ...), custom_call_target="tpu_custom_call" | custom-call | flops 2264924160 | bytes 40000000 | tf_op jit(solution)/shard_map/pallas_call | solution.py:374
  204.3 2.7 fusion.74
  207.0 2.9 collective-permute-start.29
  209.9 2.2 fusion.73
  213.4 24.7 %shard_map.114 = (bf16[6,2,272,512]{3,2,1,0:T(8,128)(2,1)}, f32[16,5,8,384]{3,2,1,0:T(8,128)}) custom-call(s32[12]{0:T(128)} %get-tuple-element.87.refs_0_, s32[12]{0:T(128)} %select_reduce_fusion.3.refs_1_, s32[12]{0:T(128)} %get-tuple-element.85.refs_2_, s32[12]{0:T(128)} %get-tuple-element.84.refs_3_, f32[48]{0:T(128)} %reshape.372.refs_4_, ...), custom_call_target="tpu_custom_call" | custom-call | flops 2717908992 | bytes 48000000 | tf_op jit(solution)/shard_map/pallas_call | solution.py:374
  239.7 8.1 %collective-permute-start.36 = (bf16[1,272,512]{2,1,0:T(8,128)(2,1)}, bf16[1,272,512]{2,1,0:T(8,128)(2,1)S(1)}, u32[]{:S(2)}, u32[]{:S(2)}) collective-permute-start(bf16[1,272,512]{2,1,0:T(8,128)(2,1)} %get-tuple-element.54), channel_id=1, source_target_pairs={{0,8},{8,16},{16,24},{24,0},{32,40},{40,48},{48,56},{56,32},{64,72... | collective-permute-start | bytes 835592 | tf_op jit(solution)/shard_map/ppermute | solution.py:405
  248.5 1.6 add_add_fusion
  250.4 2.1 collective-permute-done.36
  252.5 5.9 %collective-permute-done.37 = bf16[1,272,512]{2,1,0:T(8,128)(2,1)S(1)} collective-permute-done((bf16[1,272,512]{2,1,0:T(8,128)(2,1)}, bf16[1,272,512]{2,1,0:T(8,128)(2,1)S(1)}, u32[]{:S(2)}, u32[]{:S(2)}) %collective-permute-start.37) | collective-permute-done | bytes 278560 | tf_op jit(solution)/shard_map/ppermute | solution.py:405
  258.5 1.9 fusion.29
  261.4 3.4 %collective-permute-start.38 = (bf16[3,272,512]{2,1,0:T(8,128)(2,1)}, bf16[3,272,512]{2,1,0:T(8,128)(2,1)S(1)}, u32[]{:S(2)}, u32[]{:S(2)}) collective-permute-start(bf16[3,272,512]{2,1,0:T(8,128)(2,1)} %pad_maximum_fusion.10), channel_id=1, source_target_pairs={{0,8},{8,16},{16,24},{24,0},{32,40},{40,48},{48,56},{56,32},{64,72... | collective-permute-start | bytes 2506760 | tf_op jit(solution)/shard_map/ppermute | solution.py:405
  269.8 12.8 %collective-permute-done.38 = bf16[3,272,512]{2,1,0:T(8,128)(2,1)S(1)} collective-permute-done((bf16[3,272,512]{2,1,0:T(8,128)(2,1)}, bf16[3,272,512]{2,1,0:T(8,128)(2,1)S(1)}, u32[]{:S(2)}, u32[]{:S(2)}) %collective-permute-start.38) | collective-permute-done | bytes 835616 | tf_op jit(solution)/shard_map/ppermute | solution.py:405
  282.6 4.1 %collective-permute-done.30 = bf16[3,272,512]{2,1,0:T(8,128)(2,1)} collective-permute-done((bf16[3,272,512]{2,1,0:T(8,128)(2,1)}, bf16[3,272,512]{2,1,0:T(8,128)(2,1)}, u32[]{:S(2)}, u32[]{:S(2)}) %collective-permute-start.30) | collective-permute-done | bytes 835616 | tf_op jit(solution)/shard_map/ppermute | solution.py:405
  288.0 2.8 fusion.34
  291.0 2.7 collective-permute-start.39
  296.9 4.9 %all-to-all-start.1 = ((f32[16,1,7]{2,1,0:T(1,128)}), f32[16,1,7]{2,1,0:T(1,128)S(1)}, u32[]{:S(2)}, u32[]{:S(2)}) async-start(f32[16,1,7]{2,1,0:T(1,128)} %copy.31), calls=%async_computation.1 | async-start | bytes 16384 | tf_op jit(solution)/shard_map/all_to_all | solution.py:655
  301.8 2.2 collective-permute-done.34
  305.2 2.3 collective-permute-done.41
  307.5 2.1 fusion.6
  310.1 1.9 collective-permute-start.42
  312.0 5.5 %collective-permute-start.43 = (f32[512]{0:T(512)S(1)}, f32[512]{0:T(512)S(1)}, u32[]{:S(2)}, u32[]{:S(2)}) collective-permute-start(f32[512]{0:T(512)S(1)} %bitcast.204), channel_id=1, source_target_pairs={{0,8},{8,16},{16,24},{24,32},{32,40},{40,48},{48,56},{56,64},{64,7... | collective-permute-start | bytes 6152 | tf_op jit(solution)/shard_map/ppermute | solution.py:528
  317.5 6.4 %collective-permute-start.44 = (f32[512]{0:T(512)S(1)}, f32[512]{0:T(512)S(1)}, u32[]{:S(2)}, u32[]{:S(2)}) collective-permute-start(f32[512]{0:T(512)S(1)} %bitcast.203), channel_id=1, source_target_pairs={{1,0},{2,1},{3,2},{4,3},{5,4},{6,5},{7,6},{9,8},{10,9},{11,10},{12... | collective-permute-start | bytes 6152 | tf_op jit(solution)/shard_map/ppermute | solution.py:528
  323.9 2.0 collective-permute-start.45
  326.0 1.7 fusion.1
  328.4 2.4 fusion.9
  (197 shorter events, 51.2 us)
Async XLA Ops:
  2.0 29.9 %all-to-all-start = ((s32[16,2,2]{2,1,0:T(2,128)}), s32[16,2,2]{2,1,0:T(2,128)S(1)}, u32[]{:S(2)}, u32[]{:S(2)}) async-start(s32[16,2,2]{2,1,0:T(2,128)} %copy.26), calls=%async_computation | async-start | bytes 32768 | tf_op jit(solution)/shard_map/all_to_all | solution.py:584
  9.6 22.7 %collective-permute-start.3 = (f32[2,512]{1,0:T(2,128)S(1)}, f32[2,512]{1,0:T(2,128)S(1)}, u32[]{:S(2)}, u32[]{:S(2)}) collective-permute-start(f32[2,512]{1,0:T(2,128)S(1)} %get-tuple-element.67), channel_id=1, source_target_pairs={{8,0},{16,8},{24,16},{32,24},{40,32},{48,40},{56,48},{64,56},{72,6... | collective-permute-start | bytes 12296 | tf_op jit(solution)/shard_map/ppermute | solution.py:528
  12.1 20.3 %collective-permute-start.2 = (f32[2,512]{1,0:T(2,128)S(1)}, f32[2,512]{1,0:T(2,128)S(1)}, u32[]{:S(2)}, u32[]{:S(2)}) collective-permute-start(f32[2,512]{1,0:T(2,128)S(1)} %get-tuple-element.66), channel_id=1, source_target_pairs={{0,8},{8,16},{16,24},{24,32},{32,40},{40,48},{48,56},{56,64},{64,7... | collective-permute-start | bytes 12296 | tf_op jit(solution)/shard_map/ppermute | solution.py:528
  18.4 13.9 %collective-permute-start = (f32[512]{0:T(512)S(1)}, f32[512]{0:T(512)S(1)}, u32[]{:S(2)}, u32[]{:S(2)}) collective-permute-start(f32[512]{0:T(512)S(1)} %get-tuple-element.14), channel_id=1, source_target_pairs={{0,1},{1,2},{2,3},{3,4},{4,5},{5,6},{6,7},{8,9},{9,10},{10,11},{11... | collective-permute-start | bytes 6152 | tf_op jit(solution)/shard_map/ppermute | solution.py:528
  23.6 8.7 %collective-permute-start.1 = (f32[512]{0:T(512)S(1)}, f32[512]{0:T(512)S(1)}, u32[]{:S(2)}, u32[]{:S(2)}) collective-permute-start(f32[512]{0:T(512)S(1)} %get-tuple-element.15), channel_id=1, source_target_pairs={{1,0},{2,1},{3,2},{4,3},{5,4},{6,5},{7,6},{9,8},{10,9},{11,10},{12... | collective-permute-start | bytes 6152 | tf_op jit(solution)/shard_map/ppermute | solution.py:528
  32.6 13.1 %collective-permute-start.4 = (s32[1,264,512]{2,1,0:T(8,128)S(1)}, s32[1,264,512]{2,1,0:T(8,128)S(1)}, u32[]{:S(2)}, u32[]{:S(2)}) collective-permute-start(s32[1,264,512]{2,1,0:T(8,128)S(1)} %get-tuple-element.80.refs_6_), channel_id=1, source_target_pairs={{0,8},{8,16},{16,24},{24,0},{32,40},{40,48},{48,56},{56,32},{64,72... | collective-permute-start | bytes 1622024 | tf_op jit(solution)/shard_map/ppermute | solution.py:405
  32.7 17.4 %collective-permute-start.5 = (s32[1,264,512]{2,1,0:T(8,128)S(1)}, s32[1,264,512]{2,1,0:T(8,128)S(1)}, u32[]{:S(2)}, u32[]{:S(2)}) collective-permute-start(s32[1,264,512]{2,1,0:T(8,128)S(1)} %get-tuple-element.80.refs_6_), channel_id=1, source_target_pairs={{0,24},{8,0},{16,8},{24,16},{32,56},{40,32},{48,40},{56,48},{64,88... | collective-permute-start | bytes 1622024 | tf_op jit(solution)/shard_map/ppermute | solution.py:405
  34.2 15.4 %collective-permute-start.10 = (s32[1,264,512]{2,1,0:T(8,128)S(1)}, s32[1,264,512]{2,1,0:T(8,128)}, u32[]{:S(2)}, u32[]{:S(2)}) collective-permute-start(s32[1,264,512]{2,1,0:T(8,128)S(1)} %get-tuple-element.81.refs_11_), channel_id=1, source_target_pairs={{0,32},{8,40},{16,48},{24,56},{32,64},{40,72},{48,80},{56,88},{64,... | collective-permute-start | bytes 1622024 | tf_op jit(solution)/shard_map/ppermute | solution.py:405
  42.2 14.5 %collective-permute-start.11 = (s32[1,264,512]{2,1,0:T(8,128)S(1)}, s32[1,264,512]{2,1,0:T(8,128)}, u32[]{:S(2)}, u32[]{:S(2)}) collective-permute-start(s32[1,264,512]{2,1,0:T(8,128)S(1)} %get-tuple-element.81.refs_11_), channel_id=1, source_target_pairs={{0,96},{8,104},{16,112},{24,120},{32,0},{40,8},{48,16},{56,24},{64... | collective-permute-start | bytes 1622024 | tf_op jit(solution)/shard_map/ppermute | solution.py:405
  44.5 23.0 %collective-permute-start.6 = (s32[1,264,512]{2,1,0:T(8,128)S(1)}, s32[1,264,512]{2,1,0:T(8,128)}, u32[]{:S(2)}, u32[]{:S(2)}) collective-permute-start(s32[1,264,512]{2,1,0:T(8,128)S(1)} %get-tuple-element.80.refs_6_), channel_id=1, source_target_pairs={{0,32},{8,40},{16,48},{24,56},{32,64},{40,72},{48,80},{56,88},{64,... | collective-permute-start | bytes 1622024 | tf_op jit(solution)/shard_map/ppermute | solution.py:405
  45.7 21.8 %collective-permute-start.9 = (s32[1,264,512]{2,1,0:T(8,128)S(1)}, s32[1,264,512]{2,1,0:T(8,128)}, u32[]{:S(2)}, u32[]{:S(2)}) collective-permute-start(s32[1,264,512]{2,1,0:T(8,128)S(1)} %get-tuple-element.81.refs_11_), channel_id=1, source_target_pairs={{0,24},{8,0},{16,8},{24,16},{32,56},{40,32},{48,40},{56,48},{64,88... | collective-permute-start | bytes 1622024 | tf_op jit(solution)/shard_map/ppermute | solution.py:405
  49.6 22.0 %collective-permute-start.7 = (s32[1,264,512]{2,1,0:T(8,128)S(1)}, s32[1,264,512]{2,1,0:T(8,128)}, u32[]{:S(2)}, u32[]{:S(2)}) collective-permute-start(s32[1,264,512]{2,1,0:T(8,128)S(1)} %get-tuple-element.80.refs_6_), channel_id=1, source_target_pairs={{0,96},{8,104},{16,112},{24,120},{32,0},{40,8},{48,16},{56,24},{64... | collective-permute-start | bytes 1622024 | tf_op jit(solution)/shard_map/ppermute | solution.py:405
  50.1 21.6 %collective-permute-start.8 = (s32[1,264,512]{2,1,0:T(8,128)S(1)}, s32[1,264,512]{2,1,0:T(8,128)}, u32[]{:S(2)}, u32[]{:S(2)}) collective-permute-start(s32[1,264,512]{2,1,0:T(8,128)S(1)} %get-tuple-element.81.refs_11_), channel_id=1, source_target_pairs={{0,8},{8,16},{16,24},{24,0},{32,40},{40,48},{48,56},{56,32},{64,72... | collective-permute-start | bytes 1622024 | tf_op jit(solution)/shard_map/ppermute | solution.py:405
  56.7 8.4 %collective-permute-start.47 = (f32[516,2]{1,0:T(8,128)S(1)}, f32[516,2]{1,0:T(8,128)S(1)}, u32[]{:S(2)}, u32[]{:S(2)}) collective-permute-start(f32[516,2]{1,0:T(8,128)S(1)} %copy-done.22), channel_id=1, source_target_pairs={{1,0},{2,1},{3,2},{4,3},{5,4},{6,5},{7,6},{9,8},{10,9},{11,10},{12... | collective-permute-start | bytes 12392 | tf_op jit(solution)/shard_map/ppermute | solution.py:528
  65.1 40.7 %collective-permute-start.15 = (s32[2,264,512]{2,1,0:T(8,128)}, s32[2,264,512]{2,1,0:T(8,128)}, u32[]{:S(2)}, u32[]{:S(2)}) collective-permute-start(s32[2,264,512]{2,1,0:T(8,128)} %constant_dynamic-update-slice_fusion.2), channel_id=1, source_target_pairs={{0,96},{8,104},{16,112},{24,120},{32,0},{40,8},{48,16},{56,24},{64... | collective-permute-start | bytes 3244040 | tf_op jit(solution)/shard_map/ppermute | solution.py:405
  67.5 39.6 %collective-permute-start.13 = (s32[2,264,512]{2,1,0:T(8,128)}, s32[2,264,512]{2,1,0:T(8,128)}, u32[]{:S(2)}, u32[]{:S(2)}) collective-permute-start(s32[2,264,512]{2,1,0:T(8,128)} %constant_dynamic-update-slice_fusion), channel_id=1, source_target_pairs={{0,24},{8,0},{16,8},{24,16},{32,56},{40,32},{48,40},{56,48},{64,88... | collective-permute-start | bytes 3244040 | tf_op jit(solution)/shard_map/ppermute | solution.py:405
  67.6 11.1 %collective-permute-start.16 = (s32[1,264,512]{2,1,0:T(8,128)S(1)}, s32[1,264,512]{2,1,0:T(8,128)}, u32[]{:S(2)}, u32[]{:S(2)}) collective-permute-start(s32[1,264,512]{2,1,0:T(8,128)S(1)} %collective-permute-done.4.refs_7_), channel_id=1, source_target_pairs={{0,8},{8,16},{16,24},{24,0},{32,40},{40,48},{48,56},{56,32},{64,72... | collective-permute-start | bytes 1622024 | tf_op jit(solution)/shard_map/ppermute | solution.py:405
  71.6 29.5 %collective-permute-start.19 = (s32[1,264,512]{2,1,0:T(8,128)}, s32[1,264,512]{2,1,0:T(8,128)S(1)}, u32[]{:S(2)}, u32[]{:S(2)}) collective-permute-start(s32[1,264,512]{2,1,0:T(8,128)} %collective-permute-done.11.refs_15_), channel_id=1, source_target_pairs={{0,96},{8,104},{16,112},{24,120},{32,0},{40,8},{48,16},{56,24},{64... | collective-permute-start | bytes 1622024 | tf_op jit(solution)/shard_map/ppermute | solution.py:405
  71.7 30.5 %collective-permute-start.18 = (s32[1,264,512]{2,1,0:T(8,128)}, s32[1,264,512]{2,1,0:T(8,128)S(1)}, u32[]{:S(2)}, u32[]{:S(2)}) collective-permute-start(s32[1,264,512]{2,1,0:T(8,128)} %collective-permute-done.6.refs_9_), channel_id=1, source_target_pairs={{0,32},{8,40},{16,48},{24,56},{32,64},{40,72},{48,80},{56,88},{64,... | collective-permute-start | bytes 1622024 | tf_op jit(solution)/shard_map/ppermute | solution.py:405
  78.6 25.9 %collective-permute-start.17 = (s32[1,264,512]{2,1,0:T(8,128)}, s32[1,264,512]{2,1,0:T(8,128)}, u32[]{:S(2)}, u32[]{:S(2)}) collective-permute-start(s32[1,264,512]{2,1,0:T(8,128)} %collective-permute-done.9.refs_13_), channel_id=1, source_target_pairs={{0,24},{8,0},{16,8},{24,16},{32,56},{40,32},{48,40},{56,48},{64,88... | collective-permute-start | bytes 1622024 | tf_op jit(solution)/shard_map/ppermute | solution.py:405
  101.1 15.4 %collective-permute-start.22 = (s32[1,264,512]{2,1,0:T(8,128)}, s32[1,264,512]{2,1,0:T(8,128)S(1)}, u32[]{:S(2)}, u32[]{:S(2)}) collective-permute-start(s32[1,264,512]{2,1,0:T(8,128)} %collective-permute-done.16.refs_10_), channel_id=1, source_target_pairs={{0,32},{8,40},{16,48},{24,56},{32,64},{40,72},{48,80},{56,88},{64,... | collective-permute-start | bytes 1622024 | tf_op jit(solution)/shard_map/ppermute | solution.py:405
  102.2 14.6 %collective-permute-start.23 = (s32[1,264,512]{2,1,0:T(8,128)}, s32[1,264,512]{2,1,0:T(8,128)S(1)}, u32[]{:S(2)}, u32[]{:S(2)}) collective-permute-start(s32[1,264,512]{2,1,0:T(8,128)} %collective-permute-done.16.refs_10_), channel_id=1, source_target_pairs={{0,96},{8,104},{16,112},{24,120},{32,0},{40,8},{48,16},{56,24},{64... | collective-permute-start | bytes 1622024 | tf_op jit(solution)/shard_map/ppermute | solution.py:405
  104.5 16.5 %collective-permute-start.24 = (s32[1,264,512]{2,1,0:T(8,128)S(1)}, s32[1,264,512]{2,1,0:T(8,128)S(1)}, u32[]{:S(2)}, u32[]{:S(2)}) collective-permute-start(s32[1,264,512]{2,1,0:T(8,128)S(1)} %collective-permute-done.19.refs_13_), channel_id=1, source_target_pairs={{0,8},{8,16},{16,24},{24,0},{32,40},{40,48},{48,56},{56,32},{64,72... | collective-permute-start | bytes 1622024 | tf_op jit(solution)/shard_map/ppermute | solution.py:405
  105.8 76.0 %collective-permute-start.21 = (s32[2,264,512]{2,1,0:T(8,128)}, s32[2,264,512]{2,1,0:T(8,128)}, u32[]{:S(2)}, u32[]{:S(2)}) collective-permute-start(s32[2,264,512]{2,1,0:T(8,128)} %collective-permute-done.15.refs_9_), channel_id=1, source_target_pairs={{0,96},{8,104},{16,112},{24,120},{32,0},{40,8},{48,16},{56,24},{64... | collective-permute-start | bytes 3244040 | tf_op jit(solution)/shard_map/ppermute | solution.py:405
  107.2 74.6 %collective-permute-start.20 = (s32[2,264,512]{2,1,0:T(8,128)}, s32[2,264,512]{2,1,0:T(8,128)}, u32[]{:S(2)}, u32[]{:S(2)}) collective-permute-start(s32[2,264,512]{2,1,0:T(8,128)} %collective-permute-done.13.refs_7_), channel_id=1, source_target_pairs={{0,24},{8,0},{16,8},{24,16},{32,56},{40,32},{48,40},{56,48},{64,88... | collective-permute-start | bytes 3244040 | tf_op jit(solution)/shard_map/ppermute | solution.py:405
  116.4 41.0 %collective-permute-start.25 = (s32[1,264,512]{2,1,0:T(8,128)S(1)}, s32[1,264,512]{2,1,0:T(8,128)S(1)}, u32[]{:S(2)}, u32[]{:S(2)}) collective-permute-start(s32[1,264,512]{2,1,0:T(8,128)S(1)} %collective-permute-done.19.refs_13_), channel_id=1, source_target_pairs={{0,24},{8,0},{16,8},{24,16},{32,56},{40,32},{48,40},{56,48},{64,88... | collective-permute-start | bytes 1622024 | tf_op jit(solution)/shard_map/ppermute | solution.py:405
  116.9 40.6 %collective-permute-start.26 = (s32[1,264,512]{2,1,0:T(8,128)S(1)}, s32[1,264,512]{2,1,0:T(8,128)S(1)}, u32[]{:S(2)}, u32[]{:S(2)}) collective-permute-start(s32[1,264,512]{2,1,0:T(8,128)S(1)} %collective-permute-done.18.refs_12_), channel_id=1, source_target_pairs={{0,16},{8,24},{16,0},{24,8},{32,48},{40,56},{48,32},{56,40},{64,80... | collective-permute-start | bytes 1622024 | tf_op jit(solution)/shard_map/ppermute | solution.py:405
  121.9 59.9 %collective-permute-start.27 = (s32[1,264,512]{2,1,0:T(8,128)}, s32[1,264,512]{2,1,0:T(8,128)}, u32[]{:S(2)}, u32[]{:S(2)}) collective-permute-start(s32[1,264,512]{2,1,0:T(8,128)} %collective-permute-done.17.refs_11_), channel_id=1, source_target_pairs={{0,64},{8,72},{16,80},{24,88},{32,96},{40,104},{48,112},{56,120},{... | collective-permute-start | bytes 1622024 | tf_op jit(solution)/shard_map/ppermute | solution.py:405
  157.5 55.9 %collective-permute-start.14 = (s32[2,264,512]{2,1,0:T(8,128)}, s32[2,264,512]{2,1,0:T(8,128)}, u32[]{:S(2)}, u32[]{:S(2)}) collective-permute-start(s32[2,264,512]{2,1,0:T(8,128)} %constant_dynamic-update-slice_fusion.2), channel_id=1, source_target_pairs={{0,32},{8,40},{16,48},{24,56},{32,64},{40,72},{48,80},{56,88},{64,... | collective-permute-start | bytes 3244040 | tf_op jit(solution)/shard_map/ppermute | solution.py:405
  158.3 55.1 %collective-permute-start.12 = (s32[2,264,512]{2,1,0:T(8,128)}, s32[2,264,512]{2,1,0:T(8,128)}, u32[]{:S(2)}, u32[]{:S(2)}) collective-permute-start(s32[2,264,512]{2,1,0:T(8,128)} %constant_dynamic-update-slice_fusion), channel_id=1, source_target_pairs={{0,8},{8,16},{16,24},{24,0},{32,40},{40,48},{48,56},{56,32},{64,72... | collective-permute-start | bytes 3244040 | tf_op jit(solution)/shard_map/ppermute | solution.py:405
  207.0 51.5 %collective-permute-start.28 = (bf16[3,272,512]{2,1,0:T(8,128)(2,1)}, bf16[3,272,512]{2,1,0:T(8,128)(2,1)S(1)}, u32[]{:S(2)}, u32[]{:S(2)}) collective-permute-start(bf16[3,272,512]{2,1,0:T(8,128)(2,1)} %get-tuple-element.57), channel_id=1, source_target_pairs={{0,24},{8,0},{16,8},{24,16},{32,56},{40,32},{48,40},{56,48},{64,88... | collective-permute-start | bytes 2506760 | tf_op jit(solution)/shard_map/ppermute | solution.py:405
  207.0 51.5 %collective-permute-start.29 = (bf16[3,272,512]{2,1,0:T(8,128)(2,1)}, bf16[3,272,512]{2,1,0:T(8,128)(2,1)}, u32[]{:S(2)}, u32[]{:S(2)}) collective-permute-start(bf16[3,272,512]{2,1,0:T(8,128)(2,1)} %get-tuple-element.56), channel_id=1, source_target_pairs={{0,96},{8,104},{16,112},{24,120},{32,0},{40,8},{48,16},{56,24},{64... | collective-permute-start | bytes 2506760 | tf_op jit(solution)/shard_map/ppermute | solution.py:405
  212.1 35.7 %collective-permute-start.31 = (bf16[1,272,512]{2,1,0:T(8,128)(2,1)S(1)}, bf16[1,272,512]{2,1,0:T(8,128)(2,1)S(1)}, u32[]{:S(2)}, u32[]{:S(2)}) collective-permute-start(bf16[1,272,512]{2,1,0:T(8,128)(2,1)S(1)} %get-tuple-element.52), channel_id=1, source_target_pairs={{0,16},{8,24},{16,0},{24,8},{32,48},{40,56},{48,32},{56,40},{64,80... | collective-permute-start | bytes 835592 | tf_op jit(solution)/shard_map/ppermute | solution.py:405
  239.6 10.8 %collective-permute-start.35 = (bf16[1,272,512]{2,1,0:T(8,128)(2,1)}, bf16[1,272,512]{2,1,0:T(8,128)(2,1)S(1)}, u32[]{:S(2)}, u32[]{:S(2)}) collective-permute-start(bf16[1,272,512]{2,1,0:T(8,128)(2,1)} %get-tuple-element.55), channel_id=1, source_target_pairs={{0,64},{8,72},{16,80},{24,88},{32,96},{40,104},{48,112},{56,120},{... | collective-permute-start | bytes 835592 | tf_op jit(solution)/shard_map/ppermute | solution.py:405
  239.7 12.8 %collective-permute-start.36 = (bf16[1,272,512]{2,1,0:T(8,128)(2,1)}, bf16[1,272,512]{2,1,0:T(8,128)(2,1)S(1)}, u32[]{:S(2)}, u32[]{:S(2)}) collective-permute-start(bf16[1,272,512]{2,1,0:T(8,128)(2,1)} %get-tuple-element.54), channel_id=1, source_target_pairs={{0,8},{8,16},{16,24},{24,0},{32,40},{40,48},{48,56},{56,32},{64,72... | collective-permute-start | bytes 835592 | tf_op jit(solution)/shard_map/ppermute | solution.py:405
  247.8 10.7 %collective-permute-start.37 = (bf16[1,272,512]{2,1,0:T(8,128)(2,1)}, bf16[1,272,512]{2,1,0:T(8,128)(2,1)S(1)}, u32[]{:S(2)}, u32[]{:S(2)}) collective-permute-start(bf16[1,272,512]{2,1,0:T(8,128)(2,1)} %get-tuple-element.53), channel_id=1, source_target_pairs={{0,32},{8,40},{16,48},{24,56},{32,64},{40,72},{48,80},{56,88},{64,... | collective-permute-start | bytes 835592 | tf_op jit(solution)/shard_map/ppermute | solution.py:405
  261.4 21.2 %collective-permute-start.38 = (bf16[3,272,512]{2,1,0:T(8,128)(2,1)}, bf16[3,272,512]{2,1,0:T(8,128)(2,1)S(1)}, u32[]{:S(2)}, u32[]{:S(2)}) collective-permute-start(bf16[3,272,512]{2,1,0:T(8,128)(2,1)} %pad_maximum_fusion.10), channel_id=1, source_target_pairs={{0,8},{8,16},{16,24},{24,0},{32,40},{40,48},{48,56},{56,32},{64,72... | collective-permute-start | bytes 2506760 | tf_op jit(solution)/shard_map/ppermute | solution.py:405
  265.8 20.9 %collective-permute-start.30 = (bf16[3,272,512]{2,1,0:T(8,128)(2,1)}, bf16[3,272,512]{2,1,0:T(8,128)(2,1)}, u32[]{:S(2)}, u32[]{:S(2)}) collective-permute-start(bf16[3,272,512]{2,1,0:T(8,128)(2,1)} %pad_maximum_fusion.7), channel_id=1, source_target_pairs={{0,24},{8,0},{16,8},{24,16},{32,56},{40,32},{48,40},{56,48},{64,88... | collective-permute-start | bytes 2506760 | tf_op jit(solution)/shard_map/ppermute | solution.py:405
  266.9 19.8 %collective-permute-start.32 = (bf16[3,272,512]{2,1,0:T(8,128)(2,1)}, bf16[3,272,512]{2,1,0:T(8,128)(2,1)}, u32[]{:S(2)}, u32[]{:S(2)}) collective-permute-start(bf16[3,272,512]{2,1,0:T(8,128)(2,1)} %pad_maximum_fusion.8), channel_id=1, source_target_pairs={{0,96},{8,104},{16,112},{24,120},{32,0},{40,8},{48,16},{56,24},{64... | collective-permute-start | bytes 2506760 | tf_op jit(solution)/shard_map/ppermute | solution.py:405
  267.9 20.1 %collective-permute-start.33 = (bf16[3,272,512]{2,1,0:T(8,128)(2,1)}, bf16[3,272,512]{2,1,0:T(8,128)(2,1)}, u32[]{:S(2)}, u32[]{:S(2)}) collective-permute-start(bf16[3,272,512]{2,1,0:T(8,128)(2,1)} %pad_maximum_fusion.9), channel_id=1, source_target_pairs={{0,32},{8,40},{16,48},{24,56},{32,64},{40,72},{48,80},{56,88},{64,... | collective-permute-start | bytes 2506760 | tf_op jit(solution)/shard_map/ppermute | solution.py:405
  290.9 13.1 %collective-permute-start.34 = (bf16[2,272,512]{2,1,0:T(8,128)(2,1)S(1)}, bf16[2,272,512]{2,1,0:T(8,128)(2,1)}, u32[]{:S(2)}, u32[]{:S(2)}) collective-permute-start(bf16[2,272,512]{2,1,0:T(8,128)(2,1)S(1)} %pad_maximum_fusion.11), channel_id=1, source_target_pairs={{0,24},{8,0},{16,8},{24,16},{32,56},{40,32},{48,40},{56,48},{64,88... | collective-permute-start | bytes 1671176 | tf_op jit(solution)/shard_map/ppermute | solution.py:405
  291.0 13.0 %collective-permute-start.39 = (bf16[2,272,512]{2,1,0:T(8,128)(2,1)S(1)}, bf16[2,272,512]{2,1,0:T(8,128)(2,1)}, u32[]{:S(2)}, u32[]{:S(2)}) collective-permute-start(bf16[2,272,512]{2,1,0:T(8,128)(2,1)S(1)} %pad_maximum_fusion.12), channel_id=1, source_target_pairs={{0,8},{8,16},{16,24},{24,0},{32,40},{40,48},{48,56},{56,32},{64,72... | collective-permute-start | bytes 1671176 | tf_op jit(solution)/shard_map/ppermute | solution.py:405
  293.8 11.4 %collective-permute-start.40 = (bf16[2,272,512]{2,1,0:T(8,128)(2,1)S(1)}, bf16[2,272,512]{2,1,0:T(8,128)(2,1)}, u32[]{:S(2)}, u32[]{:S(2)}) collective-permute-start(bf16[2,272,512]{2,1,0:T(8,128)(2,1)S(1)} %pad_maximum_fusion.13), channel_id=1, source_target_pairs={{0,96},{8,104},{16,112},{24,120},{32,0},{40,8},{48,16},{56,24},{64... | collective-permute-start | bytes 1671176 | tf_op jit(solution)/shard_map/ppermute | solution.py:405
  294.7 12.7 %collective-permute-start.41 = (bf16[2,272,512]{2,1,0:T(8,128)(2,1)}, bf16[2,272,512]{2,1,0:T(8,128)(2,1)}, u32[]{:S(2)}, u32[]{:S(2)}) collective-permute-start(bf16[2,272,512]{2,1,0:T(8,128)(2,1)} %pad_maximum_fusion.14), channel_id=1, source_target_pairs={{0,32},{8,40},{16,48},{24,56},{32,64},{40,72},{48,80},{56,88},{64,... | collective-permute-start | bytes 1671176 | tf_op jit(solution)/shard_map/ppermute | solution.py:405
  296.9 30.8 %all-to-all-start.1 = ((f32[16,1,7]{2,1,0:T(1,128)}), f32[16,1,7]{2,1,0:T(1,128)S(1)}, u32[]{:S(2)}, u32[]{:S(2)}) async-start(f32[16,1,7]{2,1,0:T(1,128)} %copy.31), calls=%async_computation.1 | async-start | bytes 16384 | tf_op jit(solution)/shard_map/all_to_all | solution.py:655
  310.1 18.2 %collective-permute-start.42 = (f32[512]{0:T(512)}, f32[512]{0:T(512)S(1)}, u32[]{:S(2)}, u32[]{:S(2)}) collective-permute-start(f32[512]{0:T(512)} %bitcast.53), channel_id=1, source_target_pairs={{8,0},{16,8},{24,16},{32,24},{40,32},{48,40},{56,48},{64,56},{72,6... | collective-permute-start | bytes 6152 | tf_op jit(solution)/shard_map/ppermute | solution.py:528
  312.0 16.3 %collective-permute-start.43 = (f32[512]{0:T(512)S(1)}, f32[512]{0:T(512)S(1)}, u32[]{:S(2)}, u32[]{:S(2)}) collective-permute-start(f32[512]{0:T(512)S(1)} %bitcast.204), channel_id=1, source_target_pairs={{0,8},{8,16},{16,24},{24,32},{32,40},{40,48},{48,56},{56,64},{64,7... | collective-permute-start | bytes 6152 | tf_op jit(solution)/shard_map/ppermute | solution.py:528
  317.5 10.8 %collective-permute-start.44 = (f32[512]{0:T(512)S(1)}, f32[512]{0:T(512)S(1)}, u32[]{:S(2)}, u32[]{:S(2)}) collective-permute-start(f32[512]{0:T(512)S(1)} %bitcast.203), channel_id=1, source_target_pairs={{1,0},{2,1},{3,2},{4,3},{5,4},{6,5},{7,6},{9,8},{10,9},{11,10},{12... | collective-permute-start | bytes 6152 | tf_op jit(solution)/shard_map/ppermute | solution.py:528
  (28 other events, 400.5 us)

commit v8 on v7

--- a/solution.py
+++ b/solution.py
@@ -484,10 +484,7 @@
             "y+": jnp.stack([near[4, 0], total(near[4, 1], xm[2], xp[2], yp[0])]),
         }
     )
-    result = wide(near[0])
-    for way in WAYS_BACK:
-        result = result + wide(got[way])
-    return result
+    return [near[0]] + [got[way] for way in WAYS_BACK]
 
 
 def next_images(used, image):
@@ -585,21 +582,23 @@
     row_off = offsets[:, 0].reshape(-1)
     col_off = offsets[:, 1].reshape(-1)
     slots = jnp.arange(32, dtype=I32)
-    match = recv_plan[0, 0][None, :] == slots[:, None]
-    used = jnp.any(match, axis=1).astype(I32)
-    image = jnp.sum(jnp.where(match, jnp.arange(16, dtype=I32)[None, :], 0), axis=1)
-    table = jnp.stack([used, image, row_off, col_off])
     relative = jnp.array(NEAR + MIDDLE + FAR, I32)
     place = lax.axis_index("dy")
     tile_ids = ((place // 4 + relative[:, 1]) % 4) * 4 + (place % 4 + relative[:, 0]) % 4
     slot_ids = (2 * tile_ids[:, None] + jnp.arange(2, dtype=I32)[None, :]).reshape(-1)
-    table = jnp.sum(
-        jnp.where(slot_ids[None, :, None] == slots[None, None, :], table[:, None, :], 0), axis=2
-    )
-
-    def plan_of(first, count):
+    match = recv_plan[0, 0][None, :] == slot_ids[:, None]
+    used = jnp.any(match, axis=1).astype(I32)
+    image = jnp.sum(jnp.where(match, jnp.arange(16, dtype=I32)[None, :], 0), axis=1)
+    owned = []
+    for low, high in ((0, 10), (10, 22), (22, 32)):
+        part = used[low:high]
+        owned.append((part, next_images(part, image[low:high])))
+    chosen = slot_ids[:, None] == slots[None, :]
+    table = jnp.sum(jnp.where(chosen[None], jnp.stack([row_off, col_off])[:, None, :], 0), axis=2)
+
+    def plan_of(group, first, count):
         part = table[:, 2 * first : 2 * (first + count)]
-        return part[0], next_images(part[0], part[1]), part[2], part[3]
+        return owned[group] + (part[0], part[1])
 
     sun = sun_vectors(sun_azimuth[0], sun_elevation[0]).reshape(-1)
     gain = jnp.exp(exposure[0])
@@ -623,7 +622,7 @@
     out_near, parts = run_tiles(
         [upper] + [near_a[k] for k in WAYS] + [lower] + [near_b[k] for k in WAYS],
         [((n, 0), (n + 5, 0)) for n in range(5)],
-        resample, observed, plan_of(0, 5), sun, gain,
+        resample, observed, plan_of(0, 0, 5), sun, gain,
     )
     out_middle, more = run_tiles(
         [aside[k] for k in WAYS] + [ahead[k] for k in WAYS],
@@ -635,7 +634,7 @@
             ((4, 0), (5, 0)),
             ((6, 0), (7, 0)),
         ],
-        resample, observed, plan_of(5, 6), sun, gain,
+        resample, observed, plan_of(1, 5, 6), sun, gain,
     )
     parts = parts + more
     out_far, more = run_tiles(
@@ -647,21 +646,24 @@
             ((1, 1), (5, 0)),
             ((6, 0), (7, 0)),
         ],
-        resample, observed, plan_of(11, 5), sun, gain,
+        resample, observed, plan_of(2, 11, 5), sun, gain,
     )
     parts = parts + more
     smooth = smoothness(heights, top, bottom)
     crop_sums = finish_sums(parts)
-    arrived = lax.all_to_all(crop_sums[:, None], "dy", split_axis=0, concat_axis=0, tiled=True)
+    arrived = lax.all_to_all(
+        crop_sums[:, None], "dy", split_axis=0, concat_axis=0, tiled=True
+    )
     camera = arrived.sum(axis=0)
-    own = return_sums(out_near, out_middle, out_far)
-    from_below = shifted(own[0, HALF], "dy", False)
-    from_above = shifted(own[1, HALF], "dy", True)
-    from_right = shifted(own[:, HALF + 1, :HALF].reshape(-1), "dx", False)
-    from_left = shifted(own[:, HALF + 2, :HALF].reshape(-1), "dx", True)
+    arrived = return_sums(out_near, out_middle, out_far)
+    rim = sum(v[:, HALF : HALF + 3].astype(F32) for v in arrived)
+    from_below = shifted(rim[0, 0], "dy", False)
+    from_above = shifted(rim[1, 0], "dy", True)
+    from_right = shifted(rim[:, 1, :HALF].reshape(-1), "dx", False)
+    from_left = shifted(rim[:, 2, :HALF].reshape(-1), "dx", True)
     row_ids = lax.broadcasted_iota(I32, (T, T), 0)
     col_ids = lax.broadcasted_iota(I32, (T, T), 1)
-    data = own[:, :HALF].reshape(T, T)
+    data = sum(v[:, :HALF].astype(F32) for v in arrived).reshape(T, T)
     data = data + jnp.where(row_ids == T - 1, from_below[None, :], 0.0)
     data = data + jnp.where(row_ids == 0, from_above[None, :], 0.0)
     data = data + jnp.where(col_ids == T - 1, from_right[:, None], 0.0)

time: 337 us -> 324 us (0.961); the launches traced: 331 us -> 323 us
  waiting for transfers between devices: 112 us -> 99.1 us
  starting transfers between devices: 92.3 us -> 103 us
  local copies, waits for them, and re-layouts: 24.5 us -> 19.4 us
    ppermute x38, waiting for transfers between devices: 107 us -> 91.5 us  [send(): lax.ppermute(v, 'dy', STEPS[way])]
    ppermute x38, starting transfers between devices: 43.8 us -> 53.2 us  [send(): lax.ppermute(v, 'dy', STEPS[way])]
    all_to_all x1, waiting for transfers between devices: 0.01 us -> 4.79 us  [per_device(): lax.all_to_all(crop_sums[:, None], 'dy', split_axis=0, concat_axis=0, til...]
  transfers between devices with their start and end apart: 50 -> 50, of which waited for: 17 -> 14; matrix products, arithmetic and copies ran while one was open for 12% -> 11% of each run, Pallas kernels for 21% -> 14%
where the time goes in v8:
time: 324 us; the launch traced here: 323 us
  starting transfers between devices  103 us (32%)
  waiting for transfers between devices  99.1 us (31%)
  Pallas kernels  69.1 us (21%)
  other arithmetic  29.2 us (9%)
  local copies, waits for them, and re-layouts  19.4 us (6%)
  between operations  3.26 us (1%)
    ppermute x38, waiting for transfers between devices, send(): lax.ppermute(v, 'dy', STEPS[way])  91.5 us
    pallas_call x3, Pallas kernels, run_tiles(): pl.pallas_call(functools.partial(tile_kernel, pieces, len(arrays)), grid_...  69.1 us
    ppermute x38, starting transfers between devices, send(): lax.ppermute(v, 'dy', STEPS[way])  53.2 us
    ppermute x10, starting transfers between devices, shifted(): lax.ppermute(value, axis, pairs if up else [(b, a) for a, b in pairs])  36.1 us
    all_to_all x1, starting transfers between devices, per_device(): lax.all_to_all(offsets, 'dy', split_axis=0, concat_axis=0, tiled=True)  6.86 us
  transfers between devices with their start and end apart: 50, of which 14 were waited for; matrix products, arithmetic and copies ran while one was open for 11% of the time, Pallas kernels for 14%

profile of v8, /device:TPU:7, one launch (start us, length us, event | category | flops | bytes accessed | tf_op | source)
XLA Modules:
  0.0 322.7 jit_solution(15290460154872901697)
XLA Ops:
  2.0 6.9 %all-to-all-start = ((s32[16,2,2]{2,1,0:T(2,128)}), s32[16,2,2]{2,1,0:T(2,128)S(1)}, u32[]{:S(2)}, u32[]{:S(2)}) async-start(s32[16,2,2]{2,1,0:T(2,128)} %copy.26), calls=%async_computation | async-start | bytes 32768 | tf_op jit(solution)/shard_map/all_to_all | solution.py:581
  9.6 2.5 collective-permute-start.3
  12.1 4.9 %collective-permute-start.2 = (f32[2,512]{1,0:T(2,128)S(1)}, f32[2,512]{1,0:T(2,128)S(1)}, u32[]{:S(2)}, u32[]{:S(2)}) collective-permute-start(f32[2,512]{1,0:T(2,128)S(1)} %get-tuple-element.62), channel_id=1, source_target_pairs={{0,8},{8,16},{16,24},{24,32},{32,40},{40,48},{48,56},{56,64},{64,7... | collective-permute-start | bytes 12296 | tf_op jit(solution)/shard_map/ppermute | solution.py:525
  18.3 5.2 %collective-permute-start = (f32[512]{0:T(512)S(1)}, f32[512]{0:T(512)S(1)}, u32[]{:S(2)}, u32[]{:S(2)}) collective-permute-start(f32[512]{0:T(512)S(1)} %get-tuple-element.14), channel_id=1, source_target_pairs={{0,1},{1,2},{2,3},{3,4},{4,5},{5,6},{6,7},{8,9},{9,10},{10,11},{11... | collective-permute-start | bytes 6152 | tf_op jit(solution)/shard_map/ppermute | solution.py:525
  23.6 1.9 collective-permute-start.1
  31.4 1.8 and_or_fusion
  37.9 3.6 %collective-permute-start.46 = (f32[516,2]{1,0:T(8,128)S(1)}, f32[516,2]{1,0:T(8,128)S(1)}, u32[]{:S(2)}, u32[]{:S(2)}) collective-permute-start(f32[516,2]{1,0:T(8,128)S(1)} %get-tuple-element.58), channel_id=1, source_target_pairs={{0,1},{1,2},{2,3},{3,4},{4,5},{5,6},{6,7},{8,9},{9,10},{10,11},{11... | collective-permute-start | bytes 12392 | tf_op jit(solution)/shard_map/ppermute | solution.py:525
  41.6 1.9 collective-permute-start.47
  46.7 2.9 collective-permute-done.47
  51.5 5.2 %collective-permute-done.11.refs_15_ = s32[1,264,512]{2,1,0:T(8,128)S(1)} collective-permute-done((s32[1,264,512]{2,1,0:T(8,128)S(1)}, s32[1,264,512]{2,1,0:T(8,128)S(1)}, u32[]{:S(2)}, u32[]{:S(2)}) %collective-permute-start.11) | collective-permute-done | bytes 540704 | tf_op jit(solution)/shard_map/ppermute | solution.py:405
  56.7 2.1 collective-permute-done.4.refs_7_
  60.1 2.3 collective-permute-start.8
  62.5 7.3 %collective-permute-done.6.refs_9_ = s32[1,264,512]{2,1,0:T(8,128)} collective-permute-done((s32[1,264,512]{2,1,0:T(8,128)S(1)}, s32[1,264,512]{2,1,0:T(8,128)}, u32[]{:S(2)}, u32[]{:S(2)}) %collective-permute-start.6) | collective-permute-done | bytes 540704 | tf_op jit(solution)/shard_map/ppermute | solution.py:405
  69.8 1.7 collective-permute-start.19
  76.5 9.5 %collective-permute-done.16.refs_10_ = s32[1,264,512]{2,1,0:T(8,128)} collective-permute-done((s32[1,264,512]{2,1,0:T(8,128)S(1)}, s32[1,264,512]{2,1,0:T(8,128)}, u32[]{:S(2)}, u32[]{:S(2)}) %collective-permute-start.16) | collective-permute-done | bytes 540704 | tf_op jit(solution)/shard_map/ppermute | solution.py:405
  86.0 3.0 collective-permute-start.12
  90.1 23.8 %collective-permute-done.18.refs_12_ = s32[1,264,512]{2,1,0:T(8,128)} collective-permute-done((s32[1,264,512]{2,1,0:T(8,128)}, s32[1,264,512]{2,1,0:T(8,128)}, u32[]{:S(2)}, u32[]{:S(2)}) %collective-permute-start.18) | collective-permute-done | bytes 540704 | tf_op jit(solution)/shard_map/ppermute | solution.py:405
  115.1 1.6 pad_maximum_fusion.6
  116.7 11.6 %collective-permute-done.17.refs_11_ = s32[1,264,512]{2,1,0:T(8,128)S(1)} collective-permute-done((s32[1,264,512]{2,1,0:T(8,128)}, s32[1,264,512]{2,1,0:T(8,128)S(1)}, u32[]{:S(2)}, u32[]{:S(2)}) %collective-permute-start.17) | collective-permute-done | bytes 540704 | tf_op jit(solution)/shard_map/ppermute | solution.py:405
  128.3 2.7 collective-permute-start.23
  131.2 1.6 collective-permute-start.20
  132.8 1.7 fusion.1
  134.5 21.9 %shard_map.113 = (bf16[5,2,272,512]{3,2,1,0:T(8,128)(2,1)}, f32[16,5,8,384]{3,2,1,0:T(8,128)}) custom-call(s32[10]{0:T(128)} %get-tuple-element.86.refs_0_, s32[10]{0:T(128)} %select_reduce_fusion.5.refs_1_, s32[10]{0:T(128)} %get-tuple-element.77.refs_2_, s32[10]{0:T(128)} %get-tuple-element.74.refs_3_, f32[48]{0:T(128)} %reshape.363.refs_4_, ...), custom_call_target="tpu_custom_call" | custom-call | flops 2264924160 | bytes 40000000 | tf_op jit(solution)/shard_map/pallas_call | solution.py:374
  157.7 8.6 %collective-permute-start.26 = (s32[1,264,512]{2,1,0:T(8,128)}, s32[1,264,512]{2,1,0:T(8,128)}, u32[]{:S(2)}, u32[]{:S(2)}) collective-permute-start(s32[1,264,512]{2,1,0:T(8,128)} %collective-permute-done.18.refs_12_), channel_id=1, source_target_pairs={{0,16},{8,24},{16,0},{24,8},{32,48},{40,56},{48,32},{56,40},{64,80... | collective-permute-start | bytes 1622024 | tf_op jit(solution)/shard_map/ppermute | solution.py:405
  167.4 24.7 %shard_map.114 = (bf16[6,2,272,512]{3,2,1,0:T(8,128)(2,1)}, f32[16,5,8,384]{3,2,1,0:T(8,128)}) custom-call(s32[12]{0:T(128)} %get-tuple-element.91.refs_0_, s32[12]{0:T(128)} %select_reduce_fusion.3.refs_1_, s32[12]{0:T(128)} %get-tuple-element.81.refs_2_, s32[12]{0:T(128)} %get-tuple-element.80.refs_3_, f32[48]{0:T(128)} %reshape.363.refs_4_, ...), custom_call_target="tpu_custom_call" | custom-call | flops 2717908992 | bytes 48000000 | tf_op jit(solution)/shard_map/pallas_call | solution.py:374
  192.1 2.2 slice_bitcast_fusion.7
  195.2 22.5 %shard_map.115 = (bf16[5,2,272,512]{3,2,1,0:T(8,128)(2,1)}, f32[16,5,8,384]{3,2,1,0:T(8,128)}) custom-call(s32[10]{0:T(128)} %get-tuple-element.87.refs_0_, s32[10]{0:T(128)} %select_reduce_fusion.1.refs_1_, s32[10]{0:T(128)} %get-tuple-element.76.refs_2_, s32[10]{0:T(128)} %get-tuple-element.75.refs_3_, f32[48]{0:T(128)} %reshape.363.refs_4_, ...), custom_call_target="tpu_custom_call" | custom-call | flops 2264924160 | bytes 40000000 | tf_op jit(solution)/shard_map/pallas_call | solution.py:374
  217.7 1.6 fusion.68
  222.1 6.4 %collective-permute-start.31 = (bf16[1,272,512]{2,1,0:T(8,128)(2,1)S(1)}, bf16[1,272,512]{2,1,0:T(8,128)(2,1)S(1)}, u32[]{:S(2)}, u32[]{:S(2)}) collective-permute-start(bf16[1,272,512]{2,1,0:T(8,128)(2,1)S(1)} %get-tuple-element.52), channel_id=1, source_target_pairs={{0,16},{8,24},{16,0},{24,8},{32,48},{40,56},{48,32},{56,40},{64,80... | collective-permute-start | bytes 835592 | tf_op jit(solution)/shard_map/ppermute | solution.py:405
  228.5 5.5 %collective-permute-start.35 = (bf16[1,272,512]{2,1,0:T(8,128)(2,1)S(1)}, bf16[1,272,512]{2,1,0:T(8,128)(2,1)S(1)}, u32[]{:S(2)}, u32[]{:S(2)}) collective-permute-start(bf16[1,272,512]{2,1,0:T(8,128)(2,1)S(1)} %get-tuple-element.55), channel_id=1, source_target_pairs={{0,64},{8,72},{16,80},{24,88},{32,96},{40,104},{48,112},{56,120},{... | collective-permute-start | bytes 835592 | tf_op jit(solution)/shard_map/ppermute | solution.py:405
  234.2 10.0 %collective-permute-done.31 = bf16[1,272,512]{2,1,0:T(8,128)(2,1)S(1)} collective-permute-done((bf16[1,272,512]{2,1,0:T(8,128)(2,1)S(1)}, bf16[1,272,512]{2,1,0:T(8,128)(2,1)S(1)}, u32[]{:S(2)}, u32[]{:S(2)}) %collective-permute-start.31) | collective-permute-done | bytes 278560 | tf_op jit(solution)/shard_map/ppermute | solution.py:405
  244.5 6.3 %collective-permute-done.37 = bf16[1,272,512]{2,1,0:T(8,128)(2,1)S(1)} collective-permute-done((bf16[1,272,512]{2,1,0:T(8,128)(2,1)S(1)}, bf16[1,272,512]{2,1,0:T(8,128)(2,1)S(1)}, u32[]{:S(2)}, u32[]{:S(2)}) %collective-permute-start.37) | collective-permute-done | bytes 278560 | tf_op jit(solution)/shard_map/ppermute | solution.py:405
  256.2 1.9 collective-permute-start.32
  260.4 8.1 %collective-permute-done.38 = bf16[3,272,512]{2,1,0:T(8,128)(2,1)} collective-permute-done((bf16[3,272,512]{2,1,0:T(8,128)(2,1)}, bf16[3,272,512]{2,1,0:T(8,128)(2,1)}, u32[]{:S(2)}, u32[]{:S(2)}) %collective-permute-start.38) | collective-permute-done | bytes 835616 | tf_op jit(solution)/shard_map/ppermute | solution.py:405
  268.5 3.3 %collective-permute-done.30 = bf16[3,272,512]{2,1,0:T(8,128)(2,1)} collective-permute-done((bf16[3,272,512]{2,1,0:T(8,128)(2,1)}, bf16[3,272,512]{2,1,0:T(8,128)(2,1)}, u32[]{:S(2)}, u32[]{:S(2)}) %collective-permute-start.30) | collective-permute-done | bytes 835616 | tf_op jit(solution)/shard_map/ppermute | solution.py:405
  271.8 2.3 collective-permute-done.32
  274.1 1.8 collective-permute-done.33
  275.9 3.1 fusion.31
  279.9 2.8 collective-permute-start.39
  283.6 3.6 %collective-permute-start.40 = (bf16[2,272,512]{2,1,0:T(8,128)(2,1)}, bf16[2,272,512]{2,1,0:T(8,128)(2,1)}, u32[]{:S(2)}, u32[]{:S(2)}) collective-permute-start(bf16[2,272,512]{2,1,0:T(8,128)(2,1)} %pad_maximum_fusion.13), channel_id=1, source_target_pairs={{0,96},{8,104},{16,112},{24,120},{32,0},{40,8},{48,16},{56,24},{64... | collective-permute-start | bytes 1671176 | tf_op jit(solution)/shard_map/ppermute | solution.py:405
  288.7 6.4 %all-to-all-start.1 = ((f32[16,1,7]{2,1,0:T(1,128)}), f32[16,1,7]{2,1,0:T(1,128)S(1)}, u32[]{:S(2)}, u32[]{:S(2)}) async-start(f32[16,1,7]{2,1,0:T(1,128)} %copy.31), calls=%async_computation.1 | async-start | bytes 16384 | tf_op jit(solution)/shard_map/all_to_all | solution.py:654
  296.2 4.8 %all-to-all-done.1 = f32[16,1,7]{2,1,0:T(1,128)S(1)} async-done(((f32[16,1,7]{2,1,0:T(1,128)}), f32[16,1,7]{2,1,0:T(1,128)S(1)}, u32[]{:S(2)}, u32[]{:S(2)}) %all-to-all-start.1) | async-done | bytes 480 | tf_op jit(solution)/shard_map/all_to_all | solution.py:654
  302.3 2.2 collective-permute-start.42
  304.5 5.2 %collective-permute-start.43 = (f32[512]{0:T(512)S(1)}, f32[512]{0:T(512)S(1)}, u32[]{:S(2)}, u32[]{:S(2)}) collective-permute-start(f32[512]{0:T(512)S(1)} %bitcast.176), channel_id=1, source_target_pairs={{0,8},{8,16},{16,24},{24,32},{32,40},{40,48},{48,56},{56,64},{64,7... | collective-permute-start | bytes 6152 | tf_op jit(solution)/shard_map/ppermute | solution.py:525
  309.8 6.7 %collective-permute-start.44 = (f32[512]{0:T(512)S(1)}, f32[512]{0:T(512)S(1)}, u32[]{:S(2)}, u32[]{:S(2)}) collective-permute-start(f32[512]{0:T(512)S(1)} %bitcast.175), channel_id=1, source_target_pairs={{1,0},{2,1},{3,2},{4,3},{5,4},{6,5},{7,6},{9,8},{10,9},{11,10},{12... | collective-permute-start | bytes 6152 | tf_op jit(solution)/shard_map/ppermute | solution.py:525
  316.5 1.9 collective-permute-start.45
  318.4 1.8 convert_add_fusion
  320.3 2.4 fusion.6
  (206 shorter events, 45.6 us)
Async XLA Ops:
  2.0 87.7 %all-to-all-start = ((s32[16,2,2]{2,1,0:T(2,128)}), s32[16,2,2]{2,1,0:T(2,128)S(1)}, u32[]{:S(2)}, u32[]{:S(2)}) async-start(s32[16,2,2]{2,1,0:T(2,128)} %copy.26), calls=%async_computation | async-start | bytes 32768 | tf_op jit(solution)/shard_map/all_to_all | solution.py:581
  9.6 28.1 %collective-permute-start.3 = (f32[2,512]{1,0:T(2,128)S(1)}, f32[2,512]{1,0:T(2,128)S(1)}, u32[]{:S(2)}, u32[]{:S(2)}) collective-permute-start(f32[2,512]{1,0:T(2,128)S(1)} %get-tuple-element.63), channel_id=1, source_target_pairs={{8,0},{16,8},{24,16},{32,24},{40,32},{48,40},{56,48},{64,56},{72,6... | collective-permute-start | bytes 12296 | tf_op jit(solution)/shard_map/ppermute | solution.py:525
  12.1 25.7 %collective-permute-start.2 = (f32[2,512]{1,0:T(2,128)S(1)}, f32[2,512]{1,0:T(2,128)S(1)}, u32[]{:S(2)}, u32[]{:S(2)}) collective-permute-start(f32[2,512]{1,0:T(2,128)S(1)} %get-tuple-element.62), channel_id=1, source_target_pairs={{0,8},{8,16},{16,24},{24,32},{32,40},{40,48},{48,56},{56,64},{64,7... | collective-permute-start | bytes 12296 | tf_op jit(solution)/shard_map/ppermute | solution.py:525
  18.3 19.4 %collective-permute-start = (f32[512]{0:T(512)S(1)}, f32[512]{0:T(512)S(1)}, u32[]{:S(2)}, u32[]{:S(2)}) collective-permute-start(f32[512]{0:T(512)S(1)} %get-tuple-element.14), channel_id=1, source_target_pairs={{0,1},{1,2},{2,3},{3,4},{4,5},{5,6},{6,7},{8,9},{9,10},{10,11},{11... | collective-permute-start | bytes 6152 | tf_op jit(solution)/shard_map/ppermute | solution.py:525
  23.6 14.2 %collective-permute-start.1 = (f32[512]{0:T(512)S(1)}, f32[512]{0:T(512)S(1)}, u32[]{:S(2)}, u32[]{:S(2)}) collective-permute-start(f32[512]{0:T(512)S(1)} %get-tuple-element.15), channel_id=1, source_target_pairs={{1,0},{2,1},{3,2},{4,3},{5,4},{6,5},{7,6},{9,8},{10,9},{11,10},{12... | collective-permute-start | bytes 6152 | tf_op jit(solution)/shard_map/ppermute | solution.py:525
  37.9 7.4 %collective-permute-start.46 = (f32[516,2]{1,0:T(8,128)S(1)}, f32[516,2]{1,0:T(8,128)S(1)}, u32[]{:S(2)}, u32[]{:S(2)}) collective-permute-start(f32[516,2]{1,0:T(8,128)S(1)} %get-tuple-element.58), channel_id=1, source_target_pairs={{0,1},{1,2},{2,3},{3,4},{4,5},{5,6},{6,7},{8,9},{9,10},{10,11},{11... | collective-permute-start | bytes 12392 | tf_op jit(solution)/shard_map/ppermute | solution.py:525
  41.6 8.0 %collective-permute-start.47 = (f32[516,2]{1,0:T(8,128)S(1)}, f32[516,2]{1,0:T(8,128)S(1)}, u32[]{:S(2)}, u32[]{:S(2)}) collective-permute-start(f32[516,2]{1,0:T(8,128)S(1)} %get-tuple-element.59), channel_id=1, source_target_pairs={{1,0},{2,1},{3,2},{4,3},{5,4},{6,5},{7,6},{9,8},{10,9},{11,10},{12... | collective-permute-start | bytes 12392 | tf_op jit(solution)/shard_map/ppermute | solution.py:525
  43.7 13.0 %collective-permute-start.11 = (s32[1,264,512]{2,1,0:T(8,128)S(1)}, s32[1,264,512]{2,1,0:T(8,128)S(1)}, u32[]{:S(2)}, u32[]{:S(2)}) collective-permute-start(s32[1,264,512]{2,1,0:T(8,128)S(1)} %get-tuple-element.71.refs_11_), channel_id=1, source_target_pairs={{0,96},{8,104},{16,112},{24,120},{32,0},{40,8},{48,16},{56,24},{64... | collective-permute-start | bytes 1622024 | tf_op jit(solution)/shard_map/ppermute | solution.py:405
  43.8 16.3 %collective-permute-start.10 = (s32[1,264,512]{2,1,0:T(8,128)S(1)}, s32[1,264,512]{2,1,0:T(8,128)S(1)}, u32[]{:S(2)}, u32[]{:S(2)}) collective-permute-start(s32[1,264,512]{2,1,0:T(8,128)S(1)} %get-tuple-element.71.refs_11_), channel_id=1, source_target_pairs={{0,32},{8,40},{16,48},{24,56},{32,64},{40,72},{48,80},{56,88},{64,... | collective-permute-start | bytes 1622024 | tf_op jit(solution)/shard_map/ppermute | solution.py:405
  45.3 13.6 %collective-permute-start.4 = (s32[1,264,512]{2,1,0:T(8,128)S(1)}, s32[1,264,512]{2,1,0:T(8,128)S(1)}, u32[]{:S(2)}, u32[]{:S(2)}) collective-permute-start(s32[1,264,512]{2,1,0:T(8,128)S(1)} %get-tuple-element.70.refs_6_), channel_id=1, source_target_pairs={{0,8},{8,16},{16,24},{24,0},{32,40},{40,48},{48,56},{56,32},{64,72... | collective-permute-start | bytes 1622024 | tf_op jit(solution)/shard_map/ppermute | solution.py:405
  45.3 17.1 %collective-permute-start.5 = (s32[1,264,512]{2,1,0:T(8,128)S(1)}, s32[1,264,512]{2,1,0:T(8,128)S(1)}, u32[]{:S(2)}, u32[]{:S(2)}) collective-permute-start(s32[1,264,512]{2,1,0:T(8,128)S(1)} %get-tuple-element.70.refs_6_), channel_id=1, source_target_pairs={{0,24},{8,0},{16,8},{24,16},{32,56},{40,32},{48,40},{56,48},{64,88... | collective-permute-start | bytes 1622024 | tf_op jit(solution)/shard_map/ppermute | solution.py:405
  49.6 20.2 %collective-permute-start.6 = (s32[1,264,512]{2,1,0:T(8,128)S(1)}, s32[1,264,512]{2,1,0:T(8,128)}, u32[]{:S(2)}, u32[]{:S(2)}) collective-permute-start(s32[1,264,512]{2,1,0:T(8,128)S(1)} %get-tuple-element.70.refs_6_), channel_id=1, source_target_pairs={{0,32},{8,40},{16,48},{24,56},{32,64},{40,72},{48,80},{56,88},{64,... | collective-permute-start | bytes 1622024 | tf_op jit(solution)/shard_map/ppermute | solution.py:405
  56.7 18.2 %collective-permute-start.9 = (s32[1,264,512]{2,1,0:T(8,128)S(1)}, s32[1,264,512]{2,1,0:T(8,128)S(1)}, u32[]{:S(2)}, u32[]{:S(2)}) collective-permute-start(s32[1,264,512]{2,1,0:T(8,128)S(1)} %get-tuple-element.71.refs_11_), channel_id=1, source_target_pairs={{0,24},{8,0},{16,8},{24,16},{32,56},{40,32},{48,40},{56,48},{64,88... | collective-permute-start | bytes 1622024 | tf_op jit(solution)/shard_map/ppermute | solution.py:405
  58.9 16.4 %collective-permute-start.7 = (s32[1,264,512]{2,1,0:T(8,128)S(1)}, s32[1,264,512]{2,1,0:T(8,128)S(1)}, u32[]{:S(2)}, u32[]{:S(2)}) collective-permute-start(s32[1,264,512]{2,1,0:T(8,128)S(1)} %get-tuple-element.70.refs_6_), channel_id=1, source_target_pairs={{0,96},{8,104},{16,112},{24,120},{32,0},{40,8},{48,16},{56,24},{64... | collective-permute-start | bytes 1622024 | tf_op jit(solution)/shard_map/ppermute | solution.py:405
  60.1 16.4 %collective-permute-start.8 = (s32[1,264,512]{2,1,0:T(8,128)S(1)}, s32[1,264,512]{2,1,0:T(8,128)S(1)}, u32[]{:S(2)}, u32[]{:S(2)}) collective-permute-start(s32[1,264,512]{2,1,0:T(8,128)S(1)} %get-tuple-element.71.refs_11_), channel_id=1, source_target_pairs={{0,8},{8,16},{16,24},{24,0},{32,40},{40,48},{48,56},{56,32},{64,72... | collective-permute-start | bytes 1622024 | tf_op jit(solution)/shard_map/ppermute | solution.py:405
  62.4 23.6 %collective-permute-start.16 = (s32[1,264,512]{2,1,0:T(8,128)S(1)}, s32[1,264,512]{2,1,0:T(8,128)}, u32[]{:S(2)}, u32[]{:S(2)}) collective-permute-start(s32[1,264,512]{2,1,0:T(8,128)S(1)} %collective-permute-done.4.refs_7_), channel_id=1, source_target_pairs={{0,8},{8,16},{16,24},{24,0},{32,40},{40,48},{48,56},{56,32},{64,72... | collective-permute-start | bytes 1622024 | tf_op jit(solution)/shard_map/ppermute | solution.py:405
  69.8 19.2 %collective-permute-start.19 = (s32[1,264,512]{2,1,0:T(8,128)S(1)}, s32[1,264,512]{2,1,0:T(8,128)}, u32[]{:S(2)}, u32[]{:S(2)}) collective-permute-start(s32[1,264,512]{2,1,0:T(8,128)S(1)} %collective-permute-done.11.refs_15_), channel_id=1, source_target_pairs={{0,96},{8,104},{16,112},{24,120},{32,0},{40,8},{48,16},{56,24},{64... | collective-permute-start | bytes 1622024 | tf_op jit(solution)/shard_map/ppermute | solution.py:405
  74.9 53.4 %collective-permute-start.15 = (s32[2,264,512]{2,1,0:T(8,128)}, s32[2,264,512]{2,1,0:T(8,128)}, u32[]{:S(2)}, u32[]{:S(2)}) collective-permute-start(s32[2,264,512]{2,1,0:T(8,128)} %constant_dynamic-update-slice_fusion.2), channel_id=1, source_target_pairs={{0,96},{8,104},{16,112},{24,120},{32,0},{40,8},{48,16},{56,24},{64... | collective-permute-start | bytes 3244040 | tf_op jit(solution)/shard_map/ppermute | solution.py:405
  75.2 55.8 %collective-permute-start.14 = (s32[2,264,512]{2,1,0:T(8,128)}, s32[2,264,512]{2,1,0:T(8,128)S(1)}, u32[]{:S(2)}, u32[]{:S(2)}) collective-permute-start(s32[2,264,512]{2,1,0:T(8,128)} %constant_dynamic-update-slice_fusion.2), channel_id=1, source_target_pairs={{0,32},{8,40},{16,48},{24,56},{32,64},{40,72},{48,80},{56,88},{64,... | collective-permute-start | bytes 3244040 | tf_op jit(solution)/shard_map/ppermute | solution.py:405
  76.5 54.5 %collective-permute-start.13 = (s32[2,264,512]{2,1,0:T(8,128)}, s32[2,264,512]{2,1,0:T(8,128)}, u32[]{:S(2)}, u32[]{:S(2)}) collective-permute-start(s32[2,264,512]{2,1,0:T(8,128)} %constant_dynamic-update-slice_fusion), channel_id=1, source_target_pairs={{0,24},{8,0},{16,8},{24,16},{32,56},{40,32},{48,40},{56,48},{64,88... | collective-permute-start | bytes 3244040 | tf_op jit(solution)/shard_map/ppermute | solution.py:405
  86.0 45.2 %collective-permute-start.12 = (s32[2,264,512]{2,1,0:T(8,128)}, s32[2,264,512]{2,1,0:T(8,128)S(1)}, u32[]{:S(2)}, u32[]{:S(2)}) collective-permute-start(s32[2,264,512]{2,1,0:T(8,128)} %constant_dynamic-update-slice_fusion), channel_id=1, source_target_pairs={{0,8},{8,16},{16,24},{24,0},{32,40},{40,48},{48,56},{56,32},{64,72... | collective-permute-start | bytes 3244040 | tf_op jit(solution)/shard_map/ppermute | solution.py:405
  89.0 24.9 %collective-permute-start.18 = (s32[1,264,512]{2,1,0:T(8,128)}, s32[1,264,512]{2,1,0:T(8,128)}, u32[]{:S(2)}, u32[]{:S(2)}) collective-permute-start(s32[1,264,512]{2,1,0:T(8,128)} %collective-permute-done.6.refs_9_), channel_id=1, source_target_pairs={{0,32},{8,40},{16,48},{24,56},{32,64},{40,72},{48,80},{56,88},{64,... | collective-permute-start | bytes 1622024 | tf_op jit(solution)/shard_map/ppermute | solution.py:405
  113.9 14.4 %collective-permute-start.17 = (s32[1,264,512]{2,1,0:T(8,128)}, s32[1,264,512]{2,1,0:T(8,128)S(1)}, u32[]{:S(2)}, u32[]{:S(2)}) collective-permute-start(s32[1,264,512]{2,1,0:T(8,128)} %copy-done.22), channel_id=1, source_target_pairs={{0,24},{8,0},{16,8},{24,16},{32,56},{40,32},{48,40},{56,48},{64,88... | collective-permute-start | bytes 1622024 | tf_op jit(solution)/shard_map/ppermute | solution.py:405
  128.3 28.1 %collective-permute-start.22 = (s32[1,264,512]{2,1,0:T(8,128)}, s32[1,264,512]{2,1,0:T(8,128)}, u32[]{:S(2)}, u32[]{:S(2)}) collective-permute-start(s32[1,264,512]{2,1,0:T(8,128)} %collective-permute-done.16.refs_10_), channel_id=1, source_target_pairs={{0,32},{8,40},{16,48},{24,56},{32,64},{40,72},{48,80},{56,88},{64,... | collective-permute-start | bytes 1622024 | tf_op jit(solution)/shard_map/ppermute | solution.py:405
  128.3 29.4 %collective-permute-start.23 = (s32[1,264,512]{2,1,0:T(8,128)}, s32[1,264,512]{2,1,0:T(8,128)}, u32[]{:S(2)}, u32[]{:S(2)}) collective-permute-start(s32[1,264,512]{2,1,0:T(8,128)} %collective-permute-done.16.refs_10_), channel_id=1, source_target_pairs={{0,96},{8,104},{16,112},{24,120},{32,0},{40,8},{48,16},{56,24},{64... | collective-permute-start | bytes 1622024 | tf_op jit(solution)/shard_map/ppermute | solution.py:405
  131.0 35.3 %collective-permute-start.24 = (s32[1,264,512]{2,1,0:T(8,128)}, s32[1,264,512]{2,1,0:T(8,128)}, u32[]{:S(2)}, u32[]{:S(2)}) collective-permute-start(s32[1,264,512]{2,1,0:T(8,128)} %collective-permute-done.19.refs_13_), channel_id=1, source_target_pairs={{0,8},{8,16},{16,24},{24,0},{32,40},{40,48},{48,56},{56,32},{64,72... | collective-permute-start | bytes 1622024 | tf_op jit(solution)/shard_map/ppermute | solution.py:405
  131.0 63.4 %collective-permute-start.21 = (s32[2,264,512]{2,1,0:T(8,128)}, s32[2,264,512]{2,1,0:T(8,128)}, u32[]{:S(2)}, u32[]{:S(2)}) collective-permute-start(s32[2,264,512]{2,1,0:T(8,128)} %collective-permute-done.15.refs_9_), channel_id=1, source_target_pairs={{0,96},{8,104},{16,112},{24,120},{32,0},{40,8},{48,16},{56,24},{64... | collective-permute-start | bytes 3244040 | tf_op jit(solution)/shard_map/ppermute | solution.py:405
  131.2 63.2 %collective-permute-start.20 = (s32[2,264,512]{2,1,0:T(8,128)}, s32[2,264,512]{2,1,0:T(8,128)}, u32[]{:S(2)}, u32[]{:S(2)}) collective-permute-start(s32[2,264,512]{2,1,0:T(8,128)} %collective-permute-done.13.refs_7_), channel_id=1, source_target_pairs={{0,24},{8,0},{16,8},{24,16},{32,56},{40,32},{48,40},{56,48},{64,88... | collective-permute-start | bytes 3244040 | tf_op jit(solution)/shard_map/ppermute | solution.py:405
  156.4 37.9 %collective-permute-start.25 = (s32[1,264,512]{2,1,0:T(8,128)}, s32[1,264,512]{2,1,0:T(8,128)S(1)}, u32[]{:S(2)}, u32[]{:S(2)}) collective-permute-start(s32[1,264,512]{2,1,0:T(8,128)} %collective-permute-done.19.refs_13_), channel_id=1, source_target_pairs={{0,24},{8,0},{16,8},{24,16},{32,56},{40,32},{48,40},{56,48},{64,88... | collective-permute-start | bytes 1622024 | tf_op jit(solution)/shard_map/ppermute | solution.py:405
  157.7 36.7 %collective-permute-start.26 = (s32[1,264,512]{2,1,0:T(8,128)}, s32[1,264,512]{2,1,0:T(8,128)}, u32[]{:S(2)}, u32[]{:S(2)}) collective-permute-start(s32[1,264,512]{2,1,0:T(8,128)} %collective-permute-done.18.refs_12_), channel_id=1, source_target_pairs={{0,16},{8,24},{16,0},{24,8},{32,48},{40,56},{48,32},{56,40},{64,80... | collective-permute-start | bytes 1622024 | tf_op jit(solution)/shard_map/ppermute | solution.py:405
  166.4 28.0 %collective-permute-start.27 = (s32[1,264,512]{2,1,0:T(8,128)S(1)}, s32[1,264,512]{2,1,0:T(8,128)}, u32[]{:S(2)}, u32[]{:S(2)}) collective-permute-start(s32[1,264,512]{2,1,0:T(8,128)S(1)} %copy-done.21), channel_id=1, source_target_pairs={{0,64},{8,72},{16,80},{24,88},{32,96},{40,104},{48,112},{56,120},{... | collective-permute-start | bytes 1622024 | tf_op jit(solution)/shard_map/ppermute | solution.py:405
  219.3 31.5 %collective-permute-start.28 = (bf16[3,272,512]{2,1,0:T(8,128)(2,1)S(1)}, bf16[3,272,512]{2,1,0:T(8,128)(2,1)S(1)}, u32[]{:S(2)}, u32[]{:S(2)}) collective-permute-start(bf16[3,272,512]{2,1,0:T(8,128)(2,1)S(1)} %get-tuple-element.57), channel_id=1, source_target_pairs={{0,24},{8,0},{16,8},{24,16},{32,56},{40,32},{48,40},{56,48},{64,88... | collective-permute-start | bytes 2506760 | tf_op jit(solution)/shard_map/ppermute | solution.py:405
  219.7 31.2 %collective-permute-start.29 = (bf16[3,272,512]{2,1,0:T(8,128)(2,1)S(1)}, bf16[3,272,512]{2,1,0:T(8,128)(2,1)S(1)}, u32[]{:S(2)}, u32[]{:S(2)}) collective-permute-start(bf16[3,272,512]{2,1,0:T(8,128)(2,1)S(1)} %get-tuple-element.56), channel_id=1, source_target_pairs={{0,96},{8,104},{16,112},{24,120},{32,0},{40,8},{48,16},{56,24},{64... | collective-permute-start | bytes 2506760 | tf_op jit(solution)/shard_map/ppermute | solution.py:405
  222.1 22.1 %collective-permute-start.31 = (bf16[1,272,512]{2,1,0:T(8,128)(2,1)S(1)}, bf16[1,272,512]{2,1,0:T(8,128)(2,1)S(1)}, u32[]{:S(2)}, u32[]{:S(2)}) collective-permute-start(bf16[1,272,512]{2,1,0:T(8,128)(2,1)S(1)} %get-tuple-element.52), channel_id=1, source_target_pairs={{0,16},{8,24},{16,0},{24,8},{32,48},{40,56},{48,32},{56,40},{64,80... | collective-permute-start | bytes 835592 | tf_op jit(solution)/shard_map/ppermute | solution.py:405
  228.5 16.1 %collective-permute-start.35 = (bf16[1,272,512]{2,1,0:T(8,128)(2,1)S(1)}, bf16[1,272,512]{2,1,0:T(8,128)(2,1)S(1)}, u32[]{:S(2)}, u32[]{:S(2)}) collective-permute-start(bf16[1,272,512]{2,1,0:T(8,128)(2,1)S(1)} %get-tuple-element.55), channel_id=1, source_target_pairs={{0,64},{8,72},{16,80},{24,88},{32,96},{40,104},{48,112},{56,120},{... | collective-permute-start | bytes 835592 | tf_op jit(solution)/shard_map/ppermute | solution.py:405
  234.0 10.5 %collective-permute-start.36 = (bf16[1,272,512]{2,1,0:T(8,128)(2,1)S(1)}, bf16[1,272,512]{2,1,0:T(8,128)(2,1)S(1)}, u32[]{:S(2)}, u32[]{:S(2)}) collective-permute-start(bf16[1,272,512]{2,1,0:T(8,128)(2,1)S(1)} %get-tuple-element.54), channel_id=1, source_target_pairs={{0,8},{8,16},{16,24},{24,0},{32,40},{40,48},{48,56},{56,32},{64,72... | collective-permute-start | bytes 835592 | tf_op jit(solution)/shard_map/ppermute | solution.py:405
  252.6 15.9 %collective-permute-start.38 = (bf16[3,272,512]{2,1,0:T(8,128)(2,1)}, bf16[3,272,512]{2,1,0:T(8,128)(2,1)}, u32[]{:S(2)}, u32[]{:S(2)}) collective-permute-start(bf16[3,272,512]{2,1,0:T(8,128)(2,1)} %pad_maximum_fusion.10), channel_id=1, source_target_pairs={{0,8},{8,16},{16,24},{24,0},{32,40},{40,48},{48,56},{56,32},{64,72... | collective-permute-start | bytes 2506760 | tf_op jit(solution)/shard_map/ppermute | solution.py:405
  253.7 18.1 %collective-permute-start.30 = (bf16[3,272,512]{2,1,0:T(8,128)(2,1)}, bf16[3,272,512]{2,1,0:T(8,128)(2,1)}, u32[]{:S(2)}, u32[]{:S(2)}) collective-permute-start(bf16[3,272,512]{2,1,0:T(8,128)(2,1)} %pad_maximum_fusion.7), channel_id=1, source_target_pairs={{0,24},{8,0},{16,8},{24,16},{32,56},{40,32},{48,40},{56,48},{64,88... | collective-permute-start | bytes 2506760 | tf_op jit(solution)/shard_map/ppermute | solution.py:405
  256.2 17.9 %collective-permute-start.32 = (bf16[3,272,512]{2,1,0:T(8,128)(2,1)}, bf16[3,272,512]{2,1,0:T(8,128)(2,1)}, u32[]{:S(2)}, u32[]{:S(2)}) collective-permute-start(bf16[3,272,512]{2,1,0:T(8,128)(2,1)} %pad_maximum_fusion.8), channel_id=1, source_target_pairs={{0,96},{8,104},{16,112},{24,120},{32,0},{40,8},{48,16},{56,24},{64... | collective-permute-start | bytes 2506760 | tf_op jit(solution)/shard_map/ppermute | solution.py:405
  259.1 16.8 %collective-permute-start.33 = (bf16[3,272,512]{2,1,0:T(8,128)(2,1)}, bf16[3,272,512]{2,1,0:T(8,128)(2,1)}, u32[]{:S(2)}, u32[]{:S(2)}) collective-permute-start(bf16[3,272,512]{2,1,0:T(8,128)(2,1)} %pad_maximum_fusion.9), channel_id=1, source_target_pairs={{0,32},{8,40},{16,48},{24,56},{32,64},{40,72},{48,80},{56,88},{64,... | collective-permute-start | bytes 2506760 | tf_op jit(solution)/shard_map/ppermute | solution.py:405
  279.0 22.5 %collective-permute-start.34 = (bf16[2,272,512]{2,1,0:T(8,128)(2,1)S(1)}, bf16[2,272,512]{2,1,0:T(8,128)(2,1)}, u32[]{:S(2)}, u32[]{:S(2)}) collective-permute-start(bf16[2,272,512]{2,1,0:T(8,128)(2,1)S(1)} %pad_maximum_fusion.11), channel_id=1, source_target_pairs={{0,24},{8,0},{16,8},{24,16},{32,56},{40,32},{48,40},{56,48},{64,88... | collective-permute-start | bytes 1671176 | tf_op jit(solution)/shard_map/ppermute | solution.py:405
  279.9 21.6 %collective-permute-start.39 = (bf16[2,272,512]{2,1,0:T(8,128)(2,1)S(1)}, bf16[2,272,512]{2,1,0:T(8,128)(2,1)}, u32[]{:S(2)}, u32[]{:S(2)}) collective-permute-start(bf16[2,272,512]{2,1,0:T(8,128)(2,1)S(1)} %pad_maximum_fusion.12), channel_id=1, source_target_pairs={{0,8},{8,16},{16,24},{24,0},{32,40},{40,48},{48,56},{56,32},{64,72... | collective-permute-start | bytes 1671176 | tf_op jit(solution)/shard_map/ppermute | solution.py:405
  283.6 17.9 %collective-permute-start.40 = (bf16[2,272,512]{2,1,0:T(8,128)(2,1)}, bf16[2,272,512]{2,1,0:T(8,128)(2,1)}, u32[]{:S(2)}, u32[]{:S(2)}) collective-permute-start(bf16[2,272,512]{2,1,0:T(8,128)(2,1)} %pad_maximum_fusion.13), channel_id=1, source_target_pairs={{0,96},{8,104},{16,112},{24,120},{32,0},{40,8},{48,16},{56,24},{64... | collective-permute-start | bytes 1671176 | tf_op jit(solution)/shard_map/ppermute | solution.py:405
  288.0 13.5 %collective-permute-start.41 = (bf16[2,272,512]{2,1,0:T(8,128)(2,1)}, bf16[2,272,512]{2,1,0:T(8,128)(2,1)}, u32[]{:S(2)}, u32[]{:S(2)}) collective-permute-start(bf16[2,272,512]{2,1,0:T(8,128)(2,1)} %pad_maximum_fusion.14), channel_id=1, source_target_pairs={{0,32},{8,40},{16,48},{24,56},{32,64},{40,72},{48,80},{56,88},{64,... | collective-permute-start | bytes 1671176 | tf_op jit(solution)/shard_map/ppermute | solution.py:405
  288.7 12.2 %all-to-all-start.1 = ((f32[16,1,7]{2,1,0:T(1,128)}), f32[16,1,7]{2,1,0:T(1,128)S(1)}, u32[]{:S(2)}, u32[]{:S(2)}) async-start(f32[16,1,7]{2,1,0:T(1,128)} %copy.31), calls=%async_computation.1 | async-start | bytes 16384 | tf_op jit(solution)/shard_map/all_to_all | solution.py:654
  302.3 17.9 %collective-permute-start.42 = (f32[512]{0:T(512)S(1)}, f32[512]{0:T(512)S(1)}, u32[]{:S(2)}, u32[]{:S(2)}) collective-permute-start(f32[512]{0:T(512)S(1)} %bitcast.177), channel_id=1, source_target_pairs={{8,0},{16,8},{24,16},{32,24},{40,32},{48,40},{56,48},{64,56},{72,6... | collective-permute-start | bytes 6152 | tf_op jit(solution)/shard_map/ppermute | solution.py:525
  304.5 15.7 %collective-permute-start.43 = (f32[512]{0:T(512)S(1)}, f32[512]{0:T(512)S(1)}, u32[]{:S(2)}, u32[]{:S(2)}) collective-permute-start(f32[512]{0:T(512)S(1)} %bitcast.176), channel_id=1, source_target_pairs={{0,8},{8,16},{16,24},{24,32},{32,40},{40,48},{48,56},{56,64},{64,7... | collective-permute-start | bytes 6152 | tf_op jit(solution)/shard_map/ppermute | solution.py:525
  309.8 10.5 %collective-permute-start.44 = (f32[512]{0:T(512)S(1)}, f32[512]{0:T(512)S(1)}, u32[]{:S(2)}, u32[]{:S(2)}) collective-permute-start(f32[512]{0:T(512)S(1)} %bitcast.175), channel_id=1, source_target_pairs={{1,0},{2,1},{3,2},{4,3},{5,4},{6,5},{7,6},{9,8},{10,9},{11,10},{12... | collective-permute-start | bytes 6152 | tf_op jit(solution)/shard_map/ppermute | solution.py:525
  (31 other events, 409.3 us)
